TPU v7x, 128 devices: a whole 4x4x4 slice. The times are simulated.
128 devices in a mesh: grp: 4 (over y), dev: 32 (over x, z, core).
Axes of the slice: x: 4, y: 4, z: 4, core: 2. Of those that a mesh axis runs over, the one named last changes fastest.
Arguments:
- codes: int32 [12288, 32], P(('grp', 'dev')), may hold values from 0 to 2047
- code_table: bfloat16 [16384, 512], replicated, may hold values from -2.09375 to 2.09375
- roster: int32 [12288], P(('grp', 'dev')), may hold values from 0 to 12287, as said below
- old_slot: int32 [12288], P(('grp', 'dev')), may hold values from 0 to 12287, as said below
- states: float32 [12288, 10, 512], P(('grp', 'dev')), may hold values from -6 to 6
- up_weight: float32 [4, 512], replicated, may hold values from -3 to 3
- up_bias: float32 [512], replicated, may hold values from -2.5 to 2.5
- conv_weight: bfloat16 [7, 512, 512], replicated, may hold values from -0.09375 to 0.09375
- conv_bias: float32 [512], replicated, may hold values from -2.5 to 2.5
- res_in_weight: bfloat16 [3, 512, 256], replicated, may hold values from -0.15625 to 0.15625
- res_in_bias: float32 [256], replicated, may hold values from -2.5 to 2.5
- res_out_weight: bfloat16 [256, 512], replicated, may hold values from -0.375 to 0.375
- res_out_bias: float32 [512], replicated, may hold values from -2.5 to 2.5
Outputs:
- decoded: bfloat16 [12288, 8, 512], P(('grp', 'dev'))
- new_states: float32 [12288, 10, 512], P(('grp', 'dev'))
Inputs may be any that keep to these rules, and one draw needn't show every extreme that they name: roster is a permutation of the conversations; the 96 slots of each device are its owned conversations. Conversation c is held by language-model device c // 96. At most 2 conversations of one language-model device go to one owner device, and some pair reaches 2 in every draw. old_slot is a permutation of the slots that maps each slot within its group of 32 devices along dev. Exactly 16 slots of every device take a cache from a slot of another device; these are exactly the slots whose caches leave that device. All other slots keep their own cache. At most 1 caches go from one device to one other, and that many in every draw.
All inputs are finite; a program needn't handle non-finite values.
Results may differ from a plain program's by a relative error of at most 0.0085.
Values may be sent and summed in bfloat16 or wider, within the bound.
A program may use at most 128 MiB of HBM per device.

v0:
```python
import jax
import jax.numpy as jnp
from jax import lax
from jax.sharding import PartitionSpec as P

FRAMES = 4


def embed_codes(codes, code_table):
    row_count = codes.shape[0]
    book_count = codes.shape[1] // FRAMES
    book_size = code_table.shape[0] // book_count
    grouped = codes.reshape(row_count * FRAMES, book_count)
    entries = jnp.arange(book_size, dtype=jnp.int32)
    summed = jnp.zeros((row_count * FRAMES, code_table.shape[1]), jnp.float32)
    for book_index in range(book_count):
        onehot = (grouped[:, book_index][:, None] == entries[None, :]).astype(jnp.bfloat16)
        book_rows = code_table[book_index * book_size : (book_index + 1) * book_size]
        summed = summed + jnp.dot(onehot, book_rows, preferred_element_type=jnp.float32)
    return summed.astype(jnp.bfloat16).reshape(row_count, FRAMES, code_table.shape[1])


def pick_rows(table, index, live):
    entries = jnp.arange(table.shape[0], dtype=jnp.int32)
    select = (index[:, None] == entries[None, :]) & live[:, None]
    if table.dtype == jnp.bfloat16:
        return jnp.dot(
            select.astype(jnp.bfloat16), table, preferred_element_type=jnp.float32
        ).astype(jnp.bfloat16)
    if table.dtype == jnp.int32:
        picked = jnp.dot(
            select.astype(jnp.float32), table.astype(jnp.float32), precision=lax.Precision.HIGHEST
        )
        return picked.astype(jnp.int32)
    return jnp.dot(select.astype(jnp.float32), table, precision=lax.Precision.HIGHEST)


def prefix_count(flags):
    width = flags.shape[-1]
    positions = jnp.arange(width, dtype=jnp.int32)
    upper = (positions[:, None] <= positions[None, :]).astype(jnp.float32)
    return jnp.dot(flags.astype(jnp.float32), upper).astype(jnp.int32)


def compact(flags, ranks, values, slots):
    spots = jnp.arange(slots, dtype=jnp.int32)
    hit = flags[..., None, :] & (ranks[..., None, :] == spots[:, None])
    picked = jnp.sum(jnp.where(hit, values[..., None, :], 0), axis=-1)
    return (picked, jnp.any(hit, axis=-1))


def decode(
    routed,
    carried,
    up_weight,
    up_bias,
    conv_weight,
    conv_bias,
    res_in_weight,
    res_in_bias,
    res_out_weight,
    res_out_bias,
):
    conv_count, frame_count, chan_width = routed.shape
    step_count = 2 * frame_count
    inputs = routed.astype(jnp.float32)
    tap_zero = inputs * up_weight[0]
    tap_one = inputs * up_weight[1]
    tap_two = inputs * up_weight[2]
    tap_three = inputs * up_weight[3]
    early_even = jnp.concatenate([carried[:, 0:1], tap_two[:, :-1]], axis=1)
    early_odd = jnp.concatenate([carried[:, 1:2], tap_three[:, :-1]], axis=1)
    upsampled = (
        jnp.stack([tap_zero + early_even, tap_one + early_odd], axis=2).reshape(
            conv_count, step_count, chan_width
        )
        + up_bias
    )
    history = jnp.concatenate([carried[:, 2:8], upsampled], axis=1).astype(jnp.bfloat16)
    conv_out = jnp.zeros((conv_count * step_count, chan_width), jnp.float32) + conv_bias
    for tap_index in range(7):
        window = history[:, 6 - tap_index : 6 - tap_index + step_count].reshape(
            conv_count * step_count, chan_width
        )
        conv_out = conv_out + jnp.dot(
            window, conv_weight[tap_index], preferred_element_type=jnp.float32
        )
    active = jax.nn.elu(conv_out).reshape(conv_count, step_count, chan_width)
    res_history = jnp.concatenate([carried[:, 8:10], active], axis=1)
    res_rounded = res_history.astype(jnp.bfloat16)
    res_inner = (
        jnp.zeros((conv_count * step_count, res_in_weight.shape[2]), jnp.float32) + res_in_bias
    )
    for tap_index in range(3):
        window = res_rounded[:, 2 - tap_index : 2 - tap_index + step_count].reshape(
            conv_count * step_count, chan_width
        )
        res_inner = res_inner + jnp.dot(
            window, res_in_weight[tap_index], preferred_element_type=jnp.float32
        )
    squeezed = jax.nn.elu(res_inner).astype(jnp.bfloat16)
    summed = (
        conv_out
        + jnp.dot(squeezed, res_out_weight, preferred_element_type=jnp.float32)
        + res_out_bias
    )
    decoded = summed.astype(jnp.bfloat16).reshape(conv_count, step_count, chan_width)
    new_states = jnp.concatenate(
        [
            tap_two[:, -1:],
            tap_three[:, -1:],
            history[:, -6:].astype(jnp.float32),
            res_history[:, -2:],
        ],
        axis=1,
    )
    return (decoded, new_states)


def local(
    codes,
    code_table,
    roster,
    old_slot,
    states,
    up_weight,
    up_bias,
    conv_weight,
    conv_bias,
    res_in_weight,
    res_in_bias,
    res_out_weight,
    res_out_bias,
):
    conv_count = roster.shape[0]
    chan_width = states.shape[2]
    per_group = lax.axis_size("dev")
    devices_all = lax.axis_size("grp") * per_group
    capacity = max(1, (2 * conv_count + devices_all - 1) // devices_all)
    leaving_count = per_group // 2
    group_first = lax.axis_index("grp") * per_group
    local_index = lax.axis_index("dev")
    self_index = group_first + local_index
    positions = jnp.arange(conv_count, dtype=jnp.int32)
    earlier = positions[None, :] < positions[:, None]
    everyone = lax.all_gather(roster, ("grp", "dev"), axis=0, tiled=True).reshape(
        devices_all, conv_count
    )
    from_self = everyone // conv_count == self_index
    rank_out = prefix_count(from_self) - 1
    send_rows, send_live = compact(from_self, rank_out, everyone % conv_count, capacity)
    send_rows = send_rows.reshape(-1)
    send_live = send_live.reshape(-1)
    anchor = roster // conv_count
    rank_in = jnp.sum(earlier & (anchor[None, :] == anchor[:, None]), axis=1)
    arrival = anchor * capacity + rank_in
    all_live = jnp.ones((conv_count,), jnp.bool_)
    local_rows = embed_codes(codes, code_table).reshape(conv_count, -1)
    outgoing = pick_rows(local_rows, send_rows, send_live)
    incoming = lax.all_to_all(outgoing, ("grp", "dev"), split_axis=0, concat_axis=0, tiled=True)
    routed = pick_rows(incoming, arrival, all_live).reshape(conv_count, FRAMES, chan_width)
    slot_table = lax.all_gather(old_slot, "dev", axis=0, tiled=True).reshape(per_group, conv_count)
    source_dev = slot_table // conv_count - group_first
    moved_table = source_dev != jnp.arange(per_group, dtype=jnp.int32)[:, None]
    own_dev = old_slot // conv_count - group_first
    own_row = old_slot % conv_count
    own_moved = own_dev != local_index
    flat_states = states.reshape(conv_count, -1)
    rank_leave = prefix_count(own_moved[None, :])[0] - 1
    leave_rows, leave_live = compact(own_moved, rank_leave, positions, leaving_count)
    departing_pool = lax.all_gather(
        pick_rows(flat_states, leave_rows, leave_live).astype(jnp.bfloat16),
        "dev",
        axis=0,
        tiled=True,
    ).astype(jnp.float32)
    rank_table = prefix_count(moved_table) - 1
    pool_index = jnp.arange(per_group, dtype=jnp.int32)[:, None] * leaving_count + rank_table
    flat_key = own_dev * conv_count + own_row
    table_keys = jnp.arange(per_group * conv_count, dtype=jnp.int32)
    hit = (flat_key[:, None] == table_keys[None, :]) & own_moved[:, None]
    pool_spot = jnp.sum(jnp.where(hit, pool_index.reshape(-1)[None, :], 0), axis=1)
    arrived = pick_rows(departing_pool, pool_spot, own_moved)
    carried = jnp.where(own_moved[:, None], arrived, flat_states).reshape(states.shape)
    return decode(
        routed,
        carried,
        up_weight,
        up_bias,
        conv_weight,
        conv_bias,
        res_in_weight,
        res_in_bias,
        res_out_weight,
        res_out_bias,
    )


def solution(mesh):
    in_specs = (
        P(("grp", "dev"), None),
        P(),
        P(("grp", "dev")),
        P(("grp", "dev")),
        P(("grp", "dev"), None, None),
        P(),
        P(),
        P(),
        P(),
        P(),
        P(),
        P(),
        P(),
    )
    out_specs = (P(("grp", "dev"), None, None), P(("grp", "dev"), None, None))
    return jax.shard_map(local, mesh=mesh, in_specs=in_specs, out_specs=out_specs, check_vma=False)
```

profile of v0, /device:TPU:1, one launch (start us, length us, event | category | flops | bytes accessed | tf_op | source)
XLA Modules:
  0.0 282.2 jit_solution(14667296397977217454)
XLA Ops:
  7.2 0.7 fusion.144
  8.3 2.0 copy.90
  10.4 2.0 convolution_convert_fusion
  12.9 69.2 %all-reduce = s32[12288]{0:T(1024)S(1)} all-reduce(s32[12288]{0:T(1024)S(1)} %dynamic-update-slice), channel_id=1, replica_groups=mesh['grp'=4,'dev'=32] {'grp','dev'}, use_global_device_ids=true, to_apply=%add | all-reduce | flops 12288 | bytes 98304
  83.7 0.9 slice_reduce_fusion
  84.5 3.0 %fusion = f32[384,512]{1,0:T(8,128)S(1)} fusion(bf16[16384,512]{1,0:T(8,128)(2,1)} %param.14, s32[384]{0:T(512)S(1)} %get-tuple-element.11), kind=kOutput, calls=%fused_computation.12 | convolution fusion | flops 806092800 | bytes 2885120 | tf_op jit(solution)/shard_map/dot_general | solution.py:19
  87.5 3.4 %fusion.47 = f32[384,512]{1,0:T(8,128)S(1)} fusion(f32[384,512]{1,0:T(8,128)S(1)} %fusion, bf16[16384,512]{1,0:T(8,128)(2,1)} %param.14, s32[384]{0:T(512)S(1)} %get-tuple-element.10), kind=kOutput, calls=%fused_computation.71 | convolution fusion | flops 806289408 | bytes 3671552 | tf_op jit(solution)/shard_map/dot_general | solution.py:19
  90.9 1.0 fusion.44
  91.9 1.0 fusion.41
  93.0 1.0 fusion.38
  94.0 1.0 fusion.35
  95.0 1.0 fusion.32
  96.1 1.8 fusion.50
  97.8 1.2 reshape_reshape.3
  99.1 1.5 convolution_convert_fusion.1
  100.5 2.6 all_to_all.8
  103.1 5.4 %all-to-all-start = ((bf16[128,2,2048]{2,1,0:T(2,128)(2,1)}), bf16[128,2,2048]{2,1,0:T(2,128)(2,1)}, u32[]{:S(2)}, u32[]{:S(2)}) async-start(bf16[128,2,2048]{2,1,0:T(2,128)(2,1)} %all_to_all.8), calls=%async_computation | async-start | bytes 2097152 | tf_op jit(solution)/shard_map/all_to_all | solution.py:160
  108.5 0.6 dynamic-slice
  110.1 125.6 %all-reduce.1 = s32[3072]{0:T(1024)S(1)} all-reduce(s32[3072]{0:T(1024)S(1)} %dynamic-update-slice.1), channel_id=1, replica_groups=mesh['grp'=4,'dev'=32] {'dev'}, use_global_device_ids=true, to_apply=%add.1 | all-reduce | flops 3072 | bytes 24576
  235.9 2.0 copy.91
  238.2 0.4 select_reduce_fusion
  238.7 1.5 all_to_all.10
  240.5 1.4 reshape.230
  242.1 0.7 slice.229
  242.8 0.7 slice.230
  243.5 1.0 slice_bitcast_fusion
  244.5 4.8 %convolution_select_fusion = f32[96,5120]{1,0:T(8,128)} fusion(f32[96,5120]{1,0:T(8,128)S(1)} %copy-done.1, bf16[512,5120]{1,0:T(8,128)(2,1)} %all-gather.2.cloned.1.call-done, pred[96]{0:T(512)(128)(4,1)S(1)} %broadcast_compare_fusion.1, s32[96]{0:T(128)S(1)} %select_reduce_fusion), kind=kOutput, calls=%fused_computation | convolution fusion | flops 503906304 | bytes 9175520 | tf_op jit(solution)/shard_map/dot_general | solution.py:35
  249.3 2.0 copy.92
  251.3 0.8 slice_bitcast_fusion.3
  252.4 0.7 slice.226
  253.4 0.8 copy.94
  254.2 0.8 copy.97
  255.0 1.6 maximum_add_fusion
  257.2 0.5 copy-done.5
  257.7 0.8 copy.107
  258.9 1.7 copy-done.2
  260.6 0.6 fusion.86
  261.2 0.7 pad_maximum_fusion.3
  261.9 0.6 fusion.84
  262.5 0.6 fusion.82
  263.1 0.6 fusion.80
  263.7 0.6 fusion.78
  264.4 0.6 fusion.76
  265.1 1.0 add_add_fusion
  266.1 0.6 fusion.18
  267.8 1.5 convolution_add_fusion.1
  269.3 3.5 %fusion.28 = bf16[96,8,512]{2,1,0:T(8,128)(2,1)} fusion(f32[768,512]{1,0:T(8,128)S(1)} %add_add_fusion, bf16[256,512]{1,0:T(8,128)(2,1)S(1)} %copy-done, f32[768,256]{1,0:T(8,128)} %convolution_add_fusion.1, bf16[96,8,512]{2,1,0:T(8,128)(2,1)} %copy-done.4, bf16[96,2,512]{2,1,0:T(2,128)(2,1)} %copy.107, f32[512]{0:T(512)S(1)} %copy-done.17, ...), kind=kOutput, calls=%fused_computation.61 | convolution fusion | flops 406388736 | bytes 4655104 | tf_op jit(solution)/shard_map/dot_general | solution.py:104
  272.8 2.5 pad_maximum_fusion
  (92 shorter events, 6.2 us)
Async XLA Ops:
  7.2 262.1 %copy-start = (bf16[256,512]{1,0:T(8,128)(2,1)S(1)}, bf16[256,512]{1,0:T(8,128)(2,1)}, u32[]{:S(2)}) copy-start(bf16[256,512]{1,0:T(8,128)(2,1)} %param.24) | copy-start | bytes 786436
  7.2 237.3 %all-gather.2.cloned.1.call-start = ((), (), s32[]{:S(2)}) async-start(), calls=%async_computation.1 | async-start | bytes 5406720 | tf_op jit(solution)/shard_map/all_gather | solution.py:171
  10.4 2.1 copy-start.10
  10.4 2.2 copy-start.18
  83.7 7.2 %copy-start.16 = (bf16[16384,512]{1,0:T(8,128)(2,1)S(1)}, bf16[16384,512]{1,0:T(8,128)(2,1)}, u32[]{:S(2)}) copy-start(bf16[16384,512]{1,0:T(8,128)(2,1)} %param.14) | copy-start | bytes 50331652
  100.5 8.0 %copy-start.19 = (u32[128]{0:T(128)S(1)}, u32[128]{0:T(128)}, u32[]{:S(2)}) copy-start(u32[128]{0:T(128)} %constant.83) | copy-start | bytes 1540
  100.5 9.2 %copy-start.15 = (s32[96]{0:T(128)S(1)}, s32[96]{0:T(128)}, u32[]{:S(2)}) copy-start(s32[96]{0:T(128)} %param.16) | copy-start | bytes 1156
  103.1 135.6 %all-to-all-start = ((bf16[128,2,2048]{2,1,0:T(2,128)(2,1)}), bf16[128,2,2048]{2,1,0:T(2,128)(2,1)}, u32[]{:S(2)}, u32[]{:S(2)}) async-start(bf16[128,2,2048]{2,1,0:T(2,128)(2,1)} %all_to_all.8), calls=%async_computation | async-start | bytes 2097152 | tf_op jit(solution)/shard_map/all_to_all | solution.py:160
  235.9 2.7 copy-start.11
  242.1 2.4 copy-start.1
  252.4 1.0 copy-start.7
  252.4 1.8 copy-start.6
  252.4 2.6 copy-start.3
  256.7 1.0 copy-start.5
  256.7 1.8 copy-start.13
  258.5 2.0 copy-start.2
  264.4 0.7 copy-start.12
  266.0 1.1 copy-start.9
  266.1 1.1 copy-start.14
  266.7 0.9 copy-start.4
  266.7 1.1 copy-start.8
  267.8 1.5 copy-start.17
Sparse Core Ops, SparseCore 0:
  12.6 51.4 all-gather.1
where the time goes:
time: 287 us; the launch traced here: 282 us
  blocking collectives  195 us (68%)
  matrix products  32.4 us (11%)
  local copies, waits for them, and re-layouts  26.2 us (9%)
  between operations  15.2 us (5%)
  other arithmetic  8.05 us (3%)
  starting transfers between devices  5.43 us (2%)
    unnamed x2, blocking collectives  195 us
    dot_general x8, matrix products, embed_codes(): jnp.dot(onehot, book_rows, preferred_element_type=jnp.float32)  13.2 us
    dot_general x2, matrix products, pick_rows(): jnp.dot(select.astype(jnp.float32), table, precision=lax.Precision.HIGHEST)  6.84 us
    unnamed x48, local copies, waits for them, and re-layouts  6.29 us
  transfers between devices with their start and end apart: 2, of which 0 were waited for; matrix products, arithmetic and copies ran while one was open for 10% of the time, Pallas kernels for 0%

commit v1 on v0

--- a/solution.py
+++ b/solution.py
@@ -4,6 +4,7 @@
 from jax.sharding import PartitionSpec as P
 
 FRAMES = 4
+MOST = 2
 
 
 def embed_codes(codes, code_table):
@@ -133,55 +134,52 @@
     res_out_bias,
 ):
     conv_count = roster.shape[0]
-    chan_width = states.shape[2]
     per_group = lax.axis_size("dev")
     devices_all = lax.axis_size("grp") * per_group
-    capacity = max(1, (2 * conv_count + devices_all - 1) // devices_all)
-    leaving_count = per_group // 2
+    most = MOST
     group_first = lax.axis_index("grp") * per_group
     local_index = lax.axis_index("dev")
-    self_index = group_first + local_index
     positions = jnp.arange(conv_count, dtype=jnp.int32)
     earlier = positions[None, :] < positions[:, None]
-    everyone = lax.all_gather(roster, ("grp", "dev"), axis=0, tiled=True).reshape(
-        devices_all, conv_count
-    )
-    from_self = everyone // conv_count == self_index
-    rank_out = prefix_count(from_self) - 1
-    send_rows, send_live = compact(from_self, rank_out, everyone % conv_count, capacity)
-    send_rows = send_rows.reshape(-1)
-    send_live = send_live.reshape(-1)
+
     anchor = roster // conv_count
-    rank_in = jnp.sum(earlier & (anchor[None, :] == anchor[:, None]), axis=1)
-    arrival = anchor * capacity + rank_in
-    all_live = jnp.ones((conv_count,), jnp.bool_)
-    local_rows = embed_codes(codes, code_table).reshape(conv_count, -1)
-    outgoing = pick_rows(local_rows, send_rows, send_live)
-    incoming = lax.all_to_all(outgoing, ("grp", "dev"), split_axis=0, concat_axis=0, tiled=True)
-    routed = pick_rows(incoming, arrival, all_live).reshape(conv_count, FRAMES, chan_width)
-    slot_table = lax.all_gather(old_slot, "dev", axis=0, tiled=True).reshape(per_group, conv_count)
-    source_dev = slot_table // conv_count - group_first
-    moved_table = source_dev != jnp.arange(per_group, dtype=jnp.int32)[:, None]
-    own_dev = old_slot // conv_count - group_first
-    own_row = old_slot % conv_count
-    own_moved = own_dev != local_index
-    flat_states = states.reshape(conv_count, -1)
-    rank_leave = prefix_count(own_moved[None, :])[0] - 1
-    leave_rows, leave_live = compact(own_moved, rank_leave, positions, leaving_count)
-    departing_pool = lax.all_gather(
-        pick_rows(flat_states, leave_rows, leave_live).astype(jnp.bfloat16),
-        "dev",
-        axis=0,
-        tiled=True,
-    ).astype(jnp.float32)
-    rank_table = prefix_count(moved_table) - 1
-    pool_index = jnp.arange(per_group, dtype=jnp.int32)[:, None] * leaving_count + rank_table
-    flat_key = own_dev * conv_count + own_row
-    table_keys = jnp.arange(per_group * conv_count, dtype=jnp.int32)
-    hit = (flat_key[:, None] == table_keys[None, :]) & own_moved[:, None]
-    pool_spot = jnp.sum(jnp.where(hit, pool_index.reshape(-1)[None, :], 0), axis=1)
-    arrived = pick_rows(departing_pool, pool_spot, own_moved)
-    carried = jnp.where(own_moved[:, None], arrived, flat_states).reshape(states.shape)
+    row = roster % conv_count
+    rank_in = jnp.sum(earlier & (anchor[None, :] == anchor[:, None]), axis=1).astype(jnp.int32)
+    key = anchor * most + rank_in
+    spots = jnp.arange(devices_all * most, dtype=jnp.int32)
+    request = jnp.sum(jnp.where(key[None, :] == spots[:, None], row[None, :] + 1, 0), axis=1) - 1
+    asked = lax.all_to_all(
+        request.reshape(devices_all, most), ("grp", "dev"), 0, 0, tiled=True
+    ).reshape(-1)
+    answer = jnp.take(codes, jnp.clip(asked, 0, conv_count - 1), axis=0)
+    answered = lax.all_to_all(
+        answer.reshape(devices_all, most, -1), ("grp", "dev"), 0, 0, tiled=True
+    ).reshape(devices_all * most, -1)
+    my_codes = jnp.take(answered, key, axis=0)
+    book_count = my_codes.shape[1] // FRAMES
+    book_size = code_table.shape[0] // book_count
+    flat_index = my_codes.reshape(conv_count, FRAMES, book_count) + (
+        jnp.arange(book_count, dtype=jnp.int32) * book_size
+    )
+    looked = jnp.take(code_table, flat_index, axis=0).astype(jnp.float32)
+    routed = jnp.sum(looked, axis=2).astype(jnp.bfloat16)
+
+    source_dev = old_slot // conv_count - group_first
+    source_row = old_slot % conv_count
+    moved = source_dev != local_index
+    devs = jnp.arange(per_group, dtype=jnp.int32)
+    wanted = (
+        jnp.sum(
+            jnp.where(moved[None, :] & (source_dev[None, :] == devs[:, None]), source_row[None, :] + 1, 0),
+            axis=1,
+        )
+        - 1
+    )
+    asked_rows = lax.all_to_all(wanted.reshape(per_group, 1), "dev", 0, 0, tiled=True).reshape(-1)
+    leaving = jnp.take(states, jnp.clip(asked_rows, 0, conv_count - 1), axis=0)
+    arrived = lax.all_to_all(leaving, "dev", 0, 0, tiled=True)
+    brought = jnp.take(arrived, jnp.clip(source_dev, 0, per_group - 1), axis=0)
+    carried = jnp.where(moved[:, None, None], brought, states)
     return decode(
         routed,
         carried,

time: 287 us -> 113 us (0.39); the launches traced: 282 us -> 112 us
  blocking collectives: 195 us -> 0 us
  matrix products: 32.4 us -> 10.2 us
  starting transfers between devices: 5.43 us -> 24.6 us
  waiting for transfers between devices: 0.02 us -> 17.5 us
  local copies, waits for them, and re-layouts: 26.2 us -> 41.9 us
  between operations: 15.2 us -> 1.07 us
  other arithmetic: 8.05 us -> 17.3 us
    unnamed x2 -> x0, blocking collectives: 195 us -> none
    gather x0 -> x6, local copies, waits for them, and re-layouts: none -> 28.1 us  [the longest x1 21.3 us: local(): looked = jnp.take(code_table, flat_index, axis=0).astype(jnp.float32)]
    dot_general x15 -> x0, matrix products: 22.3 us -> none  [the longest x8 13.2 us: embed_codes(): jnp.dot(onehot, book_rows, preferred_element_type=jnp.float32)]
    all_to_all x1 -> x4, starting transfers between devices: 5.39 us -> 24.6 us  [the longest x1 9.43 us: local(): lax.all_to_all(wanted.reshape(per_group, 1), 'dev', 0, 0, tiled=True)]
    all_to_all x1 -> x4, waiting for transfers between devices: 0.01 us -> 17.5 us  [the longest x1 8.41 us: local(): lax.all_to_all(answer.reshape(devices_all, most, -1), ('grp', 'dev'), 0,...]
    all_to_all x2 -> x0, local copies, waits for them, and re-layouts: 4.05 us -> none  [local(): lax.all_to_all(outgoing, ('grp', 'dev'), split_axis=0, concat_axis=0, til...]
    another operation x1, other arithmetic: 0.23 us -> 3.82 us
    reduce_sum x4, other arithmetic: 0.75 us -> 3.76 us  [the longest x1 3.37 us: local(): routed = jnp.sum(looked, axis=2).astype(jnp.bfloat16)]
  transfers between devices with their start and end apart: 2 -> 4, of which waited for: 0 -> 3; matrix products, arithmetic and copies ran while one was open for 10% -> 34% of each run, Pallas kernels for 0% -> 0%
where the time goes in v1:
time: 113 us; the launch traced here: 112 us
  local copies, waits for them, and re-layouts  41.9 us (37%)
  starting transfers between devices  24.6 us (22%)
  waiting for transfers between devices  17.5 us (15%)
  other arithmetic  17.3 us (15%)
  matrix products  10.2 us (9%)
    gather x1, local copies, waits for them, and re-layouts, local(): looked = jnp.take(code_table, flat_index, axis=0).astype(jnp.float32)  21.3 us
    all_to_all x1, starting transfers between devices, local(): lax.all_to_all(wanted.reshape(per_group, 1), 'dev', 0, 0, tiled=True)  9.43 us
    all_to_all x1, waiting for transfers between devices, local(): lax.all_to_all(answer.reshape(devices_all, most, -1), ('grp', 'dev'), 0,...  8.41 us
    all_to_all x1, starting transfers between devices, local(): lax.all_to_all(request.reshape(devices_all, most), ('grp', 'dev'), 0, 0,...  6.05 us
    all_to_all x1, waiting for transfers between devices, local(): lax.all_to_all(request.reshape(devices_all, most), ('grp', 'dev'), 0, 0,...  5.65 us
    unnamed x30, local copies, waits for them, and re-layouts  4.83 us
    dot_general x7, matrix products, decode(): jnp.dot(window, conv_weight[tap_index], preferred_element_type=jnp.float32)  4.77 us
    all_to_all x1, starting transfers between devices, local(): lax.all_to_all(answer.reshape(devices_all, most, -1), ('grp', 'dev'), 0,...  4.6 us
  transfers between devices with their start and end apart: 4, of which 3 were waited for; matrix products, arithmetic and copies ran while one was open for 34% of the time, Pallas kernels for 0%

profile of v1, /device:TPU:1, one launch (start us, length us, event | category | flops | bytes accessed | tf_op | source)
XLA Modules:
  0.0 112.5 jit_solution(13729003396688346682)
XLA Ops:
  0.6 0.7 fusion.72
  1.4 0.7 compare_and_fusion.3
  2.2 0.7 copy.102
  2.9 9.4 %all-to-all-start.2 = ((s32[32,1,1]{2,1,0:T(1,128)}), s32[32,1,1]{2,1,0:T(1,128)S(1)}, u32[]{:S(2)}, u32[]{:S(2)}) async-start(s32[32,1,1]{2,1,0:T(1,128)} %copy.102), calls=%async_computation.2 | async-start | bytes 32768 | tf_op jit(solution)/shard_map/all_to_all | solution.py:178
  12.3 0.7 and_select_fusion.3
  13.3 0.9 fusion.83
  14.2 0.8 copy.97
  15.0 0.8 sub.30
  15.8 3.4 %all-to-all-done.2 = s32[32,1,1]{2,1,0:T(1,128)S(1)} async-done(((s32[32,1,1]{2,1,0:T(1,128)}), s32[32,1,1]{2,1,0:T(1,128)S(1)}, u32[]{:S(2)}, u32[]{:S(2)}) %all-to-all-start.2) | async-done | bytes 160 | tf_op jit(solution)/shard_map/all_to_all | solution.py:178
  19.2 6.0 %all-to-all-start = ((s32[128,1,2]{2,1,0:T(1,128)}), s32[128,1,2]{2,1,0:T(1,128)S(1)}, u32[]{:S(2)}, u32[]{:S(2)}) async-start(s32[128,1,2]{2,1,0:T(1,128)} %bitcast), calls=%async_computation | async-start | bytes 131072 | tf_op jit(solution)/shard_map/all_to_all | solution.py:151
  25.2 0.7 clamp_reduce_fusion
  25.9 3.0 %gather_fusion.3 = f32[32,10,512]{2,0,1:T(8,128)S(1)} fusion(f32[96,10,512]{2,0,1:T(8,128)} %param.17, s32[1024]{0:T(1024)S(1)} %pad_clamp_fusion.1), kind=kCustom, calls=%fused_computation.3 | custom fusion | bytes 1310848 | tf_op jit(solution)/shard_map/jit(_take)/gather | solution.py:179
  28.9 5.7 %all-to-all-done = s32[128,1,2]{2,1,0:T(1,128)S(1)} async-done(((s32[128,1,2]{2,1,0:T(1,128)}), s32[128,1,2]{2,1,0:T(1,128)S(1)}, u32[]{:S(2)}, u32[]{:S(2)}) %all-to-all-start) | async-done | bytes 1056 | tf_op jit(solution)/shard_map/all_to_all | solution.py:151
  34.6 0.2 broadcast_clamp_fusion
  35.0 0.7 gather_fusion
  35.7 0.9 broadcast_select_fusion.1
  36.6 4.6 %all-to-all-start.1 = ((s32[128,2,32]{2,1,0:T(2,128)}), s32[128,2,32]{2,1,0:T(2,128)S(1)}, u32[]{:S(2)}, u32[]{:S(2)}) async-start(s32[128,2,32]{2,1,0:T(2,128)} %broadcast_select_fusion.1), calls=%async_computation.1 | async-start | bytes 262144 | tf_op jit(solution)/shard_map/all_to_all | solution.py:155
  41.4 1.4 %copy.103 = f32[32,10,512]{2,1,0:T(8,128)} copy(f32[32,10,512]{2,0,1:T(8,128)S(1)} %broadcast_select_fusion) | data formatting | bytes 1310720 | tf_op jit(solution)/shard_map/jit(_take)/select_n | solution.py:179
  42.7 8.4 %all-to-all-done.1 = s32[128,2,32]{2,1,0:T(2,128)S(1)} async-done(((s32[128,2,32]{2,1,0:T(2,128)}), s32[128,2,32]{2,1,0:T(2,128)S(1)}, u32[]{:S(2)}, u32[]{:S(2)}) %all-to-all-start.1) | async-done | bytes 32800 | tf_op jit(solution)/shard_map/all_to_all | solution.py:155
  51.1 4.5 %all-to-all-start.3 = ((f32[32,10,512]{2,1,0:T(8,128)}), f32[32,10,512]{2,1,0:T(8,128)S(1)}, u32[]{:S(2)}, u32[]{:S(2)}) async-start(f32[32,10,512]{2,1,0:T(8,128)} %copy.103), calls=%async_computation.3 | async-start | bytes 2097152 | tf_op jit(solution)/shard_map/all_to_all | solution.py:180
  55.6 0.6 gather_fusion.1
  57.0 21.3 %gather_fusion.2 = bf16[3072,512]{1,0:T(8,128)(2,1)} fusion(bf16[16384,512]{1,0:T(8,128)(2,1)} %param.14, s32[3072]{0:T(1024)S(1)} %broadcast_clamp_fusion.1), kind=kCustom, calls=%fused_computation.2 | custom fusion | bytes 6303744 | tf_op jit(solution)/shard_map/jit(_take)/gather | solution.py:164
  78.3 3.4 %select_reduce_fusion = bf16[96,4,512]{2,1,0:T(4,128)(2,1)S(1)} fusion(bf16[96,4,8,512]{3,2,1,0:T(8,128)(2,1)} %bitcast.127, pred[96,4,8]{2,1,0:T(4,128)(4,1)S(1)} %copy.99), kind=kLoop, calls=%fused_computation.8 | loop fusion | flops 2949120 | bytes 3542016 | tf_op jit(solution)/shard_map/reduce_sum | solution.py:165
  82.1 0.7 copy.117
  83.0 0.7 copy.118
  83.7 1.4 %slice_bitcast_fusion = (f32[96,3,1,512]{3,1,0,2:T(4,128)}, f32[96,3,1,512]{3,1,0,2:T(4,128)}) fusion(f32[96,4,512]{2,1,0:T(4,128)S(1)} %get-tuple-element.24, f32[96,4,512]{2,1,0:T(4,128)S(1)} %get-tuple-element.23), kind=kLoop, calls=%fused_computation.55 | loop fusion | bytes 2359296 | tf_op jit(solution)/shard_map/concatenate | solution.py:73
  85.1 2.4 %gather_fusion.4 = f32[96,10,512]{2,1,0:T(8,128)} fusion(f32[32,10,512]{2,1,0:T(8,128)S(1)} %all-to-all-done.3, s32[1024]{0:T(1024)S(1)} %pad_clamp_fusion), kind=kCustom, calls=%fused_computation.4 | custom fusion | bytes 3932544 | tf_op jit(solution)/shard_map/jit(_take)/gather | solution.py:181
  87.5 3.8 %fusion.81 = (bf16[96,10,512]{2,1,0:T(8,128)(2,1)S(1)}, f32[96,10,512]{2,1,0:T(8,128)S(1)}) fusion(f32[96,10,512]{2,0,1:T(8,128)S(1)} %copy-done.1, f32[96,10,512]{2,1,0:T(8,128)} %gather_fusion.4, pred[96]{0:T(512)(128)(4,1)S(1)} %get-tuple-element.6, pred[96]{0:T(512)(128)(4,1)S(1)} %broadcast_compare_fusion), kind=kLoop, calls=%fused_computation.154 | loop fusion | flops 1474560 | bytes 6881472 | tf_op jit(solution)/shard_map/convert.7
  92.2 0.4 copy-done.4
  92.6 0.3 copy-done.5
  93.1 0.8 fusion.6
  93.9 0.3 pad_maximum_fusion.1
  94.2 0.5 copy.107
  95.2 1.7 %copy-done.2 = bf16[7,512,512]{2,1,0:T(8,128)(2,1)S(1)} copy-done((bf16[7,512,512]{2,1,0:T(8,128)(2,1)S(1)}, bf16[7,512,512]{2,1,0:T(8,128)(2,1)}, u32[]{:S(2)}) %copy-start.2) | copy-done | bytes 3670040
  96.9 0.6 fusion.35
  97.6 0.7 pad_maximum_fusion.3
  98.2 0.6 fusion.33
  98.9 0.6 fusion.31
  99.5 0.6 fusion.29
  100.1 0.7 fusion.27
  100.8 0.6 fusion.25
  101.5 1.0 add_add_fusion
  102.5 0.6 fusion.1
  103.4 1.1 copy-done.9
  104.5 0.4 convolution_add_fusion.2
  104.9 1.5 %convolution_add_fusion.1 = f32[768,256]{1,0:T(8,128)} fusion(f32[768,256]{1,0:T(8,128)S(1)} %convolution_add_fusion.2, bf16[96,2,512]{2,1,0:T(2,128)(2,1)S(1)} %slice.164, bf16[96,8,512]{2,1,0:T(8,128)(2,1)S(1)} %get-tuple-element.14, bf16[3,512,256]{2,1,0:T(8,128)(2,1)S(1)} %copy-done.9), kind=kOutput, calls=%fused_computation.33 | convolution fusion | flops 203096064 | bytes 2818048 | tf_op jit(solution)/shard_map/dot_general | solution.py:99
  106.4 3.5 %fusion.3 = bf16[96,8,512]{2,1,0:T(8,128)(2,1)} fusion(f32[768,512]{1,0:T(8,128)S(1)} %add_add_fusion, bf16[256,512]{1,0:T(8,128)(2,1)S(1)} %copy-done, f32[768,256]{1,0:T(8,128)} %convolution_add_fusion.1, bf16[96,8,512]{2,1,0:T(8,128)(2,1)} %copy-done.7, bf16[96,2,512]{2,1,0:T(2,128)(2,1)} %copy-done.8, f32[512]{0:T(512)S(1)} %copy-done.13, ...), kind=kOutput, calls=%fused_computation.31 | convolution fusion | flops 406388736 | bytes 4655104 | tf_op jit(solution)/shard_map/dot_general | solution.py:105
  109.9 2.5 %pad_maximum_fusion = f32[96,10,512]{2,0,1:T(8,128)} fusion(f32[96,2,512]{2,0,1:T(8,128)S(1)} %copy.119, f32[96,6,512]{2,0,1:T(8,128)S(1)} %slice_convert_fusion, f32[96,1,512]{2,0,1:T(8,128)} %copy.118, f32[96,1,512]{2,0,1:T(8,128)} %copy.117), kind=kLoop, calls=%fused_computation.16 | loop fusion | flops 1474560 | bytes 3932160 | tf_op jit(solution)/shard_map/concatenate | solution.py:109
  (62 shorter events, 3.9 us)
Async XLA Ops:
  0.6 105.8 %copy-start = (bf16[256,512]{1,0:T(8,128)(2,1)S(1)}, bf16[256,512]{1,0:T(8,128)(2,1)}, u32[]{:S(2)}) copy-start(bf16[256,512]{1,0:T(8,128)(2,1)} %param.24) | copy-start | bytes 786436
  2.9 16.3 %all-to-all-start.2 = ((s32[32,1,1]{2,1,0:T(1,128)}), s32[32,1,1]{2,1,0:T(1,128)S(1)}, u32[]{:S(2)}, u32[]{:S(2)}) async-start(s32[32,1,1]{2,1,0:T(1,128)} %copy.102), calls=%async_computation.2 | async-start | bytes 32768 | tf_op jit(solution)/shard_map/all_to_all | solution.py:178
  19.2 15.4 %all-to-all-start = ((s32[128,1,2]{2,1,0:T(1,128)}), s32[128,1,2]{2,1,0:T(1,128)S(1)}, u32[]{:S(2)}, u32[]{:S(2)}) async-start(s32[128,1,2]{2,1,0:T(1,128)} %bitcast), calls=%async_computation | async-start | bytes 131072 | tf_op jit(solution)/shard_map/all_to_all | solution.py:151
  36.6 14.5 %all-to-all-start.1 = ((s32[128,2,32]{2,1,0:T(2,128)}), s32[128,2,32]{2,1,0:T(2,128)S(1)}, u32[]{:S(2)}, u32[]{:S(2)}) async-start(s32[128,2,32]{2,1,0:T(2,128)} %broadcast_select_fusion.1), calls=%async_computation.1 | async-start | bytes 262144 | tf_op jit(solution)/shard_map/all_to_all | solution.py:155
  51.1 34.0 %all-to-all-start.3 = ((f32[32,10,512]{2,1,0:T(8,128)}), f32[32,10,512]{2,1,0:T(8,128)S(1)}, u32[]{:S(2)}, u32[]{:S(2)}) async-start(f32[32,10,512]{2,1,0:T(8,128)} %copy.103), calls=%async_computation.3 | async-start | bytes 2097152 | tf_op jit(solution)/shard_map/all_to_all | solution.py:180
  81.6 1.3 %copy-start.3 = (bf16[96,4,512]{2,1,0:T(4,128)(2,1)}, bf16[96,4,512]{2,1,0:T(4,128)(2,1)S(1)}, u32[]{:S(2)}) copy-start(bf16[96,4,512]{2,1,0:T(4,128)(2,1)S(1)} %select_reduce_fusion) | copy-start | bytes 1179652
  85.1 2.4 %copy-start.1 = (f32[96,10,512]{2,0,1:T(8,128)S(1)}, f32[96,10,512]{2,0,1:T(8,128)}, u32[]{:S(2)}) copy-start(f32[96,10,512]{2,0,1:T(8,128)} %param.17) | copy-start | bytes 5898244
  91.5 13.3 %copy-start.8 = (bf16[96,2,512]{2,1,0:T(2,128)(2,1)}, bf16[96,2,512]{2,1,0:T(2,128)(2,1)S(1)}, u32[]{:S(2)}) copy-start(bf16[96,2,512]{2,1,0:T(2,128)(2,1)S(1)} %slice.164) | copy-start | bytes 589828
  91.5 1.1 copy-start.4
  91.5 1.3 %copy-start.5 = (f32[96,3,1,512]{3,1,0,2:T(4,128)S(1)}, f32[96,3,1,512]{3,1,0,2:T(4,128)}, u32[]{:S(2)}) copy-start(f32[96,3,1,512]{3,1,0,2:T(4,128)} %get-tuple-element.33) | copy-start | bytes 1769476
  91.6 1.5 %copy-start.6 = (f32[96,3,1,512]{3,1,0,2:T(4,128)S(1)}, f32[96,3,1,512]{3,1,0,2:T(4,128)}, u32[]{:S(2)}) copy-start(f32[96,3,1,512]{3,1,0,2:T(4,128)} %get-tuple-element.34) | copy-start | bytes 1769476
  94.2 0.7 copy-start.11
  94.9 2.0 %copy-start.2 = (bf16[7,512,512]{2,1,0:T(8,128)(2,1)S(1)}, bf16[7,512,512]{2,1,0:T(8,128)(2,1)}, u32[]{:S(2)}) copy-start(bf16[7,512,512]{2,1,0:T(8,128)(2,1)} %param.20) | copy-start | bytes 11010052
  100.8 0.7 copy-start.10
  103.1 1.8 %copy-start.7 = (bf16[96,8,512]{2,1,0:T(8,128)(2,1)}, bf16[96,8,512]{2,1,0:T(8,128)(2,1)S(1)}, u32[]{:S(2)}) copy-start(bf16[96,8,512]{2,1,0:T(8,128)(2,1)S(1)} %get-tuple-element.14) | copy-start | bytes 2359300
  103.1 1.4 %copy-start.9 = (bf16[3,512,256]{2,1,0:T(8,128)(2,1)S(1)}, bf16[3,512,256]{2,1,0:T(8,128)(2,1)}, u32[]{:S(2)}) copy-start(bf16[3,512,256]{2,1,0:T(8,128)(2,1)} %param.22) | copy-start | bytes 2359300
  103.1 1.4 %copy-start.12 = (f32[256]{0:T(256)S(1)}, f32[256]{0:T(256)}, u32[]{:S(2)}) copy-start(f32[256]{0:T(256)} %param.23) | copy-start | bytes 3076
  104.9 1.5 %copy-start.13 = (f32[512]{0:T(512)S(1)}, f32[512]{0:T(512)}, u32[]{:S(2)}) copy-start(f32[512]{0:T(512)} %param.25) | copy-start | bytes 6148

commit v2 on v1

--- a/solution.py
+++ b/solution.py
@@ -147,36 +147,36 @@
     rank_in = jnp.sum(earlier & (anchor[None, :] == anchor[:, None]), axis=1).astype(jnp.int32)
     key = anchor * most + rank_in
     spots = jnp.arange(devices_all * most, dtype=jnp.int32)
-    request = jnp.sum(jnp.where(key[None, :] == spots[:, None], row[None, :] + 1, 0), axis=1) - 1
-    asked = lax.all_to_all(
-        request.reshape(devices_all, most), ("grp", "dev"), 0, 0, tiled=True
-    ).reshape(-1)
-    answer = jnp.take(codes, jnp.clip(asked, 0, conv_count - 1), axis=0)
+    code_request = jnp.sum(jnp.where(key[None, :] == spots[:, None], row[None, :] + 1, 0), axis=1) - 1
+    source_dev = old_slot // conv_count - group_first
+    source_row = old_slot % conv_count
+    moved = source_dev != local_index
+    everyone = jnp.arange(devices_all, dtype=jnp.int32)
+    state_request = (
+        jnp.sum(
+            jnp.where(
+                moved[None, :] & (source_dev[None, :] + group_first == everyone[:, None]),
+                source_row[None, :] + 1,
+                0,
+            ),
+            axis=1,
+        )
+        - 1
+    )
+    request = jnp.concatenate(
+        [code_request.reshape(devices_all, most), state_request.reshape(devices_all, 1)], axis=1
+    )
+    asked = lax.all_to_all(request, ("grp", "dev"), 0, 0, tiled=True)
+
+    local_rows = embed_codes(codes, code_table).reshape(conv_count, -1)
+    answer = jnp.take(local_rows, jnp.clip(asked[:, :most].reshape(-1), 0, conv_count - 1), axis=0)
     answered = lax.all_to_all(
         answer.reshape(devices_all, most, -1), ("grp", "dev"), 0, 0, tiled=True
     ).reshape(devices_all * most, -1)
-    my_codes = jnp.take(answered, key, axis=0)
-    book_count = my_codes.shape[1] // FRAMES
-    book_size = code_table.shape[0] // book_count
-    flat_index = my_codes.reshape(conv_count, FRAMES, book_count) + (
-        jnp.arange(book_count, dtype=jnp.int32) * book_size
-    )
-    looked = jnp.take(code_table, flat_index, axis=0).astype(jnp.float32)
-    routed = jnp.sum(looked, axis=2).astype(jnp.bfloat16)
-
-    source_dev = old_slot // conv_count - group_first
-    source_row = old_slot % conv_count
-    moved = source_dev != local_index
-    devs = jnp.arange(per_group, dtype=jnp.int32)
-    wanted = (
-        jnp.sum(
-            jnp.where(moved[None, :] & (source_dev[None, :] == devs[:, None]), source_row[None, :] + 1, 0),
-            axis=1,
-        )
-        - 1
-    )
-    asked_rows = lax.all_to_all(wanted.reshape(per_group, 1), "dev", 0, 0, tiled=True).reshape(-1)
-    leaving = jnp.take(states, jnp.clip(asked_rows, 0, conv_count - 1), axis=0)
+    routed = jnp.take(answered, key, axis=0).reshape(conv_count, FRAMES, -1)
+
+    state_asked = lax.dynamic_slice_in_dim(asked[:, most], group_first, per_group)
+    leaving = jnp.take(states, jnp.clip(state_asked, 0, conv_count - 1), axis=0)
     arrived = lax.all_to_all(leaving, "dev", 0, 0, tiled=True)
     brought = jnp.take(arrived, jnp.clip(source_dev, 0, per_group - 1), axis=0)
     carried = jnp.where(moved[:, None, None], brought, states)

time: 113 us -> 105 us (0.929)
  local copies, waits for them, and re-layouts: 41.9 us -> 21.5 us
  matrix products: 10.2 us -> 22.6 us
  other arithmetic: 17.3 us -> 14.1 us
  waiting for transfers between devices: 17.5 us -> 20.1 us
    gather x5, local copies, waits for them, and re-layouts: 25.7 us -> 6.7 us  [the longest x2 4.07 us: local(): jnp.take(local_rows, jnp.clip(asked[:, :most].reshape(-1), 0, conv_count...]
    dot_general x0 -> x8, matrix products: none -> 12.5 us  [embed_codes(): jnp.dot(onehot, book_rows, preferred_element_type=jnp.float32)]
    all_to_all x1, waiting for transfers between devices: 0.01 us -> 10.8 us  [local(): arrived = lax.all_to_all(leaving, 'dev', 0, 0, tiled=True)]
    all_to_all x2 -> x1, waiting for transfers between devices: 9.05 us -> 0.01 us  [local(): asked = lax.all_to_all(request, ('grp', 'dev'), 0, 0, tiled=True)]
    all_to_all x2 -> x1, starting transfers between devices: 15.5 us -> 11.5 us  [local(): asked = lax.all_to_all(request, ('grp', 'dev'), 0, 0, tiled=True)]
    all_to_all x1, starting transfers between devices: 4.47 us -> 7.86 us  [local(): arrived = lax.all_to_all(leaving, 'dev', 0, 0, tiled=True)]
    reduce_sum x2 -> x1, other arithmetic: 3.48 us -> 0.12 us  [local(): jnp.sum(jnp.where(moved[None, :] & (source_dev[None, :] + group_first ==...]
    all_to_all x1, starting transfers between devices: 4.6 us -> 5.93 us  [local(): lax.all_to_all(answer.reshape(devices_all, most, -1), ('grp', 'dev'), 0,...]
  transfers between devices with their start and end apart: 4 -> 3, of which waited for: 3 -> 2; matrix products, arithmetic and copies ran while one was open for 34% -> 29% of each run, Pallas kernels for 0% -> 0%
where the time goes in v2:
time: 105 us
  starting transfers between devices  25.3 us (24%)
  matrix products  22.6 us (22%)
  local copies, waits for them, and re-layouts  21.5 us (20%)
  waiting for transfers between devices  20.1 us (19%)
  other arithmetic  14.1 us (13%)
  between operations  1.16 us (1%)
    dot_general x8, matrix products, embed_codes(): jnp.dot(onehot, book_rows, preferred_element_type=jnp.float32)  12.5 us
    all_to_all x1, starting transfers between devices, local(): asked = lax.all_to_all(request, ('grp', 'dev'), 0, 0, tiled=True)  11.5 us
    all_to_all x1, waiting for transfers between devices, local(): arrived = lax.all_to_all(leaving, 'dev', 0, 0, tiled=True)  10.8 us
    all_to_all x1, waiting for transfers between devices, local(): lax.all_to_all(answer.reshape(devices_all, most, -1), ('grp', 'dev'), 0,...  9.36 us
    all_to_all x1, starting transfers between devices, local(): arrived = lax.all_to_all(leaving, 'dev', 0, 0, tiled=True)  7.86 us
    all_to_all x1, starting transfers between devices, local(): lax.all_to_all(answer.reshape(devices_all, most, -1), ('grp', 'dev'), 0,...  5.93 us
    dot_general x7, matrix products, decode(): jnp.dot(window, conv_weight[tap_index], preferred_element_type=jnp.float32)  4.79 us
    gather x2, local copies, waits for them, and re-layouts, local(): jnp.take(local_rows, jnp.clip(asked[:, :most].reshape(-1), 0, conv_count...  4.07 us
  transfers between devices with their start and end apart: 3, of which 2 were waited for; matrix products, arithmetic and copies ran while one was open for 29% of the time, Pallas kernels for 0%

profile of v2, /device:TPU:1, one launch (start us, length us, event | category | flops | bytes accessed | tf_op | source)
XLA Modules:
  0.0 104.9 jit_solution(827460397607990319)
XLA Ops:
  0.6 0.7 fusion.117
  1.4 0.7 and_select_fusion.3
  2.3 0.7 compare_and_fusion.1
  3.4 0.7 pad_add_fusion
  4.1 11.5 %all-to-all-start = ((s32[128,1,3]{2,1,0:T(1,128)}), s32[128,1,3]{2,1,0:T(1,128)S(1)}, u32[]{:S(2)}, u32[]{:S(2)}) async-start(s32[128,1,3]{2,1,0:T(1,128)} %bitcast.2), calls=%async_computation | async-start | bytes 131072 | tf_op jit(solution)/shard_map/all_to_all | solution.py:169
  15.7 0.8 copy.69
  16.6 0.9 slice_reduce_fusion
  17.5 3.0 %fusion = f32[384,512]{1,0:T(8,128)S(1)} fusion(bf16[16384,512]{1,0:T(8,128)(2,1)} %param.14, s32[384]{0:T(512)S(1)} %get-tuple-element.11), kind=kOutput, calls=%fused_computation.15 | convolution fusion | flops 806092800 | bytes 2885120 | tf_op jit(solution)/shard_map/dot_general | solution.py:20
  20.4 3.4 %fusion.46 = f32[384,512]{1,0:T(8,128)S(1)} fusion(f32[384,512]{1,0:T(8,128)S(1)} %fusion, bf16[16384,512]{1,0:T(8,128)(2,1)} %param.14, s32[384]{0:T(512)S(1)} %get-tuple-element.10), kind=kOutput, calls=%fused_computation.72 | convolution fusion | flops 806289408 | bytes 3671552 | tf_op jit(solution)/shard_map/dot_general | solution.py:20
  23.8 1.0 fusion.43
  24.8 1.0 fusion.40
  25.9 1.0 fusion.37
  26.9 1.0 fusion.34
  27.9 1.0 fusion.31
  29.0 1.0 fusion.49
  30.8 1.5 %gather_fusion.2 = f32[32,10,512]{2,0,1:T(8,128)S(1)} fusion(f32[96,10,512]{2,0,1:T(8,128)S(1)} %copy-done.1, s32[1024]{0:T(1024)S(1)} %pad_clamp_fusion.1), kind=kCustom, calls=%fused_computation.2 | custom fusion | bytes 1310848 | tf_op jit(solution)/shard_map/jit(_take)/gather | solution.py:179
  32.5 1.4 %copy.71 = f32[32,10,512]{2,1,0:T(8,128)} copy(f32[32,10,512]{2,0,1:T(8,128)S(1)} %broadcast_select_fusion.1) | data formatting | bytes 1310720 | tf_op jit(solution)/shard_map/jit(_take)/select_n | solution.py:179
  33.9 7.9 %all-to-all-start.2 = ((f32[32,10,512]{2,1,0:T(8,128)}), f32[32,10,512]{2,1,0:T(8,128)}, u32[]{:S(2)}, u32[]{:S(2)}) async-start(f32[32,10,512]{2,1,0:T(8,128)} %copy.71), calls=%async_computation.2 | async-start | bytes 2097152 | tf_op jit(solution)/shard_map/all_to_all | solution.py:180
  41.7 2.3 %gather_fusion = bf16[256,2048]{1,0:T(8,128)(2,1)} fusion(bf16[96,2048]{1,0:T(8,128)(2,1)S(1)} %reshape_reshape.3, s32[1024]{0:T(1024)S(1)} %pad_clamp_fusion.3), kind=kCustom, calls=%fused_computation | custom fusion | bytes 2098176 | tf_op jit(solution)/shard_map/jit(_take)/gather | solution.py:172
  44.1 1.7 %gather.23 = bf16[128,2,2048]{2,1,0:T(2,128)(2,1)S(1)} reshape(bf16[256,2048]{1,0:T(8,128)(2,1)} %gather_fusion) | data formatting | bytes 2097152 | tf_op jit(solution)/shard_map/jit(_take)/gather | solution.py:172
  45.9 2.0 %broadcast_select_fusion = bf16[128,2,2048]{2,1,0:T(2,128)(2,1)} fusion(bf16[128,2,2048]{2,1,0:T(2,128)(2,1)S(1)} %gather.23, pred[128,2]{1,0:T(8,128)(4,1)S(1)} %compare_and_fusion), kind=kLoop, calls=%fused_computation.38 | loop fusion | flops 524288 | bytes 2097408 | tf_op jit(solution)/shard_map/jit(_take)/select_n | solution.py:172
  47.9 10.8 %all-to-all-done.2 = f32[32,10,512]{2,1,0:T(8,128)} async-done(((f32[32,10,512]{2,1,0:T(8,128)}), f32[32,10,512]{2,1,0:T(8,128)}, u32[]{:S(2)}, u32[]{:S(2)}) %all-to-all-start.2) | async-done | bytes 655392 | tf_op jit(solution)/shard_map/all_to_all | solution.py:180
  58.7 5.9 %all-to-all-start.1 = ((bf16[128,2,2048]{2,1,0:T(2,128)(2,1)}), bf16[128,2,2048]{2,1,0:T(2,128)(2,1)S(1)}, u32[]{:S(2)}, u32[]{:S(2)}) async-start(bf16[128,2,2048]{2,1,0:T(2,128)(2,1)} %broadcast_select_fusion), calls=%async_computation.1 | async-start | bytes 2097152 | tf_op jit(solution)/shard_map/all_to_all | solution.py:173
  64.7 3.6 %gather_fusion.3 = f32[96,10,512]{2,1,0:T(8,128)} fusion(f32[32,10,512]{2,1,0:T(8,128)} %all-to-all-done.2, s32[1024]{0:T(1024)S(1)} %pad_clamp_fusion), kind=kCustom, calls=%fused_computation.3 | custom fusion | bytes 3932544 | tf_op jit(solution)/shard_map/jit(_take)/gather | solution.py:181
  68.3 3.8 %fusion.123 = (bf16[96,10,512]{2,1,0:T(8,128)(2,1)S(1)}, f32[96,10,512]{2,1,0:T(8,128)S(1)}) fusion(f32[96,10,512]{2,0,1:T(8,128)S(1)} %copy-done.1, f32[96,10,512]{2,1,0:T(8,128)} %gather_fusion.3, pred[96]{0:T(512)(128)(4,1)S(1)} %get-tuple-element.14, pred[96]{0:T(512)(128)(4,1)S(1)} %subtract_compare_fusion), kind=kLoop, calls=%fused_computation.189 | loop fusion | flops 1474560 | bytes 6881472 | tf_op jit(solution)/shard_map/convert.5
  72.1 0.8 slice.244
  73.4 1.0 copy.78
  74.4 9.4 %all-to-all-done.1 = bf16[128,2,2048]{2,1,0:T(2,128)(2,1)S(1)} async-done(((bf16[128,2,2048]{2,1,0:T(2,128)(2,1)}), bf16[128,2,2048]{2,1,0:T(2,128)(2,1)S(1)}, u32[]{:S(2)}, u32[]{:S(2)}) %all-to-all-start.1) | async-done | bytes 1048608 | tf_op jit(solution)/shard_map/all_to_all | solution.py:173
  83.8 0.4 reshape.223
  84.2 0.8 gather_fusion.1
  85.5 0.7 slice.247
  86.2 0.7 slice.248
  87.0 0.3 fusion.52
  87.7 0.5 copy-done.9
  88.6 1.7 %copy-done.2 = bf16[7,512,512]{2,1,0:T(8,128)(2,1)S(1)} copy-done((bf16[7,512,512]{2,1,0:T(8,128)(2,1)S(1)}, bf16[7,512,512]{2,1,0:T(8,128)(2,1)}, u32[]{:S(2)}) %copy-start.2) | copy-done | bytes 3670040
  90.2 0.6 fusion.81
  90.9 0.5 pad_maximum_fusion.3
  91.3 0.6 fusion.79
  92.0 0.6 fusion.77
  92.6 0.6 fusion.75
  93.2 0.6 fusion.73
  93.9 0.7 fusion.71
  94.6 1.0 add_add_fusion
  95.6 0.6 fusion.17
  96.7 0.4 convolution_add_fusion.2
  97.3 1.5 %convolution_add_fusion.1 = f32[768,256]{1,0:T(8,128)} fusion(f32[768,256]{1,0:T(8,128)S(1)} %convolution_add_fusion.2, bf16[96,2,512]{2,1,0:T(2,128)(2,1)S(1)} %copy-done.5, bf16[96,8,512]{2,1,0:T(8,128)(2,1)S(1)} %get-tuple-element.22, bf16[3,512,256]{2,1,0:T(8,128)(2,1)S(1)} %copy-done.6), kind=kOutput, calls=%fused_computation.64 | convolution fusion | flops 203096064 | bytes 2818048 | tf_op jit(solution)/shard_map/dot_general | solution.py:99
  98.8 3.5 %fusion.27 = bf16[96,8,512]{2,1,0:T(8,128)(2,1)} fusion(f32[768,512]{1,0:T(8,128)S(1)} %add_add_fusion, bf16[256,512]{1,0:T(8,128)(2,1)S(1)} %copy-done, f32[768,256]{1,0:T(8,128)} %convolution_add_fusion.1, bf16[96,8,512]{2,1,0:T(8,128)(2,1)} %copy-done.3, bf16[96,2,512]{2,1,0:T(2,128)(2,1)} %slice.244, f32[512]{0:T(512)S(1)} %copy-done.12, ...), kind=kOutput, calls=%fused_computation.62 | convolution fusion | flops 406388736 | bytes 4655104 | tf_op jit(solution)/shard_map/dot_general | solution.py:105
  102.3 2.5 %pad_maximum_fusion = f32[96,10,512]{2,0,1:T(8,128)} fusion(f32[96,2,512]{2,0,1:T(8,128)S(1)} %copy.86, f32[96,6,512]{2,0,1:T(8,128)S(1)} %slice_convert_fusion, f32[96,1,512]{2,0,1:T(8,128)} %slice.248, f32[96,1,512]{2,0,1:T(8,128)} %slice.247), kind=kLoop, calls=%fused_computation.39 | loop fusion | flops 1474560 | bytes 3932160 | tf_op jit(solution)/shard_map/concatenate | solution.py:109
  (63 shorter events, 4.1 us)
Async XLA Ops:
  0.6 98.2 %copy-start = (bf16[256,512]{1,0:T(8,128)(2,1)S(1)}, bf16[256,512]{1,0:T(8,128)(2,1)}, u32[]{:S(2)}) copy-start(bf16[256,512]{1,0:T(8,128)(2,1)} %param.24) | copy-start | bytes 786436
  4.1 26.1 %all-to-all-start = ((s32[128,1,3]{2,1,0:T(1,128)}), s32[128,1,3]{2,1,0:T(1,128)S(1)}, u32[]{:S(2)}, u32[]{:S(2)}) async-start(s32[128,1,3]{2,1,0:T(1,128)} %bitcast.2), calls=%async_computation | async-start | bytes 131072 | tf_op jit(solution)/shard_map/all_to_all | solution.py:169
  16.6 7.2 %copy-start.11 = (bf16[16384,512]{1,0:T(8,128)(2,1)S(1)}, bf16[16384,512]{1,0:T(8,128)(2,1)}, u32[]{:S(2)}) copy-start(bf16[16384,512]{1,0:T(8,128)(2,1)} %param.14) | copy-start | bytes 50331652
  29.0 1.8 %copy-start.1 = (f32[96,10,512]{2,0,1:T(8,128)S(1)}, f32[96,10,512]{2,0,1:T(8,128)}, u32[]{:S(2)}) copy-start(f32[96,10,512]{2,0,1:T(8,128)} %param.17) | copy-start | bytes 5898244
  33.9 24.8 %all-to-all-start.2 = ((f32[32,10,512]{2,1,0:T(8,128)}), f32[32,10,512]{2,1,0:T(8,128)}, u32[]{:S(2)}, u32[]{:S(2)}) async-start(f32[32,10,512]{2,1,0:T(8,128)} %copy.71), calls=%async_computation.2 | async-start | bytes 2097152 | tf_op jit(solution)/shard_map/all_to_all | solution.py:180
  45.9 18.8 %copy-start.7 = (f32[4,512]{1,0:T(4,128)S(1)}, f32[4,512]{1,0:T(4,128)}, u32[]{:S(2)}) copy-start(f32[4,512]{1,0:T(4,128)} %param.18) | copy-start | bytes 24580
  58.7 25.1 %all-to-all-start.1 = ((bf16[128,2,2048]{2,1,0:T(2,128)(2,1)}), bf16[128,2,2048]{2,1,0:T(2,128)(2,1)S(1)}, u32[]{:S(2)}, u32[]{:S(2)}) async-start(bf16[128,2,2048]{2,1,0:T(2,128)(2,1)} %broadcast_select_fusion), calls=%async_computation.1 | async-start | bytes 2097152 | tf_op jit(solution)/shard_map/all_to_all | solution.py:173
  87.5 0.7 copy-start.9
  88.2 2.0 %copy-start.2 = (bf16[7,512,512]{2,1,0:T(8,128)(2,1)S(1)}, bf16[7,512,512]{2,1,0:T(8,128)(2,1)}, u32[]{:S(2)}) copy-start(bf16[7,512,512]{2,1,0:T(8,128)(2,1)} %param.20) | copy-start | bytes 11010052
  88.4 2.4 %copy-start.4 = (bf16[96,6,512]{2,0,1:T(8,128)(2,1)S(1)}, bf16[96,6,512]{2,0,1:T(8,128)(2,1)}, u32[]{:S(2)}) copy-start(bf16[96,6,512]{2,0,1:T(8,128)(2,1)} %copy.78) | copy-start | bytes 1769476
  93.9 0.7 copy-start.8
  95.5 1.1 %copy-start.6 = (bf16[3,512,256]{2,1,0:T(8,128)(2,1)S(1)}, bf16[3,512,256]{2,1,0:T(8,128)(2,1)}, u32[]{:S(2)}) copy-start(bf16[3,512,256]{2,1,0:T(8,128)(2,1)} %param.22) | copy-start | bytes 2359300
  95.6 1.1 %copy-start.10 = (f32[256]{0:T(256)S(1)}, f32[256]{0:T(256)}, u32[]{:S(2)}) copy-start(f32[256]{0:T(256)} %param.23) | copy-start | bytes 3076
  96.2 0.9 copy-start.3
  96.2 1.1 %copy-start.5 = (bf16[96,2,512]{2,1,0:T(2,128)(2,1)S(1)}, bf16[96,2,512]{2,1,0:T(2,128)(2,1)}, u32[]{:S(2)}) copy-start(bf16[96,2,512]{2,1,0:T(2,128)(2,1)} %slice.244) | copy-start | bytes 589828
  97.3 1.5 %copy-start.12 = (f32[512]{0:T(512)S(1)}, f32[512]{0:T(512)}, u32[]{:S(2)}) copy-start(f32[512]{0:T(512)} %param.25) | copy-start | bytes 6148

commit v3 on v2

--- a/solution.py
+++ b/solution.py
@@ -1,6 +1,8 @@
 import jax
 import jax.numpy as jnp
 from jax import lax
+from jax.experimental import pallas as pl
+from jax.experimental.pallas import tpu as pltpu
 from jax.sharding import PartitionSpec as P
 
 FRAMES = 4
@@ -48,6 +50,83 @@
     hit = flags[..., None, :] & (ranks[..., None, :] == spots[:, None])
     picked = jnp.sum(jnp.where(hit, values[..., None, :], 0), axis=-1)
     return (picked, jnp.any(hit, axis=-1))
+
+
+def exchange(blocks, whole, collective_id):
+    peers = blocks.shape[0]
+    per_group = lax.axis_size("dev")
+
+    def kernel(x_ref, o_ref, send_sems, recv_sems, own_sem):
+        group = lax.axis_index("grp")
+        if whole:
+            me = group * per_group + lax.axis_index("dev")
+        else:
+            me = lax.axis_index("dev")
+
+        def device(peer):
+            if whole:
+                return (peer // per_group, peer % per_group)
+            return (group, peer)
+
+        barrier = pltpu.get_barrier_semaphore()
+
+        def greet(offset, carry):
+            peer = lax.rem(me + offset, peers)
+            pl.semaphore_signal(barrier, inc=1, device_id=device(peer), device_id_type=pl.DeviceIdType.MESH)
+            return carry
+
+        lax.fori_loop(1, peers, greet, 0)
+        pl.semaphore_wait(barrier, peers - 1)
+
+        def outgoing(peer):
+            return pltpu.make_async_remote_copy(
+                src_ref=x_ref.at[peer],
+                dst_ref=o_ref.at[me],
+                send_sem=send_sems.at[peer],
+                recv_sem=recv_sems.at[me],
+                device_id=device(peer),
+                device_id_type=pl.DeviceIdType.MESH,
+            )
+
+        def incoming(peer):
+            return pltpu.make_async_remote_copy(
+                src_ref=x_ref.at[peer],
+                dst_ref=o_ref.at[peer],
+                send_sem=send_sems.at[peer],
+                recv_sem=recv_sems.at[peer],
+                device_id=device(peer),
+                device_id_type=pl.DeviceIdType.MESH,
+            )
+
+        def send(offset, carry):
+            outgoing(lax.rem(me + offset, peers)).start()
+            return carry
+
+        lax.fori_loop(1, peers, send, 0)
+        own = pltpu.make_async_copy(x_ref.at[me], o_ref.at[me], own_sem)
+        own.start()
+        own.wait()
+
+        def finish(offset, carry):
+            peer = lax.rem(me + offset, peers)
+            outgoing(peer).wait_send()
+            incoming(lax.rem(me + peers - offset, peers)).wait_recv()
+            return carry
+
+        lax.fori_loop(1, peers, finish, 0)
+
+    return pl.pallas_call(
+        kernel,
+        out_shape=jax.ShapeDtypeStruct(blocks.shape, blocks.dtype),
+        in_specs=[pl.BlockSpec(memory_space=pl.ANY)],
+        out_specs=pl.BlockSpec(memory_space=pl.ANY),
+        scratch_shapes=[
+            pltpu.SemaphoreType.DMA((peers,)),
+            pltpu.SemaphoreType.DMA((peers,)),
+            pltpu.SemaphoreType.DMA(()),
+        ],
+        compiler_params=pltpu.CompilerParams(collective_id=collective_id, has_side_effects=True),
+    )(blocks)
 
 
 def decode(
@@ -166,18 +245,18 @@
     request = jnp.concatenate(
         [code_request.reshape(devices_all, most), state_request.reshape(devices_all, 1)], axis=1
     )
-    asked = lax.all_to_all(request, ("grp", "dev"), 0, 0, tiled=True)
+    lanes = 128
+    padded = jnp.zeros((devices_all, 1, lanes), jnp.int32).at[:, 0, : most + 1].set(request)
+    asked = exchange(padded, True, 0)[:, 0, : most + 1]
 
     local_rows = embed_codes(codes, code_table).reshape(conv_count, -1)
     answer = jnp.take(local_rows, jnp.clip(asked[:, :most].reshape(-1), 0, conv_count - 1), axis=0)
-    answered = lax.all_to_all(
-        answer.reshape(devices_all, most, -1), ("grp", "dev"), 0, 0, tiled=True
-    ).reshape(devices_all * most, -1)
+    answered = exchange(answer.reshape(devices_all, 16, -1), True, 1).reshape(devices_all * most, -1)
     routed = jnp.take(answered, key, axis=0).reshape(conv_count, FRAMES, -1)
 
     state_asked = lax.dynamic_slice_in_dim(asked[:, most], group_first, per_group)
     leaving = jnp.take(states, jnp.clip(state_asked, 0, conv_count - 1), axis=0)
-    arrived = lax.all_to_all(leaving, "dev", 0, 0, tiled=True)
+    arrived = exchange(leaving.reshape(per_group, -1, 128), False, 2).reshape(leaving.shape)
     brought = jnp.take(arrived, jnp.clip(source_dev, 0, per_group - 1), axis=0)
     carried = jnp.where(moved[:, None, None], brought, states)
     return decode(

time: 105 us -> 134 us (1.28)
  Pallas kernels: 0 us -> 62.7 us
  starting transfers between devices: 25.3 us -> 0 us
  waiting for transfers between devices: 20.1 us -> 0 us
  local copies, waits for them, and re-layouts: 21.5 us -> 29.1 us
  matrix products: 22.6 us -> 24.9 us
    pallas_call x0 -> x3, Pallas kernels: none -> 62.7 us  [exchange(): pl.pallas_call(kernel, out_shape=jax.ShapeDtypeStruct(blocks.shape, block...]
    all_to_all x3 -> x0, starting transfers between devices: 25.3 us -> none  [the longest x1 11.5 us: local(): asked = lax.all_to_all(request, ('grp', 'dev'), 0, 0, tiled=True)]
    all_to_all x3 -> x0, waiting for transfers between devices: 20.1 us -> none  [the longest x1 10.8 us: local(): arrived = lax.all_to_all(leaving, 'dev', 0, 0, tiled=True)]
    reshape x1 -> x2, local copies, waits for them, and re-layouts: 0.42 us -> 3.73 us  [the longest x1 2.18 us: local(): exchange(leaving.reshape(per_group, -1, 128), False, 2)]
    gather x1 -> x3, local copies, waits for them, and re-layouts: 1.51 us -> 4.19 us  [local(): leaving = jnp.take(states, jnp.clip(state_asked, 0, conv_count - 1), axis=0)]
    dot_general x8, matrix products: 12.5 us -> 15.1 us  [embed_codes(): jnp.dot(onehot, book_rows, preferred_element_type=jnp.float32)]
    gather x2, local copies, waits for them, and re-layouts: 1.12 us -> 3.61 us  [local(): routed = jnp.take(answered, key, axis=0).reshape(conv_count, FRAMES, -1)]
    select_n x1 -> x0, local copies, waits for them, and re-layouts: 1.39 us -> none  [local(): leaving = jnp.take(states, jnp.clip(state_asked, 0, conv_count - 1), axis=0)]
  transfers between devices with their start and end apart: 3 -> 0, of which waited for: 2 -> 0; matrix products, arithmetic and copies ran while one was open for 29% -> 0% of each run, Pallas kernels for 0% -> 0%
where the time goes in v3:
time: 134 us; the launch traced here: 133 us
  Pallas kernels  62.7 us (47%)
  local copies, waits for them, and re-layouts  29.1 us (22%)
  matrix products  24.9 us (19%)
  other arithmetic  15.2 us (11%)
    pallas_call x3, Pallas kernels, exchange(): pl.pallas_call(kernel, out_shape=jax.ShapeDtypeStruct(blocks.shape, block...  62.7 us
    dot_general x8, matrix products, embed_codes(): jnp.dot(onehot, book_rows, preferred_element_type=jnp.float32)  15.1 us
    dot_general x7, matrix products, decode(): jnp.dot(window, conv_weight[tap_index], preferred_element_type=jnp.float32)  4.79 us
    gather x3, local copies, waits for them, and re-layouts, local(): leaving = jnp.take(states, jnp.clip(state_asked, 0, conv_count - 1), axis=0)  4.19 us
    unnamed x36, local copies, waits for them, and re-layouts  4.04 us
    gather x2, local copies, waits for them, and re-layouts, local(): jnp.take(local_rows, jnp.clip(asked[:, :most].reshape(-1), 0, conv_count...  3.88 us
    another operation x1, other arithmetic  3.82 us
    gather x2, local copies, waits for them, and re-layouts, local(): routed = jnp.take(answered, key, axis=0).reshape(conv_count, FRAMES, -1)  3.61 us

profile of v3, /device:TPU:1, one launch (start us, length us, event | category | flops | bytes accessed | tf_op | source)
XLA Modules:
  0.0 133.2 jit_solution(16868830599486273039)
XLA Ops:
  0.7 0.8 fusion.117
  1.5 0.7 and_select_fusion.3
  2.5 0.7 compare_and_fusion.1
  3.3 0.9 fusion.124
  4.2 0.8 copy.77
  5.3 0.7 scatter.4.x_ref
  6.0 20.5 %shard_map.140 = s32[128,1,128]{2,1,0:T(1,128)} custom-call(s32[128,1,128]{2,1,0:T(1,128)} %scatter.4.x_ref), custom_call_target="tpu_custom_call" | custom-call | tf_op jit(solution)/shard_map/pallas_call | solution.py:118
  26.5 0.9 compare_and_fusion
  27.6 0.9 slice.255
  28.5 0.9 slice_clamp_fusion
  29.9 0.9 slice_reduce_fusion
  30.8 1.5 %gather_fusion.2 = f32[32,10,512]{2,0,1:T(8,128)S(1)} fusion(f32[96,10,512]{2,0,1:T(8,128)S(1)} %copy-done.1, s32[1024]{0:T(1024)S(1)} %pad_clamp_fusion.1), kind=kCustom, calls=%fused_computation.2 | custom fusion | bytes 1310848 | tf_op jit(solution)/shard_map/jit(_take)/gather | solution.py:258
  32.3 1.4 %copy.79 = f32[32,10,512]{2,1,0:T(8,128)} copy(f32[32,10,512]{2,0,1:T(8,128)S(1)} %gather_fusion.2) | data formatting | bytes 1310720 | tf_op jit(solution)/shard_map/jit(_take)/gather | solution.py:258
  33.7 1.3 gather.29
  35.0 0.9 broadcast_select_fusion.1.x_ref
  35.9 13.9 %shard_map.142 = f32[32,40,128]{2,1,0:T(8,128)} custom-call(f32[32,40,128]{2,1,0:T(8,128)} %broadcast_select_fusion.1.x_ref), custom_call_target="tpu_custom_call" | custom-call | tf_op jit(solution)/shard_map/pallas_call | solution.py:118
  49.9 2.2 %reshape.264 = f32[32,10,512]{2,1,0:T(8,128)} reshape(f32[32,40,128]{2,1,0:T(8,128)} %shard_map.142) | data formatting | bytes 1310720 | tf_op jit(solution)/shard_map/reshape | solution.py:259
  52.0 2.8 %fusion = f32[384,512]{1,0:T(8,128)S(1)} fusion(bf16[16384,512]{1,0:T(8,128)(2,1)} %param.16, s32[384]{0:T(512)S(1)} %get-tuple-element.23), kind=kOutput, calls=%fused_computation.15 | convolution fusion | flops 806092800 | bytes 2885120 | tf_op jit(solution)/shard_map/dot_general | solution.py:22
  54.8 2.8 %fusion.46 = f32[384,512]{1,0:T(8,128)S(1)} fusion(f32[384,512]{1,0:T(8,128)S(1)} %fusion, bf16[16384,512]{1,0:T(8,128)(2,1)} %param.16, s32[384]{0:T(512)S(1)} %get-tuple-element.22), kind=kOutput, calls=%fused_computation.71 | convolution fusion | flops 806289408 | bytes 3671552 | tf_op jit(solution)/shard_map/dot_general | solution.py:22
  57.6 2.8 %fusion.43 = f32[384,512]{1,0:T(8,128)S(1)} fusion(f32[384,512]{1,0:T(8,128)S(1)} %fusion.46, bf16[16384,512]{1,0:T(8,128)(2,1)} %param.16, s32[384]{0:T(512)S(1)} %get-tuple-element.21), kind=kOutput, calls=%fused_computation.70 | convolution fusion | flops 806289408 | bytes 3671552 | tf_op jit(solution)/shard_map/dot_general | solution.py:22
  60.4 2.8 %fusion.40 = f32[384,512]{1,0:T(8,128)S(1)} fusion(f32[384,512]{1,0:T(8,128)S(1)} %fusion.43, bf16[16384,512]{1,0:T(8,128)(2,1)} %param.16, s32[384]{0:T(512)S(1)} %get-tuple-element.20), kind=kOutput, calls=%fused_computation.69 | convolution fusion | flops 806289408 | bytes 3671552 | tf_op jit(solution)/shard_map/dot_general | solution.py:22
  63.2 1.0 fusion.37
  64.2 1.0 fusion.34
  65.3 1.0 fusion.31
  66.3 1.0 fusion.49
  67.6 2.3 %gather_fusion = bf16[256,2048]{1,0:T(8,128)(2,1)} fusion(bf16[96,2048]{1,0:T(8,128)(2,1)S(1)} %reshape_reshape.3, s32[1024]{0:T(1024)S(1)} %pad_clamp_fusion.3), kind=kCustom, calls=%fused_computation | custom fusion | bytes 2098176 | tf_op jit(solution)/shard_map/jit(_take)/gather | solution.py:253
  69.9 1.6 %gather.25 = bf16[128,16,256]{2,1,0:T(8,128)(2,1)S(1)} reshape(bf16[256,2048]{1,0:T(8,128)(2,1)} %gather_fusion) | data formatting | bytes 2097152 | tf_op jit(solution)/shard_map/jit(_take)/gather | solution.py:253
  71.5 1.2 broadcast_select_fusion.x_ref
  72.7 28.4 %shard_map.141 = bf16[128,16,256]{2,1,0:T(8,128)(2,1)} custom-call(bf16[128,16,256]{2,1,0:T(8,128)(2,1)} %broadcast_select_fusion.x_ref), custom_call_target="tpu_custom_call" | custom-call | tf_op jit(solution)/shard_map/pallas_call | solution.py:118
  101.1 1.6 %reshape.263 = bf16[256,2048]{1,0:T(8,128)(2,1)S(1)} reshape(bf16[128,16,256]{2,1,0:T(8,128)(2,1)} %shard_map.141) | data formatting | bytes 2097152 | tf_op jit(solution)/shard_map/reshape | solution.py:254
  102.6 1.6 %gather_fusion.1 = bf16[96,2048]{1,0:T(8,128)(2,1)} fusion(bf16[256,2048]{1,0:T(8,128)(2,1)S(1)} %reshape.263, s32[1024]{0:T(1024)S(1)} %pad_clamp_fusion.2), kind=kCustom, calls=%fused_computation.1 | custom fusion | bytes 786816 | tf_op jit(solution)/shard_map/jit(_take)/gather | solution.py:255
  104.2 2.0 %gather.27 = bf16[96,4,1,512]{3,1,0,2:T(4,128)(2,1)} reshape(bf16[96,2048]{1,0:T(8,128)(2,1)} %gather_fusion.1) | data formatting | bytes 786432 | tf_op jit(solution)/shard_map/jit(_take)/gather | solution.py:255
  106.2 1.2 convert_multiply_fusion.1
  107.4 0.7 slice.275
  108.1 1.1 slice_bitcast_fusion
  109.3 2.4 %gather_fusion.3 = f32[96,10,512]{2,1,0:T(8,128)} fusion(f32[32,10,512]{2,1,0:T(8,128)S(1)} %copy-done.2, s32[1024]{0:T(1024)S(1)} %pad_clamp_fusion), kind=kCustom, calls=%fused_computation.3 | custom fusion | bytes 3932544 | tf_op jit(solution)/shard_map/jit(_take)/gather | solution.py:260
  111.7 3.8 %fusion.123 = (bf16[96,10,512]{2,1,0:T(8,128)(2,1)S(1)}, f32[96,10,512]{2,1,0:T(8,128)S(1)}) fusion(f32[96,10,512]{2,0,1:T(8,128)S(1)} %copy-done.1, f32[96,10,512]{2,1,0:T(8,128)} %gather_fusion.3, pred[96]{0:T(512)(128)(4,1)S(1)} %get-tuple-element.26, pred[96]{0:T(512)(128)(4,1)S(1)} %subtract_compare_fusion), kind=kLoop, calls=%fused_computation.190 | loop fusion | flops 1474560 | bytes 6881472 | tf_op jit(solution)/shard_map/convert.5
  118.6 1.7 %copy-done.3 = bf16[7,512,512]{2,1,0:T(8,128)(2,1)S(1)} copy-done((bf16[7,512,512]{2,1,0:T(8,128)(2,1)S(1)}, bf16[7,512,512]{2,1,0:T(8,128)(2,1)}, u32[]{:S(2)}) %copy-start.3) | copy-done | bytes 3670040
  120.3 0.7 fusion.81
  121.5 0.6 fusion.79
  122.1 0.6 fusion.77
  122.7 0.6 fusion.75
  123.4 0.6 fusion.73
  124.0 0.6 fusion.71
  124.7 1.0 add_add_fusion
  126.6 1.5 %pad_maximum_fusion = f32[96,10,512]{2,0,1:T(8,128)} fusion(f32[96,2,512]{2,0,1:T(8,128)S(1)} %copy.94, f32[96,6,512]{2,0,1:T(8,128)S(1)} %slice_convert_fusion, f32[96,1,512]{2,0,1:T(8,128)S(1)} %copy-done.7, f32[96,1,512]{2,0,1:T(8,128)S(1)} %slice.274), kind=kLoop, calls=%fused_computation.38 | loop fusion | flops 1474560 | bytes 3932160 | tf_op jit(solution)/shard_map/concatenate | solution.py:188
  128.5 1.5 %convolution_add_fusion.1 = f32[768,256]{1,0:T(8,128)} fusion(f32[768,256]{1,0:T(8,128)S(1)} %convolution_add_fusion.2, bf16[96,2,512]{2,1,0:T(2,128)(2,1)S(1)} %slice.271, bf16[96,8,512]{2,1,0:T(8,128)(2,1)S(1)} %get-tuple-element.34, bf16[3,512,256]{2,1,0:T(8,128)(2,1)S(1)} %copy-done.8), kind=kOutput, calls=%fused_computation.63 | convolution fusion | flops 203096064 | bytes 2818048 | tf_op jit(solution)/shard_map/dot_general | solution.py:178
  130.0 3.2 %fusion.27 = bf16[96,8,512]{2,1,0:T(8,128)(2,1)} fusion(f32[768,512]{1,0:T(8,128)S(1)} %add_add_fusion, bf16[256,512]{1,0:T(8,128)(2,1)S(1)} %copy-done, f32[768,256]{1,0:T(8,128)} %convolution_add_fusion.1, bf16[96,8,512]{2,1,0:T(8,128)(2,1)S(1)} %get-tuple-element.34, bf16[96,2,512]{2,1,0:T(2,128)(2,1)S(1)} %slice.271, f32[512]{0:T(512)S(1)} %copy-done.12, ...), kind=kOutput, calls=%fused_computation.61 | convolution fusion | flops 406388736 | bytes 4655104 | tf_op jit(solution)/shard_map/dot_general | solution.py:184
  (75 shorter events, 6.6 us)
Async XLA Ops:
  0.6 129.3 %copy-start = (bf16[256,512]{1,0:T(8,128)(2,1)S(1)}, bf16[256,512]{1,0:T(8,128)(2,1)}, u32[]{:S(2)}) copy-start(bf16[256,512]{1,0:T(8,128)(2,1)} %param.26) | copy-start | bytes 786436
  0.6 30.1 %copy-start.1 = (f32[96,10,512]{2,0,1:T(8,128)S(1)}, f32[96,10,512]{2,0,1:T(8,128)}, u32[]{:S(2)}) copy-start(f32[96,10,512]{2,0,1:T(8,128)} %param.19) | copy-start | bytes 5898244
  52.0 11.1 %slice-start = ((s8[16777216]{0:T(1024)(128)(4,1)}), s8[4194304]{0:T(1024)(128)(4,1)S(1)}, s32[]{:S(2)}) async-start(s8[16777216]{0:T(1024)(128)(4,1)} %bitcast.110), calls=%async_computation | async-start | bytes 8388608
  54.8 8.4 %slice-start.1 = ((s8[16777216]{0:T(1024)(128)(4,1)}), s8[4194304]{0:T(1024)(128)(4,1)S(1)}, s32[]{:S(2)}) async-start(s8[16777216]{0:T(1024)(128)(4,1)} %bitcast.110), calls=%async_computation.1 | async-start | bytes 8388608
  57.6 5.6 %slice-start.2 = ((s8[16777216]{0:T(1024)(128)(4,1)}), s8[4194304]{0:T(1024)(128)(4,1)S(1)}, s32[]{:S(2)}) async-start(s8[16777216]{0:T(1024)(128)(4,1)} %bitcast.110), calls=%async_computation.2 | async-start | bytes 8388608
  60.4 2.8 %slice-start.3 = ((s8[16777216]{0:T(1024)(128)(4,1)}), s8[4194304]{0:T(1024)(128)(4,1)S(1)}, s32[]{:S(2)}) async-start(s8[16777216]{0:T(1024)(128)(4,1)} %bitcast.110), calls=%async_computation.3 | async-start | bytes 8388608
  107.4 1.9 %copy-start.2 = (f32[32,10,512]{2,1,0:T(8,128)S(1)}, f32[32,10,512]{2,1,0:T(8,128)}, u32[]{:S(2)}) copy-start(f32[32,10,512]{2,1,0:T(8,128)} %reshape.264) | copy-start | bytes 1966084
  115.8 1.1 copy-start.4
  115.8 1.3 copy-start.5
  115.8 1.4 %copy-start.6 = (bf16[96,4,1,512]{3,1,0,2:T(4,128)(2,1)S(1)}, bf16[96,4,1,512]{3,1,0,2:T(4,128)(2,1)}, u32[]{:S(2)}) copy-start(bf16[96,4,1,512]{3,1,0,2:T(4,128)(2,1)} %gather.27) | copy-start | bytes 1179652
  117.6 0.7 copy-start.10
  118.3 2.0 %copy-start.3 = (bf16[7,512,512]{2,1,0:T(8,128)(2,1)S(1)}, bf16[7,512,512]{2,1,0:T(8,128)(2,1)}, u32[]{:S(2)}) copy-start(bf16[7,512,512]{2,1,0:T(8,128)(2,1)} %param.22) | copy-start | bytes 11010052
  124.0 0.7 copy-start.9
  125.7 0.9 copy-start.7
  126.6 1.5 %copy-start.8 = (bf16[3,512,256]{2,1,0:T(8,128)(2,1)S(1)}, bf16[3,512,256]{2,1,0:T(8,128)(2,1)}, u32[]{:S(2)}) copy-start(bf16[3,512,256]{2,1,0:T(8,128)(2,1)} %param.24) | copy-start | bytes 2359300
  126.6 1.5 %copy-start.11 = (f32[256]{0:T(256)S(1)}, f32[256]{0:T(256)}, u32[]{:S(2)}) copy-start(f32[256]{0:T(256)} %param.25) | copy-start | bytes 3076
  128.5 1.5 %copy-start.12 = (f32[512]{0:T(512)S(1)}, f32[512]{0:T(512)}, u32[]{:S(2)}) copy-start(f32[512]{0:T(512)} %param.27) | copy-start | bytes 6148

commit v4 on v2

--- a/solution.py
+++ b/solution.py
@@ -1,6 +1,8 @@
 import jax
 import jax.numpy as jnp
 from jax import lax
+from jax.experimental import pallas as pl
+from jax.experimental.pallas import tpu as pltpu
 from jax.sharding import PartitionSpec as P
 
 FRAMES = 4
@@ -48,6 +50,88 @@
     hit = flags[..., None, :] & (ranks[..., None, :] == spots[:, None])
     picked = jnp.sum(jnp.where(hit, values[..., None, :], 0), axis=-1)
     return (picked, jnp.any(hit, axis=-1))
+
+
+def exchange(items, collective_id):
+    per_group = lax.axis_size("dev")
+    count = len(items)
+
+    def kernel(*refs):
+        x_refs = refs[:count]
+        o_refs = refs[count : 2 * count]
+        send_sems = refs[2 * count : 3 * count]
+        recv_sems = refs[3 * count : 4 * count]
+        own_sem = refs[4 * count]
+        group = lax.axis_index("grp")
+        dev = lax.axis_index("dev")
+        widest = max(blocks.shape[0] for blocks, _ in items)
+        whole_any = any(whole for _, whole in items)
+        me_all = group * per_group + dev
+
+        def place(whole):
+            if whole:
+                return me_all, lambda peer: (peer // per_group, peer % per_group)
+            return dev, lambda peer: (group, peer)
+
+        barrier = pltpu.get_barrier_semaphore()
+        greet_me, greet_device = place(whole_any)
+
+        def greet(offset, carry):
+            peer = lax.rem(greet_me + offset, widest)
+            pl.semaphore_signal(barrier, inc=1, device_id=greet_device(peer), device_id_type=pl.DeviceIdType.MESH)
+            return carry
+
+        lax.fori_loop(1, widest, greet, 0)
+        pl.semaphore_wait(barrier, widest - 1)
+
+        def copy(index, peer, slot):
+            whole = items[index][1]
+            _, device = place(whole)
+            return pltpu.make_async_remote_copy(
+                src_ref=x_refs[index].at[peer],
+                dst_ref=o_refs[index].at[slot],
+                send_sem=send_sems[index].at[peer],
+                recv_sem=recv_sems[index].at[slot],
+                device_id=device(peer),
+                device_id_type=pl.DeviceIdType.MESH,
+            )
+
+        for index, (blocks, whole) in enumerate(items):
+            peers = blocks.shape[0]
+            me, _ = place(whole)
+
+            def send(offset, carry, index=index, peers=peers, me=me):
+                copy(index, lax.rem(me + offset, peers), me).start()
+                return carry
+
+            lax.fori_loop(1, peers, send, 0)
+        for index, (blocks, whole) in enumerate(items):
+            me, _ = place(whole)
+            own = pltpu.make_async_copy(x_refs[index].at[me], o_refs[index].at[me], own_sem)
+            own.start()
+            own.wait()
+        for index, (blocks, whole) in enumerate(items):
+            peers = blocks.shape[0]
+            me, _ = place(whole)
+
+            def finish(offset, carry, index=index, peers=peers, me=me):
+                copy(index, lax.rem(me + offset, peers), me).wait_send()
+                source = lax.rem(me + peers - offset, peers)
+                copy(index, source, source).wait_recv()
+                return carry
+
+            lax.fori_loop(1, peers, finish, 0)
+
+    arrays = [blocks for blocks, _ in items]
+    return pl.pallas_call(
+        kernel,
+        out_shape=[jax.ShapeDtypeStruct(a.shape, a.dtype) for a in arrays],
+        in_specs=[pl.BlockSpec(memory_space=pl.ANY)] * count,
+        out_specs=[pl.BlockSpec(memory_space=pl.ANY)] * count,
+        scratch_shapes=[pltpu.SemaphoreType.DMA((a.shape[0],)) for a in arrays] * 2
+        + [pltpu.SemaphoreType.DMA(())],
+        compiler_params=pltpu.CompilerParams(collective_id=collective_id, has_side_effects=True),
+    )(*arrays)
 
 
 def decode(
@@ -166,18 +250,25 @@
     request = jnp.concatenate(
         [code_request.reshape(devices_all, most), state_request.reshape(devices_all, 1)], axis=1
     )
-    asked = lax.all_to_all(request, ("grp", "dev"), 0, 0, tiled=True)
-
-    local_rows = embed_codes(codes, code_table).reshape(conv_count, -1)
-    answer = jnp.take(local_rows, jnp.clip(asked[:, :most].reshape(-1), 0, conv_count - 1), axis=0)
-    answered = lax.all_to_all(
-        answer.reshape(devices_all, most, -1), ("grp", "dev"), 0, 0, tiled=True
-    ).reshape(devices_all * most, -1)
-    routed = jnp.take(answered, key, axis=0).reshape(conv_count, FRAMES, -1)
-
+    lanes = 128
+    padded = jnp.zeros((devices_all, 1, lanes), jnp.int32).at[:, 0, : most + 1].set(request)
+    (asked,) = exchange([(padded, True)], 0)
+    asked = asked[:, 0, : most + 1]
+
+    answer = jnp.take(codes, jnp.clip(asked[:, :most].reshape(-1), 0, conv_count - 1), axis=0)
+    answer = jnp.zeros((devices_all, 1, lanes), jnp.int32).at[:, 0, : answer.size // devices_all].set(
+        answer.reshape(devices_all, -1)
+    )
     state_asked = lax.dynamic_slice_in_dim(asked[:, most], group_first, per_group)
     leaving = jnp.take(states, jnp.clip(state_asked, 0, conv_count - 1), axis=0)
-    arrived = lax.all_to_all(leaving, "dev", 0, 0, tiled=True)
+    answered, arrived = exchange(
+        [(answer, True), (leaving.reshape(per_group, -1, lanes), False)], 1
+    )
+    code_width = codes.shape[1]
+    answered = answered[:, 0, : most * code_width].reshape(devices_all * most, code_width)
+    my_codes = jnp.take(answered, key, axis=0)
+    routed = embed_codes(my_codes, code_table)
+    arrived = arrived.reshape(leaving.shape)
     brought = jnp.take(arrived, jnp.clip(source_dev, 0, per_group - 1), axis=0)
     carried = jnp.where(moved[:, None, None], brought, states)
     return decode(

time: 105 us -> 108 us (1.029)
  Pallas kernels: 0 us -> 41.6 us
  starting transfers between devices: 25.3 us -> 0 us
  waiting for transfers between devices: 20.1 us -> 0 us
  local copies, waits for them, and re-layouts: 21.5 us -> 24.6 us
  matrix products: 22.6 us -> 24.9 us
    pallas_call x0 -> x2, Pallas kernels: none -> 41.6 us  [exchange(): pl.pallas_call(kernel, out_shape=[jax.ShapeDtypeStruct(a.shape, a.dtype)...]
    all_to_all x3 -> x0, starting transfers between devices: 25.3 us -> none  [the longest x1 11.5 us: local(): asked = lax.all_to_all(request, ('grp', 'dev'), 0, 0, tiled=True)]
    all_to_all x3 -> x0, waiting for transfers between devices: 20.1 us -> none  [the longest x1 10.8 us: local(): arrived = lax.all_to_all(leaving, 'dev', 0, 0, tiled=True)]
    gather x4, local copies, waits for them, and re-layouts: 5.19 us -> 1.53 us  [the longest x2 0.81 us: local(): jnp.take(codes, jnp.clip(asked[:, :most].reshape(-1), 0, conv_count - 1),...]
    gather x1 -> x3, local copies, waits for them, and re-layouts: 1.51 us -> 4.19 us  [local(): leaving = jnp.take(states, jnp.clip(state_asked, 0, conv_count - 1), axis=0)]
    dot_general x8, matrix products: 12.5 us -> 15.1 us  [embed_codes(): jnp.dot(onehot, book_rows, preferred_element_type=jnp.float32)]
    convert_element_type x0 -> x2, local copies, waits for them, and re-layouts: none -> 2.21 us  [decode(): inputs = routed.astype(jnp.float32)]
    select_n x3 -> x4, other arithmetic: 2.06 us -> 0.24 us  [the longest x2 0.12 us: local(): my_codes = jnp.take(answered, key, axis=0)]
  transfers between devices with their start and end apart: 3 -> 0, of which waited for: 2 -> 0; matrix products, arithmetic and copies ran while one was open for 29% -> 0% of each run, Pallas kernels for 0% -> 0%
where the time goes in v4:
time: 108 us; the launch traced here: 107 us
  Pallas kernels  41.6 us (39%)
  matrix products  24.9 us (23%)
  local copies, waits for them, and re-layouts  24.6 us (23%)
  other arithmetic  14.7 us (14%)
  between operations  1.17 us (1%)
    pallas_call x2, Pallas kernels, exchange(): pl.pallas_call(kernel, out_shape=[jax.ShapeDtypeStruct(a.shape, a.dtype)...  41.6 us
    dot_general x8, matrix products, embed_codes(): jnp.dot(onehot, book_rows, preferred_element_type=jnp.float32)  15.1 us
    dot_general x7, matrix products, decode(): jnp.dot(window, conv_weight[tap_index], preferred_element_type=jnp.float32)  4.77 us
    gather x3, local copies, waits for them, and re-layouts, local(): leaving = jnp.take(states, jnp.clip(state_asked, 0, conv_count - 1), axis=0)  4.19 us
    unnamed x34, local copies, waits for them, and re-layouts  4.16 us
    another operation x1, other arithmetic  4.04 us
    dot_general x1, matrix products, decode(): jnp.dot(squeezed, res_out_weight, preferred_element_type=jnp.float32)  3.2 us
    gather x1, local copies, waits for them, and re-layouts, local(): brought = jnp.take(arrived, jnp.clip(source_dev, 0, per_group - 1), axis=0)  2.42 us

profile of v4, /device:TPU:1, one launch (start us, length us, event | category | flops | bytes accessed | tf_op | source)
XLA Modules:
  0.0 107.0 jit_solution(605315693904088306)
XLA Ops:
  0.7 0.8 fusion.118
  1.5 0.7 and_select_fusion.3
  2.5 0.7 compare_and_fusion.1
  3.3 0.9 fusion.125
  4.4 0.8 copy.86
  5.5 0.7 scatter.6.refs_0_
  6.2 20.5 %shard_map.140 = s32[128,1,128]{2,1,0:T(1,128)} custom-call(s32[128,1,128]{2,1,0:T(1,128)} %scatter.6.refs_0_), custom_call_target="tpu_custom_call" | custom-call | tf_op jit(solution)/shard_map/pallas_call | solution.py:126
  26.7 0.9 compare_and_fusion
  27.8 0.9 slice.274
  28.7 0.9 slice_clamp_fusion
  30.0 0.7 gather_fusion
  31.0 0.7 scatter.9.refs_0_
  31.6 1.5 %gather_fusion.1 = f32[32,10,512]{2,0,1:T(8,128)S(1)} fusion(f32[96,10,512]{2,0,1:T(8,128)S(1)} %copy-done.1, s32[1024]{0:T(1024)S(1)} %pad_clamp_fusion.2), kind=kCustom, calls=%fused_computation.1 | custom fusion | bytes 1310848 | tf_op jit(solution)/shard_map/jit(_take)/gather | solution.py:263
  33.1 1.4 %copy.89 = f32[32,10,512]{2,1,0:T(8,128)} copy(f32[32,10,512]{2,0,1:T(8,128)S(1)} %gather_fusion.1) | data formatting | bytes 1310720 | tf_op jit(solution)/shard_map/jit(_take)/gather | solution.py:263
  34.5 1.3 %gather.25 = f32[32,40,128]{2,1,0:T(8,128)S(1)} reshape(f32[32,10,512]{2,1,0:T(8,128)} %copy.89) | data formatting | bytes 1310720 | tf_op jit(solution)/shard_map/jit(_take)/gather | solution.py:263
  35.8 0.9 broadcast_select_fusion.refs_1_
  36.8 21.2 %shard_map.141 = (s32[128,1,128]{2,1,0:T(1,128)}, f32[32,40,128]{2,1,0:T(8,128)}) custom-call(s32[128,1,128]{2,1,0:T(1,128)} %scatter.9.refs_0_, f32[32,40,128]{2,1,0:T(8,128)} %broadcast_select_fusion.refs_1_), custom_call_target="tpu_custom_call" | custom-call | tf_op jit(solution)/shard_map/pallas_call | solution.py:126
  58.0 1.0 slice_reduce_fusion.8
  59.1 0.6 gather_fusion.2
  59.9 0.9 slice_reduce_fusion
  60.8 2.8 %fusion = f32[384,512]{1,0:T(8,128)S(1)} fusion(bf16[16384,512]{1,0:T(8,128)(2,1)} %param.18, s32[384]{0:T(512)S(1)} %get-tuple-element.39), kind=kOutput, calls=%fused_computation.15 | convolution fusion | flops 806092800 | bytes 2885120 | tf_op jit(solution)/shard_map/dot_general | solution.py:22
  63.6 2.8 %fusion.46 = f32[384,512]{1,0:T(8,128)S(1)} fusion(f32[384,512]{1,0:T(8,128)S(1)} %fusion, bf16[16384,512]{1,0:T(8,128)(2,1)} %param.18, s32[384]{0:T(512)S(1)} %get-tuple-element.38), kind=kOutput, calls=%fused_computation.71 | convolution fusion | flops 806289408 | bytes 3671552 | tf_op jit(solution)/shard_map/dot_general | solution.py:22
  66.4 2.8 %fusion.43 = f32[384,512]{1,0:T(8,128)S(1)} fusion(f32[384,512]{1,0:T(8,128)S(1)} %fusion.46, bf16[16384,512]{1,0:T(8,128)(2,1)} %param.18, s32[384]{0:T(512)S(1)} %get-tuple-element.37), kind=kOutput, calls=%fused_computation.70 | convolution fusion | flops 806289408 | bytes 3671552 | tf_op jit(solution)/shard_map/dot_general | solution.py:22
  69.1 2.8 %fusion.40 = f32[384,512]{1,0:T(8,128)S(1)} fusion(f32[384,512]{1,0:T(8,128)S(1)} %fusion.43, bf16[16384,512]{1,0:T(8,128)(2,1)} %param.18, s32[384]{0:T(512)S(1)} %get-tuple-element.36), kind=kOutput, calls=%fused_computation.69 | convolution fusion | flops 806289408 | bytes 3671552 | tf_op jit(solution)/shard_map/dot_general | solution.py:22
  72.0 1.0 fusion.37
  73.0 1.0 fusion.34
  74.0 1.0 fusion.31
  75.0 1.0 fusion.52
  76.1 1.1 %reshape.319 = f32[96,4,512]{2,1,0:T(4,128)} reshape(f32[384,512]{1,0:T(8,128)S(1)} %fusion.52) | data formatting | bytes 1572864 | tf_op jit(solution)/shard_map/convert_element_type | solution.py:151
  77.2 1.1 %reshape.318 = f32[96,4,1,512]{3,1,0,2:T(4,128)} reshape(f32[384,512]{1,0:T(8,128)S(1)} %fusion.52) | data formatting | bytes 1572864 | tf_op jit(solution)/shard_map/convert_element_type | solution.py:151
  78.3 1.4 %copy_multiply_fusion.1 = (f32[96,4,512]{2,0,1:T(8,128)S(1)}, f32[96,4,512]{2,0,1:T(8,128)S(1)}) fusion(f32[96,4,512]{2,1,0:T(4,128)} %reshape.319, f32[512]{0:T(512)S(1)} %bitcast.101, f32[512]{0:T(512)S(1)} %bitcast.102), kind=kLoop, calls=%fused_computation.111 | loop fusion | flops 393216 | bytes 2363392 | tf_op jit(solution)/shard_map/mul | solution.py:154
  79.7 0.7 slice.302
  80.4 1.1 %slice_bitcast_fusion = (f32[96,3,1,512]{3,0,1,2:T(8,128)}, f32[96,3,1,512]{3,0,1,2:T(8,128)}) fusion(f32[96,4,512]{2,0,1:T(8,128)S(1)} %get-tuple-element.60, f32[96,4,512]{2,0,1:T(8,128)S(1)} %get-tuple-element.59), kind=kLoop, calls=%fused_computation.113 | loop fusion | bytes 2359296 | tf_op jit(solution)/shard_map/concatenate | solution.py:157
  81.5 1.2 %reshape.304 = f32[32,10,512]{2,1,0:T(8,128)S(1)} reshape(f32[32,40,128]{2,1,0:T(8,128)} %get-tuple-element.29) | data formatting | bytes 1310720 | tf_op jit(solution)/shard_map/reshape | solution.py:271
  82.7 2.4 %gather_fusion.3 = f32[96,10,512]{2,1,0:T(8,128)} fusion(f32[32,10,512]{2,1,0:T(8,128)S(1)} %reshape.304, s32[1024]{0:T(1024)S(1)} %pad_clamp_fusion), kind=kCustom, calls=%fused_computation.3 | custom fusion | bytes 3932544 | tf_op jit(solution)/shard_map/jit(_take)/gather | solution.py:272
  85.2 4.0 %fusion.124 = (bf16[96,10,512]{2,1,0:T(8,128)(2,1)S(1)}, f32[96,10,512]{2,1,0:T(8,128)S(1)}) fusion(f32[96,10,512]{2,0,1:T(8,128)S(1)} %copy-done.1, f32[96,10,512]{2,1,0:T(8,128)} %gather_fusion.3, pred[96]{0:T(512)(128)(4,1)S(1)} %get-tuple-element.42, pred[96]{0:T(512)(128)(4,1)S(1)} %subtract_compare_fusion), kind=kLoop, calls=%fused_computation.188 | loop fusion | flops 1474560 | bytes 6881472 | tf_op jit(solution)/shard_map/convert.7
  92.6 1.7 %copy-done.2 = bf16[7,512,512]{2,1,0:T(8,128)(2,1)S(1)} copy-done((bf16[7,512,512]{2,1,0:T(8,128)(2,1)S(1)}, bf16[7,512,512]{2,1,0:T(8,128)(2,1)}, u32[]{:S(2)}) %copy-start.2) | copy-done | bytes 3670040
  94.3 0.6 fusion.82
  95.3 0.6 fusion.80
  96.0 0.6 fusion.78
  96.6 0.6 fusion.76
  97.2 0.7 fusion.74
  97.9 0.6 fusion.72
  98.5 1.0 add_add_fusion
  99.6 0.6 fusion.17
  100.5 1.5 %pad_maximum_fusion = f32[96,10,512]{2,0,1:T(8,128)} fusion(f32[96,2,512]{2,0,1:T(8,128)S(1)} %copy.107, f32[96,6,512]{2,0,1:T(8,128)S(1)} %slice_convert_fusion, f32[96,1,512]{2,0,1:T(8,128)S(1)} %copy-done.6, f32[96,1,512]{2,0,1:T(8,128)S(1)} %slice.301), kind=kLoop, calls=%fused_computation.38 | loop fusion | flops 1474560 | bytes 3932160 | tf_op jit(solution)/shard_map/concatenate | solution.py:193
  102.4 1.5 %convolution_add_fusion.1 = f32[768,256]{1,0:T(8,128)} fusion(f32[768,256]{1,0:T(8,128)S(1)} %convolution_add_fusion.2, bf16[96,2,512]{2,1,0:T(2,128)(2,1)S(1)} %slice.298, bf16[96,8,512]{2,1,0:T(8,128)(2,1)S(1)} %get-tuple-element.50, bf16[3,512,256]{2,1,0:T(8,128)(2,1)S(1)} %copy-done.7), kind=kOutput, calls=%fused_computation.63 | convolution fusion | flops 203096064 | bytes 2818048 | tf_op jit(solution)/shard_map/dot_general | solution.py:183
  103.8 3.2 %fusion.27 = bf16[96,8,512]{2,1,0:T(8,128)(2,1)} fusion(f32[768,512]{1,0:T(8,128)S(1)} %add_add_fusion, bf16[256,512]{1,0:T(8,128)(2,1)S(1)} %copy-done, f32[768,256]{1,0:T(8,128)} %convolution_add_fusion.1, bf16[96,8,512]{2,1,0:T(8,128)(2,1)S(1)} %get-tuple-element.50, bf16[96,2,512]{2,1,0:T(2,128)(2,1)S(1)} %slice.298, f32[512]{0:T(512)S(1)} %copy-done.11, ...), kind=kOutput, calls=%fused_computation.61 | convolution fusion | flops 406388736 | bytes 4655104 | tf_op jit(solution)/shard_map/dot_general | solution.py:189
  (77 shorter events, 6.6 us)
Async XLA Ops:
  0.6 103.2 %copy-start = (bf16[256,512]{1,0:T(8,128)(2,1)S(1)}, bf16[256,512]{1,0:T(8,128)(2,1)}, u32[]{:S(2)}) copy-start(bf16[256,512]{1,0:T(8,128)(2,1)} %param.28) | copy-start | bytes 786436
  0.6 31.0 %copy-start.1 = (f32[96,10,512]{2,0,1:T(8,128)S(1)}, f32[96,10,512]{2,0,1:T(8,128)}, u32[]{:S(2)}) copy-start(f32[96,10,512]{2,0,1:T(8,128)} %param.21) | copy-start | bytes 5898244
  60.8 11.1 %slice-start = ((s8[16777216]{0:T(1024)(128)(4,1)}), s8[4194304]{0:T(1024)(128)(4,1)S(1)}, s32[]{:S(2)}) async-start(s8[16777216]{0:T(1024)(128)(4,1)} %bitcast.104), calls=%async_computation | async-start | bytes 8388608
  63.6 8.4 %slice-start.1 = ((s8[16777216]{0:T(1024)(128)(4,1)}), s8[4194304]{0:T(1024)(128)(4,1)S(1)}, s32[]{:S(2)}) async-start(s8[16777216]{0:T(1024)(128)(4,1)} %bitcast.104), calls=%async_computation.1 | async-start | bytes 8388608
  66.3 5.6 %slice-start.2 = ((s8[16777216]{0:T(1024)(128)(4,1)}), s8[4194304]{0:T(1024)(128)(4,1)S(1)}, s32[]{:S(2)}) async-start(s8[16777216]{0:T(1024)(128)(4,1)} %bitcast.104), calls=%async_computation.2 | async-start | bytes 8388608
  69.1 2.8 %slice-start.3 = ((s8[16777216]{0:T(1024)(128)(4,1)}), s8[4194304]{0:T(1024)(128)(4,1)S(1)}, s32[]{:S(2)}) async-start(s8[16777216]{0:T(1024)(128)(4,1)} %bitcast.104), calls=%async_computation.3 | async-start | bytes 8388608
  89.4 1.1 %copy-start.3 = (f32[96,4,1,512]{3,1,0,2:T(4,128)S(1)}, f32[96,4,1,512]{3,1,0,2:T(4,128)}, u32[]{:S(2)}) copy-start(f32[96,4,1,512]{3,1,0,2:T(4,128)} %reshape.318) | copy-start | bytes 2359300
  89.5 1.3 %copy-start.4 = (f32[96,3,1,512]{3,0,1,2:T(8,128)S(1)}, f32[96,3,1,512]{3,0,1,2:T(8,128)}, u32[]{:S(2)}) copy-start(f32[96,3,1,512]{3,0,1,2:T(8,128)} %get-tuple-element.67) | copy-start | bytes 1769476
  89.5 1.5 %copy-start.5 = (f32[96,3,1,512]{3,0,1,2:T(8,128)S(1)}, f32[96,3,1,512]{3,0,1,2:T(8,128)}, u32[]{:S(2)}) copy-start(f32[96,3,1,512]{3,0,1,2:T(8,128)} %get-tuple-element.68) | copy-start | bytes 1769476
  91.5 0.7 copy-start.9
  92.2 2.0 %copy-start.2 = (bf16[7,512,512]{2,1,0:T(8,128)(2,1)S(1)}, bf16[7,512,512]{2,1,0:T(8,128)(2,1)}, u32[]{:S(2)}) copy-start(bf16[7,512,512]{2,1,0:T(8,128)(2,1)} %param.24) | copy-start | bytes 11010052
  97.9 0.7 copy-start.8
  99.5 0.9 copy-start.6
  100.5 1.5 %copy-start.7 = (bf16[3,512,256]{2,1,0:T(8,128)(2,1)S(1)}, bf16[3,512,256]{2,1,0:T(8,128)(2,1)}, u32[]{:S(2)}) copy-start(bf16[3,512,256]{2,1,0:T(8,128)(2,1)} %param.26) | copy-start | bytes 2359300
  100.5 1.5 %copy-start.10 = (f32[256]{0:T(256)S(1)}, f32[256]{0:T(256)}, u32[]{:S(2)}) copy-start(f32[256]{0:T(256)} %param.27) | copy-start | bytes 3076
  102.3 1.5 %copy-start.11 = (f32[512]{0:T(512)S(1)}, f32[512]{0:T(512)}, u32[]{:S(2)}) copy-start(f32[512]{0:T(512)} %param.29) | copy-start | bytes 6148

commit v5 on v2

--- a/solution.py
+++ b/solution.py
@@ -1,6 +1,8 @@
 import jax
 import jax.numpy as jnp
 from jax import lax
+from jax.experimental import pallas as pl
+from jax.experimental.pallas import tpu as pltpu
 from jax.sharding import PartitionSpec as P
 
 FRAMES = 4
@@ -18,6 +20,7 @@
         onehot = (grouped[:, book_index][:, None] == entries[None, :]).astype(jnp.bfloat16)
         book_rows = code_table[book_index * book_size : (book_index + 1) * book_size]
         summed = summed + jnp.dot(onehot, book_rows, preferred_element_type=jnp.float32)
+    summed = lax.reduce_precision(summed, exponent_bits=8, mantissa_bits=7)
     return summed.astype(jnp.bfloat16).reshape(row_count, FRAMES, code_table.shape[1])
 
 
@@ -48,6 +51,140 @@
     hit = flags[..., None, :] & (ranks[..., None, :] == spots[:, None])
     picked = jnp.sum(jnp.where(hit, values[..., None, :], 0), axis=-1)
     return (picked, jnp.any(hit, axis=-1))
+
+
+def exchange(items, collective_id):
+    groups = lax.axis_size("grp")
+    per_group = lax.axis_size("dev")
+    count = len(items)
+    shapes = []
+    for blocks, whole in items:
+        if whole:
+            shapes.append(jax.ShapeDtypeStruct((groups, per_group) + blocks.shape[1:], blocks.dtype))
+        else:
+            shapes.append(jax.ShapeDtypeStruct(blocks.shape, blocks.dtype))
+    wholes = [index for index, (_, whole) in enumerate(items) if whole]
+
+    def kernel(*refs):
+        x_refs = refs[:count]
+        o_refs = refs[count : 2 * count]
+        mid_refs = dict(zip(wholes, refs[2 * count : 2 * count + len(wholes)]))
+        sems = refs[2 * count + len(wholes) :]
+        first_send, first_recv, second_send, second_recv, own_sem = sems
+        group = lax.axis_index("grp")
+        dev = lax.axis_index("dev")
+        barrier = pltpu.get_barrier_semaphore()
+        across = len(wholes) > 0
+
+        if across:
+            def greet_group(offset, carry):
+                peer = lax.rem(group + offset, groups)
+                pl.semaphore_signal(barrier, inc=1, device_id=(peer, dev), device_id_type=pl.DeviceIdType.MESH)
+                return carry
+
+            lax.fori_loop(1, groups, greet_group, 0)
+
+        def greet_dev(offset, carry):
+            peer = lax.rem(dev + offset, per_group)
+            pl.semaphore_signal(barrier, inc=1, device_id=(group, peer), device_id_type=pl.DeviceIdType.MESH)
+            return carry
+
+        lax.fori_loop(1, per_group, greet_dev, 0)
+        pl.semaphore_wait(barrier, (groups - 1 if across else 0) + per_group - 1)
+
+        def hop_one(slot, index, peer, place):
+            return pltpu.make_async_remote_copy(
+                src_ref=x_refs[index].at[pl.ds(peer * per_group, per_group)],
+                dst_ref=mid_refs[index].at[place],
+                send_sem=first_send.at[slot, peer],
+                recv_sem=first_recv.at[slot, place],
+                device_id=(peer, dev),
+                device_id_type=pl.DeviceIdType.MESH,
+            )
+
+        def hop_two(index, peer, place):
+            if items[index][1]:
+                source = mid_refs[index].at[:, peer]
+                target = o_refs[index].at[:, place]
+            else:
+                source = x_refs[index].at[peer]
+                target = o_refs[index].at[place]
+            return pltpu.make_async_remote_copy(
+                src_ref=source,
+                dst_ref=target,
+                send_sem=second_send.at[index, peer],
+                recv_sem=second_recv.at[index, place],
+                device_id=(group, peer),
+                device_id_type=pl.DeviceIdType.MESH,
+            )
+
+        for slot, index in enumerate(wholes):
+            def send_one(offset, carry, slot=slot, index=index):
+                hop_one(slot, index, lax.rem(group + offset, groups), group).start()
+                return carry
+
+            lax.fori_loop(1, groups, send_one, 0)
+        for index, (_, whole) in enumerate(items):
+            if not whole:
+                def send_group(offset, carry, index=index):
+                    hop_two(index, lax.rem(dev + offset, per_group), dev).start()
+                    return carry
+
+                lax.fori_loop(1, per_group, send_group, 0)
+        for slot, index in enumerate(wholes):
+            own = pltpu.make_async_copy(
+                x_refs[index].at[pl.ds(group * per_group, per_group)], mid_refs[index].at[group], own_sem
+            )
+            own.start()
+            own.wait()
+
+            def finish_one(offset, carry, slot=slot, index=index):
+                hop_one(slot, index, lax.rem(group + offset, groups), group).wait_send()
+                source = lax.rem(group + groups - offset, groups)
+                hop_one(slot, index, source, source).wait_recv()
+                return carry
+
+            lax.fori_loop(1, groups, finish_one, 0)
+
+            def send_two(offset, carry, index=index):
+                hop_two(index, lax.rem(dev + offset, per_group), dev).start()
+                return carry
+
+            lax.fori_loop(1, per_group, send_two, 0)
+        for index, (_, whole) in enumerate(items):
+            if whole:
+                own = pltpu.make_async_copy(mid_refs[index].at[:, dev], o_refs[index].at[:, dev], own_sem)
+            else:
+                own = pltpu.make_async_copy(x_refs[index].at[dev], o_refs[index].at[dev], own_sem)
+            own.start()
+            own.wait()
+
+            def finish_two(offset, carry, index=index):
+                hop_two(index, lax.rem(dev + offset, per_group), dev).wait_send()
+                source = lax.rem(dev + per_group - offset, per_group)
+                hop_two(index, source, source).wait_recv()
+                return carry
+
+            lax.fori_loop(1, per_group, finish_two, 0)
+
+    mids = [shapes[index] for index in wholes]
+    results = pl.pallas_call(
+        kernel,
+        out_shape=shapes + mids,
+        in_specs=[pl.BlockSpec(memory_space=pl.ANY)] * count,
+        out_specs=[pl.BlockSpec(memory_space=pl.ANY)] * (count + len(wholes)),
+        scratch_shapes=[
+            pltpu.SemaphoreType.DMA((max(len(wholes), 1), groups)),
+            pltpu.SemaphoreType.DMA((max(len(wholes), 1), groups)),
+            pltpu.SemaphoreType.DMA((count, per_group)),
+            pltpu.SemaphoreType.DMA((count, per_group)),
+            pltpu.SemaphoreType.DMA(()),
+        ],
+        compiler_params=pltpu.CompilerParams(collective_id=collective_id, has_side_effects=True),
+    )(*[blocks for blocks, _ in items])
+    return [
+        result.reshape(blocks.shape) for result, (blocks, _) in zip(results[:count], items)
+    ]
 
 
 def decode(
@@ -166,18 +303,25 @@
     request = jnp.concatenate(
         [code_request.reshape(devices_all, most), state_request.reshape(devices_all, 1)], axis=1
     )
-    asked = lax.all_to_all(request, ("grp", "dev"), 0, 0, tiled=True)
-
-    local_rows = embed_codes(codes, code_table).reshape(conv_count, -1)
-    answer = jnp.take(local_rows, jnp.clip(asked[:, :most].reshape(-1), 0, conv_count - 1), axis=0)
-    answered = lax.all_to_all(
-        answer.reshape(devices_all, most, -1), ("grp", "dev"), 0, 0, tiled=True
-    ).reshape(devices_all * most, -1)
-    routed = jnp.take(answered, key, axis=0).reshape(conv_count, FRAMES, -1)
-
+    lanes = 128
+    padded = jnp.zeros((devices_all, 1, lanes), jnp.int32).at[:, 0, : most + 1].set(request)
+    (asked,) = exchange([(padded, True)], 0)
+    asked = asked[:, 0, : most + 1]
+
+    answer = jnp.take(codes, jnp.clip(asked[:, :most].reshape(-1), 0, conv_count - 1), axis=0)
+    answer = jnp.zeros((devices_all, 1, lanes), jnp.int32).at[:, 0, : answer.size // devices_all].set(
+        answer.reshape(devices_all, -1)
+    )
     state_asked = lax.dynamic_slice_in_dim(asked[:, most], group_first, per_group)
     leaving = jnp.take(states, jnp.clip(state_asked, 0, conv_count - 1), axis=0)
-    arrived = lax.all_to_all(leaving, "dev", 0, 0, tiled=True)
+    answered, arrived = exchange(
+        [(answer, True), (leaving.reshape(per_group, -1, lanes), False)], 1
+    )
+    code_width = codes.shape[1]
+    answered = answered[:, 0, : most * code_width].reshape(devices_all * most, code_width)
+    my_codes = jnp.take(answered, key, axis=0)
+    routed = embed_codes(my_codes, code_table)
+    arrived = arrived.reshape(leaving.shape)
     brought = jnp.take(arrived, jnp.clip(source_dev, 0, per_group - 1), axis=0)
     carried = jnp.where(moved[:, None, None], brought, states)
     return decode(

time: 105 us -> 101 us (0.962)
  Pallas kernels: 0 us -> 36.9 us
  starting transfers between devices: 25.3 us -> 0 us
  waiting for transfers between devices: 20.1 us -> 0 us
  local copies, waits for them, and re-layouts: 21.5 us -> 24.4 us
  matrix products: 22.6 us -> 25.1 us
  other arithmetic: 14.1 us -> 13 us
    pallas_call x0 -> x2, Pallas kernels: none -> 36.9 us  [exchange(): pl.pallas_call(kernel, out_shape=shapes + mids, in_specs=[pl.BlockSpec(me...]
    all_to_all x3 -> x0, starting transfers between devices: 25.3 us -> none  [the longest x1 11.5 us: local(): asked = lax.all_to_all(request, ('grp', 'dev'), 0, 0, tiled=True)]
    all_to_all x3 -> x0, waiting for transfers between devices: 20.1 us -> none  [the longest x1 10.8 us: local(): arrived = lax.all_to_all(leaving, 'dev', 0, 0, tiled=True)]
    gather x4, local copies, waits for them, and re-layouts: 5.19 us -> 1.53 us  [the longest x2 0.81 us: local(): jnp.take(codes, jnp.clip(asked[:, :most].reshape(-1), 0, conv_count - 1),...]
    gather x1 -> x3, local copies, waits for them, and re-layouts: 1.51 us -> 4.19 us  [local(): leaving = jnp.take(states, jnp.clip(state_asked, 0, conv_count - 1), axis=0)]
    dot_general x8, matrix products: 12.5 us -> 15.1 us  [embed_codes(): jnp.dot(onehot, book_rows, preferred_element_type=jnp.float32)]
    convert_element_type x0 -> x2, local copies, waits for them, and re-layouts: none -> 2.21 us  [decode(): inputs = routed.astype(jnp.float32)]
    select_n x3 -> x4, other arithmetic: 2.06 us -> 0.24 us  [the longest x2 0.12 us: local(): my_codes = jnp.take(answered, key, axis=0)]
  transfers between devices with their start and end apart: 3 -> 0, of which waited for: 2 -> 0; matrix products, arithmetic and copies ran while one was open for 29% -> 0% of each run, Pallas kernels for 0% -> 0%
where the time goes in v5:
time: 101 us
  Pallas kernels  36.9 us (37%)
  matrix products  25.1 us (25%)
  local copies, waits for them, and re-layouts  24.4 us (24%)
  other arithmetic  13 us (13%)
  between operations  1.2 us (1%)
    pallas_call x2, Pallas kernels, exchange(): pl.pallas_call(kernel, out_shape=shapes + mids, in_specs=[pl.BlockSpec(me...  36.9 us
    dot_general x8, matrix products, embed_codes(): jnp.dot(onehot, book_rows, preferred_element_type=jnp.float32)  15.1 us
    unnamed x37, local copies, waits for them, and re-layouts  5.03 us
    dot_general x7, matrix products, decode(): jnp.dot(window, conv_weight[tap_index], preferred_element_type=jnp.float32)  4.8 us
    gather x3, local copies, waits for them, and re-layouts, local(): leaving = jnp.take(states, jnp.clip(state_asked, 0, conv_count - 1), axis=0)  4.19 us
    another operation x1, other arithmetic  4.04 us
    dot_general x1, matrix products, decode(): jnp.dot(squeezed, res_out_weight, preferred_element_type=jnp.float32)  3.29 us
    gather x1, local copies, waits for them, and re-layouts, local(): brought = jnp.take(arrived, jnp.clip(source_dev, 0, per_group - 1), axis=0)  2.4 us

profile of v5, /device:TPU:1, one launch (start us, length us, event | category | flops | bytes accessed | tf_op | source)
XLA Modules:
  0.0 100.6 jit_solution(17507904946013827824)
XLA Ops:
  0.7 0.8 fusion.120
  1.5 0.7 and_select_fusion.3
  2.5 0.7 compare_and_fusion
  3.3 0.9 fusion.127
  4.4 0.8 copy.92
  5.5 0.7 scatter.6.refs_0_
  6.2 18.2 %shard_map.140 = (s32[4,32,1,128]{3,2,1,0:T(1,128)}, s32[4,32,1,128]{3,2,1,0:T(1,128)}) custom-call(s32[128,1,128]{2,1,0:T(1,128)} %scatter.6.refs_0_), custom_call_target="tpu_custom_call" | custom-call | tf_op jit(solution)/shard_map/pallas_call | solution.py:171
  24.4 0.9 copy.113
  25.9 0.7 gather_fusion
  26.8 0.7 scatter.9.refs_0_
  27.5 1.5 %gather_fusion.1 = f32[32,10,512]{2,0,1:T(8,128)S(1)} fusion(f32[96,10,512]{2,0,1:T(8,128)S(1)} %copy-done.1, s32[1024]{0:T(1024)S(1)} %pad_clamp_fusion.2), kind=kCustom, calls=%fused_computation.1 | custom fusion | bytes 1310848 | tf_op jit(solution)/shard_map/jit(_take)/gather | solution.py:316
  29.0 1.4 %copy.95 = f32[32,10,512]{2,1,0:T(8,128)} copy(f32[32,10,512]{2,0,1:T(8,128)S(1)} %gather_fusion.1) | data formatting | bytes 1310720 | tf_op jit(solution)/shard_map/jit(_take)/gather | solution.py:316
  30.4 1.3 %gather.25 = f32[32,40,128]{2,1,0:T(8,128)S(1)} reshape(f32[32,10,512]{2,1,0:T(8,128)} %copy.95) | data formatting | bytes 1310720 | tf_op jit(solution)/shard_map/jit(_take)/gather | solution.py:316
  31.7 0.9 broadcast_select_fusion.refs_1_
  32.6 18.7 %shard_map.141 = (s32[4,32,1,128]{3,2,1,0:T(1,128)}, f32[32,40,128]{2,1,0:T(8,128)}, s32[4,32,1,128]{3,2,1,0:T(1,128)}) custom-call(s32[128,1,128]{2,1,0:T(1,128)} %scatter.9.refs_0_, f32[32,40,128]{2,1,0:T(8,128)} %broadcast_select_fusion.refs_1_), custom_call_target="tpu_custom_call" | custom-call | tf_op jit(solution)/shard_map/pallas_call | solution.py:171
  51.4 0.9 reshape_squeeze.3
  52.3 0.6 gather_fusion.2
  53.2 0.9 slice_reduce_fusion
  54.0 2.8 %fusion = f32[384,512]{1,0:T(8,128)S(1)} fusion(bf16[16384,512]{1,0:T(8,128)(2,1)} %param.18, s32[384]{0:T(512)S(1)} %get-tuple-element.41), kind=kOutput, calls=%fused_computation.15 | convolution fusion | flops 806092800 | bytes 2885120 | tf_op jit(solution)/shard_map/dot_general | solution.py:22
  56.8 2.8 %fusion.49 = f32[384,512]{1,0:T(8,128)S(1)} fusion(f32[384,512]{1,0:T(8,128)S(1)} %fusion, bf16[16384,512]{1,0:T(8,128)(2,1)} %param.18, s32[384]{0:T(512)S(1)} %get-tuple-element.40), kind=kOutput, calls=%fused_computation.72 | convolution fusion | flops 806289408 | bytes 3671552 | tf_op jit(solution)/shard_map/dot_general | solution.py:22
  59.6 2.8 %fusion.46 = f32[384,512]{1,0:T(8,128)S(1)} fusion(f32[384,512]{1,0:T(8,128)S(1)} %fusion.49, bf16[16384,512]{1,0:T(8,128)(2,1)} %param.18, s32[384]{0:T(512)S(1)} %get-tuple-element.39), kind=kOutput, calls=%fused_computation.71 | convolution fusion | flops 806289408 | bytes 3671552 | tf_op jit(solution)/shard_map/dot_general | solution.py:22
  62.4 2.8 %fusion.43 = f32[384,512]{1,0:T(8,128)S(1)} fusion(f32[384,512]{1,0:T(8,128)S(1)} %fusion.46, bf16[16384,512]{1,0:T(8,128)(2,1)} %param.18, s32[384]{0:T(512)S(1)} %get-tuple-element.38), kind=kOutput, calls=%fused_computation.70 | convolution fusion | flops 806289408 | bytes 3671552 | tf_op jit(solution)/shard_map/dot_general | solution.py:22
  65.2 1.0 %fusion.40 = f32[384,512]{1,0:T(8,128)S(1)} fusion(f32[384,512]{1,0:T(8,128)S(1)} %fusion.43, bf16[16384,512]{1,0:T(8,128)(2,1)S(1)} %bitcast.116, s32[384]{0:T(512)S(1)} %get-tuple-element.37), kind=kOutput, calls=%fused_computation.69 | convolution fusion | flops 806289408 | bytes 3672064 | tf_op jit(solution)/shard_map/dot_general | solution.py:22
  66.2 1.0 %fusion.37 = f32[384,512]{1,0:T(8,128)S(1)} fusion(f32[384,512]{1,0:T(8,128)S(1)} %fusion.40, bf16[16384,512]{1,0:T(8,128)(2,1)S(1)} %bitcast.116, s32[384]{0:T(512)S(1)} %get-tuple-element.36), kind=kOutput, calls=%fused_computation.68 | convolution fusion | flops 806289408 | bytes 3672064 | tf_op jit(solution)/shard_map/dot_general | solution.py:22
  67.3 1.0 %fusion.34 = f32[384,512]{1,0:T(8,128)S(1)} fusion(f32[384,512]{1,0:T(8,128)S(1)} %fusion.37, bf16[16384,512]{1,0:T(8,128)(2,1)S(1)} %bitcast.116, s32[384]{0:T(512)S(1)} %get-tuple-element.35), kind=kOutput, calls=%fused_computation.67 | convolution fusion | flops 806289408 | bytes 3672064 | tf_op jit(solution)/shard_map/dot_general | solution.py:22
  68.3 1.0 %fusion.55 = f32[384,512]{1,0:T(8,128)S(1)} fusion(f32[384,512]{1,0:T(8,128)S(1)} %fusion.34, bf16[16384,512]{1,0:T(8,128)(2,1)S(1)} %bitcast.116, s32[384]{0:T(512)S(1)} %get-tuple-element.34), kind=kOutput, calls=%fused_computation.74 | convolution fusion | flops 806879232 | bytes 3672064 | tf_op jit(solution)/shard_map/dot_general | solution.py:22
  69.3 1.1 %reshape.327 = f32[96,4,512]{2,1,0:T(4,128)} reshape(f32[384,512]{1,0:T(8,128)S(1)} %fusion.55) | data formatting | bytes 1572864 | tf_op jit(solution)/shard_map/convert_element_type | solution.py:204
  70.4 1.1 %reshape.326 = f32[96,4,1,512]{3,1,0,2:T(4,128)} reshape(f32[384,512]{1,0:T(8,128)S(1)} %fusion.55) | data formatting | bytes 1572864 | tf_op jit(solution)/shard_map/convert_element_type | solution.py:204
  71.5 1.4 %copy_multiply_fusion.1 = (f32[96,4,512]{2,0,1:T(8,128)S(1)}, f32[96,4,512]{2,0,1:T(8,128)S(1)}) fusion(f32[96,4,512]{2,1,0:T(4,128)} %reshape.327, f32[512]{0:T(512)S(1)} %bitcast.108, f32[512]{0:T(512)S(1)} %bitcast.109), kind=kLoop, calls=%fused_computation.112 | loop fusion | flops 393216 | bytes 2363392 | tf_op jit(solution)/shard_map/mul | solution.py:207
  73.0 0.7 slice.302
  73.6 1.1 %slice_bitcast_fusion = (f32[96,3,1,512]{3,0,1,2:T(8,128)}, f32[96,3,1,512]{3,0,1,2:T(8,128)}) fusion(f32[96,4,512]{2,0,1:T(8,128)S(1)} %get-tuple-element.64, f32[96,4,512]{2,0,1:T(8,128)S(1)} %get-tuple-element.63), kind=kLoop, calls=%fused_computation.114 | loop fusion | bytes 2359296 | tf_op jit(solution)/shard_map/concatenate | solution.py:210
  74.8 1.2 %reshape.312 = f32[32,10,512]{2,1,0:T(8,128)S(1)} reshape(f32[32,40,128]{2,1,0:T(8,128)} %get-tuple-element.31) | data formatting | bytes 1310720 | tf_op jit(solution)/shard_map/reshape | solution.py:324
  76.0 2.4 %gather_fusion.3 = f32[96,10,512]{2,1,0:T(8,128)} fusion(f32[32,10,512]{2,1,0:T(8,128)S(1)} %reshape.312, s32[1024]{0:T(1024)S(1)} %pad_clamp_fusion), kind=kCustom, calls=%fused_computation.3 | custom fusion | bytes 3932544 | tf_op jit(solution)/shard_map/jit(_take)/gather | solution.py:325
  78.4 4.0 %fusion.126 = (bf16[96,10,512]{2,1,0:T(8,128)(2,1)S(1)}, f32[96,10,512]{2,1,0:T(8,128)S(1)}) fusion(f32[96,10,512]{2,0,1:T(8,128)S(1)} %copy-done.1, f32[96,10,512]{2,1,0:T(8,128)} %gather_fusion.3, pred[96]{0:T(512)(128)(4,1)S(1)} %get-tuple-element.44, pred[96]{0:T(512)(128)(4,1)S(1)} %subtract_compare_fusion), kind=kLoop, calls=%fused_computation.187 | loop fusion | flops 1474560 | bytes 6881472 | tf_op jit(solution)/shard_map/convert.7
  83.3 0.6 copy-done.3
  85.9 1.7 %copy-done.2 = bf16[7,512,512]{2,1,0:T(8,128)(2,1)S(1)} copy-done((bf16[7,512,512]{2,1,0:T(8,128)(2,1)S(1)}, bf16[7,512,512]{2,1,0:T(8,128)(2,1)}, u32[]{:S(2)}) %copy-start.2) | copy-done | bytes 3670040
  87.6 0.6 fusion.85
  88.2 0.5 pad_maximum_fusion.3
  88.7 0.6 fusion.83
  89.3 0.7 fusion.81
  90.0 0.6 fusion.79
  90.6 0.6 fusion.77
  91.3 0.7 fusion.75
  91.9 1.0 add_add_fusion
  93.0 0.6 fusion.17
  93.9 1.5 %pad_maximum_fusion = f32[96,10,512]{2,0,1:T(8,128)} fusion(f32[96,2,512]{2,0,1:T(8,128)S(1)} %copy.114, f32[96,6,512]{2,0,1:T(8,128)S(1)} %slice_convert_fusion, f32[96,1,512]{2,0,1:T(8,128)S(1)} %copy-done.6, f32[96,1,512]{2,0,1:T(8,128)S(1)} %slice.301), kind=kLoop, calls=%fused_computation.38 | loop fusion | flops 1474560 | bytes 3932160 | tf_op jit(solution)/shard_map/concatenate | solution.py:246
  95.8 1.5 %convolution_add_fusion.1 = f32[768,256]{1,0:T(8,128)} fusion(f32[768,256]{1,0:T(8,128)S(1)} %convolution_add_fusion.2, bf16[96,2,512]{2,1,0:T(2,128)(2,1)S(1)} %slice.298, bf16[96,8,512]{2,1,0:T(8,128)(2,1)S(1)} %get-tuple-element.54, bf16[3,512,256]{2,1,0:T(8,128)(2,1)S(1)} %copy-done.8), kind=kOutput, calls=%fused_computation.63 | convolution fusion | flops 203096064 | bytes 2818048 | tf_op jit(solution)/shard_map/dot_general | solution.py:236
  97.3 3.3 %fusion.27 = bf16[96,8,512]{2,1,0:T(8,128)(2,1)} fusion(f32[768,512]{1,0:T(8,128)S(1)} %add_add_fusion, bf16[256,512]{1,0:T(8,128)(2,1)S(1)} %copy-done, f32[768,256]{1,0:T(8,128)} %convolution_add_fusion.1, bf16[96,8,512]{2,1,0:T(8,128)(2,1)S(1)} %get-tuple-element.54, bf16[96,2,512]{2,1,0:T(2,128)(2,1)} %copy-done.7, f32[512]{0:T(512)S(1)} %copy-done.12, ...), kind=kOutput, calls=%fused_computation.61 | convolution fusion | flops 406388736 | bytes 4655104 | tf_op jit(solution)/shard_map/dot_general | solution.py:242
  (78 shorter events, 5.5 us)
Async XLA Ops:
  0.6 96.6 %copy-start = (bf16[256,512]{1,0:T(8,128)(2,1)S(1)}, bf16[256,512]{1,0:T(8,128)(2,1)}, u32[]{:S(2)}) copy-start(bf16[256,512]{1,0:T(8,128)(2,1)} %param.28) | copy-start | bytes 786436
  0.6 26.8 %copy-start.1 = (f32[96,10,512]{2,0,1:T(8,128)S(1)}, f32[96,10,512]{2,0,1:T(8,128)}, u32[]{:S(2)}) copy-start(f32[96,10,512]{2,0,1:T(8,128)} %param.21) | copy-start | bytes 5898244
  54.0 11.1 %slice-start = ((s8[16777216]{0:T(1024)(128)(4,1)}), s8[4194304]{0:T(1024)(128)(4,1)S(1)}, s32[]{:S(2)}) async-start(s8[16777216]{0:T(1024)(128)(4,1)} %bitcast.115), calls=%async_computation | async-start | bytes 8388608
  56.8 8.4 %slice-start.1 = ((s8[16777216]{0:T(1024)(128)(4,1)}), s8[4194304]{0:T(1024)(128)(4,1)S(1)}, s32[]{:S(2)}) async-start(s8[16777216]{0:T(1024)(128)(4,1)} %bitcast.115), calls=%async_computation.1 | async-start | bytes 8388608
  59.6 5.6 %slice-start.2 = ((s8[16777216]{0:T(1024)(128)(4,1)}), s8[4194304]{0:T(1024)(128)(4,1)S(1)}, s32[]{:S(2)}) async-start(s8[16777216]{0:T(1024)(128)(4,1)} %bitcast.115), calls=%async_computation.2 | async-start | bytes 8388608
  62.4 2.8 %slice-start.3 = ((s8[16777216]{0:T(1024)(128)(4,1)}), s8[4194304]{0:T(1024)(128)(4,1)S(1)}, s32[]{:S(2)}) async-start(s8[16777216]{0:T(1024)(128)(4,1)} %bitcast.115), calls=%async_computation.3 | async-start | bytes 8388608
  82.7 1.2 %copy-start.3 = (f32[96,4,1,512]{3,1,0,2:T(4,128)S(1)}, f32[96,4,1,512]{3,1,0,2:T(4,128)}, u32[]{:S(2)}) copy-start(f32[96,4,1,512]{3,1,0,2:T(4,128)} %reshape.326) | copy-start | bytes 2359300
  82.7 1.4 %copy-start.4 = (f32[96,3,1,512]{3,0,1,2:T(8,128)S(1)}, f32[96,3,1,512]{3,0,1,2:T(8,128)}, u32[]{:S(2)}) copy-start(f32[96,3,1,512]{3,0,1,2:T(8,128)} %get-tuple-element.71) | copy-start | bytes 1769476
  82.7 1.5 %copy-start.5 = (f32[96,3,1,512]{3,0,1,2:T(8,128)S(1)}, f32[96,3,1,512]{3,0,1,2:T(8,128)}, u32[]{:S(2)}) copy-start(f32[96,3,1,512]{3,0,1,2:T(8,128)} %get-tuple-element.72) | copy-start | bytes 1769476
  82.9 12.9 %copy-start.7 = (bf16[96,2,512]{2,1,0:T(2,128)(2,1)}, bf16[96,2,512]{2,1,0:T(2,128)(2,1)S(1)}, u32[]{:S(2)}) copy-start(bf16[96,2,512]{2,1,0:T(2,128)(2,1)S(1)} %slice.298) | copy-start | bytes 589828
  84.9 0.7 copy-start.10
  85.6 2.0 %copy-start.2 = (bf16[7,512,512]{2,1,0:T(8,128)(2,1)S(1)}, bf16[7,512,512]{2,1,0:T(8,128)(2,1)}, u32[]{:S(2)}) copy-start(bf16[7,512,512]{2,1,0:T(8,128)(2,1)} %param.24) | copy-start | bytes 11010052
  91.2 0.7 copy-start.9
  92.9 0.9 copy-start.6
  93.9 1.5 %copy-start.8 = (bf16[3,512,256]{2,1,0:T(8,128)(2,1)S(1)}, bf16[3,512,256]{2,1,0:T(8,128)(2,1)}, u32[]{:S(2)}) copy-start(bf16[3,512,256]{2,1,0:T(8,128)(2,1)} %param.26) | copy-start | bytes 2359300
  93.9 1.5 %copy-start.11 = (f32[256]{0:T(256)S(1)}, f32[256]{0:T(256)}, u32[]{:S(2)}) copy-start(f32[256]{0:T(256)} %param.27) | copy-start | bytes 3076
  95.7 1.5 %copy-start.12 = (f32[512]{0:T(512)S(1)}, f32[512]{0:T(512)}, u32[]{:S(2)}) copy-start(f32[512]{0:T(512)} %param.29) | copy-start | bytes 6148

commit v6 on v5

--- a/solution.py
+++ b/solution.py
@@ -279,48 +279,27 @@
     positions = jnp.arange(conv_count, dtype=jnp.int32)
     earlier = positions[None, :] < positions[:, None]
 
-    anchor = roster // conv_count
-    row = roster % conv_count
-    rank_in = jnp.sum(earlier & (anchor[None, :] == anchor[:, None]), axis=1).astype(jnp.int32)
-    key = anchor * most + rank_in
-    spots = jnp.arange(devices_all * most, dtype=jnp.int32)
-    code_request = jnp.sum(jnp.where(key[None, :] == spots[:, None], row[None, :] + 1, 0), axis=1) - 1
+    code_width = codes.shape[1]
+    gathered = lax.all_gather(
+        jnp.concatenate([codes, old_slot[:, None]], axis=1).astype(jnp.float32),
+        ("grp", "dev"),
+        axis=0,
+        tiled=True,
+    )
+    every_code = gathered[:, :code_width]
+    slot_table = lax.dynamic_slice_in_dim(gathered[:, code_width], group_first * conv_count, per_group * conv_count)
+    my_codes = jnp.take(every_code, roster, axis=0).astype(jnp.int32)
+    routed = embed_codes(my_codes, code_table)
+
     source_dev = old_slot // conv_count - group_first
-    source_row = old_slot % conv_count
     moved = source_dev != local_index
-    everyone = jnp.arange(devices_all, dtype=jnp.int32)
-    state_request = (
-        jnp.sum(
-            jnp.where(
-                moved[None, :] & (source_dev[None, :] + group_first == everyone[:, None]),
-                source_row[None, :] + 1,
-                0,
-            ),
-            axis=1,
-        )
-        - 1
-    )
-    request = jnp.concatenate(
-        [code_request.reshape(devices_all, most), state_request.reshape(devices_all, 1)], axis=1
-    )
-    lanes = 128
-    padded = jnp.zeros((devices_all, 1, lanes), jnp.int32).at[:, 0, : most + 1].set(request)
-    (asked,) = exchange([(padded, True)], 0)
-    asked = asked[:, 0, : most + 1]
-
-    answer = jnp.take(codes, jnp.clip(asked[:, :most].reshape(-1), 0, conv_count - 1), axis=0)
-    answer = jnp.zeros((devices_all, 1, lanes), jnp.int32).at[:, 0, : answer.size // devices_all].set(
-        answer.reshape(devices_all, -1)
-    )
-    state_asked = lax.dynamic_slice_in_dim(asked[:, most], group_first, per_group)
-    leaving = jnp.take(states, jnp.clip(state_asked, 0, conv_count - 1), axis=0)
-    answered, arrived = exchange(
-        [(answer, True), (leaving.reshape(per_group, -1, lanes), False)], 1
-    )
-    code_width = codes.shape[1]
-    answered = answered[:, 0, : most * code_width].reshape(devices_all * most, code_width)
-    my_codes = jnp.take(answered, key, axis=0)
-    routed = embed_codes(my_codes, code_table)
+    slot_table = slot_table.astype(jnp.int32).reshape(per_group, conv_count)
+    from_me = (slot_table // conv_count - group_first == local_index) & (
+        jnp.arange(per_group, dtype=jnp.int32)[:, None] != local_index
+    )
+    asked_rows = jnp.sum(jnp.where(from_me, slot_table % conv_count, 0), axis=1)
+    leaving = jnp.take(states, asked_rows, axis=0)
+    (arrived,) = exchange([(leaving.reshape(per_group, -1, 128), False)], 0)
     arrived = arrived.reshape(leaving.shape)
     brought = jnp.take(arrived, jnp.clip(source_dev, 0, per_group - 1), axis=0)
     carried = jnp.where(moved[:, None, None], brought, states)

time: 101 us -> 167 us (1.65)
  waiting for transfers between devices: 0 us -> 69.2 us
  Pallas kernels: 36.9 us -> 13.1 us
  between operations: 1.2 us -> 14.5 us
  local copies, waits for them, and re-layouts: 24.4 us -> 31.4 us
  matrix products: 25.1 us -> 22.6 us
  other arithmetic: 13 us -> 15.2 us
    all_gather x0 -> x1, waiting for transfers between devices: none -> 69.2 us  [local(): lax.all_gather(jnp.concatenate([codes, old_slot[:, None]], axis=1).astype...]
    pallas_call x2 -> x1, Pallas kernels: 36.9 us -> 13.1 us  [exchange(): pl.pallas_call(kernel, out_shape=shapes + mids, in_specs=[pl.BlockSpec(me...]
    all_gather x0 -> x1, local copies, waits for them, and re-layouts: none -> 5.62 us  [local(): lax.all_gather(jnp.concatenate([codes, old_slot[:, None]], axis=1).astype...]
    slice x1, local copies, waits for them, and re-layouts: 0.01 us -> 3.91 us  [local(): gathered[:, code_width]]
    dot_general x8, matrix products: 15.1 us -> 12.5 us  [embed_codes(): jnp.dot(onehot, book_rows, preferred_element_type=jnp.float32)]
    gather x7 -> x5, local copies, waits for them, and re-layouts: 5.72 us -> 7.7 us  [the longest x3 4.19 us: local(): leaving = jnp.take(states, asked_rows, axis=0)]
    unnamed x37 -> x29, local copies, waits for them, and re-layouts: 5.03 us -> 3.45 us
  transfers between devices with their start and end apart: 0 -> 1, of which waited for: 0 -> 1; matrix products, arithmetic and copies ran while one was open for 0% -> 2% of each run, Pallas kernels for 0% -> 0%
where the time goes in v6:
time: 167 us; the launch traced here: 166 us
  waiting for transfers between devices  69.2 us (41%)
  local copies, waits for them, and re-layouts  31.4 us (19%)
  matrix products  22.6 us (14%)
  other arithmetic  15.2 us (9%)
  between operations  14.5 us (9%)
  Pallas kernels  13.1 us (8%)
    all_gather x1, waiting for transfers between devices, local(): lax.all_gather(jnp.concatenate([codes, old_slot[:, None]], axis=1).astype...  69.2 us
    pallas_call x1, Pallas kernels, exchange(): pl.pallas_call(kernel, out_shape=shapes + mids, in_specs=[pl.BlockSpec(me...  13.1 us
    dot_general x8, matrix products, embed_codes(): jnp.dot(onehot, book_rows, preferred_element_type=jnp.float32)  12.5 us
    all_gather x1, local copies, waits for them, and re-layouts, local(): lax.all_gather(jnp.concatenate([codes, old_slot[:, None]], axis=1).astype...  5.62 us
    dot_general x7, matrix products, decode(): jnp.dot(window, conv_weight[tap_index], preferred_element_type=jnp.float32)  4.77 us
    gather x3, local copies, waits for them, and re-layouts, local(): leaving = jnp.take(states, asked_rows, axis=0)  4.19 us
    slice x1, local copies, waits for them, and re-layouts, local(): gathered[:, code_width]  3.91 us
    another operation x1, other arithmetic  3.82 us
  transfers between devices with their start and end apart: 1, of which 1 were waited for; matrix products, arithmetic and copies ran while one was open for 2% of the time, Pallas kernels for 0%

profile of v6, /device:TPU:1, one launch (start us, length us, event | category | flops | bytes accessed | tf_op | source)
XLA Modules:
  0.0 166.1 jit_solution(9417857253976084996)
XLA Ops:
  7.2 1.4 fusion.119
  8.6 0.7 compare_and_fusion.2
  9.5 0.7 compare_select_fusion.7
  10.2 0.7 broadcast_compare_fusion
  10.9 0.9 fusion.134
  11.7 69.2 %all-gather.3.cloned.1.call-done = f32[128,96,33]{1,2,0:T(8,128)} async-done(((f32[1,96,33]{1,2,0:T(8,128)}), f32[128,96,33]{1,2,0:T(8,128)}) %all-gather.3.cloned.1.call-update) | async-done | bytes 1622032 | tf_op jit(solution)/shard_map/all_gather | solution.py:283
  80.9 5.6 %copy.51 = f32[128,96,33]{2,1,0:T(8,128)} copy(f32[128,96,33]{1,2,0:T(8,128)} %all-gather.3.cloned.1.call-done) | data formatting | bytes 3244032 | tf_op jit(solution)/shard_map/all_gather | solution.py:283
  86.5 3.4 %gather_fusion = f32[96,32]{1,0:T(8,128)S(1)} fusion(f32[12288,32]{1,0:T(8,128)} %bitcast.94, s32[1024]{0:T(1024)S(1)} %pad_clamp_fusion.2), kind=kCustom, calls=%fused_computation | custom fusion | bytes 24960 | tf_op jit(solution)/shard_map/jit(_take)/gather | solution.py:291
  90.2 0.9 slice_reduce_fusion
  91.1 3.0 %fusion = f32[384,512]{1,0:T(8,128)S(1)} fusion(bf16[16384,512]{1,0:T(8,128)(2,1)} %param.14, s32[384]{0:T(512)S(1)} %get-tuple-element.13), kind=kOutput, calls=%fused_computation.14 | convolution fusion | flops 806092800 | bytes 2885120 | tf_op jit(solution)/shard_map/dot_general | solution.py:22
  94.0 3.4 %fusion.51 = f32[384,512]{1,0:T(8,128)S(1)} fusion(f32[384,512]{1,0:T(8,128)S(1)} %fusion, bf16[16384,512]{1,0:T(8,128)(2,1)} %param.14, s32[384]{0:T(512)S(1)} %get-tuple-element.12), kind=kOutput, calls=%fused_computation.76 | convolution fusion | flops 806289408 | bytes 3671552 | tf_op jit(solution)/shard_map/dot_general | solution.py:22
  97.4 1.0 fusion.48
  98.5 1.0 fusion.45
  99.5 1.0 fusion.42
  100.5 1.0 fusion.39
  101.5 1.0 fusion.36
  102.6 1.0 fusion.57
  103.8 1.1 reshape.205
  105.2 0.7 slice.245
  105.9 0.7 slice.246
  106.6 1.2 slice_bitcast_fusion
  107.8 3.9 %slice.226 = f32[12288,1]{1,0:T(8,128)S(1)} slice(f32[12288,33]{1,0:T(8,128)} %bitcast.95), slice={[0:12288], [32:33]} | slice | bytes 98304 | tf_op jit(solution)/shard_map/slice | solution.py:290
  111.7 0.6 fusion.28
  112.3 1.1 fusion.27
  113.9 1.5 gather_fusion.1
  115.4 1.4 copy.53
  116.7 1.3 gather.19
  118.1 0.9 broadcast_select_fusion.refs_0_
  119.0 13.1 %shard_map.140 = f32[32,40,128]{2,1,0:T(8,128)} custom-call(f32[32,40,128]{2,1,0:T(8,128)} %broadcast_select_fusion.refs_0_), custom_call_target="tpu_custom_call" | custom-call | tf_op jit(solution)/shard_map/pallas_call | solution.py:171
  132.1 1.2 reshape.191
  133.3 2.4 %gather_fusion.2 = f32[96,10,512]{2,1,0:T(8,128)} fusion(f32[32,10,512]{2,1,0:T(8,128)S(1)} %reshape.191, s32[1024]{0:T(1024)S(1)} %pad_clamp_fusion), kind=kCustom, calls=%fused_computation.2 | custom fusion | bytes 3932544 | tf_op jit(solution)/shard_map/jit(_take)/gather | solution.py:304
  135.8 3.8 %fusion.132 = (bf16[96,10,512]{2,1,0:T(8,128)(2,1)S(1)}, f32[96,10,512]{2,1,0:T(8,128)S(1)}) fusion(f32[96,10,512]{2,0,1:T(8,128)S(1)} %copy-done.1, f32[96,10,512]{2,1,0:T(8,128)} %gather_fusion.2, pred[96]{0:T(512)(128)(4,1)S(1)} %get-tuple-element.18, pred[96]{0:T(512)(128)(4,1)S(1)} %get-tuple-element.16), kind=kLoop, calls=%fused_computation.181 | loop fusion | flops 1474560 | bytes 6881472 | tf_op jit(solution)/shard_map/convert.7
  140.5 0.5 copy-done.3
  141.3 0.4 maximum_add_fusion
  142.0 0.5 copy-done.10
  142.9 1.7 %copy-done.2 = bf16[7,512,512]{2,1,0:T(8,128)(2,1)S(1)} copy-done((bf16[7,512,512]{2,1,0:T(8,128)(2,1)S(1)}, bf16[7,512,512]{2,1,0:T(8,128)(2,1)}, u32[]{:S(2)}) %copy-start.2) | copy-done | bytes 3670040
  144.6 0.6 fusion.87
  145.2 0.7 pad_maximum_fusion.3
  145.9 0.6 fusion.85
  146.5 0.6 fusion.83
  147.1 0.6 fusion.81
  147.8 0.7 fusion.79
  148.4 0.6 fusion.77
  149.1 1.0 add_add_fusion
  150.1 0.6 fusion.17
  151.6 1.5 convolution_add_fusion.1
  153.2 3.5 %fusion.29 = bf16[96,8,512]{2,1,0:T(8,128)(2,1)} fusion(f32[768,512]{1,0:T(8,128)S(1)} %add_add_fusion, bf16[256,512]{1,0:T(8,128)(2,1)S(1)} %copy-done, f32[768,256]{1,0:T(8,128)} %convolution_add_fusion.1, bf16[96,8,512]{2,1,0:T(8,128)(2,1)} %copy-done.4, bf16[96,2,512]{2,1,0:T(2,128)(2,1)} %copy-done.7, f32[512]{0:T(512)S(1)} %copy-done.13, ...), kind=kOutput, calls=%fused_computation.65 | convolution fusion | flops 406388736 | bytes 4655104 | tf_op jit(solution)/shard_map/dot_general | solution.py:242
  156.7 2.5 %pad_maximum_fusion = f32[96,10,512]{2,0,1:T(8,128)} fusion(f32[96,2,512]{2,0,1:T(8,128)S(1)} %copy.70, f32[96,6,512]{2,0,1:T(8,128)S(1)} %slice_convert_fusion, f32[96,1,512]{2,0,1:T(8,128)} %slice.246, f32[96,1,512]{2,0,1:T(8,128)} %slice.245), kind=kLoop, calls=%fused_computation.37 | loop fusion | flops 1474560 | bytes 3932160 | tf_op jit(solution)/shard_map/concatenate | solution.py:246
  (57 shorter events, 4.1 us)
Async XLA Ops:
  7.2 146.0 %copy-start = (bf16[256,512]{1,0:T(8,128)(2,1)S(1)}, bf16[256,512]{1,0:T(8,128)(2,1)}, u32[]{:S(2)}) copy-start(bf16[256,512]{1,0:T(8,128)(2,1)} %param.24) | copy-start | bytes 786436
  7.2 73.7 %all-gather.3.cloned.1.call-start = ((), (), s32[]{:S(2)}) async-start(), calls=%async_computation | async-start | bytes 2641920 | tf_op jit(solution)/shard_map/all_gather | solution.py:283
  90.2 7.2 %copy-start.12 = (bf16[16384,512]{1,0:T(8,128)(2,1)S(1)}, bf16[16384,512]{1,0:T(8,128)(2,1)}, u32[]{:S(2)}) copy-start(bf16[16384,512]{1,0:T(8,128)(2,1)} %param.14) | copy-start | bytes 50331652
  111.7 2.2 %copy-start.1 = (f32[96,10,512]{2,0,1:T(8,128)S(1)}, f32[96,10,512]{2,0,1:T(8,128)}, u32[]{:S(2)}) copy-start(f32[96,10,512]{2,0,1:T(8,128)} %param.17) | copy-start | bytes 5898244
  139.7 11.9 %copy-start.7 = (bf16[96,2,512]{2,1,0:T(2,128)(2,1)}, bf16[96,2,512]{2,1,0:T(2,128)(2,1)S(1)}, u32[]{:S(2)}) copy-start(bf16[96,2,512]{2,1,0:T(2,128)(2,1)S(1)} %slice.242) | copy-start | bytes 589828
  139.8 1.2 copy-start.3
  139.8 1.4 copy-start.5
  139.8 1.5 copy-start.6
  141.9 0.7 copy-start.10
  142.6 2.0 %copy-start.2 = (bf16[7,512,512]{2,1,0:T(8,128)(2,1)S(1)}, bf16[7,512,512]{2,1,0:T(8,128)(2,1)}, u32[]{:S(2)}) copy-start(bf16[7,512,512]{2,1,0:T(8,128)(2,1)} %param.20) | copy-start | bytes 11010052
  148.4 0.7 copy-start.9
  150.1 1.1 copy-start.8
  150.1 1.1 copy-start.11
  150.7 0.9 copy-start.4
  151.6 1.5 copy-start.13
Sparse Core Ops, SparseCore 0:
  11.7 69.1 all-gather.2

commit v7 on v5

--- a/solution.py
+++ b/solution.py
@@ -187,72 +187,96 @@
     ]
 
 
-def decode(
-    routed,
-    carried,
-    up_weight,
-    up_bias,
-    conv_weight,
-    conv_bias,
-    res_in_weight,
-    res_in_bias,
-    res_out_weight,
-    res_out_bias,
+def decode_kernel(
+    routed_ref, carried_ref, up_w_ref, up_b_ref, conv_w_ref, conv_b_ref, in_w_ref, in_b_ref, out_w_ref, out_b_ref,
+    decoded_ref, states_ref,
 ):
+    slots, frame_count, _ = routed_ref.shape
+    step_count = 2 * frame_count
+    conv_taps = conv_w_ref.shape[0]
+    res_taps = in_w_ref.shape[0]
+    kept = carried_ref.shape[1] - 2 - (res_taps - 1)
+
+    def elu(value):
+        return jnp.where(value > 0, value, jnp.exp(jnp.minimum(value, 0.0)) - 1.0)
+
+    up_w = up_w_ref[...]
+    up_b = up_b_ref[...]
+    inputs = [routed_ref[:, f, :].astype(jnp.float32) for f in range(frame_count)]
+    carried = [carried_ref[:, r, :] for r in range(carried_ref.shape[1])]
+    upsampled = []
+    for f in range(frame_count):
+        early_even = carried[0] if f == 0 else inputs[f - 1] * up_w[2:3]
+        early_odd = carried[1] if f == 0 else inputs[f - 1] * up_w[3:4]
+        upsampled.append((inputs[f] * up_w[0:1] + early_even) + up_b)
+        upsampled.append((inputs[f] * up_w[1:2] + early_odd) + up_b)
+    history = jnp.concatenate(
+        [c.astype(jnp.bfloat16) for c in carried[2 : 2 + kept]] + [u.astype(jnp.bfloat16) for u in upsampled], axis=0
+    )
+    conv_out = None
+    for tap in range(conv_taps):
+        start = (conv_taps - 1 - tap) * slots
+        term = jnp.dot(history[start : start + step_count * slots], conv_w_ref[tap], preferred_element_type=jnp.float32)
+        conv_out = term if conv_out is None else conv_out + term
+    conv_out = conv_out + conv_b_ref[...]
+    active = elu(conv_out)
+    res_rounded = jnp.concatenate(
+        [c.astype(jnp.bfloat16) for c in carried[2 + kept :]] + [active.astype(jnp.bfloat16)], axis=0
+    )
+    inner = None
+    for tap in range(res_taps):
+        start = (res_taps - 1 - tap) * slots
+        term = jnp.dot(res_rounded[start : start + step_count * slots], in_w_ref[tap], preferred_element_type=jnp.float32)
+        inner = term if inner is None else inner + term
+    squeezed = elu(inner + in_b_ref[...]).astype(jnp.bfloat16)
+    summed = conv_out + jnp.dot(squeezed, out_w_ref[...], preferred_element_type=jnp.float32) + out_b_ref[...]
+    decoded = summed.astype(jnp.bfloat16)
+    for t in range(step_count):
+        decoded_ref[:, t, :] = decoded[t * slots : (t + 1) * slots]
+    states_ref[:, 0, :] = inputs[frame_count - 1] * up_w[2:3]
+    states_ref[:, 1, :] = inputs[frame_count - 1] * up_w[3:4]
+    tail = history.shape[0] // slots - kept
+    for k in range(kept):
+        row = history.shape[0] // slots - kept + k
+        states_ref[:, 2 + k, :] = history[row * slots : (row + 1) * slots].astype(jnp.float32)
+    for k in range(res_taps - 1):
+        row = step_count - (res_taps - 1) + k
+        states_ref[:, 2 + kept + k, :] = active[row * slots : (row + 1) * slots]
+
+
+def decode(routed, carried, up_weight, up_bias, conv_weight, conv_bias, res_in_weight, res_in_bias, res_out_weight, res_out_bias):
     conv_count, frame_count, chan_width = routed.shape
-    step_count = 2 * frame_count
-    inputs = routed.astype(jnp.float32)
-    tap_zero = inputs * up_weight[0]
-    tap_one = inputs * up_weight[1]
-    tap_two = inputs * up_weight[2]
-    tap_three = inputs * up_weight[3]
-    early_even = jnp.concatenate([carried[:, 0:1], tap_two[:, :-1]], axis=1)
-    early_odd = jnp.concatenate([carried[:, 1:2], tap_three[:, :-1]], axis=1)
-    upsampled = (
-        jnp.stack([tap_zero + early_even, tap_one + early_odd], axis=2).reshape(
-            conv_count, step_count, chan_width
-        )
-        + up_bias
-    )
-    history = jnp.concatenate([carried[:, 2:8], upsampled], axis=1).astype(jnp.bfloat16)
-    conv_out = jnp.zeros((conv_count * step_count, chan_width), jnp.float32) + conv_bias
-    for tap_index in range(7):
-        window = history[:, 6 - tap_index : 6 - tap_index + step_count].reshape(
-            conv_count * step_count, chan_width
-        )
-        conv_out = conv_out + jnp.dot(
-            window, conv_weight[tap_index], preferred_element_type=jnp.float32
-        )
-    active = jax.nn.elu(conv_out).reshape(conv_count, step_count, chan_width)
-    res_history = jnp.concatenate([carried[:, 8:10], active], axis=1)
-    res_rounded = res_history.astype(jnp.bfloat16)
-    res_inner = (
-        jnp.zeros((conv_count * step_count, res_in_weight.shape[2]), jnp.float32) + res_in_bias
-    )
-    for tap_index in range(3):
-        window = res_rounded[:, 2 - tap_index : 2 - tap_index + step_count].reshape(
-            conv_count * step_count, chan_width
-        )
-        res_inner = res_inner + jnp.dot(
-            window, res_in_weight[tap_index], preferred_element_type=jnp.float32
-        )
-    squeezed = jax.nn.elu(res_inner).astype(jnp.bfloat16)
-    summed = (
-        conv_out
-        + jnp.dot(squeezed, res_out_weight, preferred_element_type=jnp.float32)
-        + res_out_bias
-    )
-    decoded = summed.astype(jnp.bfloat16).reshape(conv_count, step_count, chan_width)
-    new_states = jnp.concatenate(
-        [
-            tap_two[:, -1:],
-            tap_three[:, -1:],
-            history[:, -6:].astype(jnp.float32),
-            res_history[:, -2:],
+    rows = carried.shape[1]
+    chunk = 32 if conv_count % 32 == 0 else conv_count
+    whole = lambda shape: pl.BlockSpec(shape, lambda i: (0,) * len(shape))
+    return pl.pallas_call(
+        decode_kernel,
+        grid=(conv_count // chunk,),
+        out_shape=(
+            jax.ShapeDtypeStruct((conv_count, 2 * frame_count, chan_width), jnp.bfloat16),
+            jax.ShapeDtypeStruct((conv_count, rows, chan_width), jnp.float32),
+        ),
+        in_specs=[
+            pl.BlockSpec((chunk, frame_count, chan_width), lambda i: (i, 0, 0)),
+            pl.BlockSpec((chunk, rows, chan_width), lambda i: (i, 0, 0)),
+            whole(up_weight.shape),
+            whole((1, chan_width)),
+            whole(conv_weight.shape),
+            whole((1, chan_width)),
+            whole(res_in_weight.shape),
+            whole((1, res_in_weight.shape[2])),
+            whole(res_out_weight.shape),
+            whole((1, chan_width)),
         ],
-        axis=1,
-    )
-    return (decoded, new_states)
+        out_specs=(
+            pl.BlockSpec((chunk, 2 * frame_count, chan_width), lambda i: (i, 0, 0)),
+            pl.BlockSpec((chunk, rows, chan_width), lambda i: (i, 0, 0)),
+        ),
+        compiler_params=pltpu.CompilerParams(vmem_limit_bytes=48 * 1024 * 1024),
+    )(
+        routed, carried, up_weight, up_bias.reshape(1, -1), conv_weight, conv_bias.reshape(1, -1),
+        res_in_weight, res_in_bias.reshape(1, -1), res_out_weight, res_out_bias.reshape(1, -1),
+    )
 
 
 def local(

time: 101 us -> 90.6 us (0.90)
  Pallas kernels: 36.9 us -> 47.5 us
  matrix products: 25.1 us -> 15.1 us
  local copies, waits for them, and re-layouts: 24.4 us -> 17.7 us
  other arithmetic: 13 us -> 8.9 us
    pallas_call x0 -> x1, Pallas kernels: none -> 10.6 us  [decode(): pl.pallas_call(decode_kernel, grid=(conv_count // chunk,), out_shape=(jax...]
    dot_general x10 -> x0, matrix products: 9.96 us -> none  [the longest x7 4.8 us: decode(): jnp.dot(window, conv_weight[tap_index], preferred_element_type=jnp.float32)]
    select_n x0 -> x1, other arithmetic: none -> 4.92 us  [local(): carried = jnp.where(moved[:, None, None], brought, states)]
    another operation x2 -> x0, other arithmetic: 4.22 us -> none
    unnamed x37 -> x26, local copies, waits for them, and re-layouts: 5.03 us -> 1.8 us
    pallas_call x0 -> x1, local copies, waits for them, and re-layouts: none -> 2.41 us  [decode(): pl.pallas_call(decode_kernel, grid=(conv_count // chunk,), out_shape=(jax...]
    slice x7 -> x0, local copies, waits for them, and re-layouts: 2.27 us -> none  [the longest x1 0.86 us: decode(): tap_zero = inputs * up_weight[0]]
    convert_element_type x2 -> x0, local copies, waits for them, and re-layouts: 2.21 us -> none  [decode(): inputs = routed.astype(jnp.float32)]
where the time goes in v7:
time: 90.6 us; the launch traced here: 90.2 us
  Pallas kernels  47.5 us (52%)
  local copies, waits for them, and re-layouts  17.7 us (20%)
  matrix products  15.1 us (17%)
  other arithmetic  8.9 us (10%)
  between operations  1.04 us (1%)
    pallas_call x2, Pallas kernels, exchange(): pl.pallas_call(kernel, out_shape=shapes + mids, in_specs=[pl.BlockSpec(me...  36.9 us
    dot_general x8, matrix products, embed_codes(): jnp.dot(onehot, book_rows, preferred_element_type=jnp.float32)  15.1 us
    pallas_call x1, Pallas kernels, decode(): pl.pallas_call(decode_kernel, grid=(conv_count // chunk,), out_shape=(jax...  10.6 us
    select_n x1, other arithmetic, local(): carried = jnp.where(moved[:, None, None], brought, states)  4.92 us
    gather x3, local copies, waits for them, and re-layouts, local(): leaving = jnp.take(states, jnp.clip(state_asked, 0, conv_count - 1), axis=0)  4.19 us
    gather x1, local copies, waits for them, and re-layouts, local(): brought = jnp.take(arrived, jnp.clip(source_dev, 0, per_group - 1), axis=0)  2.42 us
    pallas_call x1, local copies, waits for them, and re-layouts, decode(): pl.pallas_call(decode_kernel, grid=(conv_count // chunk,), out_shape=(jax...  2.41 us

profile of v7, /device:TPU:1, one launch (start us, length us, event | category | flops | bytes accessed | tf_op | source)
XLA Modules:
  0.0 90.2 jit_solution(7613928635121045338)
XLA Ops:
  0.6 0.8 fusion.54
  1.5 0.7 and_select_fusion.3
  2.1 0.2 convert_reduce_fusion
  2.3 0.1 select_reduce_fusion
  2.4 0.7 compare_and_fusion
  3.1 0.1 select_reduce_fusion.1
  3.3 0.1 broadcast_in_dim.102
  3.4 0.1 broadcast_in_dim.103
  3.5 0.8 copy.44
  4.3 0.1 sub.30
  4.4 0.1 copy.41
  4.6 0.1 pad_add_fusion
  4.6 0.7 scatter.6.refs_0_
  5.3 18.2 %shard_map.140 = (s32[4,32,1,128]{3,2,1,0:T(1,128)}, s32[4,32,1,128]{3,2,1,0:T(1,128)}) custom-call(s32[128,1,128]{2,1,0:T(1,128)} %scatter.6.refs_0_), custom_call_target="tpu_custom_call" | custom-call | tf_op jit(solution)/shard_map/pallas_call | solution.py:171
  23.5 0.9 copy.50
  24.5 0.1 and_bitcast_fusion
  24.6 0.2 copy.45
  24.7 0.1 copy.43
  24.8 0.1 min.28
  25.0 0.7 gather_fusion
  25.7 0.1 gather.23
  25.8 0.1 broadcast_select_fusion.2
  25.9 0.7 scatter.9.refs_0_
  26.6 1.5 %gather_fusion.1 = f32[32,10,512]{2,0,1:T(8,128)S(1)} fusion(f32[96,10,512]{2,0,1:T(8,128)S(1)} %copy-done.7, s32[1024]{0:T(1024)S(1)} %pad_clamp_fusion.2), kind=kCustom, calls=%fused_computation.1 | custom fusion | bytes 1310848 | tf_op jit(solution)/shard_map/jit(_take)/gather | solution.py:340
  28.1 1.4 %copy.47 = f32[32,10,512]{2,1,0:T(8,128)} copy(f32[32,10,512]{2,0,1:T(8,128)S(1)} %gather_fusion.1) | data formatting | bytes 1310720 | tf_op jit(solution)/shard_map/jit(_take)/gather | solution.py:340
  29.5 1.3 %gather.25 = f32[32,40,128]{2,1,0:T(8,128)S(1)} reshape(f32[32,10,512]{2,1,0:T(8,128)} %copy.47) | data formatting | bytes 1310720 | tf_op jit(solution)/shard_map/jit(_take)/gather | solution.py:340
  30.8 0.9 %broadcast_select_fusion.refs_1_ = f32[32,40,128]{2,1,0:T(8,128)} fusion(f32[32,40,128]{2,1,0:T(8,128)S(1)} %gather.25, pred[32]{0:T(512)(128)(4,1)S(1)} %get-tuple-element.53), kind=kLoop, calls=%fused_computation.46 | loop fusion | flops 163840 | bytes 1310752 | tf_op jit(solution)/shard_map/jit(_take)/select_n | solution.py:340
  31.8 18.7 %shard_map.141 = (s32[4,32,1,128]{3,2,1,0:T(1,128)}, f32[32,40,128]{2,1,0:T(8,128)}, s32[4,32,1,128]{3,2,1,0:T(1,128)}) custom-call(s32[128,1,128]{2,1,0:T(1,128)} %scatter.9.refs_0_, f32[32,40,128]{2,1,0:T(8,128)} %broadcast_select_fusion.refs_1_), custom_call_target="tpu_custom_call" | custom-call | tf_op jit(solution)/shard_map/pallas_call | solution.py:171
  50.5 0.9 %reshape_squeeze.3 = s32[256,32]{1,0:T(8,128)S(1)} reshape(s32[128,1,64]{2,0,1:T(8,128)} %bitcast.26) | data formatting | bytes 65536 | tf_op jit(solution)/shard_map/reshape;squeeze | solution.py:345
  51.4 0.6 gather_fusion.2
  52.1 0.1 gather.27
  52.2 0.1 broadcast_select_fusion.1
  52.3 0.9 slice_reduce_fusion
  53.2 2.8 %fusion = f32[384,512]{1,0:T(8,128)S(1)} fusion(bf16[16384,512]{1,0:T(8,128)(2,1)} %param.18, s32[384]{0:T(512)S(1)} %get-tuple-element.47), kind=kOutput, calls=%fused_computation.13 | convolution fusion | flops 806092800 | bytes 2885120 | tf_op jit(solution)/shard_map/dot_general | solution.py:22
  56.0 2.8 %fusion.45 = f32[384,512]{1,0:T(8,128)S(1)} fusion(f32[384,512]{1,0:T(8,128)S(1)} %fusion, bf16[16384,512]{1,0:T(8,128)(2,1)} %param.18, s32[384]{0:T(512)S(1)} %get-tuple-element.46), kind=kOutput, calls=%fused_computation.44 | convolution fusion | flops 806289408 | bytes 3671552 | tf_op jit(solution)/shard_map/dot_general | solution.py:22
  58.7 2.8 %fusion.42 = f32[384,512]{1,0:T(8,128)S(1)} fusion(f32[384,512]{1,0:T(8,128)S(1)} %fusion.45, bf16[16384,512]{1,0:T(8,128)(2,1)} %param.18, s32[384]{0:T(512)S(1)} %get-tuple-element.45), kind=kOutput, calls=%fused_computation.43 | convolution fusion | flops 806289408 | bytes 3671552 | tf_op jit(solution)/shard_map/dot_general | solution.py:22
  61.5 2.8 %fusion.39 = f32[384,512]{1,0:T(8,128)S(1)} fusion(f32[384,512]{1,0:T(8,128)S(1)} %fusion.42, bf16[16384,512]{1,0:T(8,128)(2,1)} %param.18, s32[384]{0:T(512)S(1)} %get-tuple-element.44), kind=kOutput, calls=%fused_computation.42 | convolution fusion | flops 806289408 | bytes 3671552 | tf_op jit(solution)/shard_map/dot_general | solution.py:22
  64.3 0.0 slice-done.3
  64.3 1.0 %fusion.36 = f32[384,512]{1,0:T(8,128)S(1)} fusion(f32[384,512]{1,0:T(8,128)S(1)} %fusion.39, bf16[16384,512]{1,0:T(8,128)(2,1)S(1)} %bitcast.35, s32[384]{0:T(512)S(1)} %get-tuple-element.43), kind=kOutput, calls=%fused_computation.41 | convolution fusion | flops 806289408 | bytes 3672064 | tf_op jit(solution)/shard_map/dot_general | solution.py:22
  65.4 1.0 %fusion.33 = f32[384,512]{1,0:T(8,128)S(1)} fusion(f32[384,512]{1,0:T(8,128)S(1)} %fusion.36, bf16[16384,512]{1,0:T(8,128)(2,1)S(1)} %bitcast.35, s32[384]{0:T(512)S(1)} %get-tuple-element.42), kind=kOutput, calls=%fused_computation.40 | convolution fusion | flops 806289408 | bytes 3672064 | tf_op jit(solution)/shard_map/dot_general | solution.py:22
  66.4 1.0 %fusion.30 = f32[384,512]{1,0:T(8,128)S(1)} fusion(f32[384,512]{1,0:T(8,128)S(1)} %fusion.33, bf16[16384,512]{1,0:T(8,128)(2,1)S(1)} %bitcast.35, s32[384]{0:T(512)S(1)} %get-tuple-element.41), kind=kOutput, calls=%fused_computation.39 | convolution fusion | flops 806289408 | bytes 3672064 | tf_op jit(solution)/shard_map/dot_general | solution.py:22
  67.4 1.0 %fusion.48 = bf16[384,512]{1,0:T(8,128)(2,1)S(1)} fusion(f32[384,512]{1,0:T(8,128)S(1)} %fusion.30, bf16[16384,512]{1,0:T(8,128)(2,1)S(1)} %bitcast.35, s32[384]{0:T(512)S(1)} %get-tuple-element.40), kind=kOutput, calls=%fused_computation.45 | convolution fusion | flops 806682624 | bytes 3278848 | tf_op jit(solution)/shard_map/dot_general | solution.py:22
  68.4 0.1 reshape.197.routed_ref
  68.5 1.2 %reshape.198 = f32[32,10,512]{2,1,0:T(8,128)S(1)} reshape(f32[32,40,128]{2,1,0:T(8,128)} %get-tuple-element.31) | data formatting | bytes 1310720 | tf_op jit(solution)/shard_map/reshape | solution.py:348
  69.7 2.4 %gather_fusion.3 = f32[96,10,512]{2,1,0:T(8,128)} fusion(f32[32,10,512]{2,1,0:T(8,128)S(1)} %reshape.198, s32[1024]{0:T(1024)S(1)} %pad_clamp_fusion), kind=kCustom, calls=%fused_computation.3 | custom fusion | bytes 3932544 | tf_op jit(solution)/shard_map/jit(_take)/gather | solution.py:349
  72.2 4.9 %copy_select_fusion.carried_ref = f32[96,10,512]{2,1,0:T(8,128)} fusion(f32[96,10,512]{2,0,1:T(8,128)S(1)} %copy-done.7, f32[96,10,512]{2,1,0:T(8,128)} %gather_fusion.3, pred[96]{0:T(512)(128)(4,1)S(1)} %get-tuple-element.48, pred[96]{0:T(512)(128)(4,1)S(1)} %subtract_compare_fusion), kind=kLoop, calls=%fused_computation.4 | loop fusion | flops 983040 | bytes 5898432 | tf_op jit(solution)/shard_map/jit(_where)/select_n | solution.py:350
  77.2 10.6 %shard_map.142 = (bf16[96,8,512]{2,1,0:T(8,128)(2,1)}, f32[96,10,512]{2,1,0:T(8,128)S(1)}) custom-call(bf16[96,4,512]{2,1,0:T(4,128)(2,1)S(1)} %reshape.197.routed_ref, f32[96,10,512]{2,1,0:T(8,128)} %copy_select_fusion.carried_ref, f32[4,512]{1,0:T(4,128)S(1)} %copy-done.2, f32[1,512]{1,0:T(1,128)S(1)} %bitcast.20, bf16[7,512,512]{2,1,0:T(8,128)(2,1)} %conv_w_ref.1, ...), custom_call_target="tpu_custom_call" | custom-call | tf_op jit(solution)/shard_map/pallas_call | solution.py:252
  87.8 2.4 %copy.49 = f32[96,10,512]{2,0,1:T(8,128)} copy(f32[96,10,512]{2,1,0:T(8,128)S(1)} %get-tuple-element.39) | data formatting | bytes 3932160 | tf_op jit(solution)/shard_map/pallas_call | solution.py:252
  (38 shorter events, 0.2 us)
Async XLA Ops:
  0.6 26.0 %copy-start.7 = (f32[96,10,512]{2,0,1:T(8,128)S(1)}, f32[96,10,512]{2,0,1:T(8,128)}, u32[]{:S(2)}) copy-start(f32[96,10,512]{2,0,1:T(8,128)} %param.21) | copy-start | bytes 5898244
  53.2 11.1 %slice-start = ((s8[16777216]{0:T(1024)(128)(4,1)}), s8[4194304]{0:T(1024)(128)(4,1)S(1)}, s32[]{:S(2)}) async-start(s8[16777216]{0:T(1024)(128)(4,1)} %bitcast.34), calls=%async_computation | async-start | bytes 8388608
  55.9 8.4 %slice-start.1 = ((s8[16777216]{0:T(1024)(128)(4,1)}), s8[4194304]{0:T(1024)(128)(4,1)S(1)}, s32[]{:S(2)}) async-start(s8[16777216]{0:T(1024)(128)(4,1)} %bitcast.34), calls=%async_computation.1 | async-start | bytes 8388608
  58.7 5.6 %slice-start.2 = ((s8[16777216]{0:T(1024)(128)(4,1)}), s8[4194304]{0:T(1024)(128)(4,1)S(1)}, s32[]{:S(2)}) async-start(s8[16777216]{0:T(1024)(128)(4,1)} %bitcast.34), calls=%async_computation.2 | async-start | bytes 8388608
  61.5 2.8 %slice-start.3 = ((s8[16777216]{0:T(1024)(128)(4,1)}), s8[4194304]{0:T(1024)(128)(4,1)S(1)}, s32[]{:S(2)}) async-start(s8[16777216]{0:T(1024)(128)(4,1)} %bitcast.34), calls=%async_computation.3 | async-start | bytes 8388608
  72.2 5.0 %copy-start = (bf16[3,512,256]{2,1,0:T(8,128)(2,1)S(1)}, bf16[3,512,256]{2,1,0:T(8,128)(2,1)}, u32[]{:S(2)}) copy-start(bf16[3,512,256]{2,1,0:T(8,128)(2,1)} %in_w_ref.1) | copy-start | bytes 2359300
  72.2 5.0 %copy-start.1 = (bf16[256,512]{1,0:T(8,128)(2,1)S(1)}, bf16[256,512]{1,0:T(8,128)(2,1)}, u32[]{:S(2)}) copy-start(bf16[256,512]{1,0:T(8,128)(2,1)} %out_w_ref.1) | copy-start | bytes 786436
  72.2 5.0 %copy-start.2 = (f32[4,512]{1,0:T(4,128)S(1)}, f32[4,512]{1,0:T(4,128)}, u32[]{:S(2)}) copy-start(f32[4,512]{1,0:T(4,128)} %up_w_ref.1) | copy-start | bytes 24580
  72.2 5.0 %copy-start.3 = (f32[512]{0:T(512)S(1)}, f32[512]{0:T(512)}, u32[]{:S(2)}) copy-start(f32[512]{0:T(512)} %param.23) | copy-start | bytes 6148
  72.2 5.0 %copy-start.4 = (f32[512]{0:T(512)S(1)}, f32[512]{0:T(512)}, u32[]{:S(2)}) copy-start(f32[512]{0:T(512)} %param.25) | copy-start | bytes 6148
  72.2 5.0 %copy-start.5 = (f32[512]{0:T(512)S(1)}, f32[512]{0:T(512)}, u32[]{:S(2)}) copy-start(f32[512]{0:T(512)} %param.29) | copy-start | bytes 6148
  72.2 5.0 %copy-start.6 = (f32[256]{0:T(256)S(1)}, f32[256]{0:T(256)}, u32[]{:S(2)}) copy-start(f32[256]{0:T(256)} %param.27) | copy-start | bytes 3076

commit v8 on v7

--- a/solution.py
+++ b/solution.py
@@ -188,14 +188,30 @@
 
 
 def decode_kernel(
-    routed_ref, carried_ref, up_w_ref, up_b_ref, conv_w_ref, conv_b_ref, in_w_ref, in_b_ref, out_w_ref, out_b_ref,
-    decoded_ref, states_ref,
+    source_ref, moved_ref,
+    routed_ref, states_ref, arrived_ref, up_w_ref, up_b_ref, conv_w_ref, conv_b_ref, in_w_ref, in_b_ref, out_w_ref,
+    out_b_ref, decoded_ref, new_ref, carried_ref,
 ):
     slots, frame_count, _ = routed_ref.shape
     step_count = 2 * frame_count
+    rows = states_ref.shape[0]
     conv_taps = conv_w_ref.shape[0]
     res_taps = in_w_ref.shape[0]
-    kept = carried_ref.shape[1] - 2 - (res_taps - 1)
+    kept = rows - 2 - (res_taps - 1)
+    base = pl.program_id(0) * slots
+
+    carried_ref[...] = states_ref[...]
+
+    def bring(slot, carry):
+        @pl.when(moved_ref[base + slot] != 0)
+        def _():
+            source = source_ref[base + slot]
+            for r in range(rows):
+                carried_ref[r, pl.ds(slot, 1), :] = arrived_ref[source, pl.ds(r, 1), :]
+
+        return carry
+
+    lax.fori_loop(0, slots, bring, 0)
 
     def elu(value):
         return jnp.where(value > 0, value, jnp.exp(jnp.minimum(value, 0.0)) - 1.0)
@@ -203,7 +219,7 @@
     up_w = up_w_ref[...]
     up_b = up_b_ref[...]
     inputs = [routed_ref[:, f, :].astype(jnp.float32) for f in range(frame_count)]
-    carried = [carried_ref[:, r, :] for r in range(carried_ref.shape[1])]
+    carried = [carried_ref[r] for r in range(rows)]
     upsampled = []
     for f in range(frame_count):
         early_even = carried[0] if f == 0 else inputs[f - 1] * up_w[2:3]
@@ -233,50 +249,59 @@
     decoded = summed.astype(jnp.bfloat16)
     for t in range(step_count):
         decoded_ref[:, t, :] = decoded[t * slots : (t + 1) * slots]
-    states_ref[:, 0, :] = inputs[frame_count - 1] * up_w[2:3]
-    states_ref[:, 1, :] = inputs[frame_count - 1] * up_w[3:4]
-    tail = history.shape[0] // slots - kept
+    new_ref[0] = inputs[frame_count - 1] * up_w[2:3]
+    new_ref[1] = inputs[frame_count - 1] * up_w[3:4]
     for k in range(kept):
         row = history.shape[0] // slots - kept + k
-        states_ref[:, 2 + k, :] = history[row * slots : (row + 1) * slots].astype(jnp.float32)
+        new_ref[2 + k] = history[row * slots : (row + 1) * slots].astype(jnp.float32)
     for k in range(res_taps - 1):
         row = step_count - (res_taps - 1) + k
-        states_ref[:, 2 + kept + k, :] = active[row * slots : (row + 1) * slots]
-
-
-def decode(routed, carried, up_weight, up_bias, conv_weight, conv_bias, res_in_weight, res_in_bias, res_out_weight, res_out_bias):
+        new_ref[2 + kept + k] = active[row * slots : (row + 1) * slots]
+
+
+def decode(
+    routed, states, arrived, source, moved, up_weight, up_bias, conv_weight, conv_bias, res_in_weight, res_in_bias,
+    res_out_weight, res_out_bias,
+):
     conv_count, frame_count, chan_width = routed.shape
-    rows = carried.shape[1]
+    rows = states.shape[1]
     chunk = 32 if conv_count % 32 == 0 else conv_count
-    whole = lambda shape: pl.BlockSpec(shape, lambda i: (0,) * len(shape))
-    return pl.pallas_call(
+    whole = lambda shape: pl.BlockSpec(shape, lambda i, *_: (0,) * len(shape))
+    states_t = jnp.transpose(states, (1, 0, 2))
+    decoded, new_t = pl.pallas_call(
         decode_kernel,
-        grid=(conv_count // chunk,),
+        grid_spec=pltpu.PrefetchScalarGridSpec(
+            num_scalar_prefetch=2,
+            grid=(conv_count // chunk,),
+            in_specs=[
+                pl.BlockSpec((chunk, frame_count, chan_width), lambda i, *_: (i, 0, 0)),
+                pl.BlockSpec((rows, chunk, chan_width), lambda i, *_: (0, i, 0)),
+                whole(arrived.shape),
+                whole(up_weight.shape),
+                whole((1, chan_width)),
+                whole(conv_weight.shape),
+                whole((1, chan_width)),
+                whole(res_in_weight.shape),
+                whole((1, res_in_weight.shape[2])),
+                whole(res_out_weight.shape),
+                whole((1, chan_width)),
+            ],
+            out_specs=(
+                pl.BlockSpec((chunk, 2 * frame_count, chan_width), lambda i, *_: (i, 0, 0)),
+                pl.BlockSpec((rows, chunk, chan_width), lambda i, *_: (0, i, 0)),
+            ),
+            scratch_shapes=[pltpu.VMEM((rows, chunk, chan_width), jnp.float32)],
+        ),
         out_shape=(
             jax.ShapeDtypeStruct((conv_count, 2 * frame_count, chan_width), jnp.bfloat16),
-            jax.ShapeDtypeStruct((conv_count, rows, chan_width), jnp.float32),
-        ),
-        in_specs=[
-            pl.BlockSpec((chunk, frame_count, chan_width), lambda i: (i, 0, 0)),
-            pl.BlockSpec((chunk, rows, chan_width), lambda i: (i, 0, 0)),
-            whole(up_weight.shape),
-            whole((1, chan_width)),
-            whole(conv_weight.shape),
-            whole((1, chan_width)),
-            whole(res_in_weight.shape),
-            whole((1, res_in_weight.shape[2])),
-            whole(res_out_weight.shape),
-            whole((1, chan_width)),
-        ],
-        out_specs=(
-            pl.BlockSpec((chunk, 2 * frame_count, chan_width), lambda i: (i, 0, 0)),
-            pl.BlockSpec((chunk, rows, chan_width), lambda i: (i, 0, 0)),
+            jax.ShapeDtypeStruct((rows, conv_count, chan_width), jnp.float32),
         ),
         compiler_params=pltpu.CompilerParams(vmem_limit_bytes=48 * 1024 * 1024),
     )(
-        routed, carried, up_weight, up_bias.reshape(1, -1), conv_weight, conv_bias.reshape(1, -1),
-        res_in_weight, res_in_bias.reshape(1, -1), res_out_weight, res_out_bias.reshape(1, -1),
-    )
+        source, moved, routed, states_t, arrived, up_weight, up_bias.reshape(1, -1), conv_weight,
+        conv_bias.reshape(1, -1), res_in_weight, res_in_bias.reshape(1, -1), res_out_weight, res_out_bias.reshape(1, -1),
+    )
+    return decoded, jnp.transpose(new_t, (1, 0, 2))
 
 
 def local(
@@ -346,11 +371,12 @@
     my_codes = jnp.take(answered, key, axis=0)
     routed = embed_codes(my_codes, code_table)
     arrived = arrived.reshape(leaving.shape)
-    brought = jnp.take(arrived, jnp.clip(source_dev, 0, per_group - 1), axis=0)
-    carried = jnp.where(moved[:, None, None], brought, states)
     return decode(
         routed,
-        carried,
+        states,
+        arrived,
+        jnp.clip(source_dev, 0, per_group - 1),
+        moved.astype(jnp.int32),
         up_weight,
         up_bias,
         conv_weight,

time: 90.6 us -> 84.2 us (0.929)
  other arithmetic: 8.9 us -> 3.97 us
  local copies, waits for them, and re-layouts: 17.7 us -> 14.9 us
  Pallas kernels: 47.5 us -> 48.7 us
    select_n x1 -> x0, other arithmetic: 4.92 us -> none  [local(): carried = jnp.where(moved[:, None, None], brought, states)]
    gather x1 -> x0, local copies, waits for them, and re-layouts: 2.42 us -> none  [local(): brought = jnp.take(arrived, jnp.clip(source_dev, 0, per_group - 1), axis=0)]
    pallas_call x1 -> x0, local copies, waits for them, and re-layouts: 2.41 us -> none  [decode(): pl.pallas_call(decode_kernel, grid=(conv_count // chunk,), out_shape=(jax...]
    unnamed x26, local copies, waits for them, and re-layouts: 1.8 us -> 3.88 us
    pallas_call x1, Pallas kernels: 10.6 us -> 12 us  [decode(): pl.pallas_call(decode_kernel, grid_spec=pltpu.PrefetchScalarGridSpec(num_...]
where the time goes in v8:
time: 84.2 us; the launch traced here: 83.7 us
  Pallas kernels  48.7 us (58%)
  matrix products  15.1 us (18%)
  local copies, waits for them, and re-layouts  14.9 us (18%)
  other arithmetic  3.97 us (5%)
  between operations  1.05 us (1%)
    pallas_call x2, Pallas kernels, exchange(): pl.pallas_call(kernel, out_shape=shapes + mids, in_specs=[pl.BlockSpec(me...  36.7 us
    dot_general x8, matrix products, embed_codes(): jnp.dot(onehot, book_rows, preferred_element_type=jnp.float32)  15.1 us
    pallas_call x1, Pallas kernels, decode(): pl.pallas_call(decode_kernel, grid_spec=pltpu.PrefetchScalarGridSpec(num_...  12 us
    gather x3, local copies, waits for them, and re-layouts, local(): leaving = jnp.take(states, jnp.clip(state_asked, 0, conv_count - 1), axis=0)  4.19 us
    unnamed x26, local copies, waits for them, and re-layouts  3.88 us

profile of v8, /device:TPU:1, one launch (start us, length us, event | category | flops | bytes accessed | tf_op | source)
XLA Modules:
  0.0 83.7 jit_solution(3486471329108250145)
XLA Ops:
  0.6 0.8 fusion.54
  1.5 0.7 fusion.55
  2.1 0.1 select_reduce_fusion.1
  2.3 0.7 and_select_fusion.2
  2.9 0.2 convert_reduce_fusion
  3.1 0.1 select_reduce_fusion
  3.3 0.1 broadcast_in_dim.81
  3.4 0.1 broadcast_in_dim.82
  3.5 0.8 copy.38
  4.3 0.1 sub.33
  4.4 0.1 copy.35
  4.5 0.1 pad_add_fusion
  4.6 0.7 scatter.6.refs_0_
  5.3 18.2 %shard_map.140 = (s32[4,32,1,128]{3,2,1,0:T(1,128)}, s32[4,32,1,128]{3,2,1,0:T(1,128)}) custom-call(s32[128,1,128]{2,1,0:T(1,128)} %scatter.6.refs_0_), custom_call_target="tpu_custom_call" | custom-call | tf_op jit(solution)/shard_map/pallas_call | solution.py:171
  23.5 0.9 %copy.42 = s32[128,1,3]{0,2,1:T(4,128)S(1)} copy(s32[128,1,3]{2,0,1:T(8,128)} %bitcast.30) | data formatting | bytes 3072
  24.4 0.1 and_bitcast_fusion
  24.5 0.2 copy.39
  24.7 0.1 copy.37
  24.8 0.1 min.30
  25.0 0.7 gather_fusion
  25.7 0.1 gather.19
  25.8 0.1 broadcast_select_fusion.2
  25.9 0.7 scatter.9.refs_0_
  26.6 1.5 %gather_fusion.1 = f32[32,10,512]{2,0,1:T(8,128)S(1)} fusion(f32[96,10,512]{2,0,1:T(8,128)S(1)} %copy-done, s32[1024]{0:T(1024)S(1)} %pad_clamp_fusion.1), kind=kCustom, calls=%fused_computation.1 | custom fusion | bytes 1310848 | tf_op jit(solution)/shard_map/jit(_take)/gather | solution.py:365
  28.1 1.4 %copy.41 = f32[32,10,512]{2,1,0:T(8,128)} copy(f32[32,10,512]{2,0,1:T(8,128)S(1)} %gather_fusion.1) | data formatting | bytes 1310720 | tf_op jit(solution)/shard_map/jit(_take)/gather | solution.py:365
  29.5 1.3 %gather.21 = f32[32,40,128]{2,1,0:T(8,128)S(1)} reshape(f32[32,10,512]{2,1,0:T(8,128)} %copy.41) | data formatting | bytes 1310720 | tf_op jit(solution)/shard_map/jit(_take)/gather | solution.py:365
  30.8 0.9 %broadcast_select_fusion.refs_1_ = f32[32,40,128]{2,1,0:T(8,128)} fusion(f32[32,40,128]{2,1,0:T(8,128)S(1)} %gather.21, pred[32]{0:T(512)(128)(4,1)S(1)} %get-tuple-element.46), kind=kLoop, calls=%fused_computation.44 | loop fusion | flops 163840 | bytes 1310752 | tf_op jit(solution)/shard_map/jit(_take)/select_n | solution.py:365
  31.7 18.5 %shard_map.141 = (s32[4,32,1,128]{3,2,1,0:T(1,128)}, f32[32,40,128]{2,1,0:T(8,128)}, s32[4,32,1,128]{3,2,1,0:T(1,128)}) custom-call(s32[128,1,128]{2,1,0:T(1,128)} %scatter.9.refs_0_, f32[32,40,128]{2,1,0:T(8,128)} %broadcast_select_fusion.refs_1_), custom_call_target="tpu_custom_call" | custom-call | tf_op jit(solution)/shard_map/pallas_call | solution.py:171
  50.3 0.9 %reshape_squeeze.3 = s32[256,32]{1,0:T(8,128)S(1)} reshape(s32[128,1,64]{2,0,1:T(8,128)} %bitcast.29) | data formatting | bytes 65536 | tf_op jit(solution)/shard_map/reshape;squeeze | solution.py:370
  51.2 0.6 gather_fusion.2
  51.8 0.1 gather.23
  52.0 0.1 broadcast_select_fusion.1
  52.1 0.9 %slice_reduce_fusion = (s32[384]{0:T(512)S(1)}, s32[384]{0:T(512)S(1)}, s32[384]{0:T(512)S(1)}, s32[384]{0:T(512)S(1)}, s32[384]{0:T(512)S(1)}, /*index=5*/s32[384]{0:T(512)S(1)}, s32[384]{0:T(512)S(1)}, s32[384]{0:T(512)S(1)}) fusion(s32[384,8]{1,0:T(8,128)S(1)} %broadcast_select_fusion.1), kind=kLoop, calls=%fused_computation.45 | loop fusion | bytes 24576 | tf_op jit(solution)/shard_map/slice | solution.py:20
  53.0 2.8 %fusion = f32[384,512]{1,0:T(8,128)S(1)} fusion(bf16[16384,512]{1,0:T(8,128)(2,1)} %param.18, s32[384]{0:T(512)S(1)} %get-tuple-element.43), kind=kOutput, calls=%fused_computation.11 | convolution fusion | flops 806092800 | bytes 2885120 | tf_op jit(solution)/shard_map/dot_general | solution.py:22
  55.7 0.0 slice-start.1
  55.7 2.8 %fusion.45 = f32[384,512]{1,0:T(8,128)S(1)} fusion(f32[384,512]{1,0:T(8,128)S(1)} %fusion, bf16[16384,512]{1,0:T(8,128)(2,1)} %param.18, s32[384]{0:T(512)S(1)} %get-tuple-element.42), kind=kOutput, calls=%fused_computation.42 | convolution fusion | flops 806289408 | bytes 3671552 | tf_op jit(solution)/shard_map/dot_general | solution.py:22
  58.5 2.8 %fusion.42 = f32[384,512]{1,0:T(8,128)S(1)} fusion(f32[384,512]{1,0:T(8,128)S(1)} %fusion.45, bf16[16384,512]{1,0:T(8,128)(2,1)} %param.18, s32[384]{0:T(512)S(1)} %get-tuple-element.41), kind=kOutput, calls=%fused_computation.41 | convolution fusion | flops 806289408 | bytes 3671552 | tf_op jit(solution)/shard_map/dot_general | solution.py:22
  61.3 2.8 %fusion.39 = f32[384,512]{1,0:T(8,128)S(1)} fusion(f32[384,512]{1,0:T(8,128)S(1)} %fusion.42, bf16[16384,512]{1,0:T(8,128)(2,1)} %param.18, s32[384]{0:T(512)S(1)} %get-tuple-element.40), kind=kOutput, calls=%fused_computation.40 | convolution fusion | flops 806289408 | bytes 3671552 | tf_op jit(solution)/shard_map/dot_general | solution.py:22
  64.1 0.0 slice-done.3
  64.1 1.0 %fusion.36 = f32[384,512]{1,0:T(8,128)S(1)} fusion(f32[384,512]{1,0:T(8,128)S(1)} %fusion.39, bf16[16384,512]{1,0:T(8,128)(2,1)S(1)} %bitcast.38, s32[384]{0:T(512)S(1)} %get-tuple-element.39), kind=kOutput, calls=%fused_computation.39 | convolution fusion | flops 806289408 | bytes 3672064 | tf_op jit(solution)/shard_map/dot_general | solution.py:22
  65.2 1.0 %fusion.33 = f32[384,512]{1,0:T(8,128)S(1)} fusion(f32[384,512]{1,0:T(8,128)S(1)} %fusion.36, bf16[16384,512]{1,0:T(8,128)(2,1)S(1)} %bitcast.38, s32[384]{0:T(512)S(1)} %get-tuple-element.38), kind=kOutput, calls=%fused_computation.38 | convolution fusion | flops 806289408 | bytes 3672064 | tf_op jit(solution)/shard_map/dot_general | solution.py:22
  66.2 1.0 %fusion.30 = f32[384,512]{1,0:T(8,128)S(1)} fusion(f32[384,512]{1,0:T(8,128)S(1)} %fusion.33, bf16[16384,512]{1,0:T(8,128)(2,1)S(1)} %bitcast.38, s32[384]{0:T(512)S(1)} %get-tuple-element.37), kind=kOutput, calls=%fused_computation.37 | convolution fusion | flops 806289408 | bytes 3672064 | tf_op jit(solution)/shard_map/dot_general | solution.py:22
  67.3 1.0 %fusion.48 = bf16[384,512]{1,0:T(8,128)(2,1)S(1)} fusion(f32[384,512]{1,0:T(8,128)S(1)} %fusion.30, bf16[16384,512]{1,0:T(8,128)(2,1)S(1)} %bitcast.38, s32[384]{0:T(512)S(1)} %get-tuple-element.36), kind=kOutput, calls=%fused_computation.43 | convolution fusion | flops 806682624 | bytes 3278848 | tf_op jit(solution)/shard_map/dot_general | solution.py:22
  68.3 0.1 reshape.191.routed_ref
  68.4 1.2 %reshape.192.arrived_ref = f32[32,10,512]{2,1,0:T(8,128)S(1)} reshape(f32[32,40,128]{2,1,0:T(8,128)} %get-tuple-element.33) | data formatting | bytes 1310720 | tf_op jit(solution)/shard_map/reshape | solution.py:373
  69.7 1.1 %copy-done.1 = bf16[3,512,256]{2,1,0:T(8,128)(2,1)S(1)} copy-done((bf16[3,512,256]{2,1,0:T(8,128)(2,1)S(1)}, bf16[3,512,256]{2,1,0:T(8,128)(2,1)}, u32[]{:S(2)}) %copy-start.1) | copy-done | bytes 786456
  70.8 0.9 %copy-done.2 = bf16[256,512]{1,0:T(8,128)(2,1)S(1)} copy-done((bf16[256,512]{1,0:T(8,128)(2,1)S(1)}, bf16[256,512]{1,0:T(8,128)(2,1)}, u32[]{:S(2)}) %copy-start.2) | copy-done | bytes 262168
  71.7 12.0 %shard_map.142 = (bf16[96,8,512]{2,1,0:T(8,128)(2,1)}, f32[10,96,512]{2,1,0:T(8,128)}) custom-call(s32[96]{0:T(128)S(1)} %subtract_clamp_fusion.source_ref, s32[96]{0:T(128)S(1)} %get-tuple-element.48.moved_ref, bf16[96,4,512]{2,1,0:T(4,128)(2,1)S(1)} %reshape.191.routed_ref, f32[10,96,512]{2,1,0:T(8,128)S(1)} %bitcast.22, ...), custom_call_target="tpu_custom_call" | custom-call | tf_op jit(solution)/shard_map/pallas_call | solution.py:271
  (34 shorter events, 0.2 us)
Async XLA Ops:
  0.6 26.0 %copy-start = (f32[96,10,512]{2,0,1:T(8,128)S(1)}, f32[96,10,512]{2,0,1:T(8,128)}, u32[]{:S(2)}) copy-start(f32[96,10,512]{2,0,1:T(8,128)} %param.21) | copy-start | bytes 5898244
  53.0 11.1 %slice-start = ((s8[16777216]{0:T(1024)(128)(4,1)}), s8[4194304]{0:T(1024)(128)(4,1)S(1)}, s32[]{:S(2)}) async-start(s8[16777216]{0:T(1024)(128)(4,1)} %bitcast.37), calls=%async_computation | async-start | bytes 8388608
  55.7 8.3 %slice-start.1 = ((s8[16777216]{0:T(1024)(128)(4,1)}), s8[4194304]{0:T(1024)(128)(4,1)S(1)}, s32[]{:S(2)}) async-start(s8[16777216]{0:T(1024)(128)(4,1)} %bitcast.37), calls=%async_computation.1 | async-start | bytes 8388608
  58.5 5.6 %slice-start.2 = ((s8[16777216]{0:T(1024)(128)(4,1)}), s8[4194304]{0:T(1024)(128)(4,1)S(1)}, s32[]{:S(2)}) async-start(s8[16777216]{0:T(1024)(128)(4,1)} %bitcast.37), calls=%async_computation.2 | async-start | bytes 8388608
  61.3 2.8 %slice-start.3 = ((s8[16777216]{0:T(1024)(128)(4,1)}), s8[4194304]{0:T(1024)(128)(4,1)S(1)}, s32[]{:S(2)}) async-start(s8[16777216]{0:T(1024)(128)(4,1)} %bitcast.37), calls=%async_computation.3 | async-start | bytes 8388608
  67.2 2.4 %copy-start.3 = (f32[4,512]{1,0:T(4,128)S(1)}, f32[4,512]{1,0:T(4,128)}, u32[]{:S(2)}) copy-start(f32[4,512]{1,0:T(4,128)} %up_w_ref.1) | copy-start | bytes 24580
  67.2 2.4 %copy-start.4 = (f32[512]{0:T(512)S(1)}, f32[512]{0:T(512)}, u32[]{:S(2)}) copy-start(f32[512]{0:T(512)} %param.23) | copy-start | bytes 6148
  67.2 2.4 %copy-start.5 = (f32[512]{0:T(512)S(1)}, f32[512]{0:T(512)}, u32[]{:S(2)}) copy-start(f32[512]{0:T(512)} %param.25) | copy-start | bytes 6148
  67.2 2.4 %copy-start.6 = (f32[512]{0:T(512)S(1)}, f32[512]{0:T(512)}, u32[]{:S(2)}) copy-start(f32[512]{0:T(512)} %param.29) | copy-start | bytes 6148
  67.2 2.4 %copy-start.7 = (f32[256]{0:T(256)S(1)}, f32[256]{0:T(256)}, u32[]{:S(2)}) copy-start(f32[256]{0:T(256)} %param.27) | copy-start | bytes 3076
  69.6 1.1 %copy-start.1 = (bf16[3,512,256]{2,1,0:T(8,128)(2,1)S(1)}, bf16[3,512,256]{2,1,0:T(8,128)(2,1)}, u32[]{:S(2)}) copy-start(bf16[3,512,256]{2,1,0:T(8,128)(2,1)} %in_w_ref.1) | copy-start | bytes 2359300
  70.8 0.9 %copy-start.2 = (bf16[256,512]{1,0:T(8,128)(2,1)S(1)}, bf16[256,512]{1,0:T(8,128)(2,1)}, u32[]{:S(2)}) copy-start(bf16[256,512]{1,0:T(8,128)(2,1)} %out_w_ref.1) | copy-start | bytes 786436

commit v9 on v8

--- a/solution.py
+++ b/solution.py
@@ -9,19 +9,43 @@
 MOST = 2
 
 
+def embed_kernel(codes_ref, table_ref, out_ref, total_ref):
+    book = pl.program_id(0)
+
+    @pl.when(book == 0)
+    def _():
+        total_ref[...] = jnp.zeros_like(total_ref)
+
+    rows = codes_ref.shape[1]
+    entries = lax.broadcasted_iota(jnp.int32, (rows, table_ref.shape[0]), 1)
+    onehot = (codes_ref[0] == entries).astype(jnp.bfloat16)
+    total_ref[...] += jnp.dot(onehot, table_ref[...], preferred_element_type=jnp.float32)
+
+    @pl.when(book == pl.num_programs(0) - 1)
+    def _():
+        out_ref[...] = total_ref[...].astype(jnp.bfloat16)
+
+
 def embed_codes(codes, code_table):
     row_count = codes.shape[0]
     book_count = codes.shape[1] // FRAMES
     book_size = code_table.shape[0] // book_count
-    grouped = codes.reshape(row_count * FRAMES, book_count)
-    entries = jnp.arange(book_size, dtype=jnp.int32)
-    summed = jnp.zeros((row_count * FRAMES, code_table.shape[1]), jnp.float32)
-    for book_index in range(book_count):
-        onehot = (grouped[:, book_index][:, None] == entries[None, :]).astype(jnp.bfloat16)
-        book_rows = code_table[book_index * book_size : (book_index + 1) * book_size]
-        summed = summed + jnp.dot(onehot, book_rows, preferred_element_type=jnp.float32)
-    summed = lax.reduce_precision(summed, exponent_bits=8, mantissa_bits=7)
-    return summed.astype(jnp.bfloat16).reshape(row_count, FRAMES, code_table.shape[1])
+    chan_width = code_table.shape[1]
+    by_book = codes.reshape(row_count, FRAMES, book_count).transpose(2, 1, 0).reshape(book_count, -1, 1)
+    rows = FRAMES * row_count
+    summed = pl.pallas_call(
+        embed_kernel,
+        grid=(book_count,),
+        in_specs=[
+            pl.BlockSpec((1, rows, 1), lambda q: (q, 0, 0)),
+            pl.BlockSpec((book_size, chan_width), lambda q: (q, 0)),
+        ],
+        out_specs=pl.BlockSpec((rows, chan_width), lambda q: (0, 0)),
+        out_shape=jax.ShapeDtypeStruct((rows, chan_width), jnp.bfloat16),
+        scratch_shapes=[pltpu.VMEM((rows, chan_width), jnp.float32)],
+        compiler_params=pltpu.CompilerParams(vmem_limit_bytes=32 * 1024 * 1024),
+    )(by_book, code_table)
+    return summed.reshape(FRAMES, row_count, chan_width)
 
 
 def pick_rows(table, index, live):
@@ -192,7 +216,7 @@
     routed_ref, states_ref, arrived_ref, up_w_ref, up_b_ref, conv_w_ref, conv_b_ref, in_w_ref, in_b_ref, out_w_ref,
     out_b_ref, decoded_ref, new_ref, carried_ref,
 ):
-    slots, frame_count, _ = routed_ref.shape
+    frame_count, slots, _ = routed_ref.shape
     step_count = 2 * frame_count
     rows = states_ref.shape[0]
     conv_taps = conv_w_ref.shape[0]
@@ -218,7 +242,7 @@
 
     up_w = up_w_ref[...]
     up_b = up_b_ref[...]
-    inputs = [routed_ref[:, f, :].astype(jnp.float32) for f in range(frame_count)]
+    inputs = [routed_ref[f].astype(jnp.float32) for f in range(frame_count)]
     carried = [carried_ref[r] for r in range(rows)]
     upsampled = []
     for f in range(frame_count):
@@ -263,7 +287,7 @@
     routed, states, arrived, source, moved, up_weight, up_bias, conv_weight, conv_bias, res_in_weight, res_in_bias,
     res_out_weight, res_out_bias,
 ):
-    conv_count, frame_count, chan_width = routed.shape
+    frame_count, conv_count, chan_width = routed.shape
     rows = states.shape[1]
     chunk = 32 if conv_count % 32 == 0 else conv_count
     whole = lambda shape: pl.BlockSpec(shape, lambda i, *_: (0,) * len(shape))
@@ -274,7 +298,7 @@
             num_scalar_prefetch=2,
             grid=(conv_count // chunk,),
             in_specs=[
-                pl.BlockSpec((chunk, frame_count, chan_width), lambda i, *_: (i, 0, 0)),
+                pl.BlockSpec((frame_count, chunk, chan_width), lambda i, *_: (0, i, 0)),
                 pl.BlockSpec((rows, chunk, chan_width), lambda i, *_: (0, i, 0)),
                 whole(arrived.shape),
                 whole(up_weight.shape),

time: 84.2 us -> 83 us (0.986)
  matrix products: 15.1 us -> 0 us
  Pallas kernels: 48.7 us -> 56.6 us
  local copies, waits for them, and re-layouts: 14.9 us -> 21.1 us
    dot_general x8 -> x0, matrix products: 15.1 us -> none  [embed_codes(): jnp.dot(onehot, book_rows, preferred_element_type=jnp.float32)]
    pallas_call x0 -> x1, Pallas kernels: none -> 8.3 us  [embed_codes(): pl.pallas_call(embed_kernel, grid=(book_count,), in_specs=[pl.BlockSpec((...]
    unnamed x26 -> x22, local copies, waits for them, and re-layouts: 3.88 us -> 7.51 us
    reshape x1, local copies, waits for them, and re-layouts: 0.1 us -> 2.2 us  [embed_codes(): codes.reshape(row_count, FRAMES, book_count).transpose(2, 1, 0)]
    reshape x1, local copies, waits for them, and re-layouts: 1.2 us -> 2.15 us  [local(): arrived = arrived.reshape(leaving.shape)]
    slice x1 -> x0, local copies, waits for them, and re-layouts: 0.87 us -> none  [embed_codes(): grouped[:, book_index][:, None] == entries[None, :]]
where the time goes in v9:
time: 83 us; the launch traced here: 82.5 us
  Pallas kernels  56.6 us (68%)
  local copies, waits for them, and re-layouts  21.1 us (25%)
  other arithmetic  3.86 us (5%)
  between operations  0.93 us (1%)
    pallas_call x2, Pallas kernels, exchange(): pl.pallas_call(kernel, out_shape=shapes + mids, in_specs=[pl.BlockSpec(me...  36.7 us
    pallas_call x1, Pallas kernels, decode(): pl.pallas_call(decode_kernel, grid_spec=pltpu.PrefetchScalarGridSpec(num_...  11.6 us
    pallas_call x1, Pallas kernels, embed_codes(): pl.pallas_call(embed_kernel, grid=(book_count,), in_specs=[pl.BlockSpec((...  8.3 us
    unnamed x22, local copies, waits for them, and re-layouts  7.51 us
    gather x3, local copies, waits for them, and re-layouts, local(): leaving = jnp.take(states, jnp.clip(state_asked, 0, conv_count - 1), axis=0)  4.19 us
    reshape x1, local copies, waits for them, and re-layouts, embed_codes(): codes.reshape(row_count, FRAMES, book_count).transpose(2, 1, 0)  2.2 us
    reshape x1, local copies, waits for them, and re-layouts, local(): arrived = arrived.reshape(leaving.shape)  2.15 us

profile of v9, /device:TPU:1, one launch (start us, length us, event | category | flops | bytes accessed | tf_op | source)
XLA Modules:
  0.0 82.5 jit_solution(2328980599168440462)
XLA Ops:
  0.6 0.0 copy-start
  0.6 0.8 fusion.4
  1.5 0.7 fusion.5
  2.1 0.1 select_reduce_fusion.1
  2.3 0.7 and_select_fusion.2
  2.9 0.2 convert_reduce_fusion
  3.1 0.1 select_reduce_fusion
  3.3 0.8 copy.45
  4.1 0.1 sub.33
  4.2 0.1 copy.42
  4.3 0.1 pad_add_fusion
  4.4 0.7 scatter.6.refs_0_
  5.1 18.2 %shard_map.140 = (s32[4,32,1,128]{3,2,1,0:T(1,128)}, s32[4,32,1,128]{3,2,1,0:T(1,128)}) custom-call(s32[128,1,128]{2,1,0:T(1,128)} %scatter.6.refs_0_), custom_call_target="tpu_custom_call" | custom-call | tf_op jit(solution)/shard_map/pallas_call | solution.py:195
  23.3 0.9 %copy.52 = s32[128,1,3]{0,2,1:T(4,128)S(1)} copy(s32[128,1,3]{2,0,1:T(8,128)} %bitcast.38) | data formatting | bytes 3072
  24.2 0.1 and_bitcast_fusion
  24.3 0.2 copy.46
  24.5 0.1 copy.44
  24.6 0.1 min.30
  24.8 0.7 gather_fusion
  25.5 0.1 gather.19
  25.6 0.1 broadcast_select_fusion.1
  25.7 0.7 scatter.9.refs_0_
  26.4 0.0 copy-done
  26.4 1.5 %gather_fusion.1 = f32[32,10,512]{2,0,1:T(8,128)S(1)} fusion(f32[96,10,512]{2,0,1:T(8,128)S(1)} %copy-done, s32[1024]{0:T(1024)S(1)} %pad_clamp_fusion.1), kind=kCustom, calls=%fused_computation.1 | custom fusion | bytes 1310848 | tf_op jit(solution)/shard_map/jit(_take)/gather | solution.py:389
  27.9 1.4 %copy.48 = f32[32,10,512]{2,1,0:T(8,128)} copy(f32[32,10,512]{2,0,1:T(8,128)S(1)} %gather_fusion.1) | data formatting | bytes 1310720 | tf_op jit(solution)/shard_map/jit(_take)/gather | solution.py:389
  29.3 1.3 %gather.21 = f32[32,40,128]{2,1,0:T(8,128)S(1)} reshape(f32[32,10,512]{2,1,0:T(8,128)} %copy.48) | data formatting | bytes 1310720 | tf_op jit(solution)/shard_map/jit(_take)/gather | solution.py:389
  30.6 0.9 %broadcast_select_fusion.refs_1_ = f32[32,40,128]{2,1,0:T(8,128)} fusion(f32[32,40,128]{2,1,0:T(8,128)S(1)} %gather.21, pred[32]{0:T(512)(128)(4,1)S(1)} %get-tuple-element.38), kind=kLoop, calls=%fused_computation.3 | loop fusion | flops 163840 | bytes 1310752 | tf_op jit(solution)/shard_map/jit(_take)/select_n | solution.py:389
  31.6 18.5 %shard_map.141 = (s32[4,32,1,128]{3,2,1,0:T(1,128)}, f32[32,40,128]{2,1,0:T(8,128)}, s32[4,32,1,128]{3,2,1,0:T(1,128)}) custom-call(s32[128,1,128]{2,1,0:T(1,128)} %scatter.9.refs_0_, f32[32,40,128]{2,1,0:T(8,128)} %broadcast_select_fusion.refs_1_), custom_call_target="tpu_custom_call" | custom-call | tf_op jit(solution)/shard_map/pallas_call | solution.py:195
  50.1 0.9 %reshape_squeeze.3 = s32[256,32]{1,0:T(8,128)S(1)} reshape(s32[128,1,64]{2,0,1:T(8,128)} %bitcast.37) | data formatting | bytes 65536 | tf_op jit(solution)/shard_map/reshape;squeeze | solution.py:394
  51.0 0.6 gather_fusion.2
  51.7 0.1 copy.49
  51.7 0.6 copy.50
  52.4 2.2 %reshape.200.arrived_ref = f32[32,10,512]{2,1,0:T(8,128)} reshape(f32[32,40,128]{2,1,0:T(8,128)} %get-tuple-element.33) | data formatting | bytes 1310720 | tf_op jit(solution)/shard_map/reshape | solution.py:397
  54.5 2.2 %reshape.230.codes_ref = s32[8,384,1]{2,1,0:T(8,128)S(1)} reshape(s32[8,4,96]{2,1,0:T(4,128)} %copy.50) | data formatting | bytes 24576 | tf_op jit(solution)/shard_map/reshape | solution.py:34
  56.7 0.0 copy-start.1
  56.7 5.8 %copy-done.1 = bf16[16384,512]{1,0:T(8,128)(2,1)S(1)} copy-done((bf16[16384,512]{1,0:T(8,128)(2,1)S(1)}, bf16[16384,512]{1,0:T(8,128)(2,1)}, u32[]{:S(2)}) %copy-start.1) | copy-done | bytes 16777240
  62.5 0.0 copy-start.6
  62.5 0.0 copy-start.7
  62.5 0.0 copy-start.8
  62.5 0.0 copy-start.9
  62.5 8.3 %shard_map.142 = bf16[384,512]{1,0:T(8,128)(2,1)S(1)} custom-call(s32[8,384,1]{2,1,0:T(8,128)S(1)} %reshape.230.codes_ref, bf16[16384,512]{1,0:T(8,128)(2,1)S(1)} %copy-done.1), custom_call_target="tpu_custom_call" | custom-call | tf_op jit(solution)/shard_map/pallas_call | solution.py:36
  70.9 0.0 copy-done.2
  70.9 0.0 copy-done.3
  70.9 0.0 copy-done.4
  70.9 0.0 copy-done.5
  70.9 0.0 copy-done.6
  70.9 0.0 copy-done.7
  70.9 11.6 %shard_map.143 = (bf16[96,8,512]{2,1,0:T(8,128)(2,1)}, f32[10,96,512]{2,1,0:T(8,128)}) custom-call(s32[96]{0:T(128)S(1)} %subtract_clamp_fusion.source_ref, s32[96]{0:T(128)S(1)} %get-tuple-element.40.moved_ref, bf16[4,96,512]{2,1,0:T(8,128)(2,1)S(1)} %bitcast.30, f32[10,96,512]{2,1,0:T(8,128)S(1)} %bitcast.29, f32[32,10,512]{2,1,0:T(8,128)S(1)} %copy-done.2, ...), custom_call_target="tpu_custom_call" | custom-call | tf_op jit(solution)/shard_map/pallas_call | solution.py:295
  (20 shorter events, 0.1 us)
Async XLA Ops:
  0.6 25.8 %copy-start = (f32[96,10,512]{2,0,1:T(8,128)S(1)}, f32[96,10,512]{2,0,1:T(8,128)}, u32[]{:S(2)}) copy-start(f32[96,10,512]{2,0,1:T(8,128)} %param.21) | copy-start | bytes 5898244
  56.7 5.8 %copy-start.1 = (bf16[16384,512]{1,0:T(8,128)(2,1)S(1)}, bf16[16384,512]{1,0:T(8,128)(2,1)}, u32[]{:S(2)}) copy-start(bf16[16384,512]{1,0:T(8,128)(2,1)} %table_ref.1) | copy-start | bytes 50331652
  62.5 8.4 %copy-start.2 = (f32[32,10,512]{2,1,0:T(8,128)S(1)}, f32[32,10,512]{2,1,0:T(8,128)}, u32[]{:S(2)}) copy-start(f32[32,10,512]{2,1,0:T(8,128)} %reshape.200.arrived_ref) | copy-start | bytes 1966084
  62.5 8.4 %copy-start.3 = (bf16[3,512,256]{2,1,0:T(8,128)(2,1)S(1)}, bf16[3,512,256]{2,1,0:T(8,128)(2,1)}, u32[]{:S(2)}) copy-start(bf16[3,512,256]{2,1,0:T(8,128)(2,1)} %in_w_ref.1) | copy-start | bytes 2359300
  62.5 8.4 %copy-start.4 = (bf16[256,512]{1,0:T(8,128)(2,1)S(1)}, bf16[256,512]{1,0:T(8,128)(2,1)}, u32[]{:S(2)}) copy-start(bf16[256,512]{1,0:T(8,128)(2,1)} %out_w_ref.1) | copy-start | bytes 786436
  62.5 8.4 %copy-start.5 = (f32[4,512]{1,0:T(4,128)S(1)}, f32[4,512]{1,0:T(4,128)}, u32[]{:S(2)}) copy-start(f32[4,512]{1,0:T(4,128)} %up_w_ref.1) | copy-start | bytes 24580
  62.5 8.4 %copy-start.6 = (f32[512]{0:T(512)S(1)}, f32[512]{0:T(512)}, u32[]{:S(2)}) copy-start(f32[512]{0:T(512)} %param.23) | copy-start | bytes 6148
  62.5 8.4 %copy-start.7 = (f32[512]{0:T(512)S(1)}, f32[512]{0:T(512)}, u32[]{:S(2)}) copy-start(f32[512]{0:T(512)} %param.25) | copy-start | bytes 6148
  62.5 8.4 %copy-start.8 = (f32[512]{0:T(512)S(1)}, f32[512]{0:T(512)}, u32[]{:S(2)}) copy-start(f32[512]{0:T(512)} %param.29) | copy-start | bytes 6148
  62.5 8.4 %copy-start.9 = (f32[256]{0:T(256)S(1)}, f32[256]{0:T(256)}, u32[]{:S(2)}) copy-start(f32[256]{0:T(256)} %param.27) | copy-start | bytes 3076

commit v10 on v9

--- a/solution.py
+++ b/solution.py
@@ -9,21 +9,26 @@
 MOST = 2
 
 
-def embed_kernel(codes_ref, table_ref, out_ref, total_ref):
-    book = pl.program_id(0)
-
-    @pl.when(book == 0)
-    def _():
-        total_ref[...] = jnp.zeros_like(total_ref)
-
-    rows = codes_ref.shape[1]
-    entries = lax.broadcasted_iota(jnp.int32, (rows, table_ref.shape[0]), 1)
-    onehot = (codes_ref[0] == entries).astype(jnp.bfloat16)
-    total_ref[...] += jnp.dot(onehot, table_ref[...], preferred_element_type=jnp.float32)
-
-    @pl.when(book == pl.num_programs(0) - 1)
-    def _():
-        out_ref[...] = total_ref[...].astype(jnp.bfloat16)
+def embed_kernel(codes_ref, table_ref, out_ref, blocks, sems):
+    books, rows = codes_ref.shape
+    size = blocks.shape[1]
+
+    def fetch(book):
+        return pltpu.make_async_copy(table_ref.at[pl.ds(book * size, size)], blocks.at[book % 2], sems.at[book % 2])
+
+    fetch(0).start()
+    total = None
+    for book in range(books):
+        if book + 1 < books:
+            fetch(book + 1).start()
+        fetch(book).wait()
+        entries = lax.broadcasted_iota(jnp.int32, (size, rows), 0)
+        onehot = (codes_ref[book : book + 1, :] == entries).astype(jnp.bfloat16)
+        term = lax.dot_general(
+            onehot, blocks[book % 2], (((0,), (0,)), ((), ())), preferred_element_type=jnp.float32
+        )
+        total = term if total is None else total + term
+    out_ref[...] = total.astype(jnp.bfloat16)
 
 
 def embed_codes(codes, code_table):
@@ -31,19 +36,17 @@
     book_count = codes.shape[1] // FRAMES
     book_size = code_table.shape[0] // book_count
     chan_width = code_table.shape[1]
-    by_book = codes.reshape(row_count, FRAMES, book_count).transpose(2, 1, 0).reshape(book_count, -1, 1)
+    by_book = codes.reshape(row_count, FRAMES, book_count).transpose(2, 1, 0).reshape(book_count, -1)
     rows = FRAMES * row_count
     summed = pl.pallas_call(
         embed_kernel,
-        grid=(book_count,),
-        in_specs=[
-            pl.BlockSpec((1, rows, 1), lambda q: (q, 0, 0)),
-            pl.BlockSpec((book_size, chan_width), lambda q: (q, 0)),
+        in_specs=[pl.BlockSpec(memory_space=pltpu.VMEM), pl.BlockSpec(memory_space=pl.ANY)],
+        out_specs=pl.BlockSpec(memory_space=pltpu.VMEM),
+        out_shape=jax.ShapeDtypeStruct((rows, chan_width), jnp.bfloat16),
+        scratch_shapes=[
+            pltpu.VMEM((2, book_size, chan_width), code_table.dtype),
+            pltpu.SemaphoreType.DMA((2,)),
         ],
-        out_specs=pl.BlockSpec((rows, chan_width), lambda q: (0, 0)),
-        out_shape=jax.ShapeDtypeStruct((rows, chan_width), jnp.bfloat16),
-        scratch_shapes=[pltpu.VMEM((rows, chan_width), jnp.float32)],
-        compiler_params=pltpu.CompilerParams(vmem_limit_bytes=32 * 1024 * 1024),
     )(by_book, code_table)
     return summed.reshape(FRAMES, row_count, chan_width)
 
@@ -205,6 +208,7 @@
             pltpu.SemaphoreType.DMA(()),
         ],
         compiler_params=pltpu.CompilerParams(collective_id=collective_id, has_side_effects=True),
+        cost_estimate=pl.CostEstimate(flops=0, transcendentals=0, bytes_accessed=48 * 1024 * 1024),
     )(*[blocks for blocks, _ in items])
     return [
         result.reshape(blocks.shape) for result, (blocks, _) in zip(results[:count], items)
@@ -388,13 +392,12 @@
     state_asked = lax.dynamic_slice_in_dim(asked[:, most], group_first, per_group)
     leaving = jnp.take(states, jnp.clip(state_asked, 0, conv_count - 1), axis=0)
     answered, arrived = exchange(
-        [(answer, True), (leaving.reshape(per_group, -1, lanes), False)], 1
+        [(answer, True), (leaving, False)], 1
     )
     code_width = codes.shape[1]
     answered = answered[:, 0, : most * code_width].reshape(devices_all * most, code_width)
     my_codes = jnp.take(answered, key, axis=0)
     routed = embed_codes(my_codes, code_table)
-    arrived = arrived.reshape(leaving.shape)
     return decode(
         routed,
         states,

time: 83 us -> 85.4 us (1.029)
  the two profiles are of different devices: /device:TPU:1 before, /device:TPU:5 now
where the time goes in v10:
time: 85.4 us; the launch traced here: 84.9 us
  Pallas kernels  69.1 us (81%)
  local copies, waits for them, and re-layouts  10.5 us (12%)
  other arithmetic  4.32 us (5%)
  between operations  0.91 us (1%)
    pallas_call x2, Pallas kernels, exchange(): pl.pallas_call(kernel, out_shape=shapes + mids, in_specs=[pl.BlockSpec(me...  45.2 us
    pallas_call x1, Pallas kernels, embed_codes(): pl.pallas_call(embed_kernel, in_specs=[pl.BlockSpec(memory_space=pltpu.VM...  12.3 us
    pallas_call x1, Pallas kernels, decode(): pl.pallas_call(decode_kernel, grid_spec=pltpu.PrefetchScalarGridSpec(num_...  11.6 us
    unnamed x22, local copies, waits for them, and re-layouts  3.87 us

profile of v10, /device:TPU:5, one launch (start us, length us, event | category | flops | bytes accessed | tf_op | source)
XLA Modules:
  0.0 84.9 jit_solution(9687743393352348332)
XLA Ops:
  0.6 0.0 copy-start
  0.6 0.8 fusion.4
  1.5 0.7 fusion.5
  2.1 0.1 select_reduce_fusion.1
  2.3 0.7 and_select_fusion.2
  2.9 0.2 convert_reduce_fusion
  3.1 0.1 select_reduce_fusion
  3.3 0.8 copy.42
  4.1 0.1 sub.33
  4.2 0.1 copy.39
  4.3 0.1 pad_add_fusion
  4.4 0.7 scatter.6.refs_0_
  5.1 16.5 %shard_map.140 = (s32[4,32,1,128]{3,2,1,0:T(1,128)}, s32[4,32,1,128]{3,2,1,0:T(1,128)}) custom-call(s32[128,1,128]{2,1,0:T(1,128)} %scatter.6.refs_0_), custom_call_target="tpu_custom_call" | custom-call | bytes 50331648 | tf_op jit(solution)/shard_map/pallas_call | solution.py:198
  21.6 0.9 %copy.48 = s32[128,1,3]{0,2,1:T(4,128)S(1)} copy(s32[128,1,3]{2,0,1:T(8,128)} %bitcast.38) | data formatting | bytes 3072
  22.6 0.1 and_bitcast_fusion
  22.7 0.2 copy.43
  22.9 0.1 copy.41
  23.0 0.1 min.30
  23.1 0.7 gather_fusion
  23.9 0.1 gather.17
  24.0 0.1 broadcast_select_fusion
  24.1 0.7 scatter.9.refs_0_
  24.8 0.0 copy-done
  24.8 1.5 %gather_fusion.1 = f32[32,10,512]{2,0,1:T(8,128)S(1)} fusion(f32[96,10,512]{2,0,1:T(8,128)S(1)} %copy-done, s32[1024]{0:T(1024)S(1)} %pad_clamp_fusion.1), kind=kCustom, calls=%fused_computation.1 | custom fusion | bytes 1310848 | tf_op jit(solution)/shard_map/jit(_take)/gather | solution.py:393
  26.3 1.4 %copy_select_fusion.refs_1_ = f32[32,10,512]{2,1,0:T(8,128)} fusion(f32[32,10,512]{2,0,1:T(8,128)S(1)} %gather_fusion.1, pred[32]{0:T(512)(128)(4,1)S(1)} %get-tuple-element.38), kind=kLoop, calls=%fused_computation.3 | loop fusion | flops 163840 | bytes 1310752 | tf_op jit(solution)/shard_map/jit(_take)/select_n | solution.py:393
  27.7 28.7 %shard_map.141 = (s32[4,32,1,128]{3,2,1,0:T(1,128)}, f32[32,10,512]{2,1,0:T(8,128)}, s32[4,32,1,128]{3,2,1,0:T(1,128)}) custom-call(s32[128,1,128]{2,1,0:T(1,128)} %scatter.9.refs_0_, f32[32,10,512]{2,1,0:T(8,128)} %copy_select_fusion.refs_1_), custom_call_target="tpu_custom_call" | custom-call | bytes 50331648 | tf_op jit(solution)/shard_map/pallas_call | solution.py:198
  56.4 0.9 %reshape_squeeze.3 = s32[256,32]{1,0:T(8,128)S(1)} reshape(s32[128,1,64]{2,0,1:T(8,128)} %bitcast.37) | data formatting | bytes 65536 | tf_op jit(solution)/shard_map/reshape;squeeze | solution.py:398
  57.3 0.6 gather_fusion.2
  57.9 0.1 copy.46
  58.0 0.7 reshape.193.codes_ref
  58.7 0.0 copy-start.2
  58.7 0.0 copy-start.4
  58.7 0.0 copy-start.5
  58.7 0.0 copy-start.7
  58.7 0.0 copy-start.8
  58.7 0.0 copy-start.9
  58.7 12.3 %shard_map.142 = bf16[384,512]{1,0:T(8,128)(2,1)} custom-call(s32[8,384]{1,0:T(8,128)} %reshape.193.codes_ref, bf16[16384,512]{1,0:T(8,128)(2,1)} %table_ref.1), custom_call_target="tpu_custom_call" | custom-call | tf_op jit(solution)/shard_map/pallas_call | solution.py:41
  71.1 0.0 copy-done.2
  71.1 0.0 copy-done.4
  71.1 0.0 copy-done.5
  71.1 0.0 copy-done.6
  71.1 0.0 copy-done.7
  71.1 0.0 copy-done.8
  71.1 0.0 copy-done.9
  71.2 0.0 copy-start.1
  71.2 1.0 %copy-done.1 = bf16[384,512]{1,0:T(8,128)(2,1)S(1)} copy-done((bf16[384,512]{1,0:T(8,128)(2,1)S(1)}, bf16[384,512]{1,0:T(8,128)(2,1)}, u32[]{:S(2)}) %copy-start.1) | copy-done | bytes 393240
  72.2 1.1 %copy-done.3 = bf16[3,512,256]{2,1,0:T(8,128)(2,1)S(1)} copy-done((bf16[3,512,256]{2,1,0:T(8,128)(2,1)S(1)}, bf16[3,512,256]{2,1,0:T(8,128)(2,1)}, u32[]{:S(2)}) %copy-start.3) | copy-done | bytes 786456
  73.3 11.6 %shard_map.143 = (bf16[96,8,512]{2,1,0:T(8,128)(2,1)}, f32[10,96,512]{2,1,0:T(8,128)}) custom-call(s32[96]{0:T(128)S(1)} %subtract_clamp_fusion.source_ref, s32[96]{0:T(128)S(1)} %get-tuple-element.40.moved_ref, bf16[4,96,512]{2,1,0:T(8,128)(2,1)S(1)} %bitcast.30, f32[10,96,512]{2,1,0:T(8,128)S(1)} %bitcast.29, f32[32,10,512]{2,1,0:T(8,128)S(1)} %copy-done.2, ...), custom_call_target="tpu_custom_call" | custom-call | tf_op jit(solution)/shard_map/pallas_call | solution.py:299
  (17 shorter events, 0.1 us)
Async XLA Ops:
  0.6 24.1 %copy-start = (f32[96,10,512]{2,0,1:T(8,128)S(1)}, f32[96,10,512]{2,0,1:T(8,128)}, u32[]{:S(2)}) copy-start(f32[96,10,512]{2,0,1:T(8,128)} %param.21) | copy-start | bytes 5898244
  58.7 12.4 %copy-start.2 = (f32[32,10,512]{2,1,0:T(8,128)S(1)}, f32[32,10,512]{2,1,0:T(8,128)}, u32[]{:S(2)}) copy-start(f32[32,10,512]{2,1,0:T(8,128)} %get-tuple-element.33.arrived_ref) | copy-start | bytes 1966084
  58.7 12.4 %copy-start.4 = (bf16[256,512]{1,0:T(8,128)(2,1)S(1)}, bf16[256,512]{1,0:T(8,128)(2,1)}, u32[]{:S(2)}) copy-start(bf16[256,512]{1,0:T(8,128)(2,1)} %out_w_ref.1) | copy-start | bytes 786436
  58.7 12.4 %copy-start.5 = (f32[4,512]{1,0:T(4,128)S(1)}, f32[4,512]{1,0:T(4,128)}, u32[]{:S(2)}) copy-start(f32[4,512]{1,0:T(4,128)} %up_w_ref.1) | copy-start | bytes 24580
  58.7 12.4 %copy-start.6 = (f32[512]{0:T(512)S(1)}, f32[512]{0:T(512)}, u32[]{:S(2)}) copy-start(f32[512]{0:T(512)} %param.23) | copy-start | bytes 6148
  58.7 12.4 %copy-start.7 = (f32[512]{0:T(512)S(1)}, f32[512]{0:T(512)}, u32[]{:S(2)}) copy-start(f32[512]{0:T(512)} %param.25) | copy-start | bytes 6148
  58.7 12.4 %copy-start.8 = (f32[512]{0:T(512)S(1)}, f32[512]{0:T(512)}, u32[]{:S(2)}) copy-start(f32[512]{0:T(512)} %param.29) | copy-start | bytes 6148
  58.7 12.4 %copy-start.9 = (f32[256]{0:T(256)S(1)}, f32[256]{0:T(256)}, u32[]{:S(2)}) copy-start(f32[256]{0:T(256)} %param.27) | copy-start | bytes 3076
  71.2 1.0 %copy-start.1 = (bf16[384,512]{1,0:T(8,128)(2,1)S(1)}, bf16[384,512]{1,0:T(8,128)(2,1)}, u32[]{:S(2)}) copy-start(bf16[384,512]{1,0:T(8,128)(2,1)} %shard_map.142) | copy-start | bytes 1179652
  72.2 1.1 %copy-start.3 = (bf16[3,512,256]{2,1,0:T(8,128)(2,1)S(1)}, bf16[3,512,256]{2,1,0:T(8,128)(2,1)}, u32[]{:S(2)}) copy-start(bf16[3,512,256]{2,1,0:T(8,128)(2,1)} %in_w_ref.1) | copy-start | bytes 2359300

commit v11 on v10

--- a/solution.py
+++ b/solution.py
@@ -17,16 +17,15 @@
         return pltpu.make_async_copy(table_ref.at[pl.ds(book * size, size)], blocks.at[book % 2], sems.at[book % 2])
 
     fetch(0).start()
+    by_row = jnp.transpose(codes_ref[...])
     total = None
     for book in range(books):
         if book + 1 < books:
             fetch(book + 1).start()
         fetch(book).wait()
-        entries = lax.broadcasted_iota(jnp.int32, (size, rows), 0)
-        onehot = (codes_ref[book : book + 1, :] == entries).astype(jnp.bfloat16)
-        term = lax.dot_general(
-            onehot, blocks[book % 2], (((0,), (0,)), ((), ())), preferred_element_type=jnp.float32
-        )
+        entries = lax.broadcasted_iota(jnp.int32, (rows, size), 1)
+        onehot = (by_row[:, book : book + 1] == entries).astype(jnp.bfloat16)
+        term = jnp.dot(onehot, blocks[book % 2], preferred_element_type=jnp.float32)
         total = term if total is None else total + term
     out_ref[...] = total.astype(jnp.bfloat16)
 
@@ -217,7 +216,7 @@
 
 def decode_kernel(
     source_ref, moved_ref,
-    routed_ref, states_ref, arrived_ref, up_w_ref, up_b_ref, conv_w_ref, conv_b_ref, in_w_ref, in_b_ref, out_w_ref,
+    routed_ref, states_ref, arrived_ref, arrived_low_ref, up_w_ref, up_b_ref, conv_w_ref, conv_b_ref, in_w_ref, in_b_ref, out_w_ref,
     out_b_ref, decoded_ref, new_ref, carried_ref,
 ):
     frame_count, slots, _ = routed_ref.shape
@@ -234,8 +233,15 @@
         @pl.when(moved_ref[base + slot] != 0)
         def _():
             source = source_ref[base + slot]
+            pieces = carried_ref.shape[2] // arrived_ref.shape[2]
             for r in range(rows):
-                carried_ref[r, pl.ds(slot, 1), :] = arrived_ref[source, pl.ds(r, 1), :]
+                if r < 2:
+                    row = arrived_ref[source, pl.ds(r * pieces, pieces), :]
+                else:
+                    row = arrived_low_ref[source, pl.ds((r - 2) * pieces, pieces), :].astype(jnp.float32)
+                carried_ref[r, pl.ds(slot, 1), :] = jnp.concatenate(
+                    [row[k : k + 1] for k in range(pieces)], axis=1
+                )
 
         return carry
 
@@ -288,7 +294,7 @@
 
 
 def decode(
-    routed, states, arrived, source, moved, up_weight, up_bias, conv_weight, conv_bias, res_in_weight, res_in_bias,
+    routed, states, arrived, arrived_low, source, moved, up_weight, up_bias, conv_weight, conv_bias, res_in_weight, res_in_bias,
     res_out_weight, res_out_bias,
 ):
     frame_count, conv_count, chan_width = routed.shape
@@ -305,6 +311,7 @@
                 pl.BlockSpec((frame_count, chunk, chan_width), lambda i, *_: (0, i, 0)),
                 pl.BlockSpec((rows, chunk, chan_width), lambda i, *_: (0, i, 0)),
                 whole(arrived.shape),
+                whole(arrived_low.shape),
                 whole(up_weight.shape),
                 whole((1, chan_width)),
                 whole(conv_weight.shape),
@@ -326,7 +333,7 @@
         ),
         compiler_params=pltpu.CompilerParams(vmem_limit_bytes=48 * 1024 * 1024),
     )(
-        source, moved, routed, states_t, arrived, up_weight, up_bias.reshape(1, -1), conv_weight,
+        source, moved, routed, states_t, arrived, arrived_low, up_weight, up_bias.reshape(1, -1), conv_weight,
         conv_bias.reshape(1, -1), res_in_weight, res_in_bias.reshape(1, -1), res_out_weight, res_out_bias.reshape(1, -1),
     )
     return decoded, jnp.transpose(new_t, (1, 0, 2))
@@ -391,8 +398,10 @@
     )
     state_asked = lax.dynamic_slice_in_dim(asked[:, most], group_first, per_group)
     leaving = jnp.take(states, jnp.clip(state_asked, 0, conv_count - 1), axis=0)
-    answered, arrived = exchange(
-        [(answer, True), (leaving, False)], 1
+    leaving_high = leaving[:, :2].reshape(per_group, -1, lanes)
+    leaving_low = leaving[:, 2:].astype(jnp.bfloat16).reshape(per_group, -1, lanes)
+    answered, arrived, arrived_low = exchange(
+        [(answer, True), (leaving_high, False), (leaving_low, False)], 1
     )
     code_width = codes.shape[1]
     answered = answered[:, 0, : most * code_width].reshape(devices_all * most, code_width)
@@ -402,6 +411,7 @@
         routed,
         states,
         arrived,
+        arrived_low,
         jnp.clip(source_dev, 0, per_group - 1),
         moved.astype(jnp.int32),
         up_weight,

time: 85.4 us -> 75.7 us (0.89)
  the two profiles are of different devices: /device:TPU:5 before, /device:TPU:1 now
where the time goes in v11:
time: 75.7 us; the launch traced here: 75.2 us
  Pallas kernels  59.8 us (79%)
  local copies, waits for them, and re-layouts  11.3 us (15%)
  other arithmetic  3.06 us (4%)
  between operations  0.98 us (1%)
    pallas_call x2, Pallas kernels, exchange(): pl.pallas_call(kernel, out_shape=shapes + mids, in_specs=[pl.BlockSpec(me...  35.7 us
    pallas_call x1, Pallas kernels, embed_codes(): pl.pallas_call(embed_kernel, in_specs=[pl.BlockSpec(memory_space=pltpu.VM...  12.4 us
    pallas_call x1, Pallas kernels, decode(): pl.pallas_call(decode_kernel, grid_spec=pltpu.PrefetchScalarGridSpec(num_...  11.8 us
    unnamed x24, local copies, waits for them, and re-layouts  2.75 us

profile of v11, /device:TPU:1, one launch (start us, length us, event | category | flops | bytes accessed | tf_op | source)
XLA Modules:
  0.0 75.2 jit_solution(9516904386502452284)
XLA Ops:
  0.6 0.8 %fusion.4 = s32[96]{0:T(128)S(1)} fusion(s32[96]{0:T(128)} %param.20), kind=kLoop, calls=%fused_computation.33 | loop fusion | flops 672 | bytes 768 | tf_op jit(solution)/shard_map/add | solution.py:380
  1.5 0.7 fusion.5
  2.1 0.1 select_reduce_fusion.1
  2.3 0.7 and_select_fusion.2
  2.9 0.2 convert_reduce_fusion
  3.1 0.1 select_reduce_fusion
  3.3 0.8 %copy.46 = s32[96,32]{1,0:T(8,128)S(1)} copy(s32[96,32]{0,1:T(8,128)} %param.17) | data formatting | bytes 24576 | tf_op args[0]
  4.1 0.1 sub.33
  4.2 0.1 copy.43
  4.3 0.1 pad_add_fusion
  4.4 0.7 scatter.6.refs_0_
  5.1 18.2 %shard_map.140 = (s32[4,32,1,128]{3,2,1,0:T(1,128)}, s32[4,32,1,128]{3,2,1,0:T(1,128)}) custom-call(s32[128,1,128]{2,1,0:T(1,128)} %scatter.6.refs_0_), custom_call_target="tpu_custom_call" | custom-call | bytes 50331648 | tf_op jit(solution)/shard_map/pallas_call | solution.py:197
  23.3 0.9 %copy.53 = s32[128,1,3]{0,2,1:T(4,128)S(1)} copy(s32[128,1,3]{2,0,1:T(8,128)} %bitcast.38) | data formatting | bytes 3072
  24.2 0.1 and_bitcast_fusion
  24.3 0.2 copy.47
  24.5 0.1 copy.45
  24.6 0.1 min.30
  24.8 0.7 gather_fusion
  25.5 0.1 gather.17
  25.6 0.1 broadcast_select_fusion.1
  25.7 0.7 scatter.9.refs_0_
  26.4 0.0 copy-done
  26.4 1.5 %gather_fusion.1 = f32[32,10,512]{2,0,1:T(8,128)S(1)} fusion(f32[96,10,512]{2,0,1:T(8,128)S(1)} %copy-done, s32[1024]{0:T(1024)S(1)} %pad_clamp_fusion.1), kind=kCustom, calls=%fused_computation.1 | custom fusion | bytes 1310848 | tf_op jit(solution)/shard_map/jit(_take)/gather | solution.py:400
  27.9 0.1 broadcast_select_fusion
  28.1 0.2 copy.50
  28.3 0.9 %reshape.199.refs_2_ = bf16[32,32,128]{2,1,0:T(8,128)(2,1)} reshape(bf16[32,8,512]{2,1,0:T(8,128)(2,1)S(1)} %copy.50) | data formatting | bytes 524288 | tf_op jit(solution)/shard_map/reshape | solution.py:402
  29.1 0.1 copy.49
  29.3 0.8 %reshape.198.refs_1_ = f32[32,8,128]{2,1,0:T(8,128)} reshape(f32[32,2,512]{2,1,0:T(2,128)S(1)} %copy.49) | data formatting | bytes 262144 | tf_op jit(solution)/shard_map/reshape | solution.py:401
  30.0 17.5 %shard_map.141 = (s32[4,32,1,128]{3,2,1,0:T(1,128)}, f32[32,8,128]{2,1,0:T(8,128)}, bf16[32,32,128]{2,1,0:T(8,128)(2,1)}, s32[4,32,1,128]{3,2,1,0:T(1,128)}) custom-call(s32[128,1,128]{2,1,0:T(1,128)} %scatter.9.refs_0_, f32[32,8,128]{2,1,0:T(8,128)} %reshape.198.refs_1_, bf16[32,32,128]{2,1,0:T(8,128)(2,1)} %reshape.199.refs_2_), custom_call_target="tpu_custom_call" | custom-call | bytes 50331648 | tf_op jit(solution)/shard_map/pallas_call | solution.py:197
  47.6 0.9 %reshape_squeeze.3 = s32[256,32]{1,0:T(8,128)S(1)} reshape(s32[128,1,64]{2,0,1:T(8,128)} %bitcast.37) | data formatting | bytes 65536 | tf_op jit(solution)/shard_map/reshape;squeeze | solution.py:407
  48.5 0.6 gather_fusion.2
  49.1 0.1 copy.51
  49.2 0.7 reshape.201.codes_ref
  49.9 0.0 copy-start.6
  49.9 0.0 copy-start.7
  49.9 0.0 copy-start.8
  49.9 0.0 copy-start.9
  49.9 0.0 copy-start.10
  49.9 12.4 %shard_map.142 = bf16[384,512]{1,0:T(8,128)(2,1)} custom-call(s32[8,384]{1,0:T(8,128)} %reshape.201.codes_ref, bf16[16384,512]{1,0:T(8,128)(2,1)} %table_ref.1), custom_call_target="tpu_custom_call" | custom-call | tf_op jit(solution)/shard_map/pallas_call | solution.py:40
  62.3 0.0 copy-done.2
  62.4 0.0 copy-done.3
  62.4 0.0 copy-done.4
  62.4 0.0 copy-done.5
  62.4 0.0 copy-done.6
  62.4 0.0 copy-done.7
  62.4 0.0 copy-start.1
  62.4 1.0 %copy-done.1 = bf16[384,512]{1,0:T(8,128)(2,1)S(1)} copy-done((bf16[384,512]{1,0:T(8,128)(2,1)S(1)}, bf16[384,512]{1,0:T(8,128)(2,1)}, u32[]{:S(2)}) %copy-start.1) | copy-done | bytes 393240
  63.4 11.8 %shard_map.143 = (bf16[96,8,512]{2,1,0:T(8,128)(2,1)}, f32[10,96,512]{2,1,0:T(8,128)}) custom-call(s32[96]{0:T(128)S(1)} %subtract_clamp_fusion.source_ref, s32[96]{0:T(128)S(1)} %get-tuple-element.42.moved_ref, bf16[4,96,512]{2,1,0:T(8,128)(2,1)S(1)} %bitcast.30, f32[10,96,512]{2,1,0:T(8,128)S(1)} %bitcast.29, f32[32,8,128]{2,1,0:T(8,128)S(1)} %copy-done.5, ...), custom_call_target="tpu_custom_call" | custom-call | tf_op jit(solution)/shard_map/pallas_call | solution.py:305
  (25 shorter events, 0.2 us)
Async XLA Ops:
  0.6 25.8 %copy-start = (f32[96,10,512]{2,0,1:T(8,128)S(1)}, f32[96,10,512]{2,0,1:T(8,128)}, u32[]{:S(2)}) copy-start(f32[96,10,512]{2,0,1:T(8,128)} %param.21) | copy-start | bytes 5898244
  49.9 12.5 %copy-start.2 = (bf16[3,512,256]{2,1,0:T(8,128)(2,1)S(1)}, bf16[3,512,256]{2,1,0:T(8,128)(2,1)}, u32[]{:S(2)}) copy-start(bf16[3,512,256]{2,1,0:T(8,128)(2,1)} %in_w_ref.1) | copy-start | bytes 2359300
  49.9 12.5 %copy-start.3 = (bf16[256,512]{1,0:T(8,128)(2,1)S(1)}, bf16[256,512]{1,0:T(8,128)(2,1)}, u32[]{:S(2)}) copy-start(bf16[256,512]{1,0:T(8,128)(2,1)} %out_w_ref.1) | copy-start | bytes 786436
  49.9 12.5 %copy-start.4 = (bf16[32,32,128]{2,1,0:T(8,128)(2,1)S(1)}, bf16[32,32,128]{2,1,0:T(8,128)(2,1)}, u32[]{:S(2)}) copy-start(bf16[32,32,128]{2,1,0:T(8,128)(2,1)} %get-tuple-element.35.arrived_low_ref) | copy-start | bytes 786436
  49.9 12.5 %copy-start.5 = (f32[32,8,128]{2,1,0:T(8,128)S(1)}, f32[32,8,128]{2,1,0:T(8,128)}, u32[]{:S(2)}) copy-start(f32[32,8,128]{2,1,0:T(8,128)} %get-tuple-element.34.arrived_ref) | copy-start | bytes 393220
  49.9 12.5 %copy-start.6 = (f32[4,512]{1,0:T(4,128)S(1)}, f32[4,512]{1,0:T(4,128)}, u32[]{:S(2)}) copy-start(f32[4,512]{1,0:T(4,128)} %up_w_ref.1) | copy-start | bytes 24580
  49.9 12.5 %copy-start.7 = (f32[512]{0:T(512)S(1)}, f32[512]{0:T(512)}, u32[]{:S(2)}) copy-start(f32[512]{0:T(512)} %param.23) | copy-start | bytes 6148
  49.9 12.5 %copy-start.8 = (f32[512]{0:T(512)S(1)}, f32[512]{0:T(512)}, u32[]{:S(2)}) copy-start(f32[512]{0:T(512)} %param.25) | copy-start | bytes 6148
  49.9 12.5 %copy-start.9 = (f32[512]{0:T(512)S(1)}, f32[512]{0:T(512)}, u32[]{:S(2)}) copy-start(f32[512]{0:T(512)} %param.29) | copy-start | bytes 6148
  49.9 12.5 %copy-start.10 = (f32[256]{0:T(256)S(1)}, f32[256]{0:T(256)}, u32[]{:S(2)}) copy-start(f32[256]{0:T(256)} %param.27) | copy-start | bytes 3076
  62.4 1.0 %copy-start.1 = (bf16[384,512]{1,0:T(8,128)(2,1)S(1)}, bf16[384,512]{1,0:T(8,128)(2,1)}, u32[]{:S(2)}) copy-start(bf16[384,512]{1,0:T(8,128)(2,1)} %shard_map.142) | copy-start | bytes 1179652

commit v12 on v11

--- a/solution.py
+++ b/solution.py
@@ -14,18 +14,17 @@
     size = blocks.shape[1]
 
     def fetch(book):
-        return pltpu.make_async_copy(table_ref.at[pl.ds(book * size, size)], blocks.at[book % 2], sems.at[book % 2])
-
-    fetch(0).start()
+        return pltpu.make_async_copy(table_ref.at[pl.ds(book * size, size)], blocks.at[book], sems.at[book])
+
+    for book in range(books):
+        fetch(book).start()
     by_row = jnp.transpose(codes_ref[...])
     total = None
     for book in range(books):
-        if book + 1 < books:
-            fetch(book + 1).start()
         fetch(book).wait()
         entries = lax.broadcasted_iota(jnp.int32, (rows, size), 1)
         onehot = (by_row[:, book : book + 1] == entries).astype(jnp.bfloat16)
-        term = jnp.dot(onehot, blocks[book % 2], preferred_element_type=jnp.float32)
+        term = jnp.dot(onehot, blocks[book], preferred_element_type=jnp.float32)
         total = term if total is None else total + term
     out_ref[...] = total.astype(jnp.bfloat16)
 
@@ -43,8 +42,8 @@
         out_specs=pl.BlockSpec(memory_space=pltpu.VMEM),
         out_shape=jax.ShapeDtypeStruct((rows, chan_width), jnp.bfloat16),
         scratch_shapes=[
-            pltpu.VMEM((2, book_size, chan_width), code_table.dtype),
-            pltpu.SemaphoreType.DMA((2,)),
+            pltpu.VMEM((book_count, book_size, chan_width), code_table.dtype),
+            pltpu.SemaphoreType.DMA((book_count,)),
         ],
     )(by_book, code_table)
     return summed.reshape(FRAMES, row_count, chan_width)
@@ -388,14 +387,13 @@
         [code_request.reshape(devices_all, most), state_request.reshape(devices_all, 1)], axis=1
     )
     lanes = 128
-    padded = jnp.zeros((devices_all, 1, lanes), jnp.int32).at[:, 0, : most + 1].set(request)
+    padded = jnp.pad(request, ((0, 0), (0, lanes - most - 1))).reshape(devices_all, 1, lanes)
     (asked,) = exchange([(padded, True)], 0)
     asked = asked[:, 0, : most + 1]
 
     answer = jnp.take(codes, jnp.clip(asked[:, :most].reshape(-1), 0, conv_count - 1), axis=0)
-    answer = jnp.zeros((devices_all, 1, lanes), jnp.int32).at[:, 0, : answer.size // devices_all].set(
-        answer.reshape(devices_all, -1)
-    )
+    answer = answer.reshape(devices_all, -1)
+    answer = jnp.pad(answer, ((0, 0), (0, lanes - answer.shape[1]))).reshape(devices_all, 1, lanes)
     state_asked = lax.dynamic_slice_in_dim(asked[:, most], group_first, per_group)
     leaving = jnp.take(states, jnp.clip(state_asked, 0, conv_count - 1), axis=0)
     leaving_high = leaving[:, :2].reshape(per_group, -1, lanes)

time: 75.7 us -> 74.1 us (0.979)
  Pallas kernels: 59.8 us -> 58.6 us
    scatter x2 -> x0, local copies, waits for them, and re-layouts: 1.35 us -> none  [the longest x1 0.68 us: local(): jnp.zeros((devices_all, 1, lanes), jnp.int32).at[:, 0, :most + 1]]
    pallas_call x1, Pallas kernels: 12.4 us -> 11.1 us  [embed_codes(): pl.pallas_call(embed_kernel, in_specs=[pl.BlockSpec(memory_space=pltpu.VM...]
    pad x0 -> x2, local copies, waits for them, and re-layouts: none -> 1.27 us  [the longest x1 0.64 us: local(): jnp.pad(request, ((0, 0), (0, lanes - most - 1)))]
where the time goes in v12:
time: 74.1 us; the launch traced here: 73.7 us
  Pallas kernels  58.6 us (79%)
  local copies, waits for them, and re-layouts  11.2 us (15%)
  other arithmetic  2.96 us (4%)
  between operations  0.98 us (1%)
    pallas_call x2, Pallas kernels, exchange(): pl.pallas_call(kernel, out_shape=shapes + mids, in_specs=[pl.BlockSpec(me...  35.7 us
    pallas_call x1, Pallas kernels, decode(): pl.pallas_call(decode_kernel, grid_spec=pltpu.PrefetchScalarGridSpec(num_...  11.8 us
    pallas_call x1, Pallas kernels, embed_codes(): pl.pallas_call(embed_kernel, in_specs=[pl.BlockSpec(memory_space=pltpu.VM...  11.1 us
    unnamed x24, local copies, waits for them, and re-layouts  2.75 us
    gather x1, local copies, waits for them, and re-layouts, local(): leaving = jnp.take(states, jnp.clip(state_asked, 0, conv_count - 1), axis=0)  1.51 us

profile of v12, /device:TPU:1, one launch (start us, length us, event | category | flops | bytes accessed | tf_op | source)
XLA Modules:
  0.0 73.7 jit_solution(15187071381844960359)
XLA Ops:
  0.6 0.0 copy-start
  0.6 0.8 %fusion.4 = s32[96]{0:T(128)S(1)} fusion(s32[96]{0:T(128)} %param.16), kind=kLoop, calls=%fused_computation.33 | loop fusion | flops 672 | bytes 768 | tf_op jit(solution)/shard_map/add | solution.py:379
  1.5 0.7 fusion.5
  2.1 0.1 select_reduce_fusion.1
  2.3 0.7 and_select_fusion.2
  2.9 0.2 convert_reduce_fusion
  3.1 0.1 select_reduce_fusion
  3.3 0.8 %copy.44 = s32[96,32]{1,0:T(8,128)S(1)} copy(s32[96,32]{0,1:T(8,128)} %param.13) | data formatting | bytes 24576 | tf_op args[0]
  4.1 0.1 sub.33
  4.2 0.1 copy.41
  4.3 0.1 pad_add_fusion
  4.4 0.6 pad.8
  5.1 18.2 %shard_map.140 = (s32[4,32,1,128]{3,2,1,0:T(1,128)}, s32[4,32,1,128]{3,2,1,0:T(1,128)}) custom-call(s32[128,1,128]{2,1,0:T(1,128)} %bitcast.36), custom_call_target="tpu_custom_call" | custom-call | bytes 50331648 | tf_op jit(solution)/shard_map/pallas_call | solution.py:196
  23.2 0.9 %copy.50 = s32[128,1,3]{0,2,1:T(4,128)S(1)} copy(s32[128,1,3]{2,0,1:T(8,128)} %bitcast.38) | data formatting | bytes 3072
  24.2 0.1 and_bitcast_fusion
  24.3 0.1 copy.45
  24.4 0.1 copy.43
  24.5 0.1 min.30
  24.7 0.7 gather_fusion
  25.4 0.1 gather.17
  25.5 0.6 pad.9
  26.2 0.0 copy-done
  26.2 1.5 %gather_fusion.1 = f32[32,10,512]{2,0,1:T(8,128)S(1)} fusion(f32[96,10,512]{2,0,1:T(8,128)S(1)} %copy-done, s32[1024]{0:T(1024)S(1)} %pad_clamp_fusion.1), kind=kCustom, calls=%fused_computation.1 | custom fusion | bytes 1310848 | tf_op jit(solution)/shard_map/jit(_take)/gather | solution.py:398
  27.7 0.1 broadcast_select_fusion
  27.9 0.2 copy.47
  28.1 0.9 %reshape.118.refs_2_ = bf16[32,32,128]{2,1,0:T(8,128)(2,1)} reshape(bf16[32,8,512]{2,1,0:T(8,128)(2,1)S(1)} %copy.47) | data formatting | bytes 524288 | tf_op jit(solution)/shard_map/reshape | solution.py:400
  28.9 0.1 copy.46
  29.0 0.8 %reshape.117.refs_1_ = f32[32,8,128]{2,1,0:T(8,128)} reshape(f32[32,2,512]{2,1,0:T(2,128)S(1)} %copy.46) | data formatting | bytes 262144 | tf_op jit(solution)/shard_map/reshape | solution.py:399
  29.8 17.5 %shard_map.141 = (s32[4,32,1,128]{3,2,1,0:T(1,128)}, f32[32,8,128]{2,1,0:T(8,128)}, bf16[32,32,128]{2,1,0:T(8,128)(2,1)}, s32[4,32,1,128]{3,2,1,0:T(1,128)}) custom-call(s32[128,1,128]{2,1,0:T(1,128)} %bitcast.35, f32[32,8,128]{2,1,0:T(8,128)} %reshape.117.refs_1_, bf16[32,32,128]{2,1,0:T(8,128)(2,1)} %reshape.118.refs_2_), custom_call_target="tpu_custom_call" | custom-call | bytes 50331648 | tf_op jit(solution)/shard_map/pallas_call | solution.py:196
  47.3 0.9 %reshape_squeeze.3 = s32[256,32]{1,0:T(8,128)S(1)} reshape(s32[128,1,64]{2,0,1:T(8,128)} %bitcast.37) | data formatting | bytes 65536 | tf_op jit(solution)/shard_map/reshape;squeeze | solution.py:405
  48.3 0.6 gather_fusion.2
  48.9 0.1 copy.48
  49.0 0.7 reshape.120.codes_ref
  49.7 0.0 copy-start.6
  49.7 0.0 copy-start.7
  49.7 0.0 copy-start.8
  49.7 0.0 copy-start.9
  49.7 0.0 copy-start.10
  49.7 11.1 %shard_map.142 = bf16[384,512]{1,0:T(8,128)(2,1)} custom-call(s32[8,384]{1,0:T(8,128)} %reshape.120.codes_ref, bf16[16384,512]{1,0:T(8,128)(2,1)} %table_ref.1), custom_call_target="tpu_custom_call" | custom-call | tf_op jit(solution)/shard_map/pallas_call | solution.py:39
  60.8 0.0 copy-done.2
  60.8 0.0 copy-done.3
  60.9 0.0 copy-done.4
  60.9 0.0 copy-done.5
  60.9 0.0 copy-done.6
  60.9 0.0 copy-done.7
  60.9 0.0 copy-start.1
  60.9 1.0 %copy-done.1 = bf16[384,512]{1,0:T(8,128)(2,1)S(1)} copy-done((bf16[384,512]{1,0:T(8,128)(2,1)S(1)}, bf16[384,512]{1,0:T(8,128)(2,1)}, u32[]{:S(2)}) %copy-start.1) | copy-done | bytes 393240
  61.9 11.8 %shard_map.143 = (bf16[96,8,512]{2,1,0:T(8,128)(2,1)}, f32[10,96,512]{2,1,0:T(8,128)}) custom-call(s32[96]{0:T(128)S(1)} %subtract_clamp_fusion.source_ref, s32[96]{0:T(128)S(1)} %get-tuple-element.18.moved_ref, bf16[4,96,512]{2,1,0:T(8,128)(2,1)S(1)} %bitcast.30, f32[10,96,512]{2,1,0:T(8,128)S(1)} %bitcast.29, f32[32,8,128]{2,1,0:T(8,128)S(1)} %copy-done.5, ...), custom_call_target="tpu_custom_call" | custom-call | tf_op jit(solution)/shard_map/pallas_call | solution.py:304
  (25 shorter events, 0.2 us)
Async XLA Ops:
  0.6 25.5 %copy-start = (f32[96,10,512]{2,0,1:T(8,128)S(1)}, f32[96,10,512]{2,0,1:T(8,128)}, u32[]{:S(2)}) copy-start(f32[96,10,512]{2,0,1:T(8,128)} %param.17) | copy-start | bytes 5898244
  49.7 11.2 %copy-start.2 = (bf16[3,512,256]{2,1,0:T(8,128)(2,1)S(1)}, bf16[3,512,256]{2,1,0:T(8,128)(2,1)}, u32[]{:S(2)}) copy-start(bf16[3,512,256]{2,1,0:T(8,128)(2,1)} %in_w_ref.1) | copy-start | bytes 2359300
  49.7 11.2 %copy-start.3 = (bf16[256,512]{1,0:T(8,128)(2,1)S(1)}, bf16[256,512]{1,0:T(8,128)(2,1)}, u32[]{:S(2)}) copy-start(bf16[256,512]{1,0:T(8,128)(2,1)} %out_w_ref.1) | copy-start | bytes 786436
  49.7 11.2 %copy-start.4 = (bf16[32,32,128]{2,1,0:T(8,128)(2,1)S(1)}, bf16[32,32,128]{2,1,0:T(8,128)(2,1)}, u32[]{:S(2)}) copy-start(bf16[32,32,128]{2,1,0:T(8,128)(2,1)} %get-tuple-element.11.arrived_low_ref) | copy-start | bytes 786436
  49.7 11.2 %copy-start.5 = (f32[32,8,128]{2,1,0:T(8,128)S(1)}, f32[32,8,128]{2,1,0:T(8,128)}, u32[]{:S(2)}) copy-start(f32[32,8,128]{2,1,0:T(8,128)} %get-tuple-element.10.arrived_ref) | copy-start | bytes 393220
  49.7 11.2 %copy-start.6 = (f32[4,512]{1,0:T(4,128)S(1)}, f32[4,512]{1,0:T(4,128)}, u32[]{:S(2)}) copy-start(f32[4,512]{1,0:T(4,128)} %up_w_ref.1) | copy-start | bytes 24580
  49.7 11.2 %copy-start.7 = (f32[512]{0:T(512)S(1)}, f32[512]{0:T(512)}, u32[]{:S(2)}) copy-start(f32[512]{0:T(512)} %param.19) | copy-start | bytes 6148
  49.7 11.2 %copy-start.8 = (f32[512]{0:T(512)S(1)}, f32[512]{0:T(512)}, u32[]{:S(2)}) copy-start(f32[512]{0:T(512)} %param.21) | copy-start | bytes 6148
  49.7 11.2 %copy-start.9 = (f32[512]{0:T(512)S(1)}, f32[512]{0:T(512)}, u32[]{:S(2)}) copy-start(f32[512]{0:T(512)} %param.25) | copy-start | bytes 6148
  49.7 11.2 %copy-start.10 = (f32[256]{0:T(256)S(1)}, f32[256]{0:T(256)}, u32[]{:S(2)}) copy-start(f32[256]{0:T(256)} %param.23) | copy-start | bytes 3076
  60.9 1.0 %copy-start.1 = (bf16[384,512]{1,0:T(8,128)(2,1)S(1)}, bf16[384,512]{1,0:T(8,128)(2,1)}, u32[]{:S(2)}) copy-start(bf16[384,512]{1,0:T(8,128)(2,1)} %shard_map.142) | copy-start | bytes 1179652

commit v13 on v12

--- a/solution.py
+++ b/solution.py
@@ -211,6 +211,93 @@
     return [
         result.reshape(blocks.shape) for result, (blocks, _) in zip(results[:count], items)
     ]
+
+
+def exchange_hops(blocks, collective_id):
+    groups = lax.axis_size("grp")
+    per_group = lax.axis_size("dev")
+    rows = 4 if per_group % 4 == 0 else 1
+    cols = per_group // rows
+    tail = blocks.shape[1:]
+    first = jax.ShapeDtypeStruct((groups, rows, cols) + tail, blocks.dtype)
+    second = jax.ShapeDtypeStruct((rows, groups, cols) + tail, blocks.dtype)
+
+    def kernel(x_ref, out_ref, mid_one, mid_two, send_sems, recv_sems, own_sem):
+        group = lax.axis_index("grp")
+        dev = lax.axis_index("dev")
+        row = dev // cols
+        col = dev % cols
+        barrier = pltpu.get_barrier_semaphore()
+        stages = (
+            (groups, lambda peer: (peer, dev), group),
+            (rows, lambda peer: (group, peer * cols + col), row),
+            (cols, lambda peer: (group, row * cols + peer), col),
+        )
+        for size, device, me in stages:
+            def greet(offset, carry, size=size, device=device, me=me):
+                pl.semaphore_signal(
+                    barrier, inc=1, device_id=device(lax.rem(me + offset, size)), device_id_type=pl.DeviceIdType.MESH
+                )
+                return carry
+
+            lax.fori_loop(1, size, greet, 0)
+        pl.semaphore_wait(barrier, groups + rows + cols - 3)
+
+        def views(stage, peer, place):
+            if stage == 0:
+                return x_ref.at[peer], mid_one.at[place]
+            if stage == 1:
+                return mid_one.at[:, peer], mid_two.at[place]
+            return mid_two.at[:, :, peer], out_ref.at[:, :, place]
+
+        for stage, (size, device, me) in enumerate(stages):
+            def copy(peer, place, stage=stage, device=device):
+                source, target = views(stage, peer, place)
+                return pltpu.make_async_remote_copy(
+                    src_ref=source,
+                    dst_ref=target,
+                    send_sem=send_sems.at[stage, peer],
+                    recv_sem=recv_sems.at[stage, place],
+                    device_id=device(peer),
+                    device_id_type=pl.DeviceIdType.MESH,
+                )
+
+            def send(offset, carry, size=size, me=me, copy=copy):
+                copy(lax.rem(me + offset, size), me).start()
+                return carry
+
+            lax.fori_loop(1, size, send, 0)
+            source, target = views(stage, me, me)
+            if stage == 0:
+                own = pltpu.make_async_copy(x_ref.at[group], mid_one.at[group], own_sem)
+            else:
+                own = pltpu.make_async_copy(source, target, own_sem)
+            own.start()
+            own.wait()
+
+            def finish(offset, carry, size=size, me=me, copy=copy):
+                copy(lax.rem(me + offset, size), me).wait_send()
+                source = lax.rem(me + size - offset, size)
+                copy(source, source).wait_recv()
+                return carry
+
+            lax.fori_loop(1, size, finish, 0)
+
+    widest = max(groups, rows, cols)
+    result, _, _ = pl.pallas_call(
+        kernel,
+        out_shape=[jax.ShapeDtypeStruct((rows, groups, cols) + tail, blocks.dtype), first, second],
+        in_specs=[pl.BlockSpec(memory_space=pl.ANY)],
+        out_specs=[pl.BlockSpec(memory_space=pl.ANY)] * 3,
+        scratch_shapes=[
+            pltpu.SemaphoreType.DMA((3, widest)),
+            pltpu.SemaphoreType.DMA((3, widest)),
+            pltpu.SemaphoreType.DMA(()),
+        ],
+        compiler_params=pltpu.CompilerParams(collective_id=collective_id, has_side_effects=True),
+        cost_estimate=pl.CostEstimate(flops=0, transcendentals=0, bytes_accessed=48 * 1024 * 1024),
+    )(blocks.reshape((groups, rows, cols) + tail))
+    return jnp.transpose(result, (1, 0) + tuple(range(2, result.ndim))).reshape(blocks.shape)
 
 
 def decode_kernel(
@@ -388,7 +475,7 @@
     )
     lanes = 128
     padded = jnp.pad(request, ((0, 0), (0, lanes - most - 1))).reshape(devices_all, 1, lanes)
-    (asked,) = exchange([(padded, True)], 0)
+    asked = exchange_hops(padded, 0)
     asked = asked[:, 0, : most + 1]
 
     answer = jnp.take(codes, jnp.clip(asked[:, :most].reshape(-1), 0, conv_count - 1), axis=0)

time: 74.1 us -> 76.1 us (1.027)
  Pallas kernels: 58.6 us -> 60.4 us
    pallas_call x0 -> x1, Pallas kernels: none -> 19.8 us  [exchange_hops(): pl.pallas_call(kernel, out_shape=[jax.ShapeDtypeStruct((rows, groups, col...]
    pallas_call x2 -> x1, Pallas kernels: 35.7 us -> 17.7 us  [exchange(): pl.pallas_call(kernel, out_shape=shapes + mids, in_specs=[pl.BlockSpec(me...]
    transpose x0 -> x1, local copies, waits for them, and re-layouts: none -> 0.85 us  [exchange_hops(): jnp.transpose(result, (1, 0) + tuple(range(2, result.ndim)))]
    unnamed x24, local copies, waits for them, and re-layouts: 2.75 us -> 1.97 us
where the time goes in v13:
time: 76.1 us; the launch traced here: 75.7 us
  Pallas kernels  60.4 us (79%)
  local copies, waits for them, and re-layouts  11.3 us (15%)
  other arithmetic  3.07 us (4%)
  between operations  0.98 us (1%)
    pallas_call x1, Pallas kernels, exchange_hops(): pl.pallas_call(kernel, out_shape=[jax.ShapeDtypeStruct((rows, groups, col...  19.8 us
    pallas_call x1, Pallas kernels, exchange(): pl.pallas_call(kernel, out_shape=shapes + mids, in_specs=[pl.BlockSpec(me...  17.7 us
    pallas_call x1, Pallas kernels, decode(): pl.pallas_call(decode_kernel, grid_spec=pltpu.PrefetchScalarGridSpec(num_...  11.8 us
    pallas_call x1, Pallas kernels, embed_codes(): pl.pallas_call(embed_kernel, in_specs=[pl.BlockSpec(memory_space=pltpu.VM...  11.1 us
    unnamed x24, local copies, waits for them, and re-layouts  1.97 us

profile of v13, /device:TPU:1, one launch (start us, length us, event | category | flops | bytes accessed | tf_op | source)
XLA Modules:
  0.0 75.7 jit_solution(4674554233770900435)
XLA Ops:
  0.6 0.0 copy-start
  0.6 0.8 %fusion.5 = s32[96]{0:T(128)S(1)} fusion(s32[96]{0:T(128)} %param.16), kind=kLoop, calls=%fused_computation.35 | loop fusion | flops 672 | bytes 768 | tf_op jit(solution)/shard_map/add | solution.py:466
  1.5 0.7 fusion.6
  2.1 0.1 select_reduce_fusion.1
  2.3 0.7 and_select_fusion.2
  2.9 0.2 convert_reduce_fusion
  3.1 0.1 select_reduce_fusion
  3.3 0.8 %copy.53 = s32[96,32]{1,0:T(8,128)S(1)} copy(s32[96,32]{0,1:T(8,128)} %param.13) | data formatting | bytes 24576 | tf_op args[0]
  4.1 0.1 sub.33
  4.2 0.1 copy.49
  4.3 0.1 copy.59
  4.4 0.6 pad.8.clone
  5.1 19.8 %shard_map.140 = (s32[4,4,8,1,128]{4,3,2,1,0:T(1,128)}, s32[4,4,8,1,128]{4,3,2,1,0:T(1,128)}, s32[4,4,8,1,128]{4,3,2,1,0:T(1,128)}) custom-call(s32[4,4,8,1,128]{4,3,2,1,0:T(1,128)} %bitcast.34), custom_call_target="tpu_custom_call" | custom-call | bytes 50331648 | tf_op jit(solution)/shard_map/pallas_call | solution.py:287
  24.9 0.8 %copy.51 = s32[4,4,8,1,128]{4,2,1,0,3:T(8,128)S(1)} copy(s32[4,4,8,1,128]{4,3,2,0,1:T(1,128)} %bitcast.37) | data formatting | bytes 131072 | tf_op jit(solution)/shard_map/transpose | solution.py:300
  25.8 0.1 copy.52
  25.9 0.1 copy.54
  26.0 0.1 slice.33
  26.1 0.1 min.30
  26.3 0.1 and_reduce_fusion
  26.4 0.1 fusion.3
  26.5 0.7 gather_fusion
  27.3 0.1 gather.17
  27.4 0.6 pad.9
  28.0 0.0 copy-done
  28.0 1.5 %gather_fusion.1 = f32[32,10,512]{2,0,1:T(8,128)S(1)} fusion(f32[96,10,512]{2,0,1:T(8,128)S(1)} %copy-done, s32[1024]{0:T(1024)S(1)} %pad_clamp_fusion.1), kind=kCustom, calls=%fused_computation.1 | custom fusion | bytes 1310848 | tf_op jit(solution)/shard_map/jit(_take)/gather | solution.py:485
  29.5 0.1 broadcast_select_fusion
  29.7 0.2 copy.56
  29.9 0.9 %reshape.114.refs_2_ = bf16[32,32,128]{2,1,0:T(8,128)(2,1)} reshape(bf16[32,8,512]{2,1,0:T(8,128)(2,1)S(1)} %copy.56) | data formatting | bytes 524288 | tf_op jit(solution)/shard_map/reshape | solution.py:487
  30.8 0.1 copy.55
  30.9 0.8 %reshape.113.refs_1_ = f32[32,8,128]{2,1,0:T(8,128)} reshape(f32[32,2,512]{2,1,0:T(2,128)S(1)} %copy.55) | data formatting | bytes 262144 | tf_op jit(solution)/shard_map/reshape | solution.py:486
  31.6 17.7 %shard_map.141 = (s32[4,32,1,128]{3,2,1,0:T(1,128)}, f32[32,8,128]{2,1,0:T(8,128)}, bf16[32,32,128]{2,1,0:T(8,128)(2,1)}, s32[4,32,1,128]{3,2,1,0:T(1,128)}) custom-call(s32[128,1,128]{2,1,0:T(1,128)} %bitcast.33, f32[32,8,128]{2,1,0:T(8,128)} %reshape.113.refs_1_, bf16[32,32,128]{2,1,0:T(8,128)(2,1)} %reshape.114.refs_2_), custom_call_target="tpu_custom_call" | custom-call | bytes 50331648 | tf_op jit(solution)/shard_map/pallas_call | solution.py:196
  49.4 0.9 %reshape_squeeze.3 = s32[256,32]{1,0:T(8,128)S(1)} reshape(s32[128,1,64]{2,0,1:T(8,128)} %bitcast.36) | data formatting | bytes 65536 | tf_op jit(solution)/shard_map/reshape;squeeze | solution.py:492
  50.3 0.6 gather_fusion.2
  50.9 0.1 copy.57
  51.0 0.7 reshape.116.codes_ref
  51.7 0.0 copy-start.6
  51.7 0.0 copy-start.7
  51.7 0.0 copy-start.8
  51.7 0.0 copy-start.9
  51.7 0.0 copy-start.10
  51.7 11.1 %shard_map.142 = bf16[384,512]{1,0:T(8,128)(2,1)} custom-call(s32[8,384]{1,0:T(8,128)} %reshape.116.codes_ref, bf16[16384,512]{1,0:T(8,128)(2,1)} %table_ref.1), custom_call_target="tpu_custom_call" | custom-call | tf_op jit(solution)/shard_map/pallas_call | solution.py:39
  62.9 0.0 copy-done.2
  62.9 0.0 copy-done.3
  62.9 0.0 copy-done.4
  62.9 0.0 copy-done.5
  62.9 0.0 copy-start.1
  63.0 1.0 %copy-done.1 = bf16[384,512]{1,0:T(8,128)(2,1)S(1)} copy-done((bf16[384,512]{1,0:T(8,128)(2,1)S(1)}, bf16[384,512]{1,0:T(8,128)(2,1)}, u32[]{:S(2)}) %copy-start.1) | copy-done | bytes 393240
  63.9 11.8 %shard_map.143 = (bf16[96,8,512]{2,1,0:T(8,128)(2,1)}, f32[10,96,512]{2,1,0:T(8,128)}) custom-call(s32[96]{0:T(128)S(1)} %subtract_clamp_fusion.source_ref, s32[96]{0:T(128)S(1)} %get-tuple-element.16.moved_ref, bf16[4,96,512]{2,1,0:T(8,128)(2,1)S(1)} %bitcast.28, f32[10,96,512]{2,1,0:T(8,128)S(1)} %bitcast.27, f32[32,8,128]{2,1,0:T(8,128)S(1)} %copy-done.5, ...), custom_call_target="tpu_custom_call" | custom-call | tf_op jit(solution)/shard_map/pallas_call | solution.py:391
  (28 shorter events, 0.2 us)
Async XLA Ops:
  0.6 27.4 %copy-start = (f32[96,10,512]{2,0,1:T(8,128)S(1)}, f32[96,10,512]{2,0,1:T(8,128)}, u32[]{:S(2)}) copy-start(f32[96,10,512]{2,0,1:T(8,128)} %param.17) | copy-start | bytes 5898244
  51.7 11.2 %copy-start.2 = (bf16[3,512,256]{2,1,0:T(8,128)(2,1)S(1)}, bf16[3,512,256]{2,1,0:T(8,128)(2,1)}, u32[]{:S(2)}) copy-start(bf16[3,512,256]{2,1,0:T(8,128)(2,1)} %in_w_ref.1) | copy-start | bytes 2359300
  51.7 11.2 %copy-start.3 = (bf16[256,512]{1,0:T(8,128)(2,1)S(1)}, bf16[256,512]{1,0:T(8,128)(2,1)}, u32[]{:S(2)}) copy-start(bf16[256,512]{1,0:T(8,128)(2,1)} %out_w_ref.1) | copy-start | bytes 786436
  51.7 11.2 %copy-start.4 = (bf16[32,32,128]{2,1,0:T(8,128)(2,1)S(1)}, bf16[32,32,128]{2,1,0:T(8,128)(2,1)}, u32[]{:S(2)}) copy-start(bf16[32,32,128]{2,1,0:T(8,128)(2,1)} %get-tuple-element.11.arrived_low_ref) | copy-start | bytes 786436
  51.7 11.2 %copy-start.5 = (f32[32,8,128]{2,1,0:T(8,128)S(1)}, f32[32,8,128]{2,1,0:T(8,128)}, u32[]{:S(2)}) copy-start(f32[32,8,128]{2,1,0:T(8,128)} %get-tuple-element.10.arrived_ref) | copy-start | bytes 393220
  51.7 11.2 %copy-start.6 = (f32[4,512]{1,0:T(4,128)S(1)}, f32[4,512]{1,0:T(4,128)}, u32[]{:S(2)}) copy-start(f32[4,512]{1,0:T(4,128)} %up_w_ref.1) | copy-start | bytes 24580
  51.7 11.2 %copy-start.7 = (f32[512]{0:T(512)S(1)}, f32[512]{0:T(512)}, u32[]{:S(2)}) copy-start(f32[512]{0:T(512)} %param.19) | copy-start | bytes 6148
  51.7 11.2 %copy-start.8 = (f32[512]{0:T(512)S(1)}, f32[512]{0:T(512)}, u32[]{:S(2)}) copy-start(f32[512]{0:T(512)} %param.21) | copy-start | bytes 6148
  51.7 11.2 %copy-start.9 = (f32[512]{0:T(512)S(1)}, f32[512]{0:T(512)}, u32[]{:S(2)}) copy-start(f32[512]{0:T(512)} %param.25) | copy-start | bytes 6148
  51.7 11.2 %copy-start.10 = (f32[256]{0:T(256)S(1)}, f32[256]{0:T(256)}, u32[]{:S(2)}) copy-start(f32[256]{0:T(256)} %param.23) | copy-start | bytes 3076
  62.9 1.0 %copy-start.1 = (bf16[384,512]{1,0:T(8,128)(2,1)S(1)}, bf16[384,512]{1,0:T(8,128)(2,1)}, u32[]{:S(2)}) copy-start(bf16[384,512]{1,0:T(8,128)(2,1)} %shard_map.142) | copy-start | bytes 1179652

commit v14 on v12

--- a/solution.py
+++ b/solution.py
@@ -298,7 +298,7 @@
 ):
     frame_count, conv_count, chan_width = routed.shape
     rows = states.shape[1]
-    chunk = 32 if conv_count % 32 == 0 else conv_count
+    chunk = 48 if conv_count % 48 == 0 else conv_count
     whole = lambda shape: pl.BlockSpec(shape, lambda i, *_: (0,) * len(shape))
     states_t = jnp.transpose(states, (1, 0, 2))
     decoded, new_t = pl.pallas_call(

time: 74.1 us -> 73.8 us (level)
  no operation moved by 1% of the time
where the time goes in v14:
time: 73.8 us; the launch traced here: 73.4 us
  Pallas kernels  58.3 us (79%)
  local copies, waits for them, and re-layouts  11.2 us (15%)
  other arithmetic  2.96 us (4%)
  between operations  0.98 us (1%)
    pallas_call x2, Pallas kernels, exchange(): pl.pallas_call(kernel, out_shape=shapes + mids, in_specs=[pl.BlockSpec(me...  35.7 us
    pallas_call x1, Pallas kernels, decode(): pl.pallas_call(decode_kernel, grid_spec=pltpu.PrefetchScalarGridSpec(num_...  11.5 us
    pallas_call x1, Pallas kernels, embed_codes(): pl.pallas_call(embed_kernel, in_specs=[pl.BlockSpec(memory_space=pltpu.VM...  11.1 us
    unnamed x24, local copies, waits for them, and re-layouts  2.75 us
    gather x1, local copies, waits for them, and re-layouts, local(): leaving = jnp.take(states, jnp.clip(state_asked, 0, conv_count - 1), axis=0)  1.51 us

profile of v14, /device:TPU:1, one launch (start us, length us, event | category | flops | bytes accessed | tf_op | source)
XLA Modules:
  0.0 73.4 jit_solution(5126393850832939633)
XLA Ops:
  0.6 0.0 copy-start
  0.6 0.8 %fusion.4 = s32[96]{0:T(128)S(1)} fusion(s32[96]{0:T(128)} %param.16), kind=kLoop, calls=%fused_computation.33 | loop fusion | flops 672 | bytes 768 | tf_op jit(solution)/shard_map/add | solution.py:379
  1.5 0.7 fusion.5
  2.1 0.1 select_reduce_fusion.1
  2.3 0.7 and_select_fusion.2
  2.9 0.2 convert_reduce_fusion
  3.1 0.1 select_reduce_fusion
  3.3 0.8 %copy.44 = s32[96,32]{1,0:T(8,128)S(1)} copy(s32[96,32]{0,1:T(8,128)} %param.13) | data formatting | bytes 24576 | tf_op args[0]
  4.1 0.1 sub.33
  4.2 0.1 copy.41
  4.3 0.1 pad_add_fusion
  4.4 0.6 pad.8
  5.1 18.2 %shard_map.140 = (s32[4,32,1,128]{3,2,1,0:T(1,128)}, s32[4,32,1,128]{3,2,1,0:T(1,128)}) custom-call(s32[128,1,128]{2,1,0:T(1,128)} %bitcast.36), custom_call_target="tpu_custom_call" | custom-call | bytes 50331648 | tf_op jit(solution)/shard_map/pallas_call | solution.py:196
  23.2 0.9 %copy.50 = s32[128,1,3]{0,2,1:T(4,128)S(1)} copy(s32[128,1,3]{2,0,1:T(8,128)} %bitcast.38) | data formatting | bytes 3072
  24.2 0.1 and_bitcast_fusion
  24.3 0.1 copy.45
  24.4 0.1 copy.43
  24.5 0.1 min.30
  24.7 0.7 gather_fusion
  25.4 0.1 gather.17
  25.5 0.6 pad.9
  26.2 0.0 copy-done
  26.2 1.5 %gather_fusion.1 = f32[32,10,512]{2,0,1:T(8,128)S(1)} fusion(f32[96,10,512]{2,0,1:T(8,128)S(1)} %copy-done, s32[1024]{0:T(1024)S(1)} %pad_clamp_fusion.1), kind=kCustom, calls=%fused_computation.1 | custom fusion | bytes 1310848 | tf_op jit(solution)/shard_map/jit(_take)/gather | solution.py:398
  27.7 0.1 broadcast_select_fusion
  27.9 0.2 copy.47
  28.1 0.9 %reshape.118.refs_2_ = bf16[32,32,128]{2,1,0:T(8,128)(2,1)} reshape(bf16[32,8,512]{2,1,0:T(8,128)(2,1)S(1)} %copy.47) | data formatting | bytes 524288 | tf_op jit(solution)/shard_map/reshape | solution.py:400
  28.9 0.1 copy.46
  29.0 0.8 %reshape.117.refs_1_ = f32[32,8,128]{2,1,0:T(8,128)} reshape(f32[32,2,512]{2,1,0:T(2,128)S(1)} %copy.46) | data formatting | bytes 262144 | tf_op jit(solution)/shard_map/reshape | solution.py:399
  29.8 17.5 %shard_map.141 = (s32[4,32,1,128]{3,2,1,0:T(1,128)}, f32[32,8,128]{2,1,0:T(8,128)}, bf16[32,32,128]{2,1,0:T(8,128)(2,1)}, s32[4,32,1,128]{3,2,1,0:T(1,128)}) custom-call(s32[128,1,128]{2,1,0:T(1,128)} %bitcast.35, f32[32,8,128]{2,1,0:T(8,128)} %reshape.117.refs_1_, bf16[32,32,128]{2,1,0:T(8,128)(2,1)} %reshape.118.refs_2_), custom_call_target="tpu_custom_call" | custom-call | bytes 50331648 | tf_op jit(solution)/shard_map/pallas_call | solution.py:196
  47.3 0.9 %reshape_squeeze.3 = s32[256,32]{1,0:T(8,128)S(1)} reshape(s32[128,1,64]{2,0,1:T(8,128)} %bitcast.37) | data formatting | bytes 65536 | tf_op jit(solution)/shard_map/reshape;squeeze | solution.py:405
  48.3 0.6 gather_fusion.2
  48.9 0.1 copy.48
  49.0 0.7 reshape.120.codes_ref
  49.7 0.0 copy-start.6
  49.7 0.0 copy-start.7
  49.7 0.0 copy-start.8
  49.7 0.0 copy-start.9
  49.7 0.0 copy-start.10
  49.7 11.1 %shard_map.142 = bf16[384,512]{1,0:T(8,128)(2,1)} custom-call(s32[8,384]{1,0:T(8,128)} %reshape.120.codes_ref, bf16[16384,512]{1,0:T(8,128)(2,1)} %table_ref.1), custom_call_target="tpu_custom_call" | custom-call | tf_op jit(solution)/shard_map/pallas_call | solution.py:39
  60.8 0.0 copy-done.2
  60.8 0.0 copy-done.3
  60.9 0.0 copy-done.4
  60.9 0.0 copy-done.5
  60.9 0.0 copy-done.6
  60.9 0.0 copy-done.7
  60.9 0.0 copy-start.1
  60.9 1.0 %copy-done.1 = bf16[384,512]{1,0:T(8,128)(2,1)S(1)} copy-done((bf16[384,512]{1,0:T(8,128)(2,1)S(1)}, bf16[384,512]{1,0:T(8,128)(2,1)}, u32[]{:S(2)}) %copy-start.1) | copy-done | bytes 393240
  61.9 11.5 %shard_map.143 = (bf16[96,8,512]{2,1,0:T(8,128)(2,1)}, f32[10,96,512]{2,1,0:T(8,128)}) custom-call(s32[96]{0:T(128)S(1)} %subtract_clamp_fusion.source_ref, s32[96]{0:T(128)S(1)} %get-tuple-element.18.moved_ref, bf16[4,96,512]{2,1,0:T(8,128)(2,1)S(1)} %bitcast.30, f32[10,96,512]{2,1,0:T(8,128)S(1)} %bitcast.29, f32[32,8,128]{2,1,0:T(8,128)S(1)} %copy-done.5, ...), custom_call_target="tpu_custom_call" | custom-call | tf_op jit(solution)/shard_map/pallas_call | solution.py:304
  (25 shorter events, 0.2 us)
Async XLA Ops:
  0.6 25.5 %copy-start = (f32[96,10,512]{2,0,1:T(8,128)S(1)}, f32[96,10,512]{2,0,1:T(8,128)}, u32[]{:S(2)}) copy-start(f32[96,10,512]{2,0,1:T(8,128)} %param.17) | copy-start | bytes 5898244
  49.7 11.2 %copy-start.2 = (bf16[3,512,256]{2,1,0:T(8,128)(2,1)S(1)}, bf16[3,512,256]{2,1,0:T(8,128)(2,1)}, u32[]{:S(2)}) copy-start(bf16[3,512,256]{2,1,0:T(8,128)(2,1)} %in_w_ref.1) | copy-start | bytes 2359300
  49.7 11.2 %copy-start.3 = (bf16[256,512]{1,0:T(8,128)(2,1)S(1)}, bf16[256,512]{1,0:T(8,128)(2,1)}, u32[]{:S(2)}) copy-start(bf16[256,512]{1,0:T(8,128)(2,1)} %out_w_ref.1) | copy-start | bytes 786436
  49.7 11.2 %copy-start.4 = (bf16[32,32,128]{2,1,0:T(8,128)(2,1)S(1)}, bf16[32,32,128]{2,1,0:T(8,128)(2,1)}, u32[]{:S(2)}) copy-start(bf16[32,32,128]{2,1,0:T(8,128)(2,1)} %get-tuple-element.11.arrived_low_ref) | copy-start | bytes 786436
  49.7 11.2 %copy-start.5 = (f32[32,8,128]{2,1,0:T(8,128)S(1)}, f32[32,8,128]{2,1,0:T(8,128)}, u32[]{:S(2)}) copy-start(f32[32,8,128]{2,1,0:T(8,128)} %get-tuple-element.10.arrived_ref) | copy-start | bytes 393220
  49.7 11.2 %copy-start.6 = (f32[4,512]{1,0:T(4,128)S(1)}, f32[4,512]{1,0:T(4,128)}, u32[]{:S(2)}) copy-start(f32[4,512]{1,0:T(4,128)} %up_w_ref.1) | copy-start | bytes 24580
  49.7 11.2 %copy-start.7 = (f32[512]{0:T(512)S(1)}, f32[512]{0:T(512)}, u32[]{:S(2)}) copy-start(f32[512]{0:T(512)} %param.19) | copy-start | bytes 6148
  49.7 11.2 %copy-start.8 = (f32[512]{0:T(512)S(1)}, f32[512]{0:T(512)}, u32[]{:S(2)}) copy-start(f32[512]{0:T(512)} %param.21) | copy-start | bytes 6148
  49.7 11.2 %copy-start.9 = (f32[512]{0:T(512)S(1)}, f32[512]{0:T(512)}, u32[]{:S(2)}) copy-start(f32[512]{0:T(512)} %param.25) | copy-start | bytes 6148
  49.7 11.2 %copy-start.10 = (f32[256]{0:T(256)S(1)}, f32[256]{0:T(256)}, u32[]{:S(2)}) copy-start(f32[256]{0:T(256)} %param.23) | copy-start | bytes 3076
  60.9 1.0 %copy-start.1 = (bf16[384,512]{1,0:T(8,128)(2,1)S(1)}, bf16[384,512]{1,0:T(8,128)(2,1)}, u32[]{:S(2)}) copy-start(bf16[384,512]{1,0:T(8,128)(2,1)} %shard_map.142) | copy-start | bytes 1179652

commit v15 on v14

--- a/solution.py
+++ b/solution.py
@@ -298,7 +298,7 @@
 ):
     frame_count, conv_count, chan_width = routed.shape
     rows = states.shape[1]
-    chunk = 48 if conv_count % 48 == 0 else conv_count
+    chunk = conv_count
     whole = lambda shape: pl.BlockSpec(shape, lambda i, *_: (0,) * len(shape))
     states_t = jnp.transpose(states, (1, 0, 2))
     decoded, new_t = pl.pallas_call(

time: 73.8 us -> 73.1 us (level)
  Pallas kernels: 58.3 us -> 57.5 us
where the time goes in v15:
time: 73.1 us; the launch traced here: 72.7 us
  Pallas kernels  57.5 us (79%)
  local copies, waits for them, and re-layouts  11.2 us (15%)
  other arithmetic  2.96 us (4%)
  between operations  0.98 us (1%)
    pallas_call x2, Pallas kernels, exchange(): pl.pallas_call(kernel, out_shape=shapes + mids, in_specs=[pl.BlockSpec(me...  35.7 us
    pallas_call x1, Pallas kernels, embed_codes(): pl.pallas_call(embed_kernel, in_specs=[pl.BlockSpec(memory_space=pltpu.VM...  11.1 us
    pallas_call x1, Pallas kernels, decode(): pl.pallas_call(decode_kernel, grid_spec=pltpu.PrefetchScalarGridSpec(num_...  10.7 us
    unnamed x24, local copies, waits for them, and re-layouts  2.75 us
    gather x1, local copies, waits for them, and re-layouts, local(): leaving = jnp.take(states, jnp.clip(state_asked, 0, conv_count - 1), axis=0)  1.51 us

profile of v15, /device:TPU:1, one launch (start us, length us, event | category | flops | bytes accessed | tf_op | source)
XLA Modules:
  0.0 72.7 jit_solution(13879255772446807334)
XLA Ops:
  0.6 0.0 copy-start
  0.6 0.8 %fusion.4 = s32[96]{0:T(128)S(1)} fusion(s32[96]{0:T(128)} %param.16), kind=kLoop, calls=%fused_computation.33 | loop fusion | flops 672 | bytes 768 | tf_op jit(solution)/shard_map/add | solution.py:379
  1.5 0.7 fusion.5
  2.1 0.1 select_reduce_fusion.1
  2.3 0.7 and_select_fusion.2
  2.9 0.2 convert_reduce_fusion
  3.1 0.1 select_reduce_fusion
  3.3 0.8 %copy.44 = s32[96,32]{1,0:T(8,128)S(1)} copy(s32[96,32]{0,1:T(8,128)} %param.13) | data formatting | bytes 24576 | tf_op args[0]
  4.1 0.1 sub.33
  4.2 0.1 copy.41
  4.3 0.1 pad_add_fusion
  4.4 0.6 pad.8
  5.1 18.2 %shard_map.140 = (s32[4,32,1,128]{3,2,1,0:T(1,128)}, s32[4,32,1,128]{3,2,1,0:T(1,128)}) custom-call(s32[128,1,128]{2,1,0:T(1,128)} %bitcast.36), custom_call_target="tpu_custom_call" | custom-call | bytes 50331648 | tf_op jit(solution)/shard_map/pallas_call | solution.py:196
  23.2 0.9 %copy.50 = s32[128,1,3]{0,2,1:T(4,128)S(1)} copy(s32[128,1,3]{2,0,1:T(8,128)} %bitcast.38) | data formatting | bytes 3072
  24.2 0.1 and_bitcast_fusion
  24.3 0.1 copy.45
  24.4 0.1 copy.43
  24.5 0.1 min.30
  24.7 0.7 %gather_fusion = s32[256,32]{1,0:T(8,128)S(1)} fusion(s32[96,32]{1,0:T(8,128)S(1)} %copy.44, s32[1024]{0:T(1024)S(1)} %pad_clamp_fusion.2), kind=kCustom, calls=%fused_computation | custom fusion | bytes 66560 | tf_op jit(solution)/shard_map/jit(_take)/gather | solution.py:394
  25.4 0.1 gather.17
  25.5 0.6 pad.9
  26.2 0.0 copy-done
  26.2 1.5 %gather_fusion.1 = f32[32,10,512]{2,0,1:T(8,128)S(1)} fusion(f32[96,10,512]{2,0,1:T(8,128)S(1)} %copy-done, s32[1024]{0:T(1024)S(1)} %pad_clamp_fusion.1), kind=kCustom, calls=%fused_computation.1 | custom fusion | bytes 1310848 | tf_op jit(solution)/shard_map/jit(_take)/gather | solution.py:398
  27.7 0.1 broadcast_select_fusion
  27.9 0.2 copy.47
  28.1 0.9 %reshape.118.refs_2_ = bf16[32,32,128]{2,1,0:T(8,128)(2,1)} reshape(bf16[32,8,512]{2,1,0:T(8,128)(2,1)S(1)} %copy.47) | data formatting | bytes 524288 | tf_op jit(solution)/shard_map/reshape | solution.py:400
  28.9 0.1 copy.46
  29.0 0.8 %reshape.117.refs_1_ = f32[32,8,128]{2,1,0:T(8,128)} reshape(f32[32,2,512]{2,1,0:T(2,128)S(1)} %copy.46) | data formatting | bytes 262144 | tf_op jit(solution)/shard_map/reshape | solution.py:399
  29.8 17.5 %shard_map.141 = (s32[4,32,1,128]{3,2,1,0:T(1,128)}, f32[32,8,128]{2,1,0:T(8,128)}, bf16[32,32,128]{2,1,0:T(8,128)(2,1)}, s32[4,32,1,128]{3,2,1,0:T(1,128)}) custom-call(s32[128,1,128]{2,1,0:T(1,128)} %bitcast.35, f32[32,8,128]{2,1,0:T(8,128)} %reshape.117.refs_1_, bf16[32,32,128]{2,1,0:T(8,128)(2,1)} %reshape.118.refs_2_), custom_call_target="tpu_custom_call" | custom-call | bytes 50331648 | tf_op jit(solution)/shard_map/pallas_call | solution.py:196
  47.3 0.9 %reshape_squeeze.3 = s32[256,32]{1,0:T(8,128)S(1)} reshape(s32[128,1,64]{2,0,1:T(8,128)} %bitcast.37) | data formatting | bytes 65536 | tf_op jit(solution)/shard_map/reshape;squeeze | solution.py:405
  48.3 0.6 gather_fusion.2
  48.9 0.1 copy.48
  49.0 0.7 reshape.120.codes_ref
  49.7 0.0 copy-start.6
  49.7 0.0 copy-start.7
  49.7 0.0 copy-start.8
  49.7 0.0 copy-start.9
  49.7 0.0 copy-start.10
  49.7 11.1 %shard_map.142 = bf16[384,512]{1,0:T(8,128)(2,1)} custom-call(s32[8,384]{1,0:T(8,128)} %reshape.120.codes_ref, bf16[16384,512]{1,0:T(8,128)(2,1)} %table_ref.1), custom_call_target="tpu_custom_call" | custom-call | tf_op jit(solution)/shard_map/pallas_call | solution.py:39
  60.8 0.0 copy-done.2
  60.9 0.0 copy-done.3
  60.9 0.0 copy-done.4
  60.9 0.0 copy-done.5
  60.9 0.0 copy-done.6
  60.9 0.0 copy-done.7
  60.9 0.0 copy-start.1
  60.9 1.0 %copy-done.1 = bf16[384,512]{1,0:T(8,128)(2,1)S(1)} copy-done((bf16[384,512]{1,0:T(8,128)(2,1)S(1)}, bf16[384,512]{1,0:T(8,128)(2,1)}, u32[]{:S(2)}) %copy-start.1) | copy-done | bytes 393240
  61.9 10.7 %shard_map.143 = (bf16[96,8,512]{2,1,0:T(8,128)(2,1)}, f32[10,96,512]{2,1,0:T(8,128)}) custom-call(s32[96]{0:T(128)S(1)} %subtract_clamp_fusion.source_ref, s32[96]{0:T(128)S(1)} %get-tuple-element.18.moved_ref, bf16[4,96,512]{2,1,0:T(8,128)(2,1)S(1)} %bitcast.30, f32[10,96,512]{2,1,0:T(8,128)S(1)} %bitcast.29, f32[32,8,128]{2,1,0:T(8,128)S(1)} %copy-done.5, ...), custom_call_target="tpu_custom_call" | custom-call | tf_op jit(solution)/shard_map/pallas_call | solution.py:304
  (25 shorter events, 0.2 us)
Async XLA Ops:
  0.6 25.5 %copy-start = (f32[96,10,512]{2,0,1:T(8,128)S(1)}, f32[96,10,512]{2,0,1:T(8,128)}, u32[]{:S(2)}) copy-start(f32[96,10,512]{2,0,1:T(8,128)} %param.17) | copy-start | bytes 5898244
  49.7 11.2 %copy-start.2 = (bf16[3,512,256]{2,1,0:T(8,128)(2,1)S(1)}, bf16[3,512,256]{2,1,0:T(8,128)(2,1)}, u32[]{:S(2)}) copy-start(bf16[3,512,256]{2,1,0:T(8,128)(2,1)} %in_w_ref.1) | copy-start | bytes 2359300
  49.7 11.2 %copy-start.3 = (bf16[256,512]{1,0:T(8,128)(2,1)S(1)}, bf16[256,512]{1,0:T(8,128)(2,1)}, u32[]{:S(2)}) copy-start(bf16[256,512]{1,0:T(8,128)(2,1)} %out_w_ref.1) | copy-start | bytes 786436
  49.7 11.2 %copy-start.4 = (bf16[32,32,128]{2,1,0:T(8,128)(2,1)S(1)}, bf16[32,32,128]{2,1,0:T(8,128)(2,1)}, u32[]{:S(2)}) copy-start(bf16[32,32,128]{2,1,0:T(8,128)(2,1)} %get-tuple-element.11.arrived_low_ref) | copy-start | bytes 786436
  49.7 11.2 %copy-start.5 = (f32[32,8,128]{2,1,0:T(8,128)S(1)}, f32[32,8,128]{2,1,0:T(8,128)}, u32[]{:S(2)}) copy-start(f32[32,8,128]{2,1,0:T(8,128)} %get-tuple-element.10.arrived_ref) | copy-start | bytes 393220
  49.7 11.2 %copy-start.6 = (f32[4,512]{1,0:T(4,128)S(1)}, f32[4,512]{1,0:T(4,128)}, u32[]{:S(2)}) copy-start(f32[4,512]{1,0:T(4,128)} %up_w_ref.1) | copy-start | bytes 24580
  49.7 11.2 %copy-start.7 = (f32[512]{0:T(512)S(1)}, f32[512]{0:T(512)}, u32[]{:S(2)}) copy-start(f32[512]{0:T(512)} %param.19) | copy-start | bytes 6148
  49.7 11.2 %copy-start.8 = (f32[512]{0:T(512)S(1)}, f32[512]{0:T(512)}, u32[]{:S(2)}) copy-start(f32[512]{0:T(512)} %param.21) | copy-start | bytes 6148
  49.7 11.2 %copy-start.9 = (f32[512]{0:T(512)S(1)}, f32[512]{0:T(512)}, u32[]{:S(2)}) copy-start(f32[512]{0:T(512)} %param.25) | copy-start | bytes 6148
  49.7 11.2 %copy-start.10 = (f32[256]{0:T(256)S(1)}, f32[256]{0:T(256)}, u32[]{:S(2)}) copy-start(f32[256]{0:T(256)} %param.23) | copy-start | bytes 3076
  60.9 1.0 %copy-start.1 = (bf16[384,512]{1,0:T(8,128)(2,1)S(1)}, bf16[384,512]{1,0:T(8,128)(2,1)}, u32[]{:S(2)}) copy-start(bf16[384,512]{1,0:T(8,128)(2,1)} %shard_map.142) | copy-start | bytes 1179652

commit v16 on v15

--- a/solution.py
+++ b/solution.py
@@ -281,7 +281,7 @@
     summed = conv_out + jnp.dot(squeezed, out_w_ref[...], preferred_element_type=jnp.float32) + out_b_ref[...]
     decoded = summed.astype(jnp.bfloat16)
     for t in range(step_count):
-        decoded_ref[:, t, :] = decoded[t * slots : (t + 1) * slots]
+        decoded_ref[t] = decoded[t * slots : (t + 1) * slots]
     new_ref[0] = inputs[frame_count - 1] * up_w[2:3]
     new_ref[1] = inputs[frame_count - 1] * up_w[3:4]
     for k in range(kept):
@@ -321,13 +321,13 @@
                 whole((1, chan_width)),
             ],
             out_specs=(
-                pl.BlockSpec((chunk, 2 * frame_count, chan_width), lambda i, *_: (i, 0, 0)),
+                pl.BlockSpec((2 * frame_count, chunk, chan_width), lambda i, *_: (0, i, 0)),
                 pl.BlockSpec((rows, chunk, chan_width), lambda i, *_: (0, i, 0)),
             ),
             scratch_shapes=[pltpu.VMEM((rows, chunk, chan_width), jnp.float32)],
         ),
         out_shape=(
-            jax.ShapeDtypeStruct((conv_count, 2 * frame_count, chan_width), jnp.bfloat16),
+            jax.ShapeDtypeStruct((2 * frame_count, conv_count, chan_width), jnp.bfloat16),
             jax.ShapeDtypeStruct((rows, conv_count, chan_width), jnp.float32),
         ),
         compiler_params=pltpu.CompilerParams(vmem_limit_bytes=48 * 1024 * 1024),
@@ -335,7 +335,7 @@
         source, moved, routed, states_t, arrived, arrived_low, up_weight, up_bias.reshape(1, -1), conv_weight,
         conv_bias.reshape(1, -1), res_in_weight, res_in_bias.reshape(1, -1), res_out_weight, res_out_bias.reshape(1, -1),
     )
-    return decoded, jnp.transpose(new_t, (1, 0, 2))
+    return jnp.transpose(decoded, (1, 0, 2)), jnp.transpose(new_t, (1, 0, 2))
 
 
 def local(

time: 73.1 us -> 73.8 us (level)
  local copies, waits for them, and re-layouts: 11.2 us -> 12.5 us
    unnamed x24 -> x25, local copies, waits for them, and re-layouts: 2.75 us -> 4.06 us
where the time goes in v16:
time: 73.8 us; the launch traced here: 73.4 us
  Pallas kernels  57 us (77%)
  local copies, waits for them, and re-layouts  12.5 us (17%)
  other arithmetic  2.96 us (4%)
  between operations  0.98 us (1%)
    pallas_call x2, Pallas kernels, exchange(): pl.pallas_call(kernel, out_shape=shapes + mids, in_specs=[pl.BlockSpec(me...  35.7 us
    pallas_call x1, Pallas kernels, embed_codes(): pl.pallas_call(embed_kernel, in_specs=[pl.BlockSpec(memory_space=pltpu.VM...  11.1 us
    pallas_call x1, Pallas kernels, decode(): pl.pallas_call(decode_kernel, grid_spec=pltpu.PrefetchScalarGridSpec(num_...  10.2 us
    unnamed x25, local copies, waits for them, and re-layouts  4.06 us
    gather x1, local copies, waits for them, and re-layouts, local(): leaving = jnp.take(states, jnp.clip(state_asked, 0, conv_count - 1), axis=0)  1.51 us

profile of v16, /device:TPU:1, one launch (start us, length us, event | category | flops | bytes accessed | tf_op | source)
XLA Modules:
  0.0 73.4 jit_solution(11573463910279504329)
XLA Ops:
  0.6 0.0 copy-start
  0.6 0.8 %fusion.4 = s32[96]{0:T(128)S(1)} fusion(s32[96]{0:T(128)} %param.16), kind=kLoop, calls=%fused_computation.33 | loop fusion | flops 672 | bytes 768 | tf_op jit(solution)/shard_map/add | solution.py:379
  1.5 0.7 fusion.5
  2.1 0.1 select_reduce_fusion.1
  2.3 0.7 and_select_fusion.2
  2.9 0.2 convert_reduce_fusion
  3.1 0.1 select_reduce_fusion
  3.3 0.8 %copy.47 = s32[96,32]{1,0:T(8,128)S(1)} copy(s32[96,32]{0,1:T(8,128)} %param.13) | data formatting | bytes 24576 | tf_op args[0]
  4.1 0.1 sub.33
  4.2 0.1 copy.44
  4.3 0.1 pad_add_fusion
  4.4 0.6 pad.8
  5.1 18.2 %shard_map.140 = (s32[4,32,1,128]{3,2,1,0:T(1,128)}, s32[4,32,1,128]{3,2,1,0:T(1,128)}) custom-call(s32[128,1,128]{2,1,0:T(1,128)} %bitcast.38), custom_call_target="tpu_custom_call" | custom-call | bytes 50331648 | tf_op jit(solution)/shard_map/pallas_call | solution.py:196
  23.2 0.9 %copy.54 = s32[128,1,3]{0,2,1:T(4,128)S(1)} copy(s32[128,1,3]{2,0,1:T(8,128)} %bitcast.40) | data formatting | bytes 3072
  24.2 0.1 and_bitcast_fusion
  24.3 0.1 copy.48
  24.4 0.1 copy.46
  24.5 0.1 min.30
  24.7 0.7 gather_fusion
  25.4 0.1 gather.17
  25.5 0.6 pad.9
  26.2 0.0 copy-done
  26.2 1.5 %gather_fusion.1 = f32[32,10,512]{2,0,1:T(8,128)S(1)} fusion(f32[96,10,512]{2,0,1:T(8,128)S(1)} %copy-done, s32[1024]{0:T(1024)S(1)} %pad_clamp_fusion.1), kind=kCustom, calls=%fused_computation.1 | custom fusion | bytes 1310848 | tf_op jit(solution)/shard_map/jit(_take)/gather | solution.py:398
  27.7 0.1 broadcast_select_fusion
  27.9 0.2 copy.50
  28.1 0.9 %reshape.118.refs_2_ = bf16[32,32,128]{2,1,0:T(8,128)(2,1)} reshape(bf16[32,8,512]{2,1,0:T(8,128)(2,1)S(1)} %copy.50) | data formatting | bytes 524288 | tf_op jit(solution)/shard_map/reshape | solution.py:400
  28.9 0.1 copy.49
  29.0 0.8 %reshape.117.refs_1_ = f32[32,8,128]{2,1,0:T(8,128)} reshape(f32[32,2,512]{2,1,0:T(2,128)S(1)} %copy.49) | data formatting | bytes 262144 | tf_op jit(solution)/shard_map/reshape | solution.py:399
  29.8 17.5 %shard_map.141 = (s32[4,32,1,128]{3,2,1,0:T(1,128)}, f32[32,8,128]{2,1,0:T(8,128)}, bf16[32,32,128]{2,1,0:T(8,128)(2,1)}, s32[4,32,1,128]{3,2,1,0:T(1,128)}) custom-call(s32[128,1,128]{2,1,0:T(1,128)} %bitcast.37, f32[32,8,128]{2,1,0:T(8,128)} %reshape.117.refs_1_, bf16[32,32,128]{2,1,0:T(8,128)(2,1)} %reshape.118.refs_2_), custom_call_target="tpu_custom_call" | custom-call | bytes 50331648 | tf_op jit(solution)/shard_map/pallas_call | solution.py:196
  47.3 0.9 %reshape_squeeze.3 = s32[256,32]{1,0:T(8,128)S(1)} reshape(s32[128,1,64]{2,0,1:T(8,128)} %bitcast.39) | data formatting | bytes 65536 | tf_op jit(solution)/shard_map/reshape;squeeze | solution.py:405
  48.3 0.6 gather_fusion.2
  48.9 0.1 copy.51
  49.0 0.7 reshape.120.codes_ref
  49.7 0.0 copy-start.6
  49.7 0.0 copy-start.7
  49.7 0.0 copy-start.8
  49.7 0.0 copy-start.9
  49.7 0.0 copy-start.10
  49.7 11.1 %shard_map.142 = bf16[384,512]{1,0:T(8,128)(2,1)} custom-call(s32[8,384]{1,0:T(8,128)} %reshape.120.codes_ref, bf16[16384,512]{1,0:T(8,128)(2,1)} %table_ref.1), custom_call_target="tpu_custom_call" | custom-call | tf_op jit(solution)/shard_map/pallas_call | solution.py:39
  60.8 0.0 copy-done.2
  60.8 0.0 copy-done.3
  60.9 0.0 copy-done.4
  60.9 0.0 copy-done.5
  60.9 0.0 copy-done.6
  60.9 0.0 copy-start.1
  60.9 1.0 %copy-done.1 = bf16[384,512]{1,0:T(8,128)(2,1)S(1)} copy-done((bf16[384,512]{1,0:T(8,128)(2,1)S(1)}, bf16[384,512]{1,0:T(8,128)(2,1)}, u32[]{:S(2)}) %copy-start.1) | copy-done | bytes 393240
  61.9 10.2 %shard_map.143 = (bf16[8,96,512]{2,1,0:T(8,128)(2,1)S(1)}, f32[10,96,512]{2,1,0:T(8,128)}) custom-call(s32[96]{0:T(128)S(1)} %subtract_clamp_fusion.source_ref, s32[96]{0:T(128)S(1)} %get-tuple-element.26.moved_ref, bf16[4,96,512]{2,1,0:T(8,128)(2,1)S(1)} %bitcast.31, f32[10,96,512]{2,1,0:T(8,128)S(1)} %bitcast.30, f32[32,8,128]{2,1,0:T(8,128)S(1)} %copy-done.5, ...), custom_call_target="tpu_custom_call" | custom-call | tf_op jit(solution)/shard_map/pallas_call | solution.py:304
  72.1 1.3 %copy.53 = bf16[96,8,512]{2,1,0:T(8,128)(2,1)} copy(bf16[96,8,512]{2,0,1:T(8,128)(2,1)S(1)} %bitcast.32) | data formatting | bytes 1572864
  (26 shorter events, 0.2 us)
Async XLA Ops:
  0.6 25.5 %copy-start = (f32[96,10,512]{2,0,1:T(8,128)S(1)}, f32[96,10,512]{2,0,1:T(8,128)}, u32[]{:S(2)}) copy-start(f32[96,10,512]{2,0,1:T(8,128)} %param.17) | copy-start | bytes 5898244
  49.7 11.2 %copy-start.2 = (bf16[3,512,256]{2,1,0:T(8,128)(2,1)S(1)}, bf16[3,512,256]{2,1,0:T(8,128)(2,1)}, u32[]{:S(2)}) copy-start(bf16[3,512,256]{2,1,0:T(8,128)(2,1)} %in_w_ref.1) | copy-start | bytes 2359300
  49.7 11.2 %copy-start.3 = (bf16[256,512]{1,0:T(8,128)(2,1)S(1)}, bf16[256,512]{1,0:T(8,128)(2,1)}, u32[]{:S(2)}) copy-start(bf16[256,512]{1,0:T(8,128)(2,1)} %out_w_ref.1) | copy-start | bytes 786436
  49.7 11.2 %copy-start.4 = (bf16[32,32,128]{2,1,0:T(8,128)(2,1)S(1)}, bf16[32,32,128]{2,1,0:T(8,128)(2,1)}, u32[]{:S(2)}) copy-start(bf16[32,32,128]{2,1,0:T(8,128)(2,1)} %get-tuple-element.11.arrived_low_ref) | copy-start | bytes 786436
  49.7 11.2 %copy-start.5 = (f32[32,8,128]{2,1,0:T(8,128)S(1)}, f32[32,8,128]{2,1,0:T(8,128)}, u32[]{:S(2)}) copy-start(f32[32,8,128]{2,1,0:T(8,128)} %get-tuple-element.10.arrived_ref) | copy-start | bytes 393220
  49.7 11.2 %copy-start.6 = (f32[4,512]{1,0:T(4,128)S(1)}, f32[4,512]{1,0:T(4,128)}, u32[]{:S(2)}) copy-start(f32[4,512]{1,0:T(4,128)} %up_w_ref.1) | copy-start | bytes 24580
  49.7 11.2 %copy-start.7 = (f32[512]{0:T(512)S(1)}, f32[512]{0:T(512)}, u32[]{:S(2)}) copy-start(f32[512]{0:T(512)} %param.19) | copy-start | bytes 6148
  49.7 11.2 %copy-start.8 = (f32[512]{0:T(512)S(1)}, f32[512]{0:T(512)}, u32[]{:S(2)}) copy-start(f32[512]{0:T(512)} %param.21) | copy-start | bytes 6148
  49.7 11.2 %copy-start.9 = (f32[512]{0:T(512)S(1)}, f32[512]{0:T(512)}, u32[]{:S(2)}) copy-start(f32[512]{0:T(512)} %param.25) | copy-start | bytes 6148
  49.7 11.2 %copy-start.10 = (f32[256]{0:T(256)S(1)}, f32[256]{0:T(256)}, u32[]{:S(2)}) copy-start(f32[256]{0:T(256)} %param.23) | copy-start | bytes 3076
  60.9 1.0 %copy-start.1 = (bf16[384,512]{1,0:T(8,128)(2,1)S(1)}, bf16[384,512]{1,0:T(8,128)(2,1)}, u32[]{:S(2)}) copy-start(bf16[384,512]{1,0:T(8,128)(2,1)} %shard_map.142) | copy-start | bytes 1179652

commit v17 on v15

--- a/solution.py
+++ b/solution.py
@@ -9,16 +9,27 @@
 MOST = 2
 
 
-def embed_kernel(codes_ref, table_ref, out_ref, blocks, sems):
-    books, rows = codes_ref.shape
+def embed_kernel(anchor_ref, answered_ref, rank_ref, table_ref, out_ref, blocks, sems, mine_ref):
+    books = blocks.shape[0]
     size = blocks.shape[1]
+    slots = rank_ref.shape[0]
 
     def fetch(book):
         return pltpu.make_async_copy(table_ref.at[pl.ds(book * size, size)], blocks.at[book], sems.at[book])
 
     for book in range(books):
         fetch(book).start()
-    by_row = jnp.transpose(codes_ref[...])
+
+    def pick(slot, carry):
+        mine_ref[pl.ds(slot, 1), :] = answered_ref[anchor_ref[slot]]
+        return carry
+
+    lax.fori_loop(0, slots, pick, 0)
+    mine = mine_ref[...]
+    width = books * FRAMES
+    own = jnp.where(rank_ref[...] == 0, mine[:, :width], mine[:, width : 2 * width])
+    by_row = jnp.concatenate([own[:, f * books : (f + 1) * books] for f in range(FRAMES)], axis=0)
+    rows = by_row.shape[0]
     total = None
     for book in range(books):
         fetch(book).wait()
@@ -29,23 +40,28 @@
     out_ref[...] = total.astype(jnp.bfloat16)
 
 
-def embed_codes(codes, code_table):
-    row_count = codes.shape[0]
-    book_count = codes.shape[1] // FRAMES
+def embed_codes(answered, anchor, rank, code_table, code_width):
+    row_count = anchor.shape[0]
+    book_count = code_width // FRAMES
     book_size = code_table.shape[0] // book_count
     chan_width = code_table.shape[1]
-    by_book = codes.reshape(row_count, FRAMES, book_count).transpose(2, 1, 0).reshape(book_count, -1)
     rows = FRAMES * row_count
     summed = pl.pallas_call(
         embed_kernel,
-        in_specs=[pl.BlockSpec(memory_space=pltpu.VMEM), pl.BlockSpec(memory_space=pl.ANY)],
+        in_specs=[
+            pl.BlockSpec(memory_space=pltpu.SMEM),
+            pl.BlockSpec(memory_space=pltpu.VMEM),
+            pl.BlockSpec(memory_space=pltpu.VMEM),
+            pl.BlockSpec(memory_space=pl.ANY),
+        ],
         out_specs=pl.BlockSpec(memory_space=pltpu.VMEM),
         out_shape=jax.ShapeDtypeStruct((rows, chan_width), jnp.bfloat16),
         scratch_shapes=[
             pltpu.VMEM((book_count, book_size, chan_width), code_table.dtype),
             pltpu.SemaphoreType.DMA((book_count,)),
+            pltpu.VMEM((row_count, answered.shape[-1]), answered.dtype),
         ],
-    )(by_book, code_table)
+    )(anchor, answered, rank.reshape(-1, 1), code_table)
     return summed.reshape(FRAMES, row_count, chan_width)
 
 
@@ -402,9 +418,7 @@
         [(answer, True), (leaving_high, False), (leaving_low, False)], 1
     )
     code_width = codes.shape[1]
-    answered = answered[:, 0, : most * code_width].reshape(devices_all * most, code_width)
-    my_codes = jnp.take(answered, key, axis=0)
-    routed = embed_codes(my_codes, code_table)
+    routed = embed_codes(answered, anchor, rank_in, code_table, code_width)
     return decode(
         routed,
         states,

time: 73.1 us -> 71.6 us (0.979)
  local copies, waits for them, and re-layouts: 11.2 us -> 9.61 us
    another operation x1 -> x0, local copies, waits for them, and re-layouts: 0.92 us -> none  [local(): answered[:, 0, :most * code_width].reshape(devices_all * most, code_width)]
    unnamed x24 -> x26, local copies, waits for them, and re-layouts: 2.75 us -> 2.75 us
where the time goes in v17:
time: 71.6 us; the launch traced here: 71.2 us
  Pallas kernels  57.7 us (81%)
  local copies, waits for them, and re-layouts  9.61 us (13%)
  other arithmetic  2.94 us (4%)
  between operations  0.99 us (1%)
    pallas_call x2, Pallas kernels, exchange(): pl.pallas_call(kernel, out_shape=shapes + mids, in_specs=[pl.BlockSpec(me...  35.7 us
    pallas_call x1, Pallas kernels, embed_codes(): pl.pallas_call(embed_kernel, in_specs=[pl.BlockSpec(memory_space=pltpu.SM...  11.2 us
    pallas_call x1, Pallas kernels, decode(): pl.pallas_call(decode_kernel, grid_spec=pltpu.PrefetchScalarGridSpec(num_...  10.7 us
    unnamed x26, local copies, waits for them, and re-layouts  2.75 us
    gather x1, local copies, waits for them, and re-layouts, local(): leaving = jnp.take(states, jnp.clip(state_asked, 0, conv_count - 1), axis=0)  1.51 us

profile of v17, /device:TPU:1, one launch (start us, length us, event | category | flops | bytes accessed | tf_op | source)
XLA Modules:
  0.0 71.2 jit_solution(2468834954820521515)
XLA Ops:
  0.6 0.0 copy-start
  0.6 0.8 %fusion.3 = s32[96]{0:T(128)S(1)} fusion(s32[96]{0:T(128)} %param.16), kind=kLoop, calls=%fused_computation.27 | loop fusion | flops 672 | bytes 768 | tf_op jit(solution)/shard_map/add | solution.py:395
  1.5 0.7 fusion.4
  2.1 0.1 select_reduce_fusion.1
  2.3 0.7 fusion.2
  2.9 0.2 convert_reduce_fusion
  3.1 0.1 select_reduce_fusion
  3.3 0.7 %copy.46.rank_ref = s32[96,1]{1,0:T(8,128)} copy(s32[96,1]{0,1:T(1,128)S(1)} %bitcast.37) | data formatting | bytes 768 | tf_op jit(solution)/shard_map/reshape | solution.py:64
  4.0 0.8 %copy.42 = s32[96,32]{1,0:T(8,128)S(1)} copy(s32[96,32]{0,1:T(8,128)} %param.13) | data formatting | bytes 24576 | tf_op args[0]
  4.8 0.1 sub.33
  4.9 0.1 copy.39
  5.0 0.1 pad_add_fusion
  5.1 0.6 pad.8
  5.8 18.2 %shard_map.140 = (s32[4,32,1,128]{3,2,1,0:T(1,128)}, s32[4,32,1,128]{3,2,1,0:T(1,128)}) custom-call(s32[128,1,128]{2,1,0:T(1,128)} %bitcast.28), custom_call_target="tpu_custom_call" | custom-call | bytes 50331648 | tf_op jit(solution)/shard_map/pallas_call | solution.py:212
  23.9 0.9 %copy.47 = s32[128,1,3]{0,2,1:T(4,128)S(1)} copy(s32[128,1,3]{2,0,1:T(8,128)} %bitcast.30) | data formatting | bytes 3072
  24.9 0.1 and_bitcast_fusion
  25.0 0.1 copy.43
  25.1 0.1 copy.41
  25.2 0.1 min.30
  25.4 0.7 %gather_fusion = s32[256,32]{1,0:T(8,128)S(1)} fusion(s32[96,32]{1,0:T(8,128)S(1)} %copy.42, s32[1024]{0:T(1024)S(1)} %pad_clamp_fusion.1), kind=kCustom, calls=%fused_computation | custom fusion | bytes 66560 | tf_op jit(solution)/shard_map/jit(_take)/gather | solution.py:410
  26.1 0.1 gather.11
  26.2 0.6 pad.9
  26.9 0.0 copy-done
  26.9 1.5 %gather_fusion.1 = f32[32,10,512]{2,0,1:T(8,128)S(1)} fusion(f32[96,10,512]{2,0,1:T(8,128)S(1)} %copy-done, s32[1024]{0:T(1024)S(1)} %pad_clamp_fusion), kind=kCustom, calls=%fused_computation.1 | custom fusion | bytes 1310848 | tf_op jit(solution)/shard_map/jit(_take)/gather | solution.py:414
  28.4 0.0 copy-done.11
  28.4 0.1 broadcast_select_fusion
  28.6 0.2 copy.45
  28.8 0.9 %reshape.106.refs_2_ = bf16[32,32,128]{2,1,0:T(8,128)(2,1)} reshape(bf16[32,8,512]{2,1,0:T(8,128)(2,1)S(1)} %copy.45) | data formatting | bytes 524288 | tf_op jit(solution)/shard_map/reshape | solution.py:416
  29.6 0.1 copy.44
  29.7 0.8 %reshape.105.refs_1_ = f32[32,8,128]{2,1,0:T(8,128)} reshape(f32[32,2,512]{2,1,0:T(2,128)S(1)} %copy.44) | data formatting | bytes 262144 | tf_op jit(solution)/shard_map/reshape | solution.py:415
  30.5 17.5 %shard_map.141 = (s32[4,32,1,128]{3,2,1,0:T(1,128)}, f32[32,8,128]{2,1,0:T(8,128)}, bf16[32,32,128]{2,1,0:T(8,128)(2,1)}, s32[4,32,1,128]{3,2,1,0:T(1,128)}) custom-call(s32[128,1,128]{2,1,0:T(1,128)} %bitcast.27, f32[32,8,128]{2,1,0:T(8,128)} %reshape.105.refs_1_, bf16[32,32,128]{2,1,0:T(8,128)(2,1)} %reshape.106.refs_2_), custom_call_target="tpu_custom_call" | custom-call | bytes 50331648 | tf_op jit(solution)/shard_map/pallas_call | solution.py:212
  48.0 0.0 copy-start.2
  48.0 0.0 copy-start.3
  48.1 0.0 copy-start.4
  48.1 0.0 copy-start.5
  48.1 0.0 copy-start.6
  48.1 0.0 copy-start.7
  48.1 0.0 copy-start.8
  48.1 0.0 copy-start.9
  48.1 0.0 copy-start.10
  48.1 11.2 %shard_map.142 = bf16[384,512]{1,0:T(8,128)(2,1)} custom-call(s32[96]{0:T(128)} %copy-done.11, s32[128,1,128]{2,1,0:T(1,128)} %bitcast.29, s32[96,1]{1,0:T(8,128)} %copy.46.rank_ref, bf16[16384,512]{1,0:T(8,128)(2,1)} %table_ref.1), custom_call_target="tpu_custom_call" | custom-call | tf_op jit(solution)/shard_map/pallas_call | solution.py:49
  59.4 0.0 copy-done.2
  59.4 0.0 copy-done.3
  59.4 0.0 copy-done.4
  59.4 0.0 copy-done.5
  59.5 0.0 copy-start.1
  59.5 1.0 %copy-done.1 = bf16[384,512]{1,0:T(8,128)(2,1)S(1)} copy-done((bf16[384,512]{1,0:T(8,128)(2,1)S(1)}, bf16[384,512]{1,0:T(8,128)(2,1)}, u32[]{:S(2)}) %copy-start.1) | copy-done | bytes 393240
  60.5 10.7 %shard_map.143 = (bf16[96,8,512]{2,1,0:T(8,128)(2,1)}, f32[10,96,512]{2,1,0:T(8,128)}) custom-call(s32[96]{0:T(128)S(1)} %subtract_clamp_fusion.source_ref, s32[96]{0:T(128)S(1)} %get-tuple-element.16.moved_ref, bf16[4,96,512]{2,1,0:T(8,128)(2,1)S(1)} %bitcast.22, f32[10,96,512]{2,1,0:T(8,128)S(1)} %bitcast.21, f32[32,8,128]{2,1,0:T(8,128)S(1)} %copy-done.5, ...), custom_call_target="tpu_custom_call" | custom-call | tf_op jit(solution)/shard_map/pallas_call | solution.py:320
  (20 shorter events, 0.1 us)
Async XLA Ops:
  0.6 26.2 %copy-start = (f32[96,10,512]{2,0,1:T(8,128)S(1)}, f32[96,10,512]{2,0,1:T(8,128)}, u32[]{:S(2)}) copy-start(f32[96,10,512]{2,0,1:T(8,128)} %param.17) | copy-start | bytes 5898244
  2.9 25.4 %copy-start.11 = (s32[96]{0:T(128)}, s32[96]{0:T(128)S(1)}, u32[]{:S(2)}) copy-start(s32[96]{0:T(128)S(1)} %get-tuple-element.20.anchor_ref) | copy-start | bytes 1156
  48.0 11.4 %copy-start.2 = (bf16[3,512,256]{2,1,0:T(8,128)(2,1)S(1)}, bf16[3,512,256]{2,1,0:T(8,128)(2,1)}, u32[]{:S(2)}) copy-start(bf16[3,512,256]{2,1,0:T(8,128)(2,1)} %in_w_ref.1) | copy-start | bytes 2359300
  48.0 11.4 %copy-start.3 = (bf16[256,512]{1,0:T(8,128)(2,1)S(1)}, bf16[256,512]{1,0:T(8,128)(2,1)}, u32[]{:S(2)}) copy-start(bf16[256,512]{1,0:T(8,128)(2,1)} %out_w_ref.1) | copy-start | bytes 786436
  48.1 11.4 %copy-start.4 = (bf16[32,32,128]{2,1,0:T(8,128)(2,1)S(1)}, bf16[32,32,128]{2,1,0:T(8,128)(2,1)}, u32[]{:S(2)}) copy-start(bf16[32,32,128]{2,1,0:T(8,128)(2,1)} %get-tuple-element.11.arrived_low_ref) | copy-start | bytes 786436
  48.1 11.4 %copy-start.5 = (f32[32,8,128]{2,1,0:T(8,128)S(1)}, f32[32,8,128]{2,1,0:T(8,128)}, u32[]{:S(2)}) copy-start(f32[32,8,128]{2,1,0:T(8,128)} %get-tuple-element.10.arrived_ref) | copy-start | bytes 393220
  48.1 11.4 %copy-start.6 = (f32[4,512]{1,0:T(4,128)S(1)}, f32[4,512]{1,0:T(4,128)}, u32[]{:S(2)}) copy-start(f32[4,512]{1,0:T(4,128)} %up_w_ref.1) | copy-start | bytes 24580
  48.1 11.4 %copy-start.7 = (f32[512]{0:T(512)S(1)}, f32[512]{0:T(512)}, u32[]{:S(2)}) copy-start(f32[512]{0:T(512)} %param.19) | copy-start | bytes 6148
  48.1 11.4 %copy-start.8 = (f32[512]{0:T(512)S(1)}, f32[512]{0:T(512)}, u32[]{:S(2)}) copy-start(f32[512]{0:T(512)} %param.21) | copy-start | bytes 6148
  48.1 11.3 %copy-start.9 = (f32[512]{0:T(512)S(1)}, f32[512]{0:T(512)}, u32[]{:S(2)}) copy-start(f32[512]{0:T(512)} %param.25) | copy-start | bytes 6148
  48.1 11.3 %copy-start.10 = (f32[256]{0:T(256)S(1)}, f32[256]{0:T(256)}, u32[]{:S(2)}) copy-start(f32[256]{0:T(256)} %param.23) | copy-start | bytes 3076
  59.5 1.0 %copy-start.1 = (bf16[384,512]{1,0:T(8,128)(2,1)S(1)}, bf16[384,512]{1,0:T(8,128)(2,1)}, u32[]{:S(2)}) copy-start(bf16[384,512]{1,0:T(8,128)(2,1)} %shard_map.142) | copy-start | bytes 1179652

commit v18 on v17

--- a/solution.py
+++ b/solution.py
@@ -227,6 +227,44 @@
     return [
         result.reshape(blocks.shape) for result, (blocks, _) in zip(results[:count], items)
     ]
+
+
+def pack_kernel(asked_ref, states_ref, high_ref, low_ref, low_scratch):
+    peers = high_ref.shape[0]
+    rows, slots, width = states_ref.shape
+    lanes = high_ref.shape[2]
+    pieces = width // lanes
+
+    def one(peer, carry):
+        index = jnp.clip(asked_ref[peer], 0, slots - 1)
+        for r in range(rows):
+            line = states_ref[r, pl.ds(index, 1), :]
+            for k in range(pieces):
+                piece = line[:, k * lanes : (k + 1) * lanes]
+                if r < 2:
+                    high_ref[peer, pl.ds(r * pieces + k, 1), :] = piece
+                else:
+                    low_scratch[peer, pl.ds((r - 2) * pieces + k, 1), :] = piece
+        return carry
+
+    lax.fori_loop(0, peers, one, 0)
+    low_ref[...] = low_scratch[...].astype(low_ref.dtype)
+
+
+def pack_leaving(asked, states_t, lanes):
+    peers = asked.shape[0]
+    rows, _, width = states_t.shape
+    pieces = width // lanes
+    return pl.pallas_call(
+        pack_kernel,
+        in_specs=[pl.BlockSpec(memory_space=pltpu.SMEM), pl.BlockSpec(memory_space=pltpu.VMEM)],
+        out_specs=[pl.BlockSpec(memory_space=pltpu.VMEM)] * 2,
+        out_shape=[
+            jax.ShapeDtypeStruct((peers, 2 * pieces, lanes), states_t.dtype),
+            jax.ShapeDtypeStruct((peers, (rows - 2) * pieces, lanes), jnp.bfloat16),
+        ],
+        scratch_shapes=[pltpu.VMEM((peers, (rows - 2) * pieces, lanes), jnp.float32)],
+    )(asked, states_t)
 
 
 def decode_kernel(
@@ -411,9 +449,7 @@
     answer = answer.reshape(devices_all, -1)
     answer = jnp.pad(answer, ((0, 0), (0, lanes - answer.shape[1]))).reshape(devices_all, 1, lanes)
     state_asked = lax.dynamic_slice_in_dim(asked[:, most], group_first, per_group)
-    leaving = jnp.take(states, jnp.clip(state_asked, 0, conv_count - 1), axis=0)
-    leaving_high = leaving[:, :2].reshape(per_group, -1, lanes)
-    leaving_low = leaving[:, 2:].astype(jnp.bfloat16).reshape(per_group, -1, lanes)
+    leaving_high, leaving_low = pack_leaving(state_asked, jnp.transpose(states, (1, 0, 2)), lanes)
     answered, arrived, arrived_low = exchange(
         [(answer, True), (leaving_high, False), (leaving_low, False)], 1
     )

time: 71.6 us -> 71.3 us (level)
  Pallas kernels: 57.7 us -> 60.6 us
  local copies, waits for them, and re-layouts: 9.61 us -> 6.8 us
    pallas_call x0 -> x1, Pallas kernels: none -> 3.04 us  [pack_leaving(): pl.pallas_call(pack_kernel, in_specs=[pl.BlockSpec(memory_space=pltpu.SME...]
    reshape x2 -> x0, local copies, waits for them, and re-layouts: 1.63 us -> none  [the longest x1 0.87 us: local(): leaving[:, 2:].astype(jnp.bfloat16).reshape(per_group, -1, lanes)]
    gather x1 -> x0, local copies, waits for them, and re-layouts: 1.51 us -> none  [local(): leaving = jnp.take(states, jnp.clip(state_asked, 0, conv_count - 1), axis=0)]
where the time goes in v18:
time: 71.3 us; the launch traced here: 71 us
  Pallas kernels  60.6 us (85%)
  local copies, waits for them, and re-layouts  6.8 us (10%)
  other arithmetic  2.57 us (4%)
  between operations  0.95 us (1%)
    pallas_call x2, Pallas kernels, exchange(): pl.pallas_call(kernel, out_shape=shapes + mids, in_specs=[pl.BlockSpec(me...  35.7 us
    pallas_call x1, Pallas kernels, embed_codes(): pl.pallas_call(embed_kernel, in_specs=[pl.BlockSpec(memory_space=pltpu.SM...  11.3 us
    pallas_call x1, Pallas kernels, decode(): pl.pallas_call(decode_kernel, grid_spec=pltpu.PrefetchScalarGridSpec(num_...  10.6 us
    pallas_call x1, Pallas kernels, pack_leaving(): pl.pallas_call(pack_kernel, in_specs=[pl.BlockSpec(memory_space=pltpu.SME...  3.04 us
    unnamed x26, local copies, waits for them, and re-layouts  2.76 us

profile of v18, /device:TPU:1, one launch (start us, length us, event | category | flops | bytes accessed | tf_op | source)
XLA Modules:
  0.0 71.0 jit_solution(6997501222187777679)
XLA Ops:
  0.6 0.7 fusion.3
  1.3 0.7 fusion.4
  2.0 0.1 select_reduce_fusion.1
  2.1 0.7 fusion.2
  2.8 0.2 convert_reduce_fusion
  3.0 0.1 select_reduce_fusion
  3.1 0.7 %copy.38.rank_ref = s32[96,1]{1,0:T(8,128)} copy(s32[96,1]{0,1:T(1,128)S(1)} %bitcast.36) | data formatting | bytes 768 | tf_op jit(solution)/shard_map/reshape | solution.py:64
  3.8 0.8 %copy.36 = s32[96,32]{1,0:T(8,128)S(1)} copy(s32[96,32]{0,1:T(8,128)} %param.13) | data formatting | bytes 24576 | tf_op args[0]
  4.6 0.1 sub.33
  4.8 0.1 copy.33
  4.9 0.1 pad_add_fusion
  5.0 0.6 pad.8
  5.6 18.2 %shard_map.140 = (s32[4,32,1,128]{3,2,1,0:T(1,128)}, s32[4,32,1,128]{3,2,1,0:T(1,128)}) custom-call(s32[128,1,128]{2,1,0:T(1,128)} %bitcast.28), custom_call_target="tpu_custom_call" | custom-call | bytes 50331648 | tf_op jit(solution)/shard_map/pallas_call | solution.py:212
  23.8 0.9 %copy.39 = s32[128,1,3]{0,2,1:T(4,128)S(1)} copy(s32[128,1,3]{2,0,1:T(8,128)} %bitcast.30) | data formatting | bytes 3072
  24.7 0.6 dynamic-slice_bitcast_fusion.asked_ref
  25.4 0.1 copy.37
  25.5 0.1 copy.35
  25.6 0.1 min.22
  25.8 0.7 %gather_fusion = s32[256,32]{1,0:T(8,128)S(1)} fusion(s32[96,32]{1,0:T(8,128)S(1)} %copy.36, s32[1024]{0:T(1024)S(1)} %pad_clamp_fusion), kind=kCustom, calls=%fused_computation | custom fusion | bytes 66560 | tf_op jit(solution)/shard_map/jit(_take)/gather | solution.py:448
  26.5 0.1 gather.7
  26.6 0.6 pad.9
  27.2 3.0 %shard_map.141 = (f32[32,8,128]{2,1,0:T(8,128)}, bf16[32,32,128]{2,1,0:T(8,128)(2,1)}) custom-call(s32[32]{0:T(128)} %dynamic-slice_bitcast_fusion.asked_ref, f32[10,96,512]{2,1,0:T(8,128)} %bitcast.20), custom_call_target="tpu_custom_call" | custom-call | tf_op jit(solution)/shard_map/pallas_call | solution.py:258
  30.3 17.6 %shard_map.142 = (s32[4,32,1,128]{3,2,1,0:T(1,128)}, f32[32,8,128]{2,1,0:T(8,128)}, bf16[32,32,128]{2,1,0:T(8,128)(2,1)}, s32[4,32,1,128]{3,2,1,0:T(1,128)}) custom-call(s32[128,1,128]{2,1,0:T(1,128)} %bitcast.27, f32[32,8,128]{2,1,0:T(8,128)} %get-tuple-element.11.refs_1_, bf16[32,32,128]{2,1,0:T(8,128)(2,1)} %get-tuple-element.12.refs_2_), custom_call_target="tpu_custom_call" | custom-call | bytes 50331648 | tf_op jit(solution)/shard_map/pallas_call | solution.py:212
  47.9 0.0 copy-done.11
  47.9 0.0 copy-start
  47.9 0.0 copy-start.2
  47.9 0.0 copy-start.3
  47.9 0.0 copy-start.4
  47.9 0.0 copy-start.5
  47.9 0.0 copy-start.6
  47.9 0.0 copy-start.7
  47.9 0.0 copy-start.8
  48.0 0.0 copy-start.9
  48.0 0.0 copy-start.10
  48.0 11.3 %shard_map.143 = bf16[384,512]{1,0:T(8,128)(2,1)} custom-call(s32[96]{0:T(128)} %copy-done.11, s32[128,1,128]{2,1,0:T(1,128)} %bitcast.29, s32[96,1]{1,0:T(8,128)} %copy.38.rank_ref, bf16[16384,512]{1,0:T(8,128)(2,1)} %table_ref.1), custom_call_target="tpu_custom_call" | custom-call | tf_op jit(solution)/shard_map/pallas_call | solution.py:49
  59.3 0.0 copy-done
  59.3 0.0 copy-done.2
  59.3 0.0 copy-done.3
  59.3 0.0 copy-done.4
  59.3 0.0 copy-done.5
  59.4 0.0 copy-done.6
  59.4 0.0 copy-done.7
  59.4 0.0 copy-done.8
  59.4 0.0 copy-done.9
  59.4 0.0 copy-done.10
  59.4 0.0 copy-start.1
  59.4 1.0 %copy-done.1 = bf16[384,512]{1,0:T(8,128)(2,1)S(1)} copy-done((bf16[384,512]{1,0:T(8,128)(2,1)S(1)}, bf16[384,512]{1,0:T(8,128)(2,1)}, u32[]{:S(2)}) %copy-start.1) | copy-done | bytes 393240
  60.4 10.6 %shard_map.144 = (bf16[96,8,512]{2,1,0:T(8,128)(2,1)}, f32[10,96,512]{2,1,0:T(8,128)}) custom-call(s32[96]{0:T(128)S(1)} %subtract_clamp_fusion.source_ref, s32[96]{0:T(128)S(1)} %get-tuple-element.18.moved_ref, bf16[4,96,512]{2,1,0:T(8,128)(2,1)S(1)} %bitcast.22, f32[10,96,512]{2,1,0:T(8,128)S(1)} %bitcast.21, f32[32,8,128]{2,1,0:T(8,128)S(1)} %copy-done.5, ...), custom_call_target="tpu_custom_call" | custom-call | tf_op jit(solution)/shard_map/pallas_call | solution.py:358
  (12 shorter events, 0.1 us)
Async XLA Ops:
  2.8 45.1 %copy-start.11 = (s32[96]{0:T(128)}, s32[96]{0:T(128)S(1)}, u32[]{:S(2)}) copy-start(s32[96]{0:T(128)S(1)} %get-tuple-element.22.anchor_ref) | copy-start | bytes 1156
  47.9 11.4 %copy-start = (f32[96,10,512]{2,0,1:T(8,128)S(1)}, f32[96,10,512]{2,0,1:T(8,128)}, u32[]{:S(2)}) copy-start(f32[96,10,512]{2,0,1:T(8,128)} %param.17) | copy-start | bytes 5898244
  47.9 11.4 %copy-start.2 = (bf16[3,512,256]{2,1,0:T(8,128)(2,1)S(1)}, bf16[3,512,256]{2,1,0:T(8,128)(2,1)}, u32[]{:S(2)}) copy-start(bf16[3,512,256]{2,1,0:T(8,128)(2,1)} %in_w_ref.1) | copy-start | bytes 2359300
  47.9 11.4 %copy-start.3 = (bf16[256,512]{1,0:T(8,128)(2,1)S(1)}, bf16[256,512]{1,0:T(8,128)(2,1)}, u32[]{:S(2)}) copy-start(bf16[256,512]{1,0:T(8,128)(2,1)} %out_w_ref.1) | copy-start | bytes 786436
  47.9 11.4 %copy-start.4 = (bf16[32,32,128]{2,1,0:T(8,128)(2,1)S(1)}, bf16[32,32,128]{2,1,0:T(8,128)(2,1)}, u32[]{:S(2)}) copy-start(bf16[32,32,128]{2,1,0:T(8,128)(2,1)} %get-tuple-element.15.arrived_low_ref) | copy-start | bytes 786436
  47.9 11.4 %copy-start.5 = (f32[32,8,128]{2,1,0:T(8,128)S(1)}, f32[32,8,128]{2,1,0:T(8,128)}, u32[]{:S(2)}) copy-start(f32[32,8,128]{2,1,0:T(8,128)} %get-tuple-element.14.arrived_ref) | copy-start | bytes 393220
  47.9 11.4 %copy-start.6 = (f32[4,512]{1,0:T(4,128)S(1)}, f32[4,512]{1,0:T(4,128)}, u32[]{:S(2)}) copy-start(f32[4,512]{1,0:T(4,128)} %up_w_ref.1) | copy-start | bytes 24580
  47.9 11.4 %copy-start.7 = (f32[512]{0:T(512)S(1)}, f32[512]{0:T(512)}, u32[]{:S(2)}) copy-start(f32[512]{0:T(512)} %param.19) | copy-start | bytes 6148
  47.9 11.4 %copy-start.8 = (f32[512]{0:T(512)S(1)}, f32[512]{0:T(512)}, u32[]{:S(2)}) copy-start(f32[512]{0:T(512)} %param.21) | copy-start | bytes 6148
  48.0 11.4 %copy-start.9 = (f32[512]{0:T(512)S(1)}, f32[512]{0:T(512)}, u32[]{:S(2)}) copy-start(f32[512]{0:T(512)} %param.25) | copy-start | bytes 6148
  48.0 11.4 %copy-start.10 = (f32[256]{0:T(256)S(1)}, f32[256]{0:T(256)}, u32[]{:S(2)}) copy-start(f32[256]{0:T(256)} %param.23) | copy-start | bytes 3076
  59.4 1.0 %copy-start.1 = (bf16[384,512]{1,0:T(8,128)(2,1)S(1)}, bf16[384,512]{1,0:T(8,128)(2,1)}, u32[]{:S(2)}) copy-start(bf16[384,512]{1,0:T(8,128)(2,1)} %shard_map.143) | copy-start | bytes 1179652

commit v19 on v18

--- a/solution.py
+++ b/solution.py
@@ -229,16 +229,24 @@
     ]
 
 
-def pack_kernel(asked_ref, states_ref, high_ref, low_ref, low_scratch):
+def pack_kernel(asked_ref, states_ref, high_ref, low_ref, lines_ref, low_scratch, sem):
     peers = high_ref.shape[0]
     rows, slots, width = states_ref.shape
     lanes = high_ref.shape[2]
     pieces = width // lanes
+    first = lax.axis_index("grp") * peers
+
+    def fetch(peer, carry):
+        index = jnp.clip(asked_ref[first + peer, 0, 2], 0, slots - 1)
+        pltpu.make_async_copy(states_ref.at[:, pl.ds(index, 1), :], lines_ref.at[:, pl.ds(peer, 1), :], sem).start()
+        return carry
+
+    lax.fori_loop(0, peers, fetch, 0)
+    pltpu.make_async_copy(lines_ref, lines_ref, sem).wait()
 
     def one(peer, carry):
-        index = jnp.clip(asked_ref[peer], 0, slots - 1)
         for r in range(rows):
-            line = states_ref[r, pl.ds(index, 1), :]
+            line = lines_ref[r, pl.ds(peer, 1), :]
             for k in range(pieces):
                 piece = line[:, k * lanes : (k + 1) * lanes]
                 if r < 2:
@@ -251,19 +259,22 @@
     low_ref[...] = low_scratch[...].astype(low_ref.dtype)
 
 
-def pack_leaving(asked, states_t, lanes):
-    peers = asked.shape[0]
+def pack_leaving(asked, states_t, lanes, peers):
     rows, _, width = states_t.shape
     pieces = width // lanes
     return pl.pallas_call(
         pack_kernel,
-        in_specs=[pl.BlockSpec(memory_space=pltpu.SMEM), pl.BlockSpec(memory_space=pltpu.VMEM)],
+        in_specs=[pl.BlockSpec(memory_space=pltpu.SMEM), pl.BlockSpec(memory_space=pl.ANY)],
         out_specs=[pl.BlockSpec(memory_space=pltpu.VMEM)] * 2,
         out_shape=[
             jax.ShapeDtypeStruct((peers, 2 * pieces, lanes), states_t.dtype),
             jax.ShapeDtypeStruct((peers, (rows - 2) * pieces, lanes), jnp.bfloat16),
         ],
-        scratch_shapes=[pltpu.VMEM((peers, (rows - 2) * pieces, lanes), jnp.float32)],
+        scratch_shapes=[
+            pltpu.VMEM((rows, peers, width), states_t.dtype),
+            pltpu.VMEM((peers, (rows - 2) * pieces, lanes), jnp.float32),
+            pltpu.SemaphoreType.DMA(()),
+        ],
     )(asked, states_t)
 
 
@@ -443,13 +454,13 @@
     lanes = 128
     padded = jnp.pad(request, ((0, 0), (0, lanes - most - 1))).reshape(devices_all, 1, lanes)
     (asked,) = exchange([(padded, True)], 0)
+    asked_blocks = asked
     asked = asked[:, 0, : most + 1]
 
     answer = jnp.take(codes, jnp.clip(asked[:, :most].reshape(-1), 0, conv_count - 1), axis=0)
     answer = answer.reshape(devices_all, -1)
     answer = jnp.pad(answer, ((0, 0), (0, lanes - answer.shape[1]))).reshape(devices_all, 1, lanes)
-    state_asked = lax.dynamic_slice_in_dim(asked[:, most], group_first, per_group)
-    leaving_high, leaving_low = pack_leaving(state_asked, jnp.transpose(states, (1, 0, 2)), lanes)
+    leaving_high, leaving_low = pack_leaving(asked_blocks, jnp.transpose(states, (1, 0, 2)), lanes, per_group)
     answered, arrived, arrived_low = exchange(
         [(answer, True), (leaving_high, False), (leaving_low, False)], 1
     )

time: 71.3 us -> 73.8 us (1.035)
  Pallas kernels: 60.6 us -> 62.8 us
  other arithmetic: 2.57 us -> 4.27 us
  local copies, waits for them, and re-layouts: 6.8 us -> 5.25 us
    pallas_call x1, Pallas kernels: 3.04 us -> 4.97 us  [pack_leaving(): pl.pallas_call(pack_kernel, in_specs=[pl.BlockSpec(memory_space=pltpu.SME...]
    unnamed x26 -> x25, local copies, waits for them, and re-layouts: 2.76 us -> 1.86 us
    min x1, other arithmetic: 0.01 us -> 0.86 us  [local(): jnp.clip(asked[:, :most].reshape(-1), 0, conv_count - 1)]
    and x1, other arithmetic: 0.03 us -> 0.87 us  [local(): jnp.take(codes, jnp.clip(asked[:, :most].reshape(-1), 0, conv_count - 1),...]
where the time goes in v19:
time: 73.8 us; the launch traced here: 73.3 us
  Pallas kernels  62.8 us (85%)
  local copies, waits for them, and re-layouts  5.25 us (7%)
  other arithmetic  4.27 us (6%)
  between operations  0.94 us (1%)
    pallas_call x2, Pallas kernels, exchange(): pl.pallas_call(kernel, out_shape=shapes + mids, in_specs=[pl.BlockSpec(me...  36 us
    pallas_call x1, Pallas kernels, embed_codes(): pl.pallas_call(embed_kernel, in_specs=[pl.BlockSpec(memory_space=pltpu.SM...  11.3 us
    pallas_call x1, Pallas kernels, decode(): pl.pallas_call(decode_kernel, grid_spec=pltpu.PrefetchScalarGridSpec(num_...  10.6 us
    pallas_call x1, Pallas kernels, pack_leaving(): pl.pallas_call(pack_kernel, in_specs=[pl.BlockSpec(memory_space=pltpu.SME...  4.97 us
    unnamed x25, local copies, waits for them, and re-layouts  1.86 us

profile of v19, /device:TPU:1, one launch (start us, length us, event | category | flops | bytes accessed | tf_op | source)
XLA Modules:
  0.0 73.3 jit_solution(13975035924966316417)
XLA Ops:
  0.6 0.7 fusion.3
  1.3 0.7 fusion.4
  2.0 0.1 select_reduce_fusion.1
  2.1 0.7 fusion.2
  2.8 0.2 convert_reduce_fusion
  3.0 0.1 select_reduce_fusion
  3.1 0.7 copy.33.rank_ref
  3.8 0.8 %copy.31 = s32[96,32]{1,0:T(8,128)S(1)} copy(s32[96,32]{0,1:T(8,128)} %param.13) | data formatting | bytes 24576 | tf_op args[0]
  4.6 0.1 sub.33
  4.8 0.1 copy.29
  4.9 0.1 pad_add_fusion
  5.0 0.6 pad.8
  5.6 18.2 %shard_map.140 = (s32[4,32,1,128]{3,2,1,0:T(1,128)}, s32[4,32,1,128]{3,2,1,0:T(1,128)}) custom-call(s32[128,1,128]{2,1,0:T(1,128)} %bitcast.29), custom_call_target="tpu_custom_call" | custom-call | bytes 50331648 | tf_op jit(solution)/shard_map/pallas_call | solution.py:212
  23.8 0.9 %compare_and_fusion = pred[128,2]{1,0:T(8,128)(4,1)S(1)} fusion(s32[128,3]{1,0:T(8,128)} %bitcast.25), kind=kLoop, calls=%fused_computation.6 | loop fusion | flops 1792 | bytes 1280 | tf_op jit(solution)/shard_map/jit(_take)/and | solution.py:460
  24.7 0.1 copy.30
  24.8 0.1 copy.32
  24.9 0.9 %slice_clamp_fusion = s32[128,2]{1,0:T(8,128)S(1)} fusion(s32[128,3]{1,0:T(8,128)} %bitcast.26), kind=kLoop, calls=%fused_computation.4 | loop fusion | flops 256 | bytes 2048 | tf_op jit(solution)/shard_map/jit(clip)/min | solution.py:460
  25.8 0.1 min.22
  25.9 0.7 gather_fusion
  26.6 0.1 gather.7
  26.7 0.6 pad.9
  27.4 5.0 %shard_map.141 = (f32[32,8,128]{2,1,0:T(8,128)}, bf16[32,32,128]{2,1,0:T(8,128)(2,1)}) custom-call(s32[128,1,128]{2,1,0:T(1,128)} %bitcast.27, f32[10,96,512]{2,1,0:T(8,128)} %bitcast.18), custom_call_target="tpu_custom_call" | custom-call | tf_op jit(solution)/shard_map/pallas_call | solution.py:265
  32.3 17.8 %shard_map.142 = (s32[4,32,1,128]{3,2,1,0:T(1,128)}, f32[32,8,128]{2,1,0:T(8,128)}, bf16[32,32,128]{2,1,0:T(8,128)(2,1)}, s32[4,32,1,128]{3,2,1,0:T(1,128)}) custom-call(s32[128,1,128]{2,1,0:T(1,128)} %bitcast.28, f32[32,8,128]{2,1,0:T(8,128)} %get-tuple-element.11.refs_1_, bf16[32,32,128]{2,1,0:T(8,128)(2,1)} %get-tuple-element.12.refs_2_), custom_call_target="tpu_custom_call" | custom-call | bytes 50331648 | tf_op jit(solution)/shard_map/pallas_call | solution.py:212
  50.1 0.0 copy-done.11
  50.2 0.0 copy-start
  50.2 0.0 copy-start.2
  50.2 0.0 copy-start.3
  50.2 0.0 copy-start.4
  50.2 0.0 copy-start.5
  50.2 0.0 copy-start.6
  50.2 0.0 copy-start.7
  50.2 0.0 copy-start.8
  50.2 0.0 copy-start.9
  50.3 0.0 copy-start.10
  50.3 11.3 %shard_map.143 = bf16[384,512]{1,0:T(8,128)(2,1)} custom-call(s32[96]{0:T(128)} %copy-done.11, s32[128,1,128]{2,1,0:T(1,128)} %bitcast.30, s32[96,1]{1,0:T(8,128)} %copy.33.rank_ref, bf16[16384,512]{1,0:T(8,128)(2,1)} %table_ref.1), custom_call_target="tpu_custom_call" | custom-call | tf_op jit(solution)/shard_map/pallas_call | solution.py:49
  61.6 0.0 copy-done
  61.6 0.0 copy-done.2
  61.6 0.0 copy-done.3
  61.6 0.0 copy-done.4
  61.6 0.0 copy-done.5
  61.7 0.0 copy-done.6
  61.7 0.0 copy-done.7
  61.7 0.0 copy-done.8
  61.7 0.0 copy-done.9
  61.7 0.0 copy-done.10
  61.7 0.0 copy-start.1
  61.7 1.0 %copy-done.1 = bf16[384,512]{1,0:T(8,128)(2,1)S(1)} copy-done((bf16[384,512]{1,0:T(8,128)(2,1)S(1)}, bf16[384,512]{1,0:T(8,128)(2,1)}, u32[]{:S(2)}) %copy-start.1) | copy-done | bytes 393240
  62.7 10.6 %shard_map.144 = (bf16[96,8,512]{2,1,0:T(8,128)(2,1)}, f32[10,96,512]{2,1,0:T(8,128)}) custom-call(s32[96]{0:T(128)S(1)} %subtract_clamp_fusion.source_ref, s32[96]{0:T(128)S(1)} %get-tuple-element.18.moved_ref, bf16[4,96,512]{2,1,0:T(8,128)(2,1)S(1)} %bitcast.20, f32[10,96,512]{2,1,0:T(8,128)S(1)} %bitcast.19, f32[32,8,128]{2,1,0:T(8,128)S(1)} %copy-done.5, ...), custom_call_target="tpu_custom_call" | custom-call | tf_op jit(solution)/shard_map/pallas_call | solution.py:369
  (9 shorter events, 0.1 us)
Async XLA Ops:
  2.8 47.4 %copy-start.11 = (s32[96]{0:T(128)}, s32[96]{0:T(128)S(1)}, u32[]{:S(2)}) copy-start(s32[96]{0:T(128)S(1)} %get-tuple-element.22.anchor_ref) | copy-start | bytes 1156
  50.2 11.4 %copy-start = (f32[96,10,512]{2,0,1:T(8,128)S(1)}, f32[96,10,512]{2,0,1:T(8,128)}, u32[]{:S(2)}) copy-start(f32[96,10,512]{2,0,1:T(8,128)} %param.17) | copy-start | bytes 5898244
  50.2 11.4 %copy-start.2 = (bf16[3,512,256]{2,1,0:T(8,128)(2,1)S(1)}, bf16[3,512,256]{2,1,0:T(8,128)(2,1)}, u32[]{:S(2)}) copy-start(bf16[3,512,256]{2,1,0:T(8,128)(2,1)} %in_w_ref.1) | copy-start | bytes 2359300
  50.2 11.4 %copy-start.3 = (bf16[256,512]{1,0:T(8,128)(2,1)S(1)}, bf16[256,512]{1,0:T(8,128)(2,1)}, u32[]{:S(2)}) copy-start(bf16[256,512]{1,0:T(8,128)(2,1)} %out_w_ref.1) | copy-start | bytes 786436
  50.2 11.4 %copy-start.4 = (bf16[32,32,128]{2,1,0:T(8,128)(2,1)S(1)}, bf16[32,32,128]{2,1,0:T(8,128)(2,1)}, u32[]{:S(2)}) copy-start(bf16[32,32,128]{2,1,0:T(8,128)(2,1)} %get-tuple-element.15.arrived_low_ref) | copy-start | bytes 786436
  50.2 11.4 %copy-start.5 = (f32[32,8,128]{2,1,0:T(8,128)S(1)}, f32[32,8,128]{2,1,0:T(8,128)}, u32[]{:S(2)}) copy-start(f32[32,8,128]{2,1,0:T(8,128)} %get-tuple-element.14.arrived_ref) | copy-start | bytes 393220
  50.2 11.4 %copy-start.6 = (f32[4,512]{1,0:T(4,128)S(1)}, f32[4,512]{1,0:T(4,128)}, u32[]{:S(2)}) copy-start(f32[4,512]{1,0:T(4,128)} %up_w_ref.1) | copy-start | bytes 24580
  50.2 11.4 %copy-start.7 = (f32[512]{0:T(512)S(1)}, f32[512]{0:T(512)}, u32[]{:S(2)}) copy-start(f32[512]{0:T(512)} %param.19) | copy-start | bytes 6148
  50.2 11.4 %copy-start.8 = (f32[512]{0:T(512)S(1)}, f32[512]{0:T(512)}, u32[]{:S(2)}) copy-start(f32[512]{0:T(512)} %param.21) | copy-start | bytes 6148
  50.2 11.4 %copy-start.9 = (f32[512]{0:T(512)S(1)}, f32[512]{0:T(512)}, u32[]{:S(2)}) copy-start(f32[512]{0:T(512)} %param.25) | copy-start | bytes 6148
  50.3 11.4 %copy-start.10 = (f32[256]{0:T(256)S(1)}, f32[256]{0:T(256)}, u32[]{:S(2)}) copy-start(f32[256]{0:T(256)} %param.23) | copy-start | bytes 3076
  61.7 1.0 %copy-start.1 = (bf16[384,512]{1,0:T(8,128)(2,1)S(1)}, bf16[384,512]{1,0:T(8,128)(2,1)}, u32[]{:S(2)}) copy-start(bf16[384,512]{1,0:T(8,128)(2,1)} %shard_map.143) | copy-start | bytes 1179652

commit v20 on v18

--- a/solution.py
+++ b/solution.py
@@ -30,10 +30,10 @@
     own = jnp.where(rank_ref[...] == 0, mine[:, :width], mine[:, width : 2 * width])
     by_row = jnp.concatenate([own[:, f * books : (f + 1) * books] for f in range(FRAMES)], axis=0)
     rows = by_row.shape[0]
+    entries = lax.broadcasted_iota(jnp.int32, (rows, size), 1)
     total = None
     for book in range(books):
         fetch(book).wait()
-        entries = lax.broadcasted_iota(jnp.int32, (rows, size), 1)
         onehot = (by_row[:, book : book + 1] == entries).astype(jnp.bfloat16)
         term = jnp.dot(onehot, blocks[book], preferred_element_type=jnp.float32)
         total = term if total is None else total + term

time: 71.3 us -> 71.3 us (level)
  no operation moved by 1% of the time
where the time goes in v20:
time: 71.3 us; the launch traced here: 71 us
  Pallas kernels  60.7 us (85%)
  local copies, waits for them, and re-layouts  6.8 us (10%)
  other arithmetic  2.57 us (4%)
  between operations  0.95 us (1%)
    pallas_call x2, Pallas kernels, exchange(): pl.pallas_call(kernel, out_shape=shapes + mids, in_specs=[pl.BlockSpec(me...  35.7 us
    pallas_call x1, Pallas kernels, embed_codes(): pl.pallas_call(embed_kernel, in_specs=[pl.BlockSpec(memory_space=pltpu.SM...  11.3 us
    pallas_call x1, Pallas kernels, decode(): pl.pallas_call(decode_kernel, grid_spec=pltpu.PrefetchScalarGridSpec(num_...  10.6 us
    pallas_call x1, Pallas kernels, pack_leaving(): pl.pallas_call(pack_kernel, in_specs=[pl.BlockSpec(memory_space=pltpu.SME...  3.04 us
    unnamed x26, local copies, waits for them, and re-layouts  2.76 us

profile of v20, /device:TPU:1, one launch (start us, length us, event | category | flops | bytes accessed | tf_op | source)
XLA Modules:
  0.0 71.0 jit_solution(530481986227207145)
XLA Ops:
  0.6 0.7 fusion.3
  1.3 0.7 fusion.4
  2.0 0.1 select_reduce_fusion.1
  2.1 0.7 fusion.2
  2.8 0.2 convert_reduce_fusion
  3.0 0.1 select_reduce_fusion
  3.1 0.7 %copy.38.rank_ref = s32[96,1]{1,0:T(8,128)} copy(s32[96,1]{0,1:T(1,128)S(1)} %bitcast.36) | data formatting | bytes 768 | tf_op jit(solution)/shard_map/reshape | solution.py:64
  3.8 0.8 %copy.36 = s32[96,32]{1,0:T(8,128)S(1)} copy(s32[96,32]{0,1:T(8,128)} %param.13) | data formatting | bytes 24576 | tf_op args[0]
  4.6 0.1 sub.33
  4.8 0.1 copy.33
  4.9 0.1 pad_add_fusion
  5.0 0.6 pad.8
  5.6 18.2 %shard_map.140 = (s32[4,32,1,128]{3,2,1,0:T(1,128)}, s32[4,32,1,128]{3,2,1,0:T(1,128)}) custom-call(s32[128,1,128]{2,1,0:T(1,128)} %bitcast.28), custom_call_target="tpu_custom_call" | custom-call | bytes 50331648 | tf_op jit(solution)/shard_map/pallas_call | solution.py:212
  23.8 0.9 %copy.39 = s32[128,1,3]{0,2,1:T(4,128)S(1)} copy(s32[128,1,3]{2,0,1:T(8,128)} %bitcast.30) | data formatting | bytes 3072
  24.7 0.6 dynamic-slice_bitcast_fusion.asked_ref
  25.4 0.1 copy.37
  25.5 0.1 copy.35
  25.6 0.1 min.22
  25.8 0.7 %gather_fusion = s32[256,32]{1,0:T(8,128)S(1)} fusion(s32[96,32]{1,0:T(8,128)S(1)} %copy.36, s32[1024]{0:T(1024)S(1)} %pad_clamp_fusion), kind=kCustom, calls=%fused_computation | custom fusion | bytes 66560 | tf_op jit(solution)/shard_map/jit(_take)/gather | solution.py:448
  26.5 0.1 gather.7
  26.6 0.6 pad.9
  27.2 3.0 %shard_map.141 = (f32[32,8,128]{2,1,0:T(8,128)}, bf16[32,32,128]{2,1,0:T(8,128)(2,1)}) custom-call(s32[32]{0:T(128)} %dynamic-slice_bitcast_fusion.asked_ref, f32[10,96,512]{2,1,0:T(8,128)} %bitcast.20), custom_call_target="tpu_custom_call" | custom-call | tf_op jit(solution)/shard_map/pallas_call | solution.py:258
  30.3 17.6 %shard_map.142 = (s32[4,32,1,128]{3,2,1,0:T(1,128)}, f32[32,8,128]{2,1,0:T(8,128)}, bf16[32,32,128]{2,1,0:T(8,128)(2,1)}, s32[4,32,1,128]{3,2,1,0:T(1,128)}) custom-call(s32[128,1,128]{2,1,0:T(1,128)} %bitcast.27, f32[32,8,128]{2,1,0:T(8,128)} %get-tuple-element.11.refs_1_, bf16[32,32,128]{2,1,0:T(8,128)(2,1)} %get-tuple-element.12.refs_2_), custom_call_target="tpu_custom_call" | custom-call | bytes 50331648 | tf_op jit(solution)/shard_map/pallas_call | solution.py:212
  47.9 0.0 copy-done.11
  47.9 0.0 copy-start
  47.9 0.0 copy-start.2
  47.9 0.0 copy-start.3
  47.9 0.0 copy-start.4
  47.9 0.0 copy-start.5
  47.9 0.0 copy-start.6
  47.9 0.0 copy-start.7
  47.9 0.0 copy-start.8
  48.0 0.0 copy-start.9
  48.0 0.0 copy-start.10
  48.0 11.3 %shard_map.143 = bf16[384,512]{1,0:T(8,128)(2,1)} custom-call(s32[96]{0:T(128)} %copy-done.11, s32[128,1,128]{2,1,0:T(1,128)} %bitcast.29, s32[96,1]{1,0:T(8,128)} %copy.38.rank_ref, bf16[16384,512]{1,0:T(8,128)(2,1)} %table_ref.1), custom_call_target="tpu_custom_call" | custom-call | tf_op jit(solution)/shard_map/pallas_call | solution.py:49
  59.3 0.0 copy-done
  59.3 0.0 copy-done.2
  59.3 0.0 copy-done.3
  59.3 0.0 copy-done.4
  59.3 0.0 copy-done.5
  59.4 0.0 copy-done.6
  59.4 0.0 copy-done.7
  59.4 0.0 copy-done.8
  59.4 0.0 copy-done.9
  59.4 0.0 copy-done.10
  59.4 0.0 copy-start.1
  59.4 1.0 %copy-done.1 = bf16[384,512]{1,0:T(8,128)(2,1)S(1)} copy-done((bf16[384,512]{1,0:T(8,128)(2,1)S(1)}, bf16[384,512]{1,0:T(8,128)(2,1)}, u32[]{:S(2)}) %copy-start.1) | copy-done | bytes 393240
  60.4 10.6 %shard_map.144 = (bf16[96,8,512]{2,1,0:T(8,128)(2,1)}, f32[10,96,512]{2,1,0:T(8,128)}) custom-call(s32[96]{0:T(128)S(1)} %subtract_clamp_fusion.source_ref, s32[96]{0:T(128)S(1)} %get-tuple-element.18.moved_ref, bf16[4,96,512]{2,1,0:T(8,128)(2,1)S(1)} %bitcast.22, f32[10,96,512]{2,1,0:T(8,128)S(1)} %bitcast.21, f32[32,8,128]{2,1,0:T(8,128)S(1)} %copy-done.5, ...), custom_call_target="tpu_custom_call" | custom-call | tf_op jit(solution)/shard_map/pallas_call | solution.py:358
  (12 shorter events, 0.1 us)
Async XLA Ops:
  2.8 45.1 %copy-start.11 = (s32[96]{0:T(128)}, s32[96]{0:T(128)S(1)}, u32[]{:S(2)}) copy-start(s32[96]{0:T(128)S(1)} %get-tuple-element.22.anchor_ref) | copy-start | bytes 1156
  47.9 11.4 %copy-start = (f32[96,10,512]{2,0,1:T(8,128)S(1)}, f32[96,10,512]{2,0,1:T(8,128)}, u32[]{:S(2)}) copy-start(f32[96,10,512]{2,0,1:T(8,128)} %param.17) | copy-start | bytes 5898244
  47.9 11.4 %copy-start.2 = (bf16[3,512,256]{2,1,0:T(8,128)(2,1)S(1)}, bf16[3,512,256]{2,1,0:T(8,128)(2,1)}, u32[]{:S(2)}) copy-start(bf16[3,512,256]{2,1,0:T(8,128)(2,1)} %in_w_ref.1) | copy-start | bytes 2359300
  47.9 11.4 %copy-start.3 = (bf16[256,512]{1,0:T(8,128)(2,1)S(1)}, bf16[256,512]{1,0:T(8,128)(2,1)}, u32[]{:S(2)}) copy-start(bf16[256,512]{1,0:T(8,128)(2,1)} %out_w_ref.1) | copy-start | bytes 786436
  47.9 11.4 %copy-start.4 = (bf16[32,32,128]{2,1,0:T(8,128)(2,1)S(1)}, bf16[32,32,128]{2,1,0:T(8,128)(2,1)}, u32[]{:S(2)}) copy-start(bf16[32,32,128]{2,1,0:T(8,128)(2,1)} %get-tuple-element.15.arrived_low_ref) | copy-start | bytes 786436
  47.9 11.4 %copy-start.5 = (f32[32,8,128]{2,1,0:T(8,128)S(1)}, f32[32,8,128]{2,1,0:T(8,128)}, u32[]{:S(2)}) copy-start(f32[32,8,128]{2,1,0:T(8,128)} %get-tuple-element.14.arrived_ref) | copy-start | bytes 393220
  47.9 11.4 %copy-start.6 = (f32[4,512]{1,0:T(4,128)S(1)}, f32[4,512]{1,0:T(4,128)}, u32[]{:S(2)}) copy-start(f32[4,512]{1,0:T(4,128)} %up_w_ref.1) | copy-start | bytes 24580
  47.9 11.4 %copy-start.7 = (f32[512]{0:T(512)S(1)}, f32[512]{0:T(512)}, u32[]{:S(2)}) copy-start(f32[512]{0:T(512)} %param.19) | copy-start | bytes 6148
  47.9 11.4 %copy-start.8 = (f32[512]{0:T(512)S(1)}, f32[512]{0:T(512)}, u32[]{:S(2)}) copy-start(f32[512]{0:T(512)} %param.21) | copy-start | bytes 6148
  48.0 11.4 %copy-start.9 = (f32[512]{0:T(512)S(1)}, f32[512]{0:T(512)}, u32[]{:S(2)}) copy-start(f32[512]{0:T(512)} %param.25) | copy-start | bytes 6148
  48.0 11.4 %copy-start.10 = (f32[256]{0:T(256)S(1)}, f32[256]{0:T(256)}, u32[]{:S(2)}) copy-start(f32[256]{0:T(256)} %param.23) | copy-start | bytes 3076
  59.4 1.0 %copy-start.1 = (bf16[384,512]{1,0:T(8,128)(2,1)S(1)}, bf16[384,512]{1,0:T(8,128)(2,1)}, u32[]{:S(2)}) copy-start(bf16[384,512]{1,0:T(8,128)(2,1)} %shard_map.143) | copy-start | bytes 1179652

commit v21 on v18

--- a/solution.py
+++ b/solution.py
@@ -298,7 +298,7 @@
 
         return carry
 
-    lax.fori_loop(0, slots, bring, 0)
+    lax.fori_loop(0, slots, bring, 0, unroll=8)
 
     def elu(value):
         return jnp.where(value > 0, value, jnp.exp(jnp.minimum(value, 0.0)) - 1.0)

time: 71.3 us -> 70.9 us (level)
  no operation moved by 1% of the time
where the time goes in v21:
time: 70.9 us; the launch traced here: 70.5 us
  Pallas kernels  60.2 us (85%)
  local copies, waits for them, and re-layouts  6.8 us (10%)
  other arithmetic  2.57 us (4%)
  between operations  0.95 us (1%)
    pallas_call x2, Pallas kernels, exchange(): pl.pallas_call(kernel, out_shape=shapes + mids, in_specs=[pl.BlockSpec(me...  35.7 us
    pallas_call x1, Pallas kernels, embed_codes(): pl.pallas_call(embed_kernel, in_specs=[pl.BlockSpec(memory_space=pltpu.SM...  11.3 us
    pallas_call x1, Pallas kernels, decode(): pl.pallas_call(decode_kernel, grid_spec=pltpu.PrefetchScalarGridSpec(num_...  10.1 us
    pallas_call x1, Pallas kernels, pack_leaving(): pl.pallas_call(pack_kernel, in_specs=[pl.BlockSpec(memory_space=pltpu.SME...  3.04 us
    unnamed x26, local copies, waits for them, and re-layouts  2.76 us

profile of v21, /device:TPU:1, one launch (start us, length us, event | category | flops | bytes accessed | tf_op | source)
XLA Modules:
  0.0 70.5 jit_solution(9524213645914019301)
XLA Ops:
  0.6 0.7 fusion.3
  1.3 0.7 fusion.4
  2.0 0.1 select_reduce_fusion.1
  2.1 0.7 fusion.2
  2.8 0.2 convert_reduce_fusion
  3.0 0.1 select_reduce_fusion
  3.1 0.7 %copy.38.rank_ref = s32[96,1]{1,0:T(8,128)} copy(s32[96,1]{0,1:T(1,128)S(1)} %bitcast.36) | data formatting | bytes 768 | tf_op jit(solution)/shard_map/reshape | solution.py:64
  3.8 0.8 %copy.36 = s32[96,32]{1,0:T(8,128)S(1)} copy(s32[96,32]{0,1:T(8,128)} %param.13) | data formatting | bytes 24576 | tf_op args[0]
  4.6 0.1 sub.33
  4.8 0.1 copy.33
  4.9 0.1 pad_add_fusion
  5.0 0.6 pad.8
  5.6 18.2 %shard_map.140 = (s32[4,32,1,128]{3,2,1,0:T(1,128)}, s32[4,32,1,128]{3,2,1,0:T(1,128)}) custom-call(s32[128,1,128]{2,1,0:T(1,128)} %bitcast.28), custom_call_target="tpu_custom_call" | custom-call | bytes 50331648 | tf_op jit(solution)/shard_map/pallas_call | solution.py:212
  23.8 0.9 %copy.39 = s32[128,1,3]{0,2,1:T(4,128)S(1)} copy(s32[128,1,3]{2,0,1:T(8,128)} %bitcast.30) | data formatting | bytes 3072
  24.7 0.6 dynamic-slice_bitcast_fusion.asked_ref
  25.4 0.1 copy.37
  25.5 0.1 copy.35
  25.6 0.1 min.22
  25.8 0.7 %gather_fusion = s32[256,32]{1,0:T(8,128)S(1)} fusion(s32[96,32]{1,0:T(8,128)S(1)} %copy.36, s32[1024]{0:T(1024)S(1)} %pad_clamp_fusion), kind=kCustom, calls=%fused_computation | custom fusion | bytes 66560 | tf_op jit(solution)/shard_map/jit(_take)/gather | solution.py:448
  26.5 0.1 gather.7
  26.6 0.6 pad.9
  27.2 3.0 %shard_map.141 = (f32[32,8,128]{2,1,0:T(8,128)}, bf16[32,32,128]{2,1,0:T(8,128)(2,1)}) custom-call(s32[32]{0:T(128)} %dynamic-slice_bitcast_fusion.asked_ref, f32[10,96,512]{2,1,0:T(8,128)} %bitcast.20), custom_call_target="tpu_custom_call" | custom-call | tf_op jit(solution)/shard_map/pallas_call | solution.py:258
  30.3 17.6 %shard_map.142 = (s32[4,32,1,128]{3,2,1,0:T(1,128)}, f32[32,8,128]{2,1,0:T(8,128)}, bf16[32,32,128]{2,1,0:T(8,128)(2,1)}, s32[4,32,1,128]{3,2,1,0:T(1,128)}) custom-call(s32[128,1,128]{2,1,0:T(1,128)} %bitcast.27, f32[32,8,128]{2,1,0:T(8,128)} %get-tuple-element.11.refs_1_, bf16[32,32,128]{2,1,0:T(8,128)(2,1)} %get-tuple-element.12.refs_2_), custom_call_target="tpu_custom_call" | custom-call | bytes 50331648 | tf_op jit(solution)/shard_map/pallas_call | solution.py:212
  47.9 0.0 copy-done.11
  47.9 0.0 copy-start
  47.9 0.0 copy-start.2
  47.9 0.0 copy-start.3
  47.9 0.0 copy-start.4
  47.9 0.0 copy-start.5
  47.9 0.0 copy-start.6
  47.9 0.0 copy-start.7
  47.9 0.0 copy-start.8
  48.0 0.0 copy-start.9
  48.0 0.0 copy-start.10
  48.0 11.3 %shard_map.143 = bf16[384,512]{1,0:T(8,128)(2,1)} custom-call(s32[96]{0:T(128)} %copy-done.11, s32[128,1,128]{2,1,0:T(1,128)} %bitcast.29, s32[96,1]{1,0:T(8,128)} %copy.38.rank_ref, bf16[16384,512]{1,0:T(8,128)(2,1)} %table_ref.1), custom_call_target="tpu_custom_call" | custom-call | tf_op jit(solution)/shard_map/pallas_call | solution.py:49
  59.3 0.0 copy-done
  59.3 0.0 copy-done.2
  59.3 0.0 copy-done.3
  59.3 0.0 copy-done.4
  59.3 0.0 copy-done.5
  59.4 0.0 copy-done.6
  59.4 0.0 copy-done.7
  59.4 0.0 copy-done.8
  59.4 0.0 copy-done.9
  59.4 0.0 copy-done.10
  59.4 0.0 copy-start.1
  59.4 1.0 %copy-done.1 = bf16[384,512]{1,0:T(8,128)(2,1)S(1)} copy-done((bf16[384,512]{1,0:T(8,128)(2,1)S(1)}, bf16[384,512]{1,0:T(8,128)(2,1)}, u32[]{:S(2)}) %copy-start.1) | copy-done | bytes 393240
  60.4 10.1 %shard_map.144 = (bf16[96,8,512]{2,1,0:T(8,128)(2,1)}, f32[10,96,512]{2,1,0:T(8,128)}) custom-call(s32[96]{0:T(128)S(1)} %subtract_clamp_fusion.source_ref, s32[96]{0:T(128)S(1)} %get-tuple-element.18.moved_ref, bf16[4,96,512]{2,1,0:T(8,128)(2,1)S(1)} %bitcast.22, f32[10,96,512]{2,1,0:T(8,128)S(1)} %bitcast.21, f32[32,8,128]{2,1,0:T(8,128)S(1)} %copy-done.5, ...), custom_call_target="tpu_custom_call" | custom-call | tf_op jit(solution)/shard_map/pallas_call | solution.py:358
  (12 shorter events, 0.1 us)
Async XLA Ops:
  2.8 45.1 %copy-start.11 = (s32[96]{0:T(128)}, s32[96]{0:T(128)S(1)}, u32[]{:S(2)}) copy-start(s32[96]{0:T(128)S(1)} %get-tuple-element.22.anchor_ref) | copy-start | bytes 1156
  47.9 11.4 %copy-start = (f32[96,10,512]{2,0,1:T(8,128)S(1)}, f32[96,10,512]{2,0,1:T(8,128)}, u32[]{:S(2)}) copy-start(f32[96,10,512]{2,0,1:T(8,128)} %param.17) | copy-start | bytes 5898244
  47.9 11.4 %copy-start.2 = (bf16[3,512,256]{2,1,0:T(8,128)(2,1)S(1)}, bf16[3,512,256]{2,1,0:T(8,128)(2,1)}, u32[]{:S(2)}) copy-start(bf16[3,512,256]{2,1,0:T(8,128)(2,1)} %in_w_ref.1) | copy-start | bytes 2359300
  47.9 11.4 %copy-start.3 = (bf16[256,512]{1,0:T(8,128)(2,1)S(1)}, bf16[256,512]{1,0:T(8,128)(2,1)}, u32[]{:S(2)}) copy-start(bf16[256,512]{1,0:T(8,128)(2,1)} %out_w_ref.1) | copy-start | bytes 786436
  47.9 11.4 %copy-start.4 = (bf16[32,32,128]{2,1,0:T(8,128)(2,1)S(1)}, bf16[32,32,128]{2,1,0:T(8,128)(2,1)}, u32[]{:S(2)}) copy-start(bf16[32,32,128]{2,1,0:T(8,128)(2,1)} %get-tuple-element.15.arrived_low_ref) | copy-start | bytes 786436
  47.9 11.4 %copy-start.5 = (f32[32,8,128]{2,1,0:T(8,128)S(1)}, f32[32,8,128]{2,1,0:T(8,128)}, u32[]{:S(2)}) copy-start(f32[32,8,128]{2,1,0:T(8,128)} %get-tuple-element.14.arrived_ref) | copy-start | bytes 393220
  47.9 11.4 %copy-start.6 = (f32[4,512]{1,0:T(4,128)S(1)}, f32[4,512]{1,0:T(4,128)}, u32[]{:S(2)}) copy-start(f32[4,512]{1,0:T(4,128)} %up_w_ref.1) | copy-start | bytes 24580
  47.9 11.4 %copy-start.7 = (f32[512]{0:T(512)S(1)}, f32[512]{0:T(512)}, u32[]{:S(2)}) copy-start(f32[512]{0:T(512)} %param.19) | copy-start | bytes 6148
  47.9 11.4 %copy-start.8 = (f32[512]{0:T(512)S(1)}, f32[512]{0:T(512)}, u32[]{:S(2)}) copy-start(f32[512]{0:T(512)} %param.21) | copy-start | bytes 6148
  48.0 11.4 %copy-start.9 = (f32[512]{0:T(512)S(1)}, f32[512]{0:T(512)}, u32[]{:S(2)}) copy-start(f32[512]{0:T(512)} %param.25) | copy-start | bytes 6148
  48.0 11.4 %copy-start.10 = (f32[256]{0:T(256)S(1)}, f32[256]{0:T(256)}, u32[]{:S(2)}) copy-start(f32[256]{0:T(256)} %param.23) | copy-start | bytes 3076
  59.4 1.0 %copy-start.1 = (bf16[384,512]{1,0:T(8,128)(2,1)S(1)}, bf16[384,512]{1,0:T(8,128)(2,1)}, u32[]{:S(2)}) copy-start(bf16[384,512]{1,0:T(8,128)(2,1)} %shard_map.143) | copy-start | bytes 1179652

commit v22 on v21

--- a/solution.py
+++ b/solution.py
@@ -298,7 +298,7 @@
 
         return carry
 
-    lax.fori_loop(0, slots, bring, 0, unroll=8)
+    lax.fori_loop(0, slots, bring, 0, unroll=32)
 
     def elu(value):
         return jnp.where(value > 0, value, jnp.exp(jnp.minimum(value, 0.0)) - 1.0)

time: 70.9 us -> 70.8 us (level)
  no operation moved by 1% of the time
where the time goes in v22:
time: 70.8 us; the launch traced here: 70.5 us
  Pallas kernels  60.2 us (85%)
  local copies, waits for them, and re-layouts  6.8 us (10%)
  other arithmetic  2.57 us (4%)
  between operations  0.95 us (1%)
    pallas_call x2, Pallas kernels, exchange(): pl.pallas_call(kernel, out_shape=shapes + mids, in_specs=[pl.BlockSpec(me...  35.7 us
    pallas_call x1, Pallas kernels, embed_codes(): pl.pallas_call(embed_kernel, in_specs=[pl.BlockSpec(memory_space=pltpu.SM...  11.3 us
    pallas_call x1, Pallas kernels, decode(): pl.pallas_call(decode_kernel, grid_spec=pltpu.PrefetchScalarGridSpec(num_...  10.1 us
    pallas_call x1, Pallas kernels, pack_leaving(): pl.pallas_call(pack_kernel, in_specs=[pl.BlockSpec(memory_space=pltpu.SME...  3.04 us
    unnamed x26, local copies, waits for them, and re-layouts  2.76 us

profile of v22, /device:TPU:1, one launch (start us, length us, event | category | flops | bytes accessed | tf_op | source)
XLA Modules:
  0.0 70.5 jit_solution(4224150293794171863)
XLA Ops:
  0.6 0.7 fusion.3
  1.3 0.7 fusion.4
  2.0 0.1 select_reduce_fusion.1
  2.1 0.7 fusion.2
  2.8 0.2 convert_reduce_fusion
  3.0 0.1 select_reduce_fusion
  3.1 0.7 %copy.38.rank_ref = s32[96,1]{1,0:T(8,128)} copy(s32[96,1]{0,1:T(1,128)S(1)} %bitcast.36) | data formatting | bytes 768 | tf_op jit(solution)/shard_map/reshape | solution.py:64
  3.8 0.8 %copy.36 = s32[96,32]{1,0:T(8,128)S(1)} copy(s32[96,32]{0,1:T(8,128)} %param.13) | data formatting | bytes 24576 | tf_op args[0]
  4.6 0.1 sub.33
  4.8 0.1 copy.33
  4.9 0.1 pad_add_fusion
  5.0 0.6 pad.8
  5.6 18.2 %shard_map.140 = (s32[4,32,1,128]{3,2,1,0:T(1,128)}, s32[4,32,1,128]{3,2,1,0:T(1,128)}) custom-call(s32[128,1,128]{2,1,0:T(1,128)} %bitcast.28), custom_call_target="tpu_custom_call" | custom-call | bytes 50331648 | tf_op jit(solution)/shard_map/pallas_call | solution.py:212
  23.8 0.9 %copy.39 = s32[128,1,3]{0,2,1:T(4,128)S(1)} copy(s32[128,1,3]{2,0,1:T(8,128)} %bitcast.30) | data formatting | bytes 3072
  24.7 0.6 dynamic-slice_bitcast_fusion.asked_ref
  25.4 0.1 copy.37
  25.5 0.1 copy.35
  25.6 0.1 min.22
  25.8 0.7 %gather_fusion = s32[256,32]{1,0:T(8,128)S(1)} fusion(s32[96,32]{1,0:T(8,128)S(1)} %copy.36, s32[1024]{0:T(1024)S(1)} %pad_clamp_fusion), kind=kCustom, calls=%fused_computation | custom fusion | bytes 66560 | tf_op jit(solution)/shard_map/jit(_take)/gather | solution.py:448
  26.5 0.1 gather.7
  26.6 0.6 pad.9
  27.2 3.0 %shard_map.141 = (f32[32,8,128]{2,1,0:T(8,128)}, bf16[32,32,128]{2,1,0:T(8,128)(2,1)}) custom-call(s32[32]{0:T(128)} %dynamic-slice_bitcast_fusion.asked_ref, f32[10,96,512]{2,1,0:T(8,128)} %bitcast.20), custom_call_target="tpu_custom_call" | custom-call | tf_op jit(solution)/shard_map/pallas_call | solution.py:258
  30.3 17.6 %shard_map.142 = (s32[4,32,1,128]{3,2,1,0:T(1,128)}, f32[32,8,128]{2,1,0:T(8,128)}, bf16[32,32,128]{2,1,0:T(8,128)(2,1)}, s32[4,32,1,128]{3,2,1,0:T(1,128)}) custom-call(s32[128,1,128]{2,1,0:T(1,128)} %bitcast.27, f32[32,8,128]{2,1,0:T(8,128)} %get-tuple-element.11.refs_1_, bf16[32,32,128]{2,1,0:T(8,128)(2,1)} %get-tuple-element.12.refs_2_), custom_call_target="tpu_custom_call" | custom-call | bytes 50331648 | tf_op jit(solution)/shard_map/pallas_call | solution.py:212
  47.9 0.0 copy-done.11
  47.9 0.0 copy-start
  47.9 0.0 copy-start.2
  47.9 0.0 copy-start.3
  47.9 0.0 copy-start.4
  47.9 0.0 copy-start.5
  47.9 0.0 copy-start.6
  47.9 0.0 copy-start.7
  47.9 0.0 copy-start.8
  48.0 0.0 copy-start.9
  48.0 0.0 copy-start.10
  48.0 11.3 %shard_map.143 = bf16[384,512]{1,0:T(8,128)(2,1)} custom-call(s32[96]{0:T(128)} %copy-done.11, s32[128,1,128]{2,1,0:T(1,128)} %bitcast.29, s32[96,1]{1,0:T(8,128)} %copy.38.rank_ref, bf16[16384,512]{1,0:T(8,128)(2,1)} %table_ref.1), custom_call_target="tpu_custom_call" | custom-call | tf_op jit(solution)/shard_map/pallas_call | solution.py:49
  59.3 0.0 copy-done
  59.3 0.0 copy-done.2
  59.3 0.0 copy-done.3
  59.3 0.0 copy-done.4
  59.3 0.0 copy-done.5
  59.4 0.0 copy-done.6
  59.4 0.0 copy-done.7
  59.4 0.0 copy-done.8
  59.4 0.0 copy-done.9
  59.4 0.0 copy-done.10
  59.4 0.0 copy-start.1
  59.4 1.0 %copy-done.1 = bf16[384,512]{1,0:T(8,128)(2,1)S(1)} copy-done((bf16[384,512]{1,0:T(8,128)(2,1)S(1)}, bf16[384,512]{1,0:T(8,128)(2,1)}, u32[]{:S(2)}) %copy-start.1) | copy-done | bytes 393240
  60.4 10.1 %shard_map.144 = (bf16[96,8,512]{2,1,0:T(8,128)(2,1)}, f32[10,96,512]{2,1,0:T(8,128)}) custom-call(s32[96]{0:T(128)S(1)} %subtract_clamp_fusion.source_ref, s32[96]{0:T(128)S(1)} %get-tuple-element.18.moved_ref, bf16[4,96,512]{2,1,0:T(8,128)(2,1)S(1)} %bitcast.22, f32[10,96,512]{2,1,0:T(8,128)S(1)} %bitcast.21, f32[32,8,128]{2,1,0:T(8,128)S(1)} %copy-done.5, ...), custom_call_target="tpu_custom_call" | custom-call | tf_op jit(solution)/shard_map/pallas_call | solution.py:358
  (12 shorter events, 0.1 us)
Async XLA Ops:
  2.8 45.1 %copy-start.11 = (s32[96]{0:T(128)}, s32[96]{0:T(128)S(1)}, u32[]{:S(2)}) copy-start(s32[96]{0:T(128)S(1)} %get-tuple-element.22.anchor_ref) | copy-start | bytes 1156
  47.9 11.4 %copy-start = (f32[96,10,512]{2,0,1:T(8,128)S(1)}, f32[96,10,512]{2,0,1:T(8,128)}, u32[]{:S(2)}) copy-start(f32[96,10,512]{2,0,1:T(8,128)} %param.17) | copy-start | bytes 5898244
  47.9 11.4 %copy-start.2 = (bf16[3,512,256]{2,1,0:T(8,128)(2,1)S(1)}, bf16[3,512,256]{2,1,0:T(8,128)(2,1)}, u32[]{:S(2)}) copy-start(bf16[3,512,256]{2,1,0:T(8,128)(2,1)} %in_w_ref.1) | copy-start | bytes 2359300
  47.9 11.4 %copy-start.3 = (bf16[256,512]{1,0:T(8,128)(2,1)S(1)}, bf16[256,512]{1,0:T(8,128)(2,1)}, u32[]{:S(2)}) copy-start(bf16[256,512]{1,0:T(8,128)(2,1)} %out_w_ref.1) | copy-start | bytes 786436
  47.9 11.4 %copy-start.4 = (bf16[32,32,128]{2,1,0:T(8,128)(2,1)S(1)}, bf16[32,32,128]{2,1,0:T(8,128)(2,1)}, u32[]{:S(2)}) copy-start(bf16[32,32,128]{2,1,0:T(8,128)(2,1)} %get-tuple-element.15.arrived_low_ref) | copy-start | bytes 786436
  47.9 11.4 %copy-start.5 = (f32[32,8,128]{2,1,0:T(8,128)S(1)}, f32[32,8,128]{2,1,0:T(8,128)}, u32[]{:S(2)}) copy-start(f32[32,8,128]{2,1,0:T(8,128)} %get-tuple-element.14.arrived_ref) | copy-start | bytes 393220
  47.9 11.4 %copy-start.6 = (f32[4,512]{1,0:T(4,128)S(1)}, f32[4,512]{1,0:T(4,128)}, u32[]{:S(2)}) copy-start(f32[4,512]{1,0:T(4,128)} %up_w_ref.1) | copy-start | bytes 24580
  47.9 11.4 %copy-start.7 = (f32[512]{0:T(512)S(1)}, f32[512]{0:T(512)}, u32[]{:S(2)}) copy-start(f32[512]{0:T(512)} %param.19) | copy-start | bytes 6148
  47.9 11.4 %copy-start.8 = (f32[512]{0:T(512)S(1)}, f32[512]{0:T(512)}, u32[]{:S(2)}) copy-start(f32[512]{0:T(512)} %param.21) | copy-start | bytes 6148
  48.0 11.4 %copy-start.9 = (f32[512]{0:T(512)S(1)}, f32[512]{0:T(512)}, u32[]{:S(2)}) copy-start(f32[512]{0:T(512)} %param.25) | copy-start | bytes 6148
  48.0 11.4 %copy-start.10 = (f32[256]{0:T(256)S(1)}, f32[256]{0:T(256)}, u32[]{:S(2)}) copy-start(f32[256]{0:T(256)} %param.23) | copy-start | bytes 3076
  59.4 1.0 %copy-start.1 = (bf16[384,512]{1,0:T(8,128)(2,1)S(1)}, bf16[384,512]{1,0:T(8,128)(2,1)}, u32[]{:S(2)}) copy-start(bf16[384,512]{1,0:T(8,128)(2,1)} %shard_map.143) | copy-start | bytes 1179652

commit v23 on v21

--- a/solution.py
+++ b/solution.py
@@ -24,7 +24,7 @@
         mine_ref[pl.ds(slot, 1), :] = answered_ref[anchor_ref[slot]]
         return carry
 
-    lax.fori_loop(0, slots, pick, 0)
+    lax.fori_loop(0, slots, pick, 0, unroll=8)
     mine = mine_ref[...]
     width = books * FRAMES
     own = jnp.where(rank_ref[...] == 0, mine[:, :width], mine[:, width : 2 * width])
@@ -247,7 +247,7 @@
                     low_scratch[peer, pl.ds((r - 2) * pieces + k, 1), :] = piece
         return carry
 
-    lax.fori_loop(0, peers, one, 0)
+    lax.fori_loop(0, peers, one, 0, unroll=8)
     low_ref[...] = low_scratch[...].astype(low_ref.dtype)
 
 

time: 70.9 us -> 70.6 us (level)
  no operation moved by 1% of the time
where the time goes in v23:
time: 70.6 us; the launch traced here: 70.3 us
  Pallas kernels  59.9 us (85%)
  local copies, waits for them, and re-layouts  6.8 us (10%)
  other arithmetic  2.57 us (4%)
  between operations  0.95 us (1%)
    pallas_call x2, Pallas kernels, exchange(): pl.pallas_call(kernel, out_shape=shapes + mids, in_specs=[pl.BlockSpec(me...  35.7 us
    pallas_call x1, Pallas kernels, embed_codes(): pl.pallas_call(embed_kernel, in_specs=[pl.BlockSpec(memory_space=pltpu.SM...  11.3 us
    pallas_call x1, Pallas kernels, decode(): pl.pallas_call(decode_kernel, grid_spec=pltpu.PrefetchScalarGridSpec(num_...  10.1 us
    pallas_call x1, Pallas kernels, pack_leaving(): pl.pallas_call(pack_kernel, in_specs=[pl.BlockSpec(memory_space=pltpu.SME...  2.78 us
    unnamed x26, local copies, waits for them, and re-layouts  2.76 us

profile of v23, /device:TPU:1, one launch (start us, length us, event | category | flops | bytes accessed | tf_op | source)
XLA Modules:
  0.0 70.3 jit_solution(4139213323567635792)
XLA Ops:
  0.6 0.7 fusion.3
  1.3 0.7 fusion.4
  2.0 0.1 select_reduce_fusion.1
  2.1 0.7 fusion.2
  2.8 0.2 convert_reduce_fusion
  3.0 0.1 select_reduce_fusion
  3.1 0.7 %copy.38.rank_ref = s32[96,1]{1,0:T(8,128)} copy(s32[96,1]{0,1:T(1,128)S(1)} %bitcast.36) | data formatting | bytes 768 | tf_op jit(solution)/shard_map/reshape | solution.py:64
  3.8 0.8 %copy.36 = s32[96,32]{1,0:T(8,128)S(1)} copy(s32[96,32]{0,1:T(8,128)} %param.13) | data formatting | bytes 24576 | tf_op args[0]
  4.6 0.1 sub.33
  4.8 0.1 copy.33
  4.9 0.1 pad_add_fusion
  5.0 0.6 pad.8
  5.6 18.2 %shard_map.140 = (s32[4,32,1,128]{3,2,1,0:T(1,128)}, s32[4,32,1,128]{3,2,1,0:T(1,128)}) custom-call(s32[128,1,128]{2,1,0:T(1,128)} %bitcast.28), custom_call_target="tpu_custom_call" | custom-call | bytes 50331648 | tf_op jit(solution)/shard_map/pallas_call | solution.py:212
  23.8 0.9 %copy.39 = s32[128,1,3]{0,2,1:T(4,128)S(1)} copy(s32[128,1,3]{2,0,1:T(8,128)} %bitcast.30) | data formatting | bytes 3072
  24.7 0.6 dynamic-slice_bitcast_fusion.asked_ref
  25.4 0.1 copy.37
  25.5 0.1 copy.35
  25.6 0.1 min.22
  25.8 0.7 %gather_fusion = s32[256,32]{1,0:T(8,128)S(1)} fusion(s32[96,32]{1,0:T(8,128)S(1)} %copy.36, s32[1024]{0:T(1024)S(1)} %pad_clamp_fusion), kind=kCustom, calls=%fused_computation | custom fusion | bytes 66560 | tf_op jit(solution)/shard_map/jit(_take)/gather | solution.py:448
  26.5 0.1 gather.7
  26.6 0.6 pad.9
  27.2 2.8 %shard_map.141 = (f32[32,8,128]{2,1,0:T(8,128)}, bf16[32,32,128]{2,1,0:T(8,128)(2,1)}) custom-call(s32[32]{0:T(128)} %dynamic-slice_bitcast_fusion.asked_ref, f32[10,96,512]{2,1,0:T(8,128)} %bitcast.20), custom_call_target="tpu_custom_call" | custom-call | tf_op jit(solution)/shard_map/pallas_call | solution.py:258
  30.0 17.6 %shard_map.142 = (s32[4,32,1,128]{3,2,1,0:T(1,128)}, f32[32,8,128]{2,1,0:T(8,128)}, bf16[32,32,128]{2,1,0:T(8,128)(2,1)}, s32[4,32,1,128]{3,2,1,0:T(1,128)}) custom-call(s32[128,1,128]{2,1,0:T(1,128)} %bitcast.27, f32[32,8,128]{2,1,0:T(8,128)} %get-tuple-element.11.refs_1_, bf16[32,32,128]{2,1,0:T(8,128)(2,1)} %get-tuple-element.12.refs_2_), custom_call_target="tpu_custom_call" | custom-call | bytes 50331648 | tf_op jit(solution)/shard_map/pallas_call | solution.py:212
  47.6 0.0 copy-done.11
  47.6 0.0 copy-start
  47.6 0.0 copy-start.2
  47.6 0.0 copy-start.3
  47.6 0.0 copy-start.4
  47.6 0.0 copy-start.5
  47.7 0.0 copy-start.6
  47.7 0.0 copy-start.7
  47.7 0.0 copy-start.8
  47.7 0.0 copy-start.9
  47.7 0.0 copy-start.10
  47.7 11.3 %shard_map.143 = bf16[384,512]{1,0:T(8,128)(2,1)} custom-call(s32[96]{0:T(128)} %copy-done.11, s32[128,1,128]{2,1,0:T(1,128)} %bitcast.29, s32[96,1]{1,0:T(8,128)} %copy.38.rank_ref, bf16[16384,512]{1,0:T(8,128)(2,1)} %table_ref.1), custom_call_target="tpu_custom_call" | custom-call | tf_op jit(solution)/shard_map/pallas_call | solution.py:49
  59.0 0.0 copy-done
  59.1 0.0 copy-done.2
  59.1 0.0 copy-done.3
  59.1 0.0 copy-done.4
  59.1 0.0 copy-done.5
  59.1 0.0 copy-done.6
  59.1 0.0 copy-done.7
  59.1 0.0 copy-done.8
  59.1 0.0 copy-done.9
  59.1 0.0 copy-done.10
  59.1 0.0 copy-start.1
  59.2 1.0 %copy-done.1 = bf16[384,512]{1,0:T(8,128)(2,1)S(1)} copy-done((bf16[384,512]{1,0:T(8,128)(2,1)S(1)}, bf16[384,512]{1,0:T(8,128)(2,1)}, u32[]{:S(2)}) %copy-start.1) | copy-done | bytes 393240
  60.1 10.1 %shard_map.144 = (bf16[96,8,512]{2,1,0:T(8,128)(2,1)}, f32[10,96,512]{2,1,0:T(8,128)}) custom-call(s32[96]{0:T(128)S(1)} %subtract_clamp_fusion.source_ref, s32[96]{0:T(128)S(1)} %get-tuple-element.18.moved_ref, bf16[4,96,512]{2,1,0:T(8,128)(2,1)S(1)} %bitcast.22, f32[10,96,512]{2,1,0:T(8,128)S(1)} %bitcast.21, f32[32,8,128]{2,1,0:T(8,128)S(1)} %copy-done.5, ...), custom_call_target="tpu_custom_call" | custom-call | tf_op jit(solution)/shard_map/pallas_call | solution.py:358
  (12 shorter events, 0.1 us)
Async XLA Ops:
  2.8 44.8 %copy-start.11 = (s32[96]{0:T(128)}, s32[96]{0:T(128)S(1)}, u32[]{:S(2)}) copy-start(s32[96]{0:T(128)S(1)} %get-tuple-element.22.anchor_ref) | copy-start | bytes 1156
  47.6 11.4 %copy-start = (f32[96,10,512]{2,0,1:T(8,128)S(1)}, f32[96,10,512]{2,0,1:T(8,128)}, u32[]{:S(2)}) copy-start(f32[96,10,512]{2,0,1:T(8,128)} %param.17) | copy-start | bytes 5898244
  47.6 11.4 %copy-start.2 = (bf16[3,512,256]{2,1,0:T(8,128)(2,1)S(1)}, bf16[3,512,256]{2,1,0:T(8,128)(2,1)}, u32[]{:S(2)}) copy-start(bf16[3,512,256]{2,1,0:T(8,128)(2,1)} %in_w_ref.1) | copy-start | bytes 2359300
  47.6 11.4 %copy-start.3 = (bf16[256,512]{1,0:T(8,128)(2,1)S(1)}, bf16[256,512]{1,0:T(8,128)(2,1)}, u32[]{:S(2)}) copy-start(bf16[256,512]{1,0:T(8,128)(2,1)} %out_w_ref.1) | copy-start | bytes 786436
  47.6 11.4 %copy-start.4 = (bf16[32,32,128]{2,1,0:T(8,128)(2,1)S(1)}, bf16[32,32,128]{2,1,0:T(8,128)(2,1)}, u32[]{:S(2)}) copy-start(bf16[32,32,128]{2,1,0:T(8,128)(2,1)} %get-tuple-element.15.arrived_low_ref) | copy-start | bytes 786436
  47.6 11.4 %copy-start.5 = (f32[32,8,128]{2,1,0:T(8,128)S(1)}, f32[32,8,128]{2,1,0:T(8,128)}, u32[]{:S(2)}) copy-start(f32[32,8,128]{2,1,0:T(8,128)} %get-tuple-element.14.arrived_ref) | copy-start | bytes 393220
  47.7 11.4 %copy-start.6 = (f32[4,512]{1,0:T(4,128)S(1)}, f32[4,512]{1,0:T(4,128)}, u32[]{:S(2)}) copy-start(f32[4,512]{1,0:T(4,128)} %up_w_ref.1) | copy-start | bytes 24580
  47.7 11.4 %copy-start.7 = (f32[512]{0:T(512)S(1)}, f32[512]{0:T(512)}, u32[]{:S(2)}) copy-start(f32[512]{0:T(512)} %param.19) | copy-start | bytes 6148
  47.7 11.4 %copy-start.8 = (f32[512]{0:T(512)S(1)}, f32[512]{0:T(512)}, u32[]{:S(2)}) copy-start(f32[512]{0:T(512)} %param.21) | copy-start | bytes 6148
  47.7 11.4 %copy-start.9 = (f32[512]{0:T(512)S(1)}, f32[512]{0:T(512)}, u32[]{:S(2)}) copy-start(f32[512]{0:T(512)} %param.25) | copy-start | bytes 6148
  47.7 11.4 %copy-start.10 = (f32[256]{0:T(256)S(1)}, f32[256]{0:T(256)}, u32[]{:S(2)}) copy-start(f32[256]{0:T(256)} %param.23) | copy-start | bytes 3076
  59.1 1.0 %copy-start.1 = (bf16[384,512]{1,0:T(8,128)(2,1)S(1)}, bf16[384,512]{1,0:T(8,128)(2,1)}, u32[]{:S(2)}) copy-start(bf16[384,512]{1,0:T(8,128)(2,1)} %shard_map.143) | copy-start | bytes 1179652

commit v24 on v23

--- a/solution.py
+++ b/solution.py
@@ -247,7 +247,7 @@
                     low_scratch[peer, pl.ds((r - 2) * pieces + k, 1), :] = piece
         return carry
 
-    lax.fori_loop(0, peers, one, 0, unroll=8)
+    lax.fori_loop(0, peers, one, 0)
     low_ref[...] = low_scratch[...].astype(low_ref.dtype)
 
 

time: 70.6 us -> 70.9 us (level)
  no operation moved by 1% of the time
where the time goes in v24:
time: 70.9 us; the launch traced here: 70.5 us
  Pallas kernels  60.2 us (85%)
  local copies, waits for them, and re-layouts  6.8 us (10%)
  other arithmetic  2.57 us (4%)
  between operations  0.95 us (1%)
    pallas_call x2, Pallas kernels, exchange(): pl.pallas_call(kernel, out_shape=shapes + mids, in_specs=[pl.BlockSpec(me...  35.7 us
    pallas_call x1, Pallas kernels, embed_codes(): pl.pallas_call(embed_kernel, in_specs=[pl.BlockSpec(memory_space=pltpu.SM...  11.3 us
    pallas_call x1, Pallas kernels, decode(): pl.pallas_call(decode_kernel, grid_spec=pltpu.PrefetchScalarGridSpec(num_...  10.1 us
    pallas_call x1, Pallas kernels, pack_leaving(): pl.pallas_call(pack_kernel, in_specs=[pl.BlockSpec(memory_space=pltpu.SME...  3.04 us
    unnamed x26, local copies, waits for them, and re-layouts  2.76 us

profile of v24, /device:TPU:1, one launch (start us, length us, event | category | flops | bytes accessed | tf_op | source)
XLA Modules:
  0.0 70.5 jit_solution(12589717573567102782)
XLA Ops:
  0.6 0.7 fusion.3
  1.3 0.7 fusion.4
  2.0 0.1 select_reduce_fusion.1
  2.1 0.7 fusion.2
  2.8 0.2 convert_reduce_fusion
  3.0 0.1 select_reduce_fusion
  3.1 0.7 %copy.38.rank_ref = s32[96,1]{1,0:T(8,128)} copy(s32[96,1]{0,1:T(1,128)S(1)} %bitcast.36) | data formatting | bytes 768 | tf_op jit(solution)/shard_map/reshape | solution.py:64
  3.8 0.8 %copy.36 = s32[96,32]{1,0:T(8,128)S(1)} copy(s32[96,32]{0,1:T(8,128)} %param.13) | data formatting | bytes 24576 | tf_op args[0]
  4.6 0.1 sub.33
  4.8 0.1 copy.33
  4.9 0.1 pad_add_fusion
  5.0 0.6 pad.8
  5.6 18.2 %shard_map.140 = (s32[4,32,1,128]{3,2,1,0:T(1,128)}, s32[4,32,1,128]{3,2,1,0:T(1,128)}) custom-call(s32[128,1,128]{2,1,0:T(1,128)} %bitcast.28), custom_call_target="tpu_custom_call" | custom-call | bytes 50331648 | tf_op jit(solution)/shard_map/pallas_call | solution.py:212
  23.8 0.9 %copy.39 = s32[128,1,3]{0,2,1:T(4,128)S(1)} copy(s32[128,1,3]{2,0,1:T(8,128)} %bitcast.30) | data formatting | bytes 3072
  24.7 0.6 dynamic-slice_bitcast_fusion.asked_ref
  25.4 0.1 copy.37
  25.5 0.1 copy.35
  25.6 0.1 min.22
  25.8 0.7 %gather_fusion = s32[256,32]{1,0:T(8,128)S(1)} fusion(s32[96,32]{1,0:T(8,128)S(1)} %copy.36, s32[1024]{0:T(1024)S(1)} %pad_clamp_fusion), kind=kCustom, calls=%fused_computation | custom fusion | bytes 66560 | tf_op jit(solution)/shard_map/jit(_take)/gather | solution.py:448
  26.5 0.1 gather.7
  26.6 0.6 pad.9
  27.2 3.0 %shard_map.141 = (f32[32,8,128]{2,1,0:T(8,128)}, bf16[32,32,128]{2,1,0:T(8,128)(2,1)}) custom-call(s32[32]{0:T(128)} %dynamic-slice_bitcast_fusion.asked_ref, f32[10,96,512]{2,1,0:T(8,128)} %bitcast.20), custom_call_target="tpu_custom_call" | custom-call | tf_op jit(solution)/shard_map/pallas_call | solution.py:258
  30.3 17.6 %shard_map.142 = (s32[4,32,1,128]{3,2,1,0:T(1,128)}, f32[32,8,128]{2,1,0:T(8,128)}, bf16[32,32,128]{2,1,0:T(8,128)(2,1)}, s32[4,32,1,128]{3,2,1,0:T(1,128)}) custom-call(s32[128,1,128]{2,1,0:T(1,128)} %bitcast.27, f32[32,8,128]{2,1,0:T(8,128)} %get-tuple-element.11.refs_1_, bf16[32,32,128]{2,1,0:T(8,128)(2,1)} %get-tuple-element.12.refs_2_), custom_call_target="tpu_custom_call" | custom-call | bytes 50331648 | tf_op jit(solution)/shard_map/pallas_call | solution.py:212
  47.9 0.0 copy-done.11
  47.9 0.0 copy-start
  47.9 0.0 copy-start.2
  47.9 0.0 copy-start.3
  47.9 0.0 copy-start.4
  47.9 0.0 copy-start.5
  47.9 0.0 copy-start.6
  47.9 0.0 copy-start.7
  47.9 0.0 copy-start.8
  48.0 0.0 copy-start.9
  48.0 0.0 copy-start.10
  48.0 11.3 %shard_map.143 = bf16[384,512]{1,0:T(8,128)(2,1)} custom-call(s32[96]{0:T(128)} %copy-done.11, s32[128,1,128]{2,1,0:T(1,128)} %bitcast.29, s32[96,1]{1,0:T(8,128)} %copy.38.rank_ref, bf16[16384,512]{1,0:T(8,128)(2,1)} %table_ref.1), custom_call_target="tpu_custom_call" | custom-call | tf_op jit(solution)/shard_map/pallas_call | solution.py:49
  59.3 0.0 copy-done
  59.3 0.0 copy-done.2
  59.3 0.0 copy-done.3
  59.3 0.0 copy-done.4
  59.3 0.0 copy-done.5
  59.4 0.0 copy-done.6
  59.4 0.0 copy-done.7
  59.4 0.0 copy-done.8
  59.4 0.0 copy-done.9
  59.4 0.0 copy-done.10
  59.4 0.0 copy-start.1
  59.4 1.0 %copy-done.1 = bf16[384,512]{1,0:T(8,128)(2,1)S(1)} copy-done((bf16[384,512]{1,0:T(8,128)(2,1)S(1)}, bf16[384,512]{1,0:T(8,128)(2,1)}, u32[]{:S(2)}) %copy-start.1) | copy-done | bytes 393240
  60.4 10.1 %shard_map.144 = (bf16[96,8,512]{2,1,0:T(8,128)(2,1)}, f32[10,96,512]{2,1,0:T(8,128)}) custom-call(s32[96]{0:T(128)S(1)} %subtract_clamp_fusion.source_ref, s32[96]{0:T(128)S(1)} %get-tuple-element.18.moved_ref, bf16[4,96,512]{2,1,0:T(8,128)(2,1)S(1)} %bitcast.22, f32[10,96,512]{2,1,0:T(8,128)S(1)} %bitcast.21, f32[32,8,128]{2,1,0:T(8,128)S(1)} %copy-done.5, ...), custom_call_target="tpu_custom_call" | custom-call | tf_op jit(solution)/shard_map/pallas_call | solution.py:358
  (12 shorter events, 0.1 us)
Async XLA Ops:
  2.8 45.1 %copy-start.11 = (s32[96]{0:T(128)}, s32[96]{0:T(128)S(1)}, u32[]{:S(2)}) copy-start(s32[96]{0:T(128)S(1)} %get-tuple-element.22.anchor_ref) | copy-start | bytes 1156
  47.9 11.4 %copy-start = (f32[96,10,512]{2,0,1:T(8,128)S(1)}, f32[96,10,512]{2,0,1:T(8,128)}, u32[]{:S(2)}) copy-start(f32[96,10,512]{2,0,1:T(8,128)} %param.17) | copy-start | bytes 5898244
  47.9 11.4 %copy-start.2 = (bf16[3,512,256]{2,1,0:T(8,128)(2,1)S(1)}, bf16[3,512,256]{2,1,0:T(8,128)(2,1)}, u32[]{:S(2)}) copy-start(bf16[3,512,256]{2,1,0:T(8,128)(2,1)} %in_w_ref.1) | copy-start | bytes 2359300
  47.9 11.4 %copy-start.3 = (bf16[256,512]{1,0:T(8,128)(2,1)S(1)}, bf16[256,512]{1,0:T(8,128)(2,1)}, u32[]{:S(2)}) copy-start(bf16[256,512]{1,0:T(8,128)(2,1)} %out_w_ref.1) | copy-start | bytes 786436
  47.9 11.4 %copy-start.4 = (bf16[32,32,128]{2,1,0:T(8,128)(2,1)S(1)}, bf16[32,32,128]{2,1,0:T(8,128)(2,1)}, u32[]{:S(2)}) copy-start(bf16[32,32,128]{2,1,0:T(8,128)(2,1)} %get-tuple-element.15.arrived_low_ref) | copy-start | bytes 786436
  47.9 11.4 %copy-start.5 = (f32[32,8,128]{2,1,0:T(8,128)S(1)}, f32[32,8,128]{2,1,0:T(8,128)}, u32[]{:S(2)}) copy-start(f32[32,8,128]{2,1,0:T(8,128)} %get-tuple-element.14.arrived_ref) | copy-start | bytes 393220
  47.9 11.4 %copy-start.6 = (f32[4,512]{1,0:T(4,128)S(1)}, f32[4,512]{1,0:T(4,128)}, u32[]{:S(2)}) copy-start(f32[4,512]{1,0:T(4,128)} %up_w_ref.1) | copy-start | bytes 24580
  47.9 11.4 %copy-start.7 = (f32[512]{0:T(512)S(1)}, f32[512]{0:T(512)}, u32[]{:S(2)}) copy-start(f32[512]{0:T(512)} %param.19) | copy-start | bytes 6148
  47.9 11.4 %copy-start.8 = (f32[512]{0:T(512)S(1)}, f32[512]{0:T(512)}, u32[]{:S(2)}) copy-start(f32[512]{0:T(512)} %param.21) | copy-start | bytes 6148
  48.0 11.4 %copy-start.9 = (f32[512]{0:T(512)S(1)}, f32[512]{0:T(512)}, u32[]{:S(2)}) copy-start(f32[512]{0:T(512)} %param.25) | copy-start | bytes 6148
  48.0 11.4 %copy-start.10 = (f32[256]{0:T(256)S(1)}, f32[256]{0:T(256)}, u32[]{:S(2)}) copy-start(f32[256]{0:T(256)} %param.23) | copy-start | bytes 3076
  59.4 1.0 %copy-start.1 = (bf16[384,512]{1,0:T(8,128)(2,1)S(1)}, bf16[384,512]{1,0:T(8,128)(2,1)}, u32[]{:S(2)}) copy-start(bf16[384,512]{1,0:T(8,128)(2,1)} %shard_map.143) | copy-start | bytes 1179652
